TPU v7x, 32 devices: a whole 2x2x4 slice. The times are simulated.
32 devices in a mesh: tm: 8 (over z, x), chan: 4 (over y, core).
Axes of the slice: x: 2, y: 2, z: 4, core: 2. Of those that a mesh axis runs over, the one named last changes fastest.
Arguments:
- inputs: bfloat16 [2048, 2048], P('tm'), may hold values from -6 to 6
- cotangent: bfloat16 [2048, 2048], P('tm'), may hold values from -6 to 6
- in_proj: bfloat16 [2048, 4096], P(None, 'chan'), may hold values from -0.125 to 0.125
- out_proj: bfloat16 [4096, 2048], P('chan'), may hold values from -0.09375 to 0.09375
- decays: float32 [4096], P('chan'), may hold values from 0 to 1, as said below
- input_scale: float32 [4096], P('chan'), may hold values from 0 to 1.5, as said below
- retain: float32 [2048], P('tm'), may hold values from 0.5 to 1, as said below
Outputs:
- in_proj_grad: float32 [2048, 4096], P('tm', 'chan')
- out_proj_grad: float32 [2048, 4096], P('tm', 'chan')
- decay_grad: float32 [4096], P('chan')
- input_grad: bfloat16 [2048, 2048], P('tm', 'chan')
Inputs may be any that keep to these rules, and one draw needn't show every extreme that they name: `decays`: each decay lies strictly between 0 and 1. `input_scale`: positive. `retain`: most steps have factor 1.
All inputs are finite; a program needn't handle non-finite values.
Results may differ from a plain program's by a relative error of at most 0.0049.
Values sent between devices are 32-bit elements; how exact they have to be, the bound alone decides.
No kernel may reach another device: no remote copies, remote signals or barrier semaphores. Data moves between devices by JAX's collectives and lax.ppermute only.
A program may use at most 128 MiB of HBM per device.

v0:
```python
import math

import jax
import jax.numpy as jnp
from jax import lax
from jax.sharding import PartitionSpec as P


def prefix(x, axis, combine, identity, reverse):
    peers, mine = (lax.axis_size(axis), lax.axis_index(axis))
    everything = jax.tree.map(lambda part: lax.all_gather(part, axis), x)
    start = jax.tree.map(
        lambda part, zero: jnp.broadcast_to(jnp.asarray(zero, part.dtype), part.shape), x, identity
    )

    def lap(k, before):
        at = peers - 1 - k if reverse else k
        reached = at > mine if reverse else at < mine
        new = combine(before, jax.tree.map(lambda part: part[at], everything))
        return jax.tree.map(lambda a, b: jnp.where(reached, a, b), new, before)

    return lax.fori_loop(0, peers, lap, start)


def compose(earlier, latter):
    return (earlier[0] * latter[0], latter[0] * earlier[1] + latter[1])


def per_device(inputs, cotangent, in_proj, out_proj, decays, input_scale, retain):
    tok_count = inputs.shape[0]
    devices = lax.axis_size("tm")
    scaling = 1.0 / math.sqrt(tok_count * devices)
    driving = jnp.dot(inputs, in_proj, preferred_element_type=jnp.float32) * input_scale
    factors = retain[:, None] * decays[None, :]
    cum_rate, local_state = lax.associative_scan(compose, (factors, driving), axis=0)
    state_cot = (
        lax.dot_general(
            cotangent, out_proj, (((1,), (1,)), ((), ())), preferred_element_type=jnp.float32
        )
        * scaling
    )
    cum_back, local_mu = lax.associative_scan(
        compose, (factors, factors * state_cot), axis=0, reverse=True
    )
    identity = (jnp.ones_like(decays), jnp.zeros_like(decays))
    entering = prefix((cum_rate[-1], local_state[-1]), "tm", compose, identity, False)[1]
    leaving = prefix((cum_back[0], local_mu[0]), "tm", compose, identity, True)[1]
    states = local_state + cum_rate * entering[None, :]
    previous = jnp.concatenate([entering[None, :], states[:-1]], axis=0)
    carry_mu = local_mu + cum_back * leaving[None, :]
    following = jnp.concatenate([carry_mu[1:], leaving[None, :]], axis=0)
    adjoint = state_cot + following
    decay_term = jnp.sum(retain[:, None] * adjoint * previous, axis=0)
    decay_grad = lax.psum(decay_term, "tm")
    scaled = (input_scale * adjoint).astype(jnp.bfloat16)
    state_low = states.astype(jnp.bfloat16)
    partial_in = lax.dot_general(
        scaled, in_proj, (((1,), (1,)), ((), ())), preferred_element_type=jnp.float32
    )
    input_grad = lax.psum_scatter(partial_in, "chan", scatter_dimension=1, tiled=True).astype(
        jnp.bfloat16
    )
    columns = inputs
    in_proj_grad = lax.psum_scatter(
        lax.dot_general(
            columns, scaled, (((0,), (0,)), ((), ())), preferred_element_type=jnp.float32
        ),
        "tm",
        scatter_dimension=0,
        tiled=True,
    )
    columns = cotangent
    out_proj_grad = lax.psum_scatter(
        lax.dot_general(
            columns, state_low, (((0,), (0,)), ((), ())), preferred_element_type=jnp.float32
        )
        * scaling,
        "tm",
        scatter_dimension=0,
        tiled=True,
    )
    return (in_proj_grad, out_proj_grad, decay_grad, input_grad)


def solution(mesh):
    return jax.shard_map(
        per_device,
        mesh=mesh,
        in_specs=(
            P("tm", None),
            P("tm", None),
            P(None, "chan"),
            P("chan", None),
            P("chan"),
            P("chan"),
            P("tm"),
        ),
        out_specs=(P("tm", "chan"), P("tm", "chan"), P("chan"), P("tm", "chan")),
        check_vma=False,
    )
```

profile of v0, /device:TPU:0, one launch (start us, length us, event | category | flops | bytes accessed | tf_op | source)
XLA Modules:
  0.0 762.6 jit_solution(17143284975590019371)
XLA Ops:
  8.4 4.5 fusion.4
  18.7 4.7 slice.500
  23.4 4.7 slice.507
  28.2 4.8 slice.502
  33.0 4.7 slice.504
  37.7 2.7 multiply_add_fusion.2
  127.5 4.8 slice.498
  132.4 4.8 slice.560
  140.1 2.6 fusion.2
  145.7 4.6 pad.211
  158.0 4.6 pad.227
  166.2 4.8 convolution_multiply_fusion
  171.1 3.3 slice.581
  174.3 3.3 slice.582
  241.3 3.3 slice.635
  244.7 8.9 %rev.9 = f32[256,1024]{1,0:T(8,128)} reverse(f32[256,1024]{1,0:T(8,128)} %add.431), dimensions={0} | reverse | bytes 2097152 | tf_op jit(solution)/shard_map/rev | solution.py:42
  253.6 5.3 rev.8
  258.9 32.5 %all-gather.1 = f32[8,1,1024]{2,1,0:T(1,128)S(1)} all-gather(f32[1,1,1024]{2,1,0:T(1,128)} %add_bitcast_fusion.2), channel_id=1, replica_groups=mesh['tm'=8,'chan'=4] {'tm'}, dimensions={0}, use_global_device_ids=true | all-gather | bytes 36864 | tf_op jit(solution)/shard_map/all_gather | solution.py:11
  291.4 30.8 %all-gather = f32[8,1,1024]{2,1,0:T(1,128)S(1)} all-gather(f32[1,1,1024]{2,1,0:T(1,128)} %add_bitcast_fusion.3), channel_id=1, replica_groups=mesh['tm'=8,'chan'=4] {'tm'}, dimensions={0}, use_global_device_ids=true | all-gather | bytes 36864 | tf_op jit(solution)/shard_map/all_gather | solution.py:11
  325.3 2.7 pad.243
  335.1 30.4 %all-gather.3 = f32[8,1,1024]{2,1,0:T(1,128)S(1)} all-gather(f32[1,1,1024]{2,1,0:T(1,128)S(1)} %add_bitcast_fusion), channel_id=1, replica_groups=mesh['tm'=8,'chan'=4] {'tm'}, dimensions={0}, use_global_device_ids=true | all-gather | bytes 36864 | tf_op jit(solution)/shard_map/all_gather | solution.py:11
  365.5 4.6 pad.259
  372.0 4.6 pad.258
  377.4 30.4 %all-gather.2 = f32[8,1,1024]{2,1,0:T(1,128)S(1)} all-gather(f32[1,1,1024]{2,1,0:T(1,128)S(1)} %add_bitcast_fusion.1), channel_id=1, replica_groups=mesh['tm'=8,'chan'=4] {'tm'}, dimensions={0}, use_global_device_ids=true | all-gather | bytes 36864 | tf_op jit(solution)/shard_map/all_gather | solution.py:11
  413.0 2.6 fusion.27
  415.7 5.9 convolution_bitcast_fusion
  421.6 4.7 multiply_bitcast_fusion
  426.4 21.6 %psum.7 = f32[1024]{0:T(1024)} all-reduce(f32[1024]{0:T(1024)S(1)} %get-tuple-element.300), channel_id=1, replica_groups=mesh['tm'=8,'chan'=4] {'tm'}, use_global_device_ids=true, to_apply=%region_7.8 | all-reduce | flops 1024 | bytes 8192 | tf_op jit(solution)/shard_map/psum | solution.py:54
  449.8 151.6 %reduce-scatter.4.cloned.1.call-done = f32[256,1024]{0,1:T(8,128)} async-done(((f32[2048,1024]{0,1:T(8,128)}), f32[256,1024]{0,1:T(8,128)}) %reduce-scatter.4.cloned.1.call-update) | async-done | bytes 1048592 | tf_op jit(solution)/shard_map/reduce_scatter | solution.py:64
  601.4 2.5 copy.13
  604.0 149.6 %reduce-scatter.6.cloned.1.call-done = f32[256,1024]{0,1:T(8,128)} async-done(((f32[2048,1024]{0,1:T(8,128)}), f32[256,1024]{0,1:T(8,128)}) %reduce-scatter.6.cloned.1.call-update) | async-done | bytes 1048592 | tf_op jit(solution)/shard_map/reduce_scatter | solution.py:73
  753.5 2.5 copy.14
  (375 shorter events, 194.4 us)
Async XLA Ops:
  7.2 440.9 %reduce-scatter.8.cloned.1.call-start = ((), (), s32[]{:S(2)}) async-start(), calls=%async_computation.5 | async-start | bytes 2621440 | tf_op jit(solution)/shard_map/reduce_scatter | solution.py:60
  100.4 17.1 %copy-start.16 = (f32[15,1024]{1,0:T(8,128)S(1)}, f32[15,1024]{1,0:T(8,128)}, u32[]{:S(2)}) copy-start(f32[15,1024]{1,0:T(8,128)} %slice.520) | copy-start | bytes 184324
  100.4 17.1 %copy-start.17 = (f32[15,1024]{1,0:T(8,128)S(1)}, f32[15,1024]{1,0:T(8,128)}, u32[]{:S(2)}) copy-start(f32[15,1024]{1,0:T(8,128)} %slice.553) | copy-start | bytes 184324
  100.4 18.7 %copy-start.13 = (f32[31,1024]{1,0:T(8,128)S(1)}, f32[31,1024]{1,0:T(8,128)}, u32[]{:S(2)}) copy-start(f32[31,1024]{1,0:T(8,128)} %slice.555) | copy-start | bytes 380932
  110.7 8.6 %copy-start.31 = (f32[1,1024]{1,0:T(1,128)S(1)}, f32[1,1024]{1,0:T(1,128)}, u32[]{:S(2)}) copy-start(f32[1,1024]{1,0:T(1,128)} %slice.656) | copy-start | bytes 12292
  132.4 10.3 %copy-start.28 = (f32[1,1024]{1,0:T(1,128)S(1)}, f32[1,1024]{1,0:T(1,128)}, u32[]{:S(2)}) copy-start(f32[1,1024]{1,0:T(1,128)} %slice.654) | copy-start | bytes 12292
  142.7 11.3 %copy-start.34 = (f32[1,1024]{1,0:T(1,128)S(1)}, f32[1,1024]{1,0:T(1,128)}, u32[]{:S(2)}) copy-start(f32[1,1024]{1,0:T(1,128)} %get-tuple-element.303) | copy-start | bytes 12292
  152.6 13.6 %copy-start.41 = (f32[1024]{0:T(1024)S(1)}, f32[1024]{0:T(1024)}, u32[]{:S(2)}) copy-start(f32[1024]{0:T(1024)} %param.16) | copy-start | bytes 12292
  166.2 11.3 %copy-start.1 = (f32[128,1024]{1,0:T(8,128)S(1)}, f32[128,1024]{1,0:T(8,128)}, u32[]{:S(2)}) copy-start(f32[128,1024]{1,0:T(8,128)} %slice.499) | copy-start | bytes 1572868
  166.2 11.3 %copy-start.2 = (f32[128,1024]{1,0:T(8,128)S(1)}, f32[128,1024]{1,0:T(8,128)}, u32[]{:S(2)}) copy-start(f32[128,1024]{1,0:T(8,128)} %slice.506) | copy-start | bytes 1572868
  187.3 66.3 %copy-start.5 = (f32[256,1024]{1,0:T(8,128)S(1)}, f32[256,1024]{1,0:T(8,128)}, u32[]{:S(2)}) copy-start(f32[256,1024]{1,0:T(8,128)} %add.423) | copy-start | bytes 3145732
  233.6 89.2 %copy-start.22 = (f32[2,1024]{1,0:T(2,128)S(1)}, f32[2,1024]{1,0:T(2,128)}, u32[]{:S(2)}) copy-start(f32[2,1024]{1,0:T(2,128)} %get-tuple-element.376) | copy-start | bytes 24580
  233.6 90.1 %copy-start.20 = (f32[3,1024]{1,0:T(4,128)S(1)}, f32[3,1024]{1,0:T(4,128)}, u32[]{:S(2)}) copy-start(f32[3,1024]{1,0:T(4,128)} %slice.608) | copy-start | bytes 36868
  233.6 90.1 %copy-start.21 = (f32[3,1024]{1,0:T(4,128)S(1)}, f32[3,1024]{1,0:T(4,128)}, u32[]{:S(2)}) copy-start(f32[3,1024]{1,0:T(4,128)} %slice.625) | copy-start | bytes 36868
  233.6 90.1 %copy-start.40 = (f32[1,1024]{1,0:T(1,128)S(1)}, f32[1,1024]{1,0:T(1,128)}, u32[]{:S(2)}) copy-start(f32[1,1024]{1,0:T(1,128)} %slice.739) | copy-start | bytes 12292
  233.6 90.2 %copy-start.39 = (f32[1,1024]{1,0:T(1,128)S(1)}, f32[1,1024]{1,0:T(1,128)}, u32[]{:S(2)}) copy-start(f32[1,1024]{1,0:T(1,128)} %slice.713) | copy-start | bytes 12292
  235.3 88.5 %copy-start.18 = (f32[7,1024]{1,0:T(8,128)S(1)}, f32[7,1024]{1,0:T(8,128)}, u32[]{:S(2)}) copy-start(f32[7,1024]{1,0:T(8,128)} %slice.602) | copy-start | bytes 86020
  235.3 88.6 %copy-start.19 = (f32[7,1024]{1,0:T(8,128)S(1)}, f32[7,1024]{1,0:T(8,128)}, u32[]{:S(2)}) copy-start(f32[7,1024]{1,0:T(8,128)} %slice.627) | copy-start | bytes 86020
  235.3 88.6 %copy-start.38 = (f32[1,1024]{1,0:T(1,128)S(1)}, f32[1,1024]{1,0:T(1,128)}, u32[]{:S(2)}) copy-start(f32[1,1024]{1,0:T(1,128)} %slice.738) | copy-start | bytes 12292
  239.8 84.2 %copy-start.37 = (f32[1,1024]{1,0:T(1,128)S(1)}, f32[1,1024]{1,0:T(1,128)}, u32[]{:S(2)}) copy-start(f32[1,1024]{1,0:T(1,128)} %slice.712) | copy-start | bytes 12292
  241.3 82.8 %copy-start.14 = (f32[15,1024]{1,0:T(8,128)S(1)}, f32[15,1024]{1,0:T(8,128)}, u32[]{:S(2)}) copy-start(f32[15,1024]{1,0:T(8,128)} %slice.596) | copy-start | bytes 184324
  241.3 82.8 %copy-start.15 = (f32[15,1024]{1,0:T(8,128)S(1)}, f32[15,1024]{1,0:T(8,128)}, u32[]{:S(2)}) copy-start(f32[15,1024]{1,0:T(8,128)} %slice.629) | copy-start | bytes 184324
  241.3 82.8 %copy-start.36 = (f32[1,1024]{1,0:T(1,128)S(1)}, f32[1,1024]{1,0:T(1,128)}, u32[]{:S(2)}) copy-start(f32[1,1024]{1,0:T(1,128)} %slice.737) | copy-start | bytes 12292
  244.6 79.6 %copy-start.35 = (f32[1,1024]{1,0:T(1,128)S(1)}, f32[1,1024]{1,0:T(1,128)}, u32[]{:S(2)}) copy-start(f32[1,1024]{1,0:T(1,128)} %slice.711) | copy-start | bytes 12292
  244.7 79.7 %copy-start.12 = (f32[31,1024]{1,0:T(8,128)S(1)}, f32[31,1024]{1,0:T(8,128)}, u32[]{:S(2)}) copy-start(f32[31,1024]{1,0:T(8,128)} %slice.631) | copy-start | bytes 380932
  253.6 70.9 %copy-start.27 = (f32[1,1024]{1,0:T(1,128)S(1)}, f32[1,1024]{1,0:T(1,128)}, u32[]{:S(2)}) copy-start(f32[1,1024]{1,0:T(1,128)} %slice.736) | copy-start | bytes 12292
  258.9 65.7 %copy-start.26 = (f32[1,1024]{1,0:T(1,128)S(1)}, f32[1,1024]{1,0:T(1,128)}, u32[]{:S(2)}) copy-start(f32[1,1024]{1,0:T(1,128)} %slice.710) | copy-start | bytes 12292
  329.0 41.1 %copy-start.33 = (f32[1,1024]{1,0:T(1,128)S(1)}, f32[1,1024]{1,0:T(1,128)}, u32[]{:S(2)}) copy-start(f32[1,1024]{1,0:T(1,128)} %get-tuple-element.302) | copy-start | bytes 12292
  331.3 77.0 %copy-start.3 = (f32[256,1024]{1,0:T(8,128)S(1)}, f32[256,1024]{1,0:T(8,128)}, u32[]{:S(2)}) copy-start(f32[256,1024]{1,0:T(8,128)} %pad.243) | copy-start | bytes 3145732
  334.3 74.0 %copy-start.4 = (f32[256,1024]{1,0:T(8,128)}, f32[256,1024]{1,0:T(8,128)S(1)}, u32[]{:S(2)}) copy-start(f32[256,1024]{1,0:T(8,128)S(1)} %pad.242) | copy-start | bytes 3145732
  415.7 185.8 %reduce-scatter.4.cloned.1.call-start = ((), (), s32[]{:S(2)}) async-start(), calls=%async_computation.3 | async-start | bytes 9437184 | tf_op jit(solution)/shard_map/reduce_scatter | solution.py:64
  421.6 331.9 %reduce-scatter.6.cloned.1.call-start = ((), (), s32[]{:S(2)}) async-start(), calls=%async_computation.4 | async-start | bytes 9437184 | tf_op jit(solution)/shard_map/reduce_scatter | solution.py:73
  (16 other events, 44.8 us)
Sparse Core Ops, SparseCore 0:
  415.8 32.0 reduce-scatter.7
  452.0 149.4 reduce-scatter.3
  605.1 148.4 reduce-scatter.5
where the time goes:
time: 771 us; the launch traced here: 763 us
  waiting for transfers between devices  301 us (39%)
  local copies, waits for them, and re-layouts  213 us (28%)
  blocking collectives  146 us (19%)
  other arithmetic  64.4 us (8%)
  matrix products  22.5 us (3%)
  between operations  14.9 us (2%)
    reduce_scatter x1, waiting for transfers between devices, per_device(): lax.psum_scatter(lax.dot_general(columns, scaled, (((0,), (0,)), ((), ())...  152 us
    reduce_scatter x1, waiting for transfers between devices, per_device(): lax.psum_scatter(lax.dot_general(columns, state_low, (((0,), (0,)), ((),...  150 us
    all_gather x4, blocking collectives, prefix(): everything = jax.tree.map(lambda part: lax.all_gather(part, axis), x)  124 us
    slice x57, local copies, waits for them, and re-layouts, per_device(): lax.associative_scan(compose, (factors, factors * state_cot), axis=0, rev...  93.2 us
    slice x51, local copies, waits for them, and re-layouts, per_device(): lax.associative_scan(compose, (factors, driving), axis=0)  62.4 us
    add x27, other arithmetic, compose(): return (earlier[0] * latter[0], latter[0] * earlier[1] + latter[1])  29.3 us
    psum x1, blocking collectives, per_device(): decay_grad = lax.psum(decay_term, 'tm')  21.6 us
    pad x28, local copies, waits for them, and re-layouts, per_device(): lax.associative_scan(compose, (factors, factors * state_cot), axis=0, rev...  19.6 us
  transfers between devices with their start and end apart: 3, of which 2 were waited for; matrix products, arithmetic and copies ran while one was open for 2% of the time, Pallas kernels for 0%

commit v1 on v0

v1 whole, which is shorter than its diff:
```python
import functools
import math

import jax
import jax.numpy as jnp
from jax import lax
from jax.experimental import pallas as pl
from jax.experimental.pallas import tpu as pltpu
from jax.sharding import PartitionSpec as P

F32 = jnp.float32
BF16 = jnp.bfloat16
SEG = 8
VMEM_LIMIT = 48 * 1024 * 1024


def swap(x, axis, bit):
    n = lax.axis_size(axis)
    return lax.ppermute(x, axis, [(k, k ^ bit) for k in range(n)])


def nn(a, b):
    return lax.dot_general(a, b, (((1,), (0,)), ((), ())), preferred_element_type=F32)


def nt(a, b):
    return lax.dot_general(a, b, (((1,), (1,)), ((), ())), preferred_element_type=F32)


def tn(a, b):
    return lax.dot_general(a, b, (((0,), (0,)), ((), ())), preferred_element_type=F32)


def tiles(row, width):
    return [row[:, 128 * l : 128 * (l + 1)] for l in range(width // 128)]


def put(dst, value):
    for l in range(dst.shape[0]):
        dst[l] = value[:, 128 * l : 128 * (l + 1)]


def joined(src):
    return jnp.concatenate([src[l] for l in range(src.shape[0])], axis=1)


def scan_ends(src, retain_ref, decays, reverse):
    count, steps = src.shape[0], src.shape[1] // SEG

    def lap(k, carry):
        j = steps - 1 - k if reverse else k
        rows = pl.ds(j, SEG, stride=steps)
        kept = retain_ref[rows, :]
        out = []
        for l in range(count):
            end, rate = carry[l]
            factor = kept * decays[l]
            value = src[l, rows, :]
            end = factor * (value + end) if reverse else factor * end + value
            out.append((end, factor * rate))
        return tuple(out)

    start = tuple((jnp.zeros((SEG, 128), F32), jnp.ones((SEG, 128), F32)) for _ in range(count))
    ends = lax.fori_loop(0, steps, lap, start, unroll=4)
    return jnp.concatenate([e[0] for e in ends], axis=1), jnp.concatenate([e[1] for e in ends], axis=1)


def seg_starts(end, rate, entering, reverse):
    now = entering
    starts = [None] * SEG
    for k in range(SEG):
        s = SEG - 1 - k if reverse else k
        starts[s] = now
        now = end[s : s + 1] + rate[s : s + 1] * now
    return jnp.concatenate(starts, axis=0), now


def summary_kernel(x_ref, c_ref, w_ref, v_ref, scale_ref, decay_ref, retain_ref, out_ref, drive, scot, *, scaling):
    width = decay_ref.shape[1]
    decays = tiles(jnp.broadcast_to(decay_ref[...], (SEG, width)), width)
    put(drive, nn(x_ref[...], w_ref[...]) * scale_ref[...])
    put(scot, nt(c_ref[...], v_ref[...]) * scaling)
    zero = jnp.zeros((1, width), F32)
    end, rate = scan_ends(drive, retain_ref, decays, False)
    _, forward = seg_starts(end, rate, zero, False)
    back, _ = scan_ends(scot, retain_ref, decays, True)
    _, backward = seg_starts(back, rate, zero, True)
    total = rate[0:1]
    for s in range(1, SEG):
        total = total * rate[s : s + 1]
    out_ref[...] = jnp.concatenate([total, forward, backward, zero], axis=0)


def summary(x, c, in_proj, out_proj, scale, decays, retain_wide, scaling, chunk):
    rows, depth = x.shape
    channels = in_proj.shape[1]
    return pl.pallas_call(
        functools.partial(summary_kernel, scaling=scaling),
        out_shape=jax.ShapeDtypeStruct((4, channels), F32),
        grid=(channels // chunk,),
        in_specs=[
            pl.BlockSpec((rows, depth), lambda j: (0, 0)),
            pl.BlockSpec((rows, depth), lambda j: (0, 0)),
            pl.BlockSpec((depth, chunk), lambda j: (0, j)),
            pl.BlockSpec((chunk, depth), lambda j: (j, 0)),
            pl.BlockSpec((1, chunk), lambda j: (0, j)),
            pl.BlockSpec((1, chunk), lambda j: (0, j)),
            pl.BlockSpec((rows, 128), lambda j: (0, 0)),
        ],
        out_specs=pl.BlockSpec((4, chunk), lambda j: (0, j)),
        scratch_shapes=[pltpu.VMEM((chunk // 128, rows, 128), F32)] * 2,
        compiler_params=pltpu.CompilerParams(vmem_limit_bytes=VMEM_LIMIT),
        cost_estimate=pl.CostEstimate(flops=4 * rows * depth * channels, transcendentals=0, bytes_accessed=4 * depth * channels),
        name="summary",
    )(x, c, in_proj, out_proj, scale, decays, retain_wide)


def carries_kernel(sum_ref, fwd_ref, bwd_ref):
    blocks = sum_ref.shape[0]
    now = jnp.zeros_like(fwd_ref[0:1, :])
    for b in range(blocks):
        fwd_ref[b : b + 1, :] = now
        row = sum_ref[b]
        now = row[1:2] + row[0:1] * now
    now = jnp.zeros_like(now)
    for b in range(blocks - 1, -1, -1):
        bwd_ref[b : b + 1, :] = now
        row = sum_ref[b]
        now = row[2:3] + row[0:1] * now


def carries(table):
    shape = jax.ShapeDtypeStruct((table.shape[0], table.shape[2]), F32)
    return pl.pallas_call(carries_kernel, out_shape=(shape, shape), name="carries")(table)


def collect(idx_ref, pieces, out_ref):
    @pl.when(pl.program_id(0) == 0)
    def _():
        if len(pieces) == 1:
            out_ref[...] = pieces[0][...].astype(BF16)
        else:
            for k, piece in enumerate(pieces):
                rows = piece.shape[0]
                at = pl.multiple_of(idx_ref[1 + k] * rows, rows)
                out_ref[pl.ds(at, rows), :] = piece[...].astype(BF16)


def forward_kernel(idx_ref, *refs, given):
    pieces = refs[:given]
    w_ref, scale_ref, decay_ref, retain_ref, enter_ref = refs[given : given + 5]
    x_ref, prev_ref, low_ref, drive, state = refs[given + 5 :]
    collect(idx_ref, pieces, x_ref)
    width = decay_ref.shape[1]
    count = drive.shape[0]
    steps = drive.shape[1] // SEG
    decays = tiles(jnp.broadcast_to(decay_ref[...], (SEG, width)), width)
    put(drive, nn(x_ref[...], w_ref[...]) * scale_ref[...])
    end, rate = scan_ends(drive, retain_ref, decays, False)
    start, _ = seg_starts(end, rate, enter_ref[pl.ds(idx_ref[0], 1), :], False)

    def lap(j, before):
        rows = pl.ds(j, SEG, stride=steps)
        kept = retain_ref[rows, :]
        out = []
        for l in range(count):
            after = kept * decays[l] * before[l] + drive[l, rows, :]
            prev_ref[l, rows, :] = before[l]
            state[l, rows, :] = after
            out.append(after)
        return tuple(out)

    lax.fori_loop(0, steps, lap, tuple(tiles(start, width)), unroll=4)
    low_ref[...] = joined(state).astype(BF16)


def backward_kernel(idx_ref, *refs, given, scaling):
    pieces = refs[:given]
    v_ref, scale_ref, decay_ref, retain_ref, enter_ref, prev_ref = refs[given : given + 6]
    x_ref, scaled_ref, grad_ref, scot, adjoint = refs[given + 6 :]
    collect(idx_ref, pieces, x_ref)
    width = decay_ref.shape[1]
    count = scot.shape[0]
    steps = scot.shape[1] // SEG
    decays = tiles(jnp.broadcast_to(decay_ref[...], (SEG, width)), width)
    put(scot, nt(x_ref[...], v_ref[...]) * scaling)
    end, rate = scan_ends(scot, retain_ref, decays, True)
    start, _ = seg_starts(end, rate, enter_ref[pl.ds(idx_ref[0], 1), :], True)

    def lap(k, carry):
        rows = pl.ds(steps - 1 - k, SEG, stride=steps)
        kept = retain_ref[rows, :]
        out = []
        for l in range(count):
            follow, grad = carry[l]
            here = scot[l, rows, :] + follow
            adjoint[l, rows, :] = here
            part = kept * here
            out.append((part * decays[l], grad + part * prev_ref[l, rows, :]))
        return tuple(out)

    begin = tuple((t, jnp.zeros((SEG, 128), F32)) for t in tiles(start, width))
    done = lax.fori_loop(0, steps, lap, begin, unroll=4)
    scaled_ref[...] = (joined(adjoint) * scale_ref[...]).astype(BF16)
    grad_ref[...] = jnp.sum(jnp.concatenate([d[1] for d in done], axis=1), axis=0, keepdims=True)


def block_call(kernel, idx, pieces, weight, across, scale, decays, retain_wide, enter, prev, chunk, name):
    channels = scale.shape[1]
    depth = pieces[0].shape[1]
    rows = sum(p.shape[0] for p in pieces)
    blocks = enter.shape[0]
    specs = [pl.BlockSpec(p.shape, lambda j, i: (0, 0)) for p in pieces]
    specs.append(
        pl.BlockSpec((depth, chunk), lambda j, i: (0, j)) if across else pl.BlockSpec((chunk, depth), lambda j, i: (j, 0))
    )
    specs += [
        pl.BlockSpec((1, chunk), lambda j, i: (0, j)),
        pl.BlockSpec((1, chunk), lambda j, i: (0, j)),
        pl.BlockSpec((rows, 128), lambda j, i: (i[0], 0)),
        pl.BlockSpec((blocks, chunk), lambda j, i: (0, j)),
    ]
    operands = [*pieces, weight, scale, decays, retain_wide, enter]
    tile = pl.BlockSpec((rows, chunk), lambda j, i: (0, j))
    outs = [(jax.ShapeDtypeStruct((rows, depth), BF16), pl.BlockSpec((rows, depth), lambda j, i: (0, 0)))]
    deep = pl.BlockSpec((chunk // 128, rows, 128), lambda j, i: (j, 0, 0))
    if prev is None:
        outs.append((jax.ShapeDtypeStruct((channels // 128, rows, 128), F32), deep))
        outs.append((jax.ShapeDtypeStruct((rows, channels), BF16), tile))
    else:
        specs.append(deep)
        operands.append(prev)
        outs.append((jax.ShapeDtypeStruct((rows, channels), BF16), tile))
        outs.append((jax.ShapeDtypeStruct((1, channels), F32), pl.BlockSpec((1, chunk), lambda j, i: (0, j))))
    return pl.pallas_call(
        functools.partial(kernel, given=len(pieces)),
        out_shape=tuple(o[0] for o in outs),
        grid_spec=pltpu.PrefetchScalarGridSpec(
            num_scalar_prefetch=1,
            grid=(channels // chunk,),
            in_specs=specs,
            out_specs=tuple(o[1] for o in outs),
            scratch_shapes=[pltpu.VMEM((chunk // 128, rows, 128), F32)] * 2,
        ),
        compiler_params=pltpu.CompilerParams(vmem_limit_bytes=VMEM_LIMIT),
        cost_estimate=pl.CostEstimate(
            flops=2 * rows * depth * channels, transcendentals=0, bytes_accessed=2 * depth * channels + 8 * rows * channels
        ),
        name=name,
    )(idx, *operands)


def grad_kernel(idx_ref, *refs, factor):
    half = (len(refs) - 1) // 2
    total = tn(refs[0][...], refs[half][...])
    for k in range(1, half):
        total += tn(refs[k][...], refs[half + k][...])
    refs[-1][...] = total * factor if factor is not None else total


def grad_rows(at, features, values, rows_out, factor, chunk, name):
    channels = values[0].shape[1]
    rows = values[0].shape[0]
    if rows_out % 128:
        total = sum(
            tn(lax.dynamic_slice_in_dim(x, at * rows_out, rows_out, axis=1), v) for x, v in zip(features, values, strict=True)
        )
        return total * factor if factor is not None else total
    return pl.pallas_call(
        functools.partial(grad_kernel, factor=factor),
        out_shape=jax.ShapeDtypeStruct((rows_out, channels), F32),
        grid_spec=pltpu.PrefetchScalarGridSpec(
            num_scalar_prefetch=1,
            grid=(channels // chunk,),
            in_specs=[pl.BlockSpec((rows, rows_out), lambda j, i: (0, i[0]))] * len(features)
            + [pl.BlockSpec((rows, chunk), lambda j, i: (0, j))] * len(values),
            out_specs=pl.BlockSpec((rows_out, chunk), lambda j, i: (0, j)),
        ),
        compiler_params=pltpu.CompilerParams(vmem_limit_bytes=VMEM_LIMIT),
        cost_estimate=pl.CostEstimate(
            flops=2 * len(values) * rows * rows_out * channels, transcendentals=0, bytes_accessed=8 * rows * channels
        ),
        name=name,
    )(jnp.reshape(at, (1,)).astype(jnp.int32), *features, *values)


def rowgrad_kernel(a_ref, w_ref, out_ref):
    out_ref[0] = nt(a_ref[...], w_ref[...])


def row_grad(scaled, in_proj, parts):
    rows, channels = scaled.shape
    depth = in_proj.shape[0]
    width = depth // parts
    return pl.pallas_call(
        rowgrad_kernel,
        out_shape=jax.ShapeDtypeStruct((parts, rows, width), F32),
        grid=(parts,),
        in_specs=[pl.BlockSpec((rows, channels), lambda j: (0, 0)), pl.BlockSpec((width, channels), lambda j: (j, 0))],
        out_specs=pl.BlockSpec((1, rows, width), lambda j: (j, 0, 0)),
        compiler_params=pltpu.CompilerParams(vmem_limit_bytes=VMEM_LIMIT),
        cost_estimate=pl.CostEstimate(flops=2 * rows * depth * channels, transcendentals=0, bytes_accessed=2 * depth * channels),
        name="row_grad",
    )(scaled, in_proj)


def gather_group(x, far, lane):
    rows = x.shape[0]
    half, quarter = rows // 2, rows // 4
    near = swap(lax.dynamic_slice_in_dim(x, (lane % 2) * half, half, axis=0).astype(F32), "tm", 1)
    away = swap(lax.dynamic_slice_in_dim(x, lane * quarter, quarter, axis=0).astype(F32), "tm", far)
    corner = swap(away, "tm", 1)
    near_rest = swap(near, "chan", 1)

    def spread(piece):
        across = swap(piece, "chan", 2)
        return [piece, swap(piece, "chan", 1), across, swap(across, "chan", 1)]

    return [near, near_rest], spread(away), spread(corner)


def per_device(inputs, cotangent, in_proj, out_proj, decays, input_scale, retain):
    rows, depth = inputs.shape
    channels = in_proj.shape[1]
    devices, lanes = lax.axis_size("tm"), lax.axis_size("chan")
    scaling = 1.0 / math.sqrt(rows * devices)
    me, lane = lax.axis_index("tm"), lax.axis_index("chan")
    far = devices // 2
    groups = devices // 4
    chunk = min(512, channels)
    scale = input_scale[None, :]
    decay_row = decays[None, :]

    in_pieces = gather_group(inputs, far, lane)
    cot_pieces = gather_group(cotangent, far, lane)

    own = summary(
        inputs, cotangent, in_proj, out_proj, scale, decay_row,
        jnp.broadcast_to(retain[:, None], (rows, 128)), scaling, chunk,
    )
    own = jnp.concatenate([own[:3], jnp.pad(retain, (0, channels - rows))[None, :]], axis=0)
    table = own[None]
    bit = 1
    while bit < devices:
        other = swap(table, "tm", bit)
        low = (me & bit) == 0
        table = jnp.where(low, jnp.concatenate([table, other]), jnp.concatenate([other, table]))
        bit *= 2
    enter_fwd, enter_bwd = carries(table)
    retain_wide = jnp.broadcast_to(table[:, 3, :rows].reshape(-1, 1), (devices * rows, 128))

    quarters = jnp.stack([lane, lane ^ 1, lane ^ 2, lane ^ 3])
    halves = jnp.stack([lane % 2, 1 - lane % 2, 0, 0])
    places = [jnp.zeros_like(halves), halves, quarters, quarters]
    blocks = [me, me ^ 1, me ^ far, me ^ far ^ 1]
    idx = [jnp.concatenate([b[None], p]).astype(jnp.int32) for b, p in zip(blocks, places, strict=True)]

    backward = functools.partial(backward_kernel, scaling=scaling)
    xs, prevs, lows = [], [], []
    for role, pieces in enumerate([[inputs], *in_pieces]):
        x, prev, low = block_call(
            forward_kernel, idx[role], pieces, in_proj, True, scale, decay_row, retain_wide, enter_fwd, None, chunk, "forward"
        )
        xs.append(x)
        prevs.append(prev)
        lows.append(low)
    cs, scaled, grads = [], [], []
    for role, pieces in enumerate([[cotangent], *cot_pieces]):
        c, s, g = block_call(
            backward, idx[role], pieces, out_proj, False, scale, decay_row, retain_wide, enter_bwd, prevs[role], chunk, "backward"
        )
        cs.append(c)
        scaled.append(s)
        grads.append(g)

    rows_out = depth // devices

    def reduced(features, values, factor, name):
        mine = grad_rows(me, features, values, rows_out, factor, chunk, name)
        for k in range(1, groups):
            mine += swap(grad_rows(me ^ (2 * k), features, values, rows_out, factor, chunk, name), "tm", 2 * k)
        return mine

    out_proj_grad = reduced(cs, lows, scaling, "out_grad")
    in_proj_grad = reduced(xs, scaled, None, "in_grad")

    decay_grad = (grads[0] + grads[1]) + (grads[2] + grads[3])
    bit = 2
    while bit < far:
        decay_grad += swap(decay_grad, "tm", bit)
        bit *= 2

    parts = row_grad(scaled[0], in_proj, lanes)
    bit = 1
    while bit < lanes:
        parts = parts.reshape(-1, 2, *parts.shape[1:])
        side = (lane // bit) % 2
        keep = lax.dynamic_index_in_dim(parts, side, axis=1, keepdims=False)
        give = lax.dynamic_index_in_dim(parts, 1 - side, axis=1, keepdims=False)
        parts = keep + swap(give, "chan", bit)
        bit *= 2
    input_grad = parts[0].astype(BF16)
    return (in_proj_grad, out_proj_grad, decay_grad[0], input_grad)


def solution(mesh):
    return jax.shard_map(
        per_device,
        mesh=mesh,
        in_specs=(
            P("tm", None),
            P("tm", None),
            P(None, "chan"),
            P("chan", None),
            P("chan"),
            P("chan"),
            P("tm"),
        ),
        out_specs=(P("tm", "chan"), P("tm", "chan"), P("chan"), P("tm", "chan")),
        check_vma=False,
    )
```

time: 771 us -> 266 us (0.35)
  local copies, waits for them, and re-layouts: 213 us -> 17.2 us
  waiting for transfers between devices: 301 us -> 121 us
  blocking collectives: 146 us -> 0 us
  Pallas kernels: 0 us -> 87.9 us
  other arithmetic: 64.4 us -> 12.2 us
  starting transfers between devices: 0.12 us -> 25.6 us
  matrix products: 22.5 us -> 0 us
  between operations: 14.9 us -> 1.24 us
    reduce_scatter x3 -> x0, waiting for transfers between devices: 301 us -> none  [the longest x1 152 us: per_device(): lax.psum_scatter(lax.dot_general(columns, scaled, (((0,), (0,)), ((), ())...]
    slice x108 -> x1, local copies, waits for them, and re-layouts: 156 us -> 0.01 us  [per_device(): table[:, 3, :rows].reshape(-1, 1)]
    all_gather x4 -> x0, blocking collectives: 124 us -> none  [prefix(): everything = jax.tree.map(lambda part: lax.all_gather(part, axis), x)]
    ppermute x0 -> x28, waiting for transfers between devices: none -> 121 us  [swap(): return lax.ppermute(x, axis, [(k, k ^ bit) for k in range(n)])]
    pallas_call x0 -> x15, Pallas kernels: none -> 87.9 us  [the longest x8 63.9 us: block_call(): pl.pallas_call(functools.partial(kernel, given=len(pieces)), out_shape=tu...]
    add x57 -> x5, other arithmetic: 42.7 us -> 7.06 us  [the longest x2 4.92 us: reduced(): mine += swap(grad_rows(me ^ 2 * k, features, values, rows_out, factor, ch...]
    pad x56 -> x1, local copies, waits for them, and re-layouts: 34.4 us -> 0.68 us  [per_device(): jnp.pad(retain, (0, channels - rows))[None, :]]
    ppermute x0 -> x28, starting transfers between devices: none -> 25.6 us  [swap(): return lax.ppermute(x, axis, [(k, k ^ bit) for k in range(n)])]
  transfers between devices with their start and end apart: 3 -> 28, of which waited for: 2 -> 8; matrix products, arithmetic and copies ran while one was open for 2% -> 4% of each run, Pallas kernels for 0% -> 30%
where the time goes in v1:
time: 266 us; the launch traced here: 265 us
  waiting for transfers between devices  121 us (45%)
  Pallas kernels  87.9 us (33%)
  starting transfers between devices  25.6 us (10%)
  local copies, waits for them, and re-layouts  17.2 us (6%)
  other arithmetic  12.2 us (5%)
    ppermute x28, waiting for transfers between devices, swap(): return lax.ppermute(x, axis, [(k, k ^ bit) for k in range(n)])  121 us
    pallas_call x8, Pallas kernels, block_call(): pl.pallas_call(functools.partial(kernel, given=len(pieces)), out_shape=tu...  63.9 us
    ppermute x28, starting transfers between devices, swap(): return lax.ppermute(x, axis, [(k, k ^ bit) for k in range(n)])  25.6 us
    unnamed x90, local copies, waits for them, and re-layouts  14.3 us
    pallas_call x4, Pallas kernels, grad_rows(): pl.pallas_call(functools.partial(grad_kernel, factor=factor), out_shape=j...  10.6 us
    pallas_call x1, Pallas kernels, summary(): pl.pallas_call(functools.partial(summary_kernel, scaling=scaling), out_sh...  7.31 us
  transfers between devices with their start and end apart: 28, of which 8 were waited for; matrix products, arithmetic and copies ran while one was open for 4% of the time, Pallas kernels for 30%

profile of v1, /device:TPU:0, one launch (start us, length us, event | category | flops | bytes accessed | tf_op | source)
XLA Modules:
  0.0 264.9 jit_solution(1638124094123408027)
XLA Ops:
  5.9 7.3 %summary.1 = f32[4,1024]{1,0:T(4,128)S(1)} custom-call(bf16[256,2048]{1,0:T(8,128)(2,1)S(1)} %copy-done, bf16[256,2048]{1,0:T(8,128)(2,1)S(1)} %copy-done.2, bf16[2048,1024]{1,0:T(8,128)(2,1)} %w_ref.3, bf16[1024,2048]{1,0:T(8,128)(2,1)} %refs_4_.7, f32[1,1024]{1,0:T(1,128)S(1)} %bitcast.28, f32[1,1024]{1,0:T(1,128)S(1)} %bitcast.37, ...), custom_call_target="tpu_custom_call" | custom-call | flops 2147483648 | bytes 8388608 | tf_op jit(solution)/shard_map/summary/pallas_call | solution.py:97
  13.3 3.0 %collective-permute-start = (f32[1,4,1024]{2,1,0:T(4,128)S(1)}, f32[1,4,1024]{2,1,0:T(4,128)S(1)}, u32[]{:S(2)}, u32[]{:S(2)}) collective-permute-start(f32[1,4,1024]{2,1,0:T(4,128)S(1)} %maximum_bitcast_fusion), channel_id=1, source_target_pairs={{0,4},{4,0},{8,12},{12,8},{16,20},{20,16},{24,28},{28,24},{1,5},{5... | collective-permute-start | bytes 49160 | tf_op jit(solution)/shard_map/ppermute | solution.py:19
  16.3 2.6 collective-permute-start.15
  20.2 1.6 collective-permute-start.1
  23.4 18.4 %collective-permute-done.1 = f32[2,4,1024]{2,1,0:T(4,128)S(1)} collective-permute-done((f32[2,4,1024]{2,1,0:T(4,128)S(1)}, f32[2,4,1024]{2,1,0:T(4,128)S(1)}, u32[]{:S(2)}, u32[]{:S(2)}) %collective-permute-start.1) | collective-permute-done | bytes 32800 | tf_op jit(solution)/shard_map/ppermute | solution.py:19
  41.9 2.4 collective-permute-start.2
  45.4 10.4 %collective-permute-done.15.refs_0_ = f32[64,2048]{1,0:T(8,128)} collective-permute-done((f32[64,2048]{1,0:T(8,128)S(1)}, f32[64,2048]{1,0:T(8,128)}, u32[]{:S(2)}, u32[]{:S(2)}) %collective-permute-start.15) | collective-permute-done | bytes 524320 | tf_op jit(solution)/shard_map/ppermute | solution.py:19
  56.3 1.6 collective-permute-start.17
  57.9 9.3 %collective-permute-done.2 = f32[4,4,1024]{2,1,0:T(4,128)S(1)} collective-permute-done((f32[4,4,1024]{2,1,0:T(4,128)S(1)}, f32[4,4,1024]{2,1,0:T(4,128)S(1)}, u32[]{:S(2)}, u32[]{:S(2)}) %collective-permute-start.2) | collective-permute-done | bytes 65568 | tf_op jit(solution)/shard_map/ppermute | solution.py:19
  70.5 6.8 %forward.4 = (bf16[256,2048]{1,0:T(8,128)(2,1)S(1)}, f32[8,256,128]{2,1,0:T(8,128)S(1)}, bf16[256,1024]{1,0:T(8,128)(2,1)S(1)}) custom-call(s32[5]{0:T(128)S(1)} %concatenate.35.idx_ref, bf16[256,2048]{1,0:T(8,128)(2,1)S(1)} %copy-done.1, bf16[2048,1024]{1,0:T(8,128)(2,1)} %w_ref.3, f32[1,1024]{1,0:T(1,128)S(1)} %bitcast.29, f32[1,1024]{1,0:T(1,128)S(1)} %bitcast.38, ...), custom_call_target="tpu_custom_call" | custom-call | flops 1073741824 | bytes 6291456 | tf_op jit(solution)/shard_map/forward/pallas_call | solution.py:235
  78.2 8.3 %backward.4 = (bf16[256,2048]{1,0:T(8,128)(2,1)S(1)}, bf16[256,1024]{1,0:T(8,128)(2,1)S(1)}, f32[1,1024]{1,0:T(1,128)S(1)}) custom-call(s32[5]{0:T(128)S(1)} %concatenate.35.idx_ref, bf16[256,2048]{1,0:T(8,128)(2,1)S(1)} %copy-done.3, bf16[1024,2048]{1,0:T(8,128)(2,1)} %refs_4_.7, f32[1,1024]{1,0:T(1,128)S(1)} %bitcast.30, f32[1,1024]{1,0:T(1,128)S(1)} %bitcast.39, ...), custom_call_target="tpu_custom_call" | custom-call | flops 1073741824 | bytes 6291456 | tf_op jit(solution)/shard_map/backward/pallas_call | solution.py:235
  86.5 4.6 %row_grad.1 = f32[4,256,512]{2,1,0:T(8,128)S(1)} custom-call(bf16[256,1024]{1,0:T(8,128)(2,1)S(1)} %get-tuple-element.37.refs_4_.a_ref, bf16[2048,1024]{1,0:T(8,128)(2,1)} %w_ref.3), custom_call_target="tpu_custom_call" | custom-call | flops 1073741824 | bytes 4194304 | tf_op jit(solution)/shard_map/row_grad/pallas_call | solution.py:295
  91.8 1.6 collective-permute-start.9
  93.4 1.6 collective-permute-start.7
  95.0 33.1 %collective-permute-done.9.refs_0_ = f32[64,2048]{1,0:T(8,128)} collective-permute-done((f32[64,2048]{1,0:T(8,128)}, f32[64,2048]{1,0:T(8,128)}, u32[]{:S(2)}, u32[]{:S(2)}) %collective-permute-start.9) | collective-permute-done | bytes 524320 | tf_op jit(solution)/shard_map/ppermute | solution.py:19
  133.7 9.5 %collective-permute-done.21.refs_2_ = f32[64,2048]{1,0:T(8,128)} collective-permute-done((f32[64,2048]{1,0:T(8,128)}, f32[64,2048]{1,0:T(8,128)}, u32[]{:S(2)}, u32[]{:S(2)}) %collective-permute-start.21) | collective-permute-done | bytes 524320 | tf_op jit(solution)/shard_map/ppermute | solution.py:19
  145.6 8.5 %collective-permute-done.11.refs_2_ = f32[64,2048]{1,0:T(8,128)} collective-permute-done((f32[64,2048]{1,0:T(8,128)}, f32[64,2048]{1,0:T(8,128)}, u32[]{:S(2)}, u32[]{:S(2)}) %collective-permute-start.11) | collective-permute-done | bytes 524320 | tf_op jit(solution)/shard_map/ppermute | solution.py:19
  155.5 7.4 %forward.6 = (bf16[256,2048]{1,0:T(8,128)(2,1)S(1)}, f32[8,256,128]{2,1,0:T(8,128)S(1)}, bf16[256,1024]{1,0:T(8,128)(2,1)S(1)}) custom-call(s32[5]{0:T(128)S(1)} %concatenate.44.idx_ref, f32[64,2048]{1,0:T(8,128)} %collective-permute-done.5.refs_0_, f32[64,2048]{1,0:T(8,128)S(1)} %copy-done.36, f32[64,2048]{1,0:T(8,128)} %collective-permute-done.7.refs_2_, ...), custom_call_target="tpu_custom_call" | custom-call | flops 1073741824 | bytes 6291456 | tf_op jit(solution)/shard_map/forward/pallas_call | solution.py:235
  162.9 8.9 %backward.6 = (bf16[256,2048]{1,0:T(8,128)(2,1)S(1)}, bf16[256,1024]{1,0:T(8,128)(2,1)S(1)}, f32[1,1024]{1,0:T(1,128)S(1)}) custom-call(s32[5]{0:T(128)S(1)} %concatenate.44.idx_ref, f32[64,2048]{1,0:T(8,128)} %collective-permute-done.15.refs_0_, f32[64,2048]{1,0:T(8,128)} %collective-permute-done.16.refs_1_, f32[64,2048]{1,0:T(8,128)} %collective-permute-done.17.refs_2_, ...), custom_call_target="tpu_custom_call" | custom-call | flops 1073741824 | bytes 6291456 | tf_op jit(solution)/shard_map/backward/pallas_call | solution.py:235
  172.8 7.5 %forward.5 = (bf16[256,2048]{1,0:T(8,128)(2,1)S(1)}, f32[8,256,128]{2,1,0:T(8,128)S(1)}, bf16[256,1024]{1,0:T(8,128)(2,1)S(1)}) custom-call(s32[5]{0:T(128)S(1)} %pad_add_fusion.idx_ref, f32[128,2048]{1,0:T(8,128)} %collective-permute-done.3.refs_0_, f32[128,2048]{1,0:T(8,128)} %collective-permute-done.4.refs_1_, bf16[2048,1024]{1,0:T(8,128)(2,1)} %w_ref.3, ...), custom_call_target="tpu_custom_call" | custom-call | flops 1073741824 | bytes 6291456 | tf_op jit(solution)/shard_map/forward/pallas_call | solution.py:235
  180.3 1.6 collective-permute-start.27
  181.9 8.9 %backward.5 = (bf16[256,2048]{1,0:T(8,128)(2,1)S(1)}, bf16[256,1024]{1,0:T(8,128)(2,1)S(1)}, f32[1,1024]{1,0:T(1,128)S(1)}) custom-call(s32[5]{0:T(128)S(1)} %pad_add_fusion.idx_ref, f32[128,2048]{1,0:T(8,128)} %collective-permute-done.13.refs_0_, f32[128,2048]{1,0:T(8,128)} %collective-permute-done.14.refs_1_, bf16[1024,2048]{1,0:T(8,128)(2,1)} %refs_4_.7, ...), custom_call_target="tpu_custom_call" | custom-call | flops 1073741824 | bytes 6291456 | tf_op jit(solution)/shard_map/backward/pallas_call | solution.py:235
  190.9 7.1 %forward.7 = (bf16[256,2048]{1,0:T(8,128)(2,1)S(1)}, f32[8,256,128]{2,1,0:T(8,128)S(1)}, bf16[256,1024]{1,0:T(8,128)(2,1)S(1)}) custom-call(s32[5]{0:T(128)S(1)} %concatenate.45.idx_ref, f32[64,2048]{1,0:T(8,128)} %collective-permute-done.9.refs_0_, f32[64,2048]{1,0:T(8,128)S(1)} %collective-permute-done.10.refs_1_, ...), custom_call_target="tpu_custom_call" | custom-call | flops 1073741824 | bytes 6291456 | tf_op jit(solution)/shard_map/forward/pallas_call | solution.py:235
  198.1 9.0 %backward.7 = (bf16[256,2048]{1,0:T(8,128)(2,1)S(1)}, bf16[256,1024]{1,0:T(8,128)(2,1)S(1)}, f32[1,1024]{1,0:T(1,128)S(1)}) custom-call(s32[5]{0:T(128)S(1)} %concatenate.45.idx_ref, f32[64,2048]{1,0:T(8,128)} %collective-permute-done.19.refs_0_, f32[64,2048]{1,0:T(8,128)S(1)} %collective-permute-done.20.refs_1_, ...), custom_call_target="tpu_custom_call" | custom-call | flops 1073741824 | bytes 6291456 | tf_op jit(solution)/shard_map/backward/pallas_call | solution.py:235
  208.2 3.2 %in_grad.3 = f32[256,1024]{1,0:T(8,128)} custom-call(s32[1]{0:T(128)} %bitcast.15.idx_ref, bf16[256,2048]{1,0:T(8,128)(2,1)S(1)} %copy-done.7, bf16[256,2048]{1,0:T(8,128)(2,1)S(1)} %get-tuple-element.32.refs_1_, bf16[256,2048]{1,0:T(8,128)(2,1)} %copy-done.10, bf16[256,2048]{1,0:T(8,128)(2,1)} %copy-done.16, bf16[256,1024]{1,0:T(8,128)(2,1)S(1)} %copy-done.5, ...), custom_call_target="tpu_custom_call" | custom-call | flops 536870912 | bytes 2097152 | tf_op jit(solution)/shard_map/in_grad/pallas_call | solution.py:269
  212.0 2.9 %out_grad.3 = f32[256,1024]{1,0:T(8,128)} custom-call(s32[1]{0:T(128)} %bitcast.15.idx_ref, bf16[256,2048]{1,0:T(8,128)(2,1)S(1)} %copy-done.9, bf16[256,2048]{1,0:T(8,128)(2,1)S(1)} %get-tuple-element.45.refs_1_, bf16[256,2048]{1,0:T(8,128)(2,1)} %copy-done.11, bf16[256,2048]{1,0:T(8,128)(2,1)} %copy-done.17, bf16[256,1024]{1,0:T(8,128)(2,1)S(1)} %copy-done.19, ...), custom_call_target="tpu_custom_call" | custom-call | flops 536870912 | bytes 2097152 | tf_op jit(solution)/shard_map/out_grad/pallas_call | solution.py:269
  216.3 2.0 fusion
  223.4 2.3 out_grad.2
  225.7 2.2 in_grad.2
  227.9 31.4 %collective-permute-done.25 = f32[1,1024]{1,0:T(1,128)S(1)} collective-permute-done((f32[1,1024]{1,0:T(1,128)S(1)}, f32[1,1024]{1,0:T(1,128)S(1)}, u32[]{:S(2)}, u32[]{:S(2)}) %collective-permute-start.25) | collective-permute-done | bytes 4128 | tf_op jit(solution)/shard_map/ppermute | solution.py:19
  260.0 2.5 add.68
  262.4 2.5 add.69
  (154 shorter events, 33.7 us)
Async XLA Ops:
  13.3 6.9 %collective-permute-start = (f32[1,4,1024]{2,1,0:T(4,128)S(1)}, f32[1,4,1024]{2,1,0:T(4,128)S(1)}, u32[]{:S(2)}, u32[]{:S(2)}) collective-permute-start(f32[1,4,1024]{2,1,0:T(4,128)S(1)} %maximum_bitcast_fusion), channel_id=1, source_target_pairs={{0,4},{4,0},{8,12},{12,8},{16,20},{20,16},{24,28},{28,24},{1,5},{5... | collective-permute-start | bytes 49160 | tf_op jit(solution)/shard_map/ppermute | solution.py:19
  16.3 39.5 %collective-permute-start.15 = (f32[64,2048]{1,0:T(8,128)S(1)}, f32[64,2048]{1,0:T(8,128)}, u32[]{:S(2)}, u32[]{:S(2)}) collective-permute-start(f32[64,2048]{1,0:T(8,128)S(1)} %dynamic-slice_convert_fusion.2), channel_id=1, source_target_pairs={{0,16},{4,20},{8,24},{12,28},{16,0},{20,4},{24,8},{28,12},{1,17},{... | collective-permute-start | bytes 1572872 | tf_op jit(solution)/shard_map/ppermute | solution.py:19
  19.8 71.3 %collective-permute-start.5 = (f32[64,2048]{1,0:T(8,128)}, f32[64,2048]{1,0:T(8,128)}, u32[]{:S(2)}, u32[]{:S(2)}) collective-permute-start(f32[64,2048]{1,0:T(8,128)} %dynamic-slice_convert_fusion.3), channel_id=1, source_target_pairs={{0,16},{4,20},{8,24},{12,28},{16,0},{20,4},{24,8},{28,12},{1,17},{... | collective-permute-start | bytes 1572872 | tf_op jit(solution)/shard_map/ppermute | solution.py:19
  20.2 49.6 %copy-start.38 = (f32[1024]{0:T(1024)S(1)}, f32[1024]{0:T(1024)}, u32[]{:S(2)}) copy-start(f32[1024]{0:T(1024)} %param.12) | copy-start | bytes 12292
  20.2 49.6 %copy-start.40 = (f32[1024]{0:T(1024)S(1)}, f32[1024]{0:T(1024)}, u32[]{:S(2)}) copy-start(f32[1024]{0:T(1024)} %param.11) | copy-start | bytes 12292
  20.2 21.7 %collective-permute-start.1 = (f32[2,4,1024]{2,1,0:T(4,128)S(1)}, f32[2,4,1024]{2,1,0:T(4,128)S(1)}, u32[]{:S(2)}, u32[]{:S(2)}) collective-permute-start(f32[2,4,1024]{2,1,0:T(4,128)S(1)} %maximum_select_fusion.2), channel_id=1, source_target_pairs={{0,8},{4,12},{8,0},{12,4},{16,24},{20,28},{24,16},{28,20},{1,9},{5... | collective-permute-start | bytes 98312 | tf_op jit(solution)/shard_map/ppermute | solution.py:19
  22.9 106.8 %collective-permute-start.3 = (f32[128,2048]{1,0:T(8,128)}, f32[128,2048]{1,0:T(8,128)}, u32[]{:S(2)}, u32[]{:S(2)}) collective-permute-start(f32[128,2048]{1,0:T(8,128)} %dynamic-slice_convert_fusion.1), channel_id=1, source_target_pairs={{0,4},{4,0},{8,12},{12,8},{16,20},{20,16},{24,28},{28,24},{1,5},{5... | collective-permute-start | bytes 3145736 | tf_op jit(solution)/shard_map/ppermute | solution.py:19
  41.9 25.3 %collective-permute-start.2 = (f32[4,4,1024]{2,1,0:T(4,128)S(1)}, f32[4,4,1024]{2,1,0:T(4,128)S(1)}, u32[]{:S(2)}, u32[]{:S(2)}) collective-permute-start(f32[4,4,1024]{2,1,0:T(4,128)S(1)} %maximum_select_fusion.1), channel_id=1, source_target_pairs={{0,16},{4,20},{8,24},{12,28},{16,0},{20,4},{24,8},{28,12},{1,17},{... | collective-permute-start | bytes 196616 | tf_op jit(solution)/shard_map/ppermute | solution.py:19
  55.8 36.0 %collective-permute-start.19 = (f32[64,2048]{1,0:T(8,128)}, f32[64,2048]{1,0:T(8,128)}, u32[]{:S(2)}, u32[]{:S(2)}) collective-permute-start(f32[64,2048]{1,0:T(8,128)} %collective-permute-done.15.refs_0_), channel_id=1, source_target_pairs={{0,4},{4,0},{8,12},{12,8},{16,20},{20,16},{24,28},{28,24},{1,5},{5... | collective-permute-start | bytes 1572872 | tf_op jit(solution)/shard_map/ppermute | solution.py:19
  56.3 37.1 %collective-permute-start.17 = (f32[64,2048]{1,0:T(8,128)}, f32[64,2048]{1,0:T(8,128)}, u32[]{:S(2)}, u32[]{:S(2)}) collective-permute-start(f32[64,2048]{1,0:T(8,128)} %collective-permute-done.15.refs_0_), channel_id=1, source_target_pairs={{0,2},{1,3},{2,0},{3,1},{4,6},{5,7},{6,4},{7,5},{8,10},{9,11},{10,... | collective-permute-start | bytes 1572872 | tf_op jit(solution)/shard_map/ppermute | solution.py:19
  67.2 26.2 %collective-permute-start.16 = (f32[64,2048]{1,0:T(8,128)}, f32[64,2048]{1,0:T(8,128)}, u32[]{:S(2)}, u32[]{:S(2)}) collective-permute-start(f32[64,2048]{1,0:T(8,128)} %collective-permute-done.15.refs_0_), channel_id=1, source_target_pairs={{0,1},{1,0},{2,3},{3,2},{4,5},{5,4},{6,7},{7,6},{8,9},{9,8},{10,11... | collective-permute-start | bytes 1572872 | tf_op jit(solution)/shard_map/ppermute | solution.py:19
  91.1 38.7 %collective-permute-start.13 = (f32[128,2048]{1,0:T(8,128)S(1)}, f32[128,2048]{1,0:T(8,128)}, u32[]{:S(2)}, u32[]{:S(2)}) collective-permute-start(f32[128,2048]{1,0:T(8,128)S(1)} %copy-done.43), channel_id=1, source_target_pairs={{0,4},{4,0},{8,12},{12,8},{16,20},{20,16},{24,28},{28,24},{1,5},{5... | collective-permute-start | bytes 3145736 | tf_op jit(solution)/shard_map/ppermute | solution.py:19
  91.8 36.3 %collective-permute-start.9 = (f32[64,2048]{1,0:T(8,128)}, f32[64,2048]{1,0:T(8,128)}, u32[]{:S(2)}, u32[]{:S(2)}) collective-permute-start(f32[64,2048]{1,0:T(8,128)} %collective-permute-done.5.refs_0_), channel_id=1, source_target_pairs={{0,4},{4,0},{8,12},{12,8},{16,20},{20,16},{24,28},{28,24},{1,5},{5... | collective-permute-start | bytes 1572872 | tf_op jit(solution)/shard_map/ppermute | solution.py:19
  93.4 37.8 %collective-permute-start.26 = (f32[2,256,512]{2,1,0:T(8,128)S(1)}, f32[2,256,512]{2,1,0:T(8,128)S(1)}, u32[]{:S(2)}, u32[]{:S(2)}) collective-permute-start(f32[2,256,512]{2,1,0:T(8,128)S(1)} %dynamic-slice_bitcast_fusion), channel_id=1, source_target_pairs={{0,1},{1,0},{2,3},{3,2},{4,5},{5,4},{6,7},{7,6},{8,9},{9,8},{10,11... | collective-permute-start | bytes 3145736 | tf_op jit(solution)/shard_map/ppermute | solution.py:19
  93.4 34.7 %collective-permute-start.7 = (f32[64,2048]{1,0:T(8,128)}, f32[64,2048]{1,0:T(8,128)}, u32[]{:S(2)}, u32[]{:S(2)}) collective-permute-start(f32[64,2048]{1,0:T(8,128)} %collective-permute-done.5.refs_0_), channel_id=1, source_target_pairs={{0,2},{1,3},{2,0},{3,1},{4,6},{5,7},{6,4},{7,5},{8,10},{9,11},{10,... | collective-permute-start | bytes 1572872 | tf_op jit(solution)/shard_map/ppermute | solution.py:19
  128.1 2.1 collective-permute-start.6
  128.1 15.0 %collective-permute-start.21 = (f32[64,2048]{1,0:T(8,128)}, f32[64,2048]{1,0:T(8,128)}, u32[]{:S(2)}, u32[]{:S(2)}) collective-permute-start(f32[64,2048]{1,0:T(8,128)} %collective-permute-done.19.refs_0_), channel_id=1, source_target_pairs={{0,2},{1,3},{2,0},{3,1},{4,6},{5,7},{6,4},{7,5},{8,10},{9,11},{10,... | collective-permute-start | bytes 1572872 | tf_op jit(solution)/shard_map/ppermute | solution.py:19
  129.7 24.9 %collective-permute-start.4 = (f32[128,2048]{1,0:T(8,128)}, f32[128,2048]{1,0:T(8,128)}, u32[]{:S(2)}, u32[]{:S(2)}) collective-permute-start(f32[128,2048]{1,0:T(8,128)} %collective-permute-done.3.refs_0_), channel_id=1, source_target_pairs={{0,1},{1,0},{2,3},{3,2},{4,5},{5,4},{6,7},{7,6},{8,9},{9,8},{10,11... | collective-permute-start | bytes 3145736 | tf_op jit(solution)/shard_map/ppermute | solution.py:19
  129.9 50.4 %collective-permute-start.14 = (f32[128,2048]{1,0:T(8,128)}, f32[128,2048]{1,0:T(8,128)}, u32[]{:S(2)}, u32[]{:S(2)}) collective-permute-start(f32[128,2048]{1,0:T(8,128)} %collective-permute-done.13.refs_0_), channel_id=1, source_target_pairs={{0,1},{1,0},{2,3},{3,2},{4,5},{5,4},{6,7},{7,6},{8,9},{9,8},{10,11... | collective-permute-start | bytes 3145736 | tf_op jit(solution)/shard_map/ppermute | solution.py:19
  131.1 13.9 %collective-permute-start.18 = (f32[64,2048]{1,0:T(8,128)}, f32[64,2048]{1,0:T(8,128)}, u32[]{:S(2)}, u32[]{:S(2)}) collective-permute-start(f32[64,2048]{1,0:T(8,128)} %collective-permute-done.17.refs_2_), channel_id=1, source_target_pairs={{0,1},{1,0},{2,3},{3,2},{4,5},{5,4},{6,7},{7,6},{8,9},{9,8},{10,11... | collective-permute-start | bytes 1572872 | tf_op jit(solution)/shard_map/ppermute | solution.py:19
  132.2 21.9 %collective-permute-start.11 = (f32[64,2048]{1,0:T(8,128)}, f32[64,2048]{1,0:T(8,128)}, u32[]{:S(2)}, u32[]{:S(2)}) collective-permute-start(f32[64,2048]{1,0:T(8,128)} %collective-permute-done.9.refs_0_), channel_id=1, source_target_pairs={{0,2},{1,3},{2,0},{3,1},{4,6},{5,7},{6,4},{7,5},{8,10},{9,11},{10,... | collective-permute-start | bytes 1572872 | tf_op jit(solution)/shard_map/ppermute | solution.py:19
  143.2 10.9 %collective-permute-start.8 = (f32[64,2048]{1,0:T(8,128)}, f32[64,2048]{1,0:T(8,128)}, u32[]{:S(2)}, u32[]{:S(2)}) collective-permute-start(f32[64,2048]{1,0:T(8,128)} %collective-permute-done.7.refs_2_), channel_id=1, source_target_pairs={{0,1},{1,0},{2,3},{3,2},{4,5},{5,4},{6,7},{7,6},{8,9},{9,8},{10,11... | collective-permute-start | bytes 1572872 | tf_op jit(solution)/shard_map/ppermute | solution.py:19
  145.0 53.0 %collective-permute-start.20 = (f32[64,2048]{1,0:T(8,128)}, f32[64,2048]{1,0:T(8,128)S(1)}, u32[]{:S(2)}, u32[]{:S(2)}) collective-permute-start(f32[64,2048]{1,0:T(8,128)} %collective-permute-done.19.refs_0_), channel_id=1, source_target_pairs={{0,1},{1,0},{2,3},{3,2},{4,5},{5,4},{6,7},{7,6},{8,9},{9,8},{10,11... | collective-permute-start | bytes 1572872 | tf_op jit(solution)/shard_map/ppermute | solution.py:19
  154.0 36.8 %collective-permute-start.10 = (f32[64,2048]{1,0:T(8,128)}, f32[64,2048]{1,0:T(8,128)S(1)}, u32[]{:S(2)}, u32[]{:S(2)}) collective-permute-start(f32[64,2048]{1,0:T(8,128)} %collective-permute-done.9.refs_0_), channel_id=1, source_target_pairs={{0,1},{1,0},{2,3},{3,2},{4,5},{5,4},{6,7},{7,6},{8,9},{9,8},{10,11... | collective-permute-start | bytes 1572872 | tf_op jit(solution)/shard_map/ppermute | solution.py:19
  154.0 44.0 %collective-permute-start.22 = (f32[64,2048]{1,0:T(8,128)}, f32[64,2048]{1,0:T(8,128)S(1)}, u32[]{:S(2)}, u32[]{:S(2)}) collective-permute-start(f32[64,2048]{1,0:T(8,128)} %collective-permute-done.21.refs_2_), channel_id=1, source_target_pairs={{0,1},{1,0},{2,3},{3,2},{4,5},{5,4},{6,7},{7,6},{8,9},{9,8},{10,11... | collective-permute-start | bytes 1572872 | tf_op jit(solution)/shard_map/ppermute | solution.py:19
  154.6 36.3 %collective-permute-start.12 = (f32[64,2048]{1,0:T(8,128)}, f32[64,2048]{1,0:T(8,128)S(1)}, u32[]{:S(2)}, u32[]{:S(2)}) collective-permute-start(f32[64,2048]{1,0:T(8,128)} %collective-permute-done.11.refs_2_), channel_id=1, source_target_pairs={{0,1},{1,0},{2,3},{3,2},{4,5},{5,4},{6,7},{7,6},{8,9},{9,8},{10,11... | collective-permute-start | bytes 1572872 | tf_op jit(solution)/shard_map/ppermute | solution.py:19
  162.9 49.2 %copy-start.22 = (bf16[256,1024]{1,0:T(8,128)(2,1)}, bf16[256,1024]{1,0:T(8,128)(2,1)S(1)}, u32[]{:S(2)}) copy-start(bf16[256,1024]{1,0:T(8,128)(2,1)S(1)} %get-tuple-element.50.refs_6_) | copy-start | bytes 1572868
  172.8 35.3 %copy-start.20 = (bf16[256,1024]{1,0:T(8,128)(2,1)}, bf16[256,1024]{1,0:T(8,128)(2,1)S(1)}, u32[]{:S(2)}) copy-start(bf16[256,1024]{1,0:T(8,128)(2,1)S(1)} %get-tuple-element.41.refs_6_) | copy-start | bytes 1572868
  180.3 36.0 %collective-permute-start.27 = (f32[1,256,512]{2,1,0:T(8,128)}, f32[1,256,512]{2,1,0:T(8,128)}, u32[]{:S(2)}, u32[]{:S(2)}) collective-permute-start(f32[1,256,512]{2,1,0:T(8,128)} %constant_dynamic-slice_fusion), channel_id=1, source_target_pairs={{0,2},{1,3},{2,0},{3,1},{4,6},{5,7},{6,4},{7,5},{8,10},{9,11},{10,... | collective-permute-start | bytes 1572872 | tf_op jit(solution)/shard_map/ppermute | solution.py:19
  211.3 48.6 %collective-permute-start.23 = (f32[256,1024]{1,0:T(8,128)}, f32[256,1024]{1,0:T(8,128)}, u32[]{:S(2)}, u32[]{:S(2)}) collective-permute-start(f32[256,1024]{1,0:T(8,128)} %in_grad.3), channel_id=1, source_target_pairs={{0,8},{4,12},{8,0},{12,4},{16,24},{20,28},{24,16},{28,20},{1,9},{5... | collective-permute-start | bytes 3145736 | tf_op jit(solution)/shard_map/ppermute | solution.py:19
  215.0 47.5 %collective-permute-start.24 = (f32[256,1024]{1,0:T(8,128)}, f32[256,1024]{1,0:T(8,128)}, u32[]{:S(2)}, u32[]{:S(2)}) collective-permute-start(f32[256,1024]{1,0:T(8,128)} %out_grad.3), channel_id=1, source_target_pairs={{0,8},{4,12},{8,0},{12,4},{16,24},{20,28},{24,16},{28,20},{1,9},{5... | collective-permute-start | bytes 3145736 | tf_op jit(solution)/shard_map/ppermute | solution.py:19
  218.3 41.0 %collective-permute-start.25 = (f32[1,1024]{1,0:T(1,128)S(1)}, f32[1,1024]{1,0:T(1,128)S(1)}, u32[]{:S(2)}, u32[]{:S(2)}) collective-permute-start(f32[1,1024]{1,0:T(1,128)S(1)} %add_add_fusion), channel_id=1, source_target_pairs={{0,8},{4,12},{8,0},{12,4},{16,24},{20,28},{24,16},{28,20},{1,9},{5... | collective-permute-start | bytes 12296 | tf_op jit(solution)/shard_map/ppermute | solution.py:19
  (41 other events, 276.5 us)

commit v2 on v0

v2 whole, which is shorter than its diff:
```python
import functools
import math

import jax
import jax.numpy as jnp
from jax import lax
from jax.experimental import pallas as pl
from jax.experimental.pallas import tpu as pltpu
from jax.sharding import PartitionSpec as P

F32 = jnp.float32
BF16 = jnp.bfloat16
SEG = 8
VMEM_LIMIT = 8 * 1024 * 1024


def swap(x, axis, bit):
    n = lax.axis_size(axis)
    return lax.ppermute(x, axis, [(k, k ^ bit) for k in range(n)])


def nn(a, b):
    return lax.dot_general(a, b, (((1,), (0,)), ((), ())), preferred_element_type=F32)


def nt(a, b):
    return lax.dot_general(a, b, (((1,), (1,)), ((), ())), preferred_element_type=F32)


def tn(a, b):
    return lax.dot_general(a, b, (((0,), (0,)), ((), ())), preferred_element_type=F32)


def order(rows, transpose=False):
    steps = rows // SEG
    r = lax.broadcasted_iota(jnp.int32, (rows, rows), 1 if transpose else 0)
    t = lax.broadcasted_iota(jnp.int32, (rows, rows), 0 if transpose else 1)
    return ((r % SEG) * steps + r // SEG == t).astype(F32).astype(BF16)


VMEM = pl.BlockSpec(memory_space=pltpu.VMEM)
SMEM = pl.BlockSpec(memory_space=pltpu.SMEM)


def resident(kernel, out_shape, operands, name, scratch=(), scalars=1):
    outs = jax.tree.map(lambda _: VMEM, out_shape)
    return pl.pallas_call(
        kernel,
        out_shape=out_shape,
        in_specs=[SMEM] * scalars + [VMEM] * (len(operands) - scalars),
        out_specs=outs,
        scratch_shapes=scratch,
        compiler_params=pltpu.CompilerParams(vmem_limit_bytes=VMEM_LIMIT),
        cost_estimate=pl.CostEstimate(flops=0, transcendentals=0, bytes_accessed=0),
        name=name,
    )(*operands)


def prep_kernel(idx_ref, x_ref, p_ref, half_ref, quarter_ref, full):
    rows = x_ref.shape[0]
    full[...] = nn(order(rows), x_ref[...])
    p_ref[...] = full[...].astype(BF16)
    half, quarter = rows // 2, rows // 4
    half_ref[...] = full[pl.ds(pl.multiple_of(idx_ref[0] * half, half), half), :]
    quarter_ref[...] = full[pl.ds(pl.multiple_of(idx_ref[1] * quarter, quarter), quarter), :]


def prep(idx, x, name):
    rows, depth = x.shape
    shapes = (
        jax.ShapeDtypeStruct((rows, depth), BF16),
        jax.ShapeDtypeStruct((rows // 2, depth), F32),
        jax.ShapeDtypeStruct((rows // 4, depth), F32),
    )
    return resident(prep_kernel, shapes, (idx, x), name, [pltpu.VMEM((rows, depth), F32)])


def lanes_of(l):
    return slice(128 * l, 128 * (l + 1))


def scan_ends(src, retain_ref, base, decays, reverse):
    count, steps = src.shape[1] // 128, src.shape[0] // SEG

    def lap(k, carry):
        j = steps - 1 - k if reverse else k
        rows = pl.ds(pl.multiple_of(j * SEG, SEG), SEG)
        kept = retain_ref[pl.ds(pl.multiple_of(base + j * SEG, SEG), SEG), :]
        out = []
        for l in range(count):
            end, rate = carry[l]
            factor = kept * decays[l]
            value = src[rows, lanes_of(l)]
            end = factor * (value + end) if reverse else factor * end + value
            out.append((end, factor * rate))
        return tuple(out)

    start = tuple((jnp.zeros((SEG, 128), F32), jnp.ones((SEG, 128), F32)) for _ in range(count))
    ends = lax.fori_loop(0, steps, lap, start, unroll=4)
    return jnp.concatenate([e[0] for e in ends], axis=1), jnp.concatenate([e[1] for e in ends], axis=1)


def seg_starts(end, rate, entering, reverse):
    now = entering
    starts = [None] * SEG
    for k in range(SEG):
        s = SEG - 1 - k if reverse else k
        starts[s] = now
        now = end[s : s + 1] + rate[s : s + 1] * now
    return jnp.concatenate(starts, axis=0), now


def decay_tiles(decay_ref):
    width = decay_ref.shape[1]
    full = jnp.broadcast_to(decay_ref[...], (SEG, width))
    return [full[:, lanes_of(l)] for l in range(width // 128)]


def summary_kernel(x_ref, c_ref, w_ref, v_ref, scale_ref, decay_ref, retain_ref, out_ref, drive, scot, *, scaling):
    decays = decay_tiles(decay_ref)
    drive[...] = nn(x_ref[...], w_ref[...]) * scale_ref[...]
    scot[...] = nt(c_ref[...], v_ref[...]) * scaling
    zero = jnp.zeros(decay_ref.shape, F32)
    end, rate = scan_ends(drive, retain_ref, 0, decays, False)
    _, forward = seg_starts(end, rate, zero, False)
    back, _ = scan_ends(scot, retain_ref, 0, decays, True)
    _, backward = seg_starts(back, rate, zero, True)
    total = rate[0:1]
    for s in range(1, SEG):
        total = total * rate[s : s + 1]
    out_ref[...] = jnp.concatenate([total, forward, backward], axis=0)


def carries_kernel(sum_ref, fwd_ref, bwd_ref):
    blocks = sum_ref.shape[0]
    now = jnp.zeros_like(fwd_ref[0:1, :])
    for b in range(blocks):
        fwd_ref[b : b + 1, :] = now
        row = sum_ref[b]
        now = row[1:2] + row[0:1] * now
    now = jnp.zeros_like(now)
    for b in range(blocks - 1, -1, -1):
        bwd_ref[b : b + 1, :] = now
        row = sum_ref[b]
        now = row[2:3] + row[0:1] * now


def carries(table):
    shape = jax.ShapeDtypeStruct((table.shape[0], table.shape[2]), F32)
    return resident(carries_kernel, (shape, shape), (table,), "carries", scalars=0)


def collect(idx_ref, role, pieces, out_ref):
    for k, piece in enumerate(pieces):
        rows = piece.shape[0]
        at = pl.multiple_of(idx_ref[role, 1 + k] * rows, rows)
        out_ref[pl.ds(at, rows), :] = piece[...].astype(BF16)


def forward_kernel(idx_ref, *refs, given):
    total = sum(given)
    pieces = refs[:total]
    w_ref, scale_ref, decay_ref, retain_ref, enter_ref = refs[total : total + 5]
    outs = list(refs[total + 5 :])
    decays = decay_tiles(decay_ref)
    count = len(decays)
    drive = outs.pop()
    rows_all = drive.shape[0]
    steps = rows_all // SEG
    at_piece = 0
    for role, number in enumerate(given):
        mine = pieces[at_piece : at_piece + number]
        at_piece += number
        if number > 1:
            x_ref = outs.pop(0)
            collect(idx_ref, role, mine, x_ref)
        else:
            x_ref = mine[0]
        track_ref, low_ref = outs.pop(0), outs.pop(0)
        block = idx_ref[role, 0]
        base = block * rows_all
        drive[...] = nn(x_ref[...], w_ref[...]) * scale_ref[...]
        end, rate = scan_ends(drive, retain_ref, base, decays, False)
        start, _ = seg_starts(end, rate, enter_ref[pl.ds(block, 1), :], False)
        track_ref[0:SEG, :] = start

        def lap(j, before, base=base, track_ref=track_ref):
            at = pl.multiple_of(j * SEG, SEG)
            kept = retain_ref[pl.ds(pl.multiple_of(base + j * SEG, SEG), SEG), :]
            out = []
            for l in range(count):
                after = kept * decays[l] * before[l] + drive[pl.ds(at, SEG), lanes_of(l)]
                track_ref[pl.ds(pl.multiple_of(at + SEG, SEG), SEG), lanes_of(l)] = after
                out.append(after)
            return tuple(out)

        lax.fori_loop(0, steps, lap, tuple(start[:, lanes_of(l)] for l in range(count)), unroll=4)
        low_ref[...] = track_ref[SEG:, :].astype(BF16)


def backward_kernel(idx_ref, *refs, given, scaling):
    total = sum(given)
    roles = len(given)
    pieces = refs[:total]
    v_ref, scale_ref, decay_ref, retain_ref, enter_ref = refs[total : total + 5]
    tracks = refs[total + 5 : total + 5 + roles]
    outs = list(refs[total + 5 + roles :])
    decays = decay_tiles(decay_ref)
    count = len(decays)
    adjoint, scot = outs.pop(), outs.pop()
    rows_all = scot.shape[0]
    steps = rows_all // SEG
    at_piece = 0
    for role, number in enumerate(given):
        mine = pieces[at_piece : at_piece + number]
        at_piece += number
        if number > 1:
            x_ref = outs.pop(0)
            collect(idx_ref, role, mine, x_ref)
        else:
            x_ref = mine[0]
        scaled_ref, grad_ref = outs.pop(0), outs.pop(0)
        block = idx_ref[role, 0]
        base = block * rows_all
        scot[...] = nt(x_ref[...], v_ref[...]) * scaling
        end, rate = scan_ends(scot, retain_ref, base, decays, True)
        start, _ = seg_starts(end, rate, enter_ref[pl.ds(block, 1), :], True)

        def lap(k, carry, base=base, track_ref=tracks[role]):
            at = (steps - 1 - k) * SEG
            rows = pl.ds(pl.multiple_of(at, SEG), SEG)
            kept = retain_ref[pl.ds(pl.multiple_of(base + at, SEG), SEG), :]
            out = []
            for l in range(count):
                follow, grad = carry[l]
                here = scot[rows, lanes_of(l)] + follow
                adjoint[rows, lanes_of(l)] = here
                part = kept * here
                out.append((part * decays[l], grad + part * track_ref[rows, lanes_of(l)]))
            return tuple(out)

        begin = tuple((start[:, lanes_of(l)], jnp.zeros((SEG, 128), F32)) for l in range(count))
        done = lax.fori_loop(0, steps, lap, begin, unroll=4)
        scaled_ref[...] = (adjoint[...] * scale_ref[...]).astype(BF16)
        grad_ref[...] = jnp.sum(jnp.concatenate([d[1] for d in done], axis=1), axis=0, keepdims=True)


def block_call(kernel, idx, blocks, operands, backward, name):
    channels = operands[1].shape[1]
    rows, depth = sum(p.shape[0] for p in blocks[0]), blocks[0][0].shape[1]
    low = jax.ShapeDtypeStruct((rows, channels), BF16)
    shapes = []
    for pieces in blocks:
        shapes += [jax.ShapeDtypeStruct((rows, depth), BF16)] if len(pieces) > 1 else []
        if backward:
            shapes += [low, jax.ShapeDtypeStruct((1, channels), F32)]
        else:
            shapes += [jax.ShapeDtypeStruct((SEG + rows, channels), F32), low]
    out = list(resident(
        functools.partial(kernel, given=tuple(len(b) for b in blocks)), tuple(shapes),
        (idx, *[p for b in blocks for p in b], *operands), name,
        [pltpu.VMEM((rows, channels), F32)] * (2 if backward else 1),
    ))
    return [(out.pop(0) if len(b) > 1 else b[0], out.pop(0), out.pop(0)) for b in blocks]


def grad_kernel(idx_ref, *refs, factor):
    half = (len(refs) - 1) // 2
    width = refs[-1].shape[0]
    at = pl.ds(pl.multiple_of(idx_ref[0] * width, width), width)
    total = tn(refs[0][:, at], refs[half][...])
    for k in range(1, half):
        total += tn(refs[k][:, at], refs[half + k][...])
    refs[-1][...] = total * factor if factor is not None else total


def grad_rows(at, features, values, rows_out, factor, name):
    channels = values[0].shape[1]
    rows = values[0].shape[0]
    if rows_out % 128:
        total = sum(
            tn(lax.dynamic_slice_in_dim(x, at * rows_out, rows_out, axis=1), v) for x, v in zip(features, values, strict=True)
        )
        return total * factor if factor is not None else total
    return resident(
        functools.partial(grad_kernel, factor=factor), jax.ShapeDtypeStruct((rows_out, channels), F32),
        (jnp.reshape(at, (1,)).astype(jnp.int32), *features, *values), name,
    )


def row_grad_kernel(a_ref, w_ref, out_ref):
    parts, rows, width = out_ref.shape
    a = nn(order(rows, True), a_ref[...]).astype(BF16)
    for k in range(parts):
        out_ref[k] = nt(a, w_ref[width * k : width * (k + 1), :])


def row_grad(scaled, in_proj, parts):
    rows, channels = scaled.shape
    depth = in_proj.shape[0]
    return resident(
        row_grad_kernel, jax.ShapeDtypeStruct((parts, rows, depth // parts), F32), (scaled, in_proj), "row_grad",
        scalars=0,
    )


def after(x, *others):
    return lax.optimization_barrier((x, *others))[0]


def spread(piece):
    across = swap(piece, "chan", 2)
    return [piece, swap(piece, "chan", 1), across, swap(across, "chan", 1)]


def per_device(inputs, cotangent, in_proj, out_proj, decays, input_scale, retain):
    rows, depth = inputs.shape
    channels = in_proj.shape[1]
    devices, lanes = lax.axis_size("tm"), lax.axis_size("chan")
    scaling = 1.0 / math.sqrt(rows * devices)
    me, lane = lax.axis_index("tm"), lax.axis_index("chan")
    far = devices // 2
    groups = devices // 4
    steps = rows // SEG
    scale = input_scale[None, :]
    decay_row = decays[None, :]

    where = jnp.stack([lane % 2, lane]).astype(jnp.int32)
    x_own, x_half, x_quarter = prep(where, inputs, "prep_inputs")
    near_x = swap(x_half, "tm", 1)
    away_x = swap(x_quarter, "tm", far)
    c_own, c_half, c_quarter = prep(where, cotangent, "prep_cotangent")
    corner_x = swap(away_x, "tm", 1)
    x_pieces = [[near_x, swap(near_x, "chan", 1)], spread(away_x), spread(corner_x)]
    away_c = swap(after(c_quarter, away_x), "tm", far)
    near_c = swap(after(c_half, corner_x), "tm", 1)
    corner_c = swap(away_c, "tm", 1)
    c_pieces = [[near_c, swap(near_c, "chan", 1)], spread(away_c), spread(corner_c)]

    def ordered(r):
        return r.reshape(-1, SEG, steps).swapaxes(1, 2).reshape(-1, 1)

    ends = resident(
        functools.partial(summary_kernel, scaling=scaling), jax.ShapeDtypeStruct((3, channels), F32),
        (x_own, c_own, in_proj, out_proj, scale, decay_row, jnp.broadcast_to(ordered(retain), (rows, 128))), "summary",
        [pltpu.VMEM((rows, channels), F32)] * 2, scalars=0,
    )
    table = jnp.concatenate([after(ends, away_x, near_x), jnp.pad(retain, (0, channels - rows))[None, :]], axis=0)[None]
    bit = 1
    while bit < devices:
        other = swap(table, "tm", bit)
        low = (me & bit) == 0
        table = jnp.where(low, jnp.concatenate([table, other]), jnp.concatenate([other, table]))
        bit *= 2
    enter_fwd, enter_bwd = carries(table)
    retain_wide = jnp.broadcast_to(ordered(table[:, 3, :rows]), (devices * rows, 128))

    quarters = jnp.stack([lane, lane ^ 1, lane ^ 2, lane ^ 3])
    halves = jnp.stack([lane % 2, 1 - lane % 2, 0, 0])
    places = [jnp.zeros_like(halves), halves, quarters, quarters]
    blocks = [me, me ^ 1, me ^ far, me ^ far ^ 1]
    idx = [jnp.concatenate([b[None], p]).astype(jnp.int32) for b, p in zip(blocks, places, strict=True)]

    own, others = jnp.stack(idx[:1]), jnp.stack(idx[1:])
    shared = (in_proj, scale, decay_row, retain_wide, enter_fwd)
    forward = block_call(forward_kernel, own, [[x_own]], shared, False, "forward_own")
    forward += block_call(forward_kernel, others, x_pieces, shared, False, "forward_group")
    xs, tracks, lows = zip(*forward, strict=True)
    shared = (out_proj, scale, decay_row, retain_wide, enter_bwd)
    kernel = functools.partial(backward_kernel, scaling=scaling)
    backward = block_call(kernel, own, [[c_own]], (*shared, tracks[0]), True, "backward_own")
    backward += block_call(kernel, others[:2], c_pieces[:2], (*shared, *tracks[1:3]), True, "backward_near")
    backward += block_call(kernel, others[2:], c_pieces[2:], (*shared, *tracks[3:]), True, "backward_far")
    cs, scaled, grads = zip(*backward, strict=True)

    rows_out = depth // devices

    def reduced(features, values, factor, name):
        given = [swap(grad_rows(me ^ (2 * k), features, values, rows_out, factor, name), "tm", 2 * k) for k in range(1, groups)]
        mine = grad_rows(me, features, values, rows_out, factor, name)
        for part in given:
            mine += part
        return mine

    out_proj_grad = reduced(cs, lows, scaling, "out_grad")
    in_proj_grad = reduced(xs, scaled, None, "in_grad")

    decay_grad = (grads[0] + grads[1]) + (grads[2] + grads[3])
    bit = 2
    while bit < far:
        decay_grad += swap(decay_grad, "tm", bit)
        bit *= 2

    parts = row_grad(scaled[0], in_proj, lanes)
    bit = 1
    while bit < lanes:
        parts = parts.reshape(-1, 2, *parts.shape[1:])
        side = (lane // bit) % 2
        keep = lax.dynamic_index_in_dim(parts, side, axis=1, keepdims=False)
        give = lax.dynamic_index_in_dim(parts, 1 - side, axis=1, keepdims=False)
        parts = keep + swap(give, "chan", bit)
        bit *= 2
    input_grad = parts[0].astype(BF16)
    return (in_proj_grad, out_proj_grad, decay_grad[0], input_grad)


def solution(mesh):
    return jax.shard_map(
        per_device,
        mesh=mesh,
        in_specs=(
            P("tm", None),
            P("tm", None),
            P(None, "chan"),
            P("chan", None),
            P("chan"),
            P("chan"),
            P("tm"),
        ),
        out_specs=(P("tm", "chan"), P("tm", "chan"), P("chan"), P("tm", "chan")),
        check_vma=False,
    )
```

time: 771 us -> 201 us (0.26)
  waiting for transfers between devices: 301 us -> 99.3 us
  local copies, waits for them, and re-layouts: 213 us -> 30.6 us
  blocking collectives: 146 us -> 0 us
  other arithmetic: 64.4 us -> 9.07 us
  Pallas kernels: 0 us -> 37.6 us
  matrix products: 22.5 us -> 0 us
  starting transfers between devices: 0.12 us -> 21.7 us
  between operations: 14.9 us -> 1.23 us
    reduce_scatter x3 -> x0, waiting for transfers between devices: 301 us -> none  [the longest x1 152 us: per_device(): lax.psum_scatter(lax.dot_general(columns, scaled, (((0,), (0,)), ((), ())...]
    slice x108 -> x1, local copies, waits for them, and re-layouts: 156 us -> 0.03 us  [per_device(): table[:, 3, :rows]]
    all_gather x4 -> x0, blocking collectives: 124 us -> none  [prefix(): everything = jax.tree.map(lambda part: lax.all_gather(part, axis), x)]
    ppermute x0 -> x28, waiting for transfers between devices: none -> 99.3 us  [swap(): return lax.ppermute(x, axis, [(k, k ^ bit) for k in range(n)])]
    pallas_call x0 -> x14, Pallas kernels: none -> 37.6 us  [resident(): pl.pallas_call(kernel, out_shape=out_shape, in_specs=[SMEM] * scalars + [...]
    add x57 -> x5, other arithmetic: 42.7 us -> 6.85 us  [the longest x2 4.78 us: reduced(): mine += part]
    pad x56 -> x1, local copies, waits for them, and re-layouts: 34.4 us -> 0.68 us  [per_device(): jnp.pad(retain, (0, channels - rows))[None, :]]
    dot_general x5 -> x0, matrix products: 22.5 us -> none  [the longest x1 5.85 us: per_device(): lax.dot_general(columns, scaled, (((0,), (0,)), ((), ())), preferred_elem...]
  transfers between devices with their start and end apart: 3 -> 28, of which waited for: 2 -> 11; matrix products, arithmetic and copies ran while one was open for 2% -> 6% of each run, Pallas kernels for 0% -> 18%
where the time goes in v2:
time: 201 us; the launch traced here: 200 us
  waiting for transfers between devices  99.3 us (49%)
  Pallas kernels  37.6 us (19%)
  local copies, waits for them, and re-layouts  30.6 us (15%)
  starting transfers between devices  21.7 us (11%)
  other arithmetic  9.07 us (5%)
    ppermute x28, waiting for transfers between devices, swap(): return lax.ppermute(x, axis, [(k, k ^ bit) for k in range(n)])  99.3 us
    pallas_call x14, Pallas kernels, resident(): pl.pallas_call(kernel, out_shape=out_shape, in_specs=[SMEM] * scalars + [...  37.6 us
    unnamed x104, local copies, waits for them, and re-layouts  26.3 us
    ppermute x28, starting transfers between devices, swap(): return lax.ppermute(x, axis, [(k, k ^ bit) for k in range(n)])  21.7 us
    add x2, other arithmetic, reduced(): mine += part  4.78 us
  transfers between devices with their start and end apart: 28, of which 11 were waited for; matrix products, arithmetic and copies ran while one was open for 6% of the time, Pallas kernels for 18%

profile of v2, /device:TPU:0, one launch (start us, length us, event | category | flops | bytes accessed | tf_op | source)
XLA Modules:
  0.0 199.6 jit_solution(3967082284226525016)
XLA Ops:
  2.0 2.1 %prep_inputs.1 = (bf16[256,2048]{1,0:T(8,128)(2,1)S(1)}, f32[128,2048]{1,0:T(8,128)}, f32[64,2048]{1,0:T(8,128)S(1)}) custom-call(s32[2]{0:T(128)S(1)} %pad_add_fusion.2.idx_ref, bf16[256,2048]{1,0:T(8,128)(2,1)S(1)} %copy-done.38), custom_call_target="tpu_custom_call" | custom-call | tf_op jit(solution)/shard_map/prep_inputs/pallas_call | solution.py:47
  4.1 2.9 %collective-permute-start = (f32[128,2048]{1,0:T(8,128)}, f32[128,2048]{1,0:T(8,128)}, u32[]{:S(2)}, u32[]{:S(2)}) collective-permute-start(f32[128,2048]{1,0:T(8,128)} %get-tuple-element.38), channel_id=1, source_target_pairs={{0,4},{4,0},{8,12},{12,8},{16,20},{20,16},{24,28},{28,24},{1,5},{5... | collective-permute-start | bytes 3145736 | tf_op jit(solution)/shard_map/ppermute | solution.py:19
  7.0 2.6 %collective-permute-start.2 = (f32[64,2048]{1,0:T(8,128)S(1)}, f32[64,2048]{1,0:T(8,128)S(1)}, u32[]{:S(2)}, u32[]{:S(2)}) collective-permute-start(f32[64,2048]{1,0:T(8,128)S(1)} %get-tuple-element.39), channel_id=1, source_target_pairs={{0,16},{4,20},{8,24},{12,28},{16,0},{20,4},{24,8},{28,12},{1,17},{... | collective-permute-start | bytes 1572872 | tf_op jit(solution)/shard_map/ppermute | solution.py:19
  9.6 22.9 %collective-permute-done.2.refs_2_ = f32[64,2048]{1,0:T(8,128)S(1)} collective-permute-done((f32[64,2048]{1,0:T(8,128)S(1)}, f32[64,2048]{1,0:T(8,128)S(1)}, u32[]{:S(2)}, u32[]{:S(2)}) %collective-permute-start.2) | collective-permute-done | bytes 524320 | tf_op jit(solution)/shard_map/ppermute | solution.py:19
  33.0 1.6 collective-permute-start.4
  37.3 2.0 prep_cotangent.1
  40.5 2.2 %copy-done = bf16[2048,1024]{1,0:T(8,128)(2,1)S(1)} copy-done((bf16[2048,1024]{1,0:T(8,128)(2,1)S(1)}, bf16[2048,1024]{1,0:T(8,128)(2,1)}, u32[]{:S(2)}) %copy-start) | copy-done | bytes 4194328
  42.7 2.2 %copy-done.4 = bf16[1024,2048]{1,0:T(8,128)(2,1)S(1)} copy-done((bf16[1024,2048]{1,0:T(8,128)(2,1)S(1)}, bf16[1024,2048]{1,0:T(8,128)(2,1)}, u32[]{:S(2)}) %copy-start.4) | copy-done | bytes 4194328
  44.9 3.0 %summary.1 = f32[3,1024]{1,0:T(4,128)S(1)} custom-call(bf16[256,2048]{1,0:T(8,128)(2,1)S(1)} %get-tuple-element.37.x_ref.refs_0_, bf16[256,2048]{1,0:T(8,128)(2,1)S(1)} %get-tuple-element.40.c_ref.refs_0_, bf16[2048,1024]{1,0:T(8,128)(2,1)S(1)} %copy-done, bf16[1024,2048]{1,0:T(8,128)(2,1)S(1)} %copy-done.4, f32[1,1024]{1,0:T(1,128)S(1)} %bitcast.34, ...), custom_call_target="tpu_custom_call" | custom-call | tf_op jit(solution)/shard_map/summary/pallas_call | solution.py:47
  50.1 1.7 collective-permute-done.10
  51.8 4.1 %collective-permute-start.11 = (f32[2,4,1024]{2,1,0:T(4,128)S(1)}, f32[2,4,1024]{2,1,0:T(4,128)S(1)}, u32[]{:S(2)}, u32[]{:S(2)}) collective-permute-start(f32[2,4,1024]{2,1,0:T(4,128)S(1)} %maximum_select_fusion.2), channel_id=1, source_target_pairs={{0,8},{4,12},{8,0},{12,4},{16,24},{20,28},{24,16},{28,20},{1,9},{5... | collective-permute-start | bytes 98312 | tf_op jit(solution)/shard_map/ppermute | solution.py:19
  55.9 5.1 %collective-permute-done.11 = f32[2,4,1024]{2,1,0:T(4,128)S(1)} collective-permute-done((f32[2,4,1024]{2,1,0:T(4,128)S(1)}, f32[2,4,1024]{2,1,0:T(4,128)S(1)}, u32[]{:S(2)}, u32[]{:S(2)}) %collective-permute-start.11) | collective-permute-done | bytes 32800 | tf_op jit(solution)/shard_map/ppermute | solution.py:19
  61.0 13.7 %collective-permute-done.15.refs_2_ = f32[64,2048]{1,0:T(8,128)} collective-permute-done((f32[64,2048]{1,0:T(8,128)}, f32[64,2048]{1,0:T(8,128)}, u32[]{:S(2)}, u32[]{:S(2)}) %collective-permute-start.15) | collective-permute-done | bytes 524320 | tf_op jit(solution)/shard_map/ppermute | solution.py:19
  74.7 5.2 %collective-permute-done.12 = f32[4,4,1024]{2,1,0:T(4,128)S(1)} collective-permute-done((f32[4,4,1024]{2,1,0:T(4,128)S(1)}, f32[4,4,1024]{2,1,0:T(4,128)S(1)}, u32[]{:S(2)}, u32[]{:S(2)}) %collective-permute-start.12) | collective-permute-done | bytes 65568 | tf_op jit(solution)/shard_map/ppermute | solution.py:19
  84.2 2.2 %copy-done.1 = bf16[2048,1024]{1,0:T(8,128)(2,1)S(1)} copy-done((bf16[2048,1024]{1,0:T(8,128)(2,1)S(1)}, bf16[2048,1024]{1,0:T(8,128)(2,1)}, u32[]{:S(2)}) %copy-start.1) | copy-done | bytes 4194328
  86.4 2.3 %forward_own.1 = (f32[264,1024]{1,0:T(8,128)S(1)}, bf16[256,1024]{1,0:T(8,128)(2,1)S(1)}) custom-call(s32[1,5]{1,0:T(1,128)S(1)} %pad_bitcast_fusion.idx_ref, bf16[256,2048]{1,0:T(8,128)(2,1)S(1)} %get-tuple-element.37.x_ref.refs_0_, bf16[2048,1024]{1,0:T(8,128)(2,1)S(1)} %copy-done.1, f32[1,1024]{1,0:T(1,128)S(1)} %bitcast.35, f32[1,1024]{1,0:T(1,128)S(1)} %bitcast.41, ...), custom_call_target="tpu_custom_call" | custom-call | tf_op jit(solution)/shard_map/forward_own/pallas_call | solution.py:47
  88.7 2.4 %backward_own.1 = (bf16[256,1024]{1,0:T(8,128)(2,1)S(1)}, f32[1,1024]{1,0:T(1,128)S(1)}) custom-call(s32[1,5]{1,0:T(1,128)S(1)} %pad_bitcast_fusion.idx_ref, bf16[256,2048]{1,0:T(8,128)(2,1)S(1)} %get-tuple-element.40.c_ref.refs_0_, bf16[1024,2048]{1,0:T(8,128)(2,1)S(1)} %copy-done.5, f32[1,1024]{1,0:T(1,128)S(1)} %bitcast.36, f32[1,1024]{1,0:T(1,128)S(1)} %bitcast.42, ...), custom_call_target="tpu_custom_call" | custom-call | tf_op jit(solution)/shard_map/backward_own/pallas_call | solution.py:47
  92.9 3.7 %collective-permute-done.8.refs_8_ = f32[64,2048]{1,0:T(8,128)} collective-permute-done((f32[64,2048]{1,0:T(8,128)}, f32[64,2048]{1,0:T(8,128)}, u32[]{:S(2)}, u32[]{:S(2)}) %collective-permute-start.8) | collective-permute-done | bytes 524320 | tf_op jit(solution)/shard_map/ppermute | solution.py:19
  97.1 10.7 %collective-permute-done.17.refs_4_ = f32[64,2048]{1,0:T(8,128)} collective-permute-done((f32[64,2048]{1,0:T(8,128)}, f32[64,2048]{1,0:T(8,128)}, u32[]{:S(2)}, u32[]{:S(2)}) %collective-permute-start.17) | collective-permute-done | bytes 524320 | tf_op jit(solution)/shard_map/ppermute | solution.py:19
  109.4 7.2 %collective-permute-done.21.refs_2_ = f32[64,2048]{1,0:T(8,128)} collective-permute-done((f32[64,2048]{1,0:T(8,128)}, f32[64,2048]{1,0:T(8,128)}, u32[]{:S(2)}, u32[]{:S(2)}) %collective-permute-start.21) | collective-permute-done | bytes 524320 | tf_op jit(solution)/shard_map/ppermute | solution.py:19
  119.0 2.2 %copy-done.3 = bf16[2048,1024]{1,0:T(8,128)(2,1)S(1)} copy-done((bf16[2048,1024]{1,0:T(8,128)(2,1)S(1)}, bf16[2048,1024]{1,0:T(8,128)(2,1)}, u32[]{:S(2)}) %copy-start.3) | copy-done | bytes 4194328
  124.3 7.9 %forward_group.1 = (bf16[256,2048]{1,0:T(8,128)(2,1)S(1)}, f32[264,1024]{1,0:T(8,128)S(1)}, bf16[256,1024]{1,0:T(8,128)(2,1)S(1)}, bf16[256,2048]{1,0:T(8,128)(2...) custom-call(s32[3,5]{1,0:T(4,128)S(1)} %pad_add_fusion.idx_ref, ...), custom_call_target="tpu_custom_call" | custom-call | tf_op jit(solution)/shard_map/forward_group/pallas_call | solution.py:47
  132.3 4.5 %backward_far.1 = (bf16[256,2048]{1,0:T(8,128)(2,1)S(1)}, bf16[256,1024]{1,0:T(8,128)(2,1)S(1)}, f32[1,1024]{1,0:T(1,128)S(1)}) custom-call(s32[1,5]{1,0:T(1,128)S(1)} %bitcast.47, f32[64,2048]{1,0:T(8,128)} %collective-permute-done.19.refs_0_, f32[64,2048]{1,0:T(8,128)S(1)} %copy-done.45, f32[64,2048]{1,0:T(8,128)} %collective-permute-done.21.refs_2_, ...), custom_call_target="tpu_custom_call" | custom-call | tf_op jit(solution)/shard_map/backward_far/pallas_call | solution.py:47
  136.8 6.8 %backward_near.1 = (bf16[256,2048]{1,0:T(8,128)(2,1)S(1)}, bf16[256,1024]{1,0:T(8,128)(2,1)S(1)}, f32[1,1024]{1,0:T(1,128)S(1)}, bf16[256,2048]{1,0:T(8,128)(2,1...) custom-call(s32[2,5]{1,0:T(2,128)S(1)} %pad_add_fusion.1.idx_ref, ...), custom_call_target="tpu_custom_call" | custom-call | tf_op jit(solution)/shard_map/backward_near/pallas_call | solution.py:47
  143.8 2.0 %in_grad.3 = f32[256,1024]{1,0:T(8,128)} custom-call(s32[1]{0:T(128)} %bitcast.20.idx_ref, bf16[256,2048]{1,0:T(8,128)(2,1)S(1)} %get-tuple-element.37.x_ref.refs_0_, bf16[256,2048]{1,0:T(8,128)(2,1)S(1)} %get-tuple-element.43.refs_1_, bf16[256,2048]{1,0:T(8,128)(2,1)S(1)} %get-tuple-element.44.refs_2_, bf16[256,2048]{1,0:T(8,128)(2,1)S(1)} %get-tuple-element.45.refs_3_, ...), custom_call_target="tpu_custom_call" | custom-call | tf_op jit(solution)/shard_map/in_grad/pallas_call | solution.py:47
  146.0 1.7 out_grad.3
  147.8 1.9 collective-permute-start.24
  153.7 13.3 %collective-permute-done.27 = f32[1,256,512]{2,1,0:T(8,128)} collective-permute-done((f32[1,256,512]{2,1,0:T(8,128)}, f32[1,256,512]{2,1,0:T(8,128)}, u32[]{:S(2)}, u32[]{:S(2)}) %collective-permute-start.27) | collective-permute-done | bytes 524320 | tf_op jit(solution)/shard_map/ppermute | solution.py:19
  167.0 2.0 fusion
  178.8 15.3 %collective-permute-done.25 = f32[1,1024]{1,0:T(1,128)S(1)} collective-permute-done((f32[1,1024]{1,0:T(1,128)S(1)}, f32[1,1024]{1,0:T(1,128)S(1)}, u32[]{:S(2)}, u32[]{:S(2)}) %collective-permute-start.25) | collective-permute-done | bytes 4128 | tf_op jit(solution)/shard_map/ppermute | solution.py:19
  194.8 2.4 %add.57 = f32[256,1024]{1,0:T(8,128)} add(f32[256,1024]{1,0:T(8,128)S(1)} %in_grad.2, f32[256,1024]{1,0:T(8,128)} %collective-permute-done.23) | non-fusion elementwise | flops 262144 | bytes 3145728 | tf_op jit(solution)/shard_map/add | solution.py:382
  197.2 2.4 %add.58 = f32[256,1024]{1,0:T(8,128)} add(f32[256,1024]{1,0:T(8,128)S(1)} %out_grad.2, f32[256,1024]{1,0:T(8,128)} %collective-permute-done.24) | non-fusion elementwise | flops 262144 | bytes 3145728 | tf_op jit(solution)/shard_map/add | solution.py:382
  (172 shorter events, 36.3 us)
Async XLA Ops:
  0.6 39.9 %copy-start.48 = (f32[1024]{0:T(1024)S(1)}, f32[1024]{0:T(1024)}, u32[]{:S(2)}) copy-start(f32[1024]{0:T(1024)} %param.12) | copy-start | bytes 12292
  0.6 39.9 %copy-start.49 = (f32[1024]{0:T(1024)S(1)}, f32[1024]{0:T(1024)}, u32[]{:S(2)}) copy-start(f32[1024]{0:T(1024)} %param.11) | copy-start | bytes 12292
  4.1 43.8 %collective-permute-start = (f32[128,2048]{1,0:T(8,128)}, f32[128,2048]{1,0:T(8,128)}, u32[]{:S(2)}, u32[]{:S(2)}) collective-permute-start(f32[128,2048]{1,0:T(8,128)} %get-tuple-element.38), channel_id=1, source_target_pairs={{0,4},{4,0},{8,12},{12,8},{16,20},{20,16},{24,28},{28,24},{1,5},{5... | collective-permute-start | bytes 3145736 | tf_op jit(solution)/shard_map/ppermute | solution.py:19
  7.0 25.5 %collective-permute-start.2 = (f32[64,2048]{1,0:T(8,128)S(1)}, f32[64,2048]{1,0:T(8,128)S(1)}, u32[]{:S(2)}, u32[]{:S(2)}) collective-permute-start(f32[64,2048]{1,0:T(8,128)S(1)} %get-tuple-element.39), channel_id=1, source_target_pairs={{0,16},{4,20},{8,24},{12,28},{16,0},{20,4},{24,8},{28,12},{1,17},{... | collective-permute-start | bytes 1572872 | tf_op jit(solution)/shard_map/ppermute | solution.py:19
  32.6 17.0 %collective-permute-start.6 = (f32[64,2048]{1,0:T(8,128)S(1)}, f32[64,2048]{1,0:T(8,128)}, u32[]{:S(2)}, u32[]{:S(2)}) collective-permute-start(f32[64,2048]{1,0:T(8,128)S(1)} %collective-permute-done.2.refs_2_), channel_id=1, source_target_pairs={{0,4},{4,0},{8,12},{12,8},{16,20},{20,16},{24,28},{28,24},{1,5},{5... | collective-permute-start | bytes 1572872 | tf_op jit(solution)/shard_map/ppermute | solution.py:19
  33.0 17.0 %collective-permute-start.4 = (f32[64,2048]{1,0:T(8,128)S(1)}, f32[64,2048]{1,0:T(8,128)S(1)}, u32[]{:S(2)}, u32[]{:S(2)}) collective-permute-start(f32[64,2048]{1,0:T(8,128)S(1)} %collective-permute-done.2.refs_2_), channel_id=1, source_target_pairs={{0,2},{1,3},{2,0},{3,1},{4,6},{5,7},{6,4},{7,5},{8,10},{9,11},{10,... | collective-permute-start | bytes 1572872 | tf_op jit(solution)/shard_map/ppermute | solution.py:19
  34.6 17.2 %collective-permute-start.3 = (f32[64,2048]{1,0:T(8,128)S(1)}, f32[64,2048]{1,0:T(8,128)}, u32[]{:S(2)}, u32[]{:S(2)}) collective-permute-start(f32[64,2048]{1,0:T(8,128)S(1)} %collective-permute-done.2.refs_2_), channel_id=1, source_target_pairs={{0,1},{1,0},{2,3},{3,2},{4,5},{5,4},{6,7},{7,6},{8,9},{9,8},{10,11... | collective-permute-start | bytes 1572872 | tf_op jit(solution)/shard_map/ppermute | solution.py:19
  47.9 26.9 %collective-permute-start.15 = (f32[64,2048]{1,0:T(8,128)}, f32[64,2048]{1,0:T(8,128)}, u32[]{:S(2)}, u32[]{:S(2)}) collective-permute-start(f32[64,2048]{1,0:T(8,128)} %get-tuple-element.52), channel_id=1, source_target_pairs={{0,16},{4,20},{8,24},{12,28},{16,0},{20,4},{24,8},{28,12},{1,17},{... | collective-permute-start | bytes 1572872 | tf_op jit(solution)/shard_map/ppermute | solution.py:19
  48.0 3.8 %collective-permute-start.10 = (f32[1,4,1024]{2,1,0:T(4,128)S(1)}, f32[1,4,1024]{2,1,0:T(4,128)S(1)}, u32[]{:S(2)}, u32[]{:S(2)}) collective-permute-start(f32[1,4,1024]{2,1,0:T(4,128)S(1)} %maximum_bitcast_fusion), channel_id=1, source_target_pairs={{0,4},{4,0},{8,12},{12,8},{16,20},{20,16},{24,28},{28,24},{1,5},{5... | collective-permute-start | bytes 49160 | tf_op jit(solution)/shard_map/ppermute | solution.py:19
  49.5 58.2 %collective-permute-start.13 = (f32[128,2048]{1,0:T(8,128)}, f32[128,2048]{1,0:T(8,128)}, u32[]{:S(2)}, u32[]{:S(2)}) collective-permute-start(f32[128,2048]{1,0:T(8,128)} %copy-done.50), channel_id=1, source_target_pairs={{0,4},{4,0},{8,12},{12,8},{16,20},{20,16},{24,28},{28,24},{1,5},{5... | collective-permute-start | bytes 3145736 | tf_op jit(solution)/shard_map/ppermute | solution.py:19
  50.1 33.6 %copy-start.42 = (f32[64,2048]{1,0:T(8,128)}, f32[64,2048]{1,0:T(8,128)S(1)}, u32[]{:S(2)}) copy-start(f32[64,2048]{1,0:T(8,128)S(1)} %collective-permute-done.4.refs_4_) | copy-start | bytes 1572868
  50.1 31.8 %collective-permute-start.7 = (f32[64,2048]{1,0:T(8,128)}, f32[64,2048]{1,0:T(8,128)}, u32[]{:S(2)}, u32[]{:S(2)}) collective-permute-start(f32[64,2048]{1,0:T(8,128)} %collective-permute-done.6.refs_6_), channel_id=1, source_target_pairs={{0,1},{1,0},{2,3},{3,2},{4,5},{5,4},{6,7},{7,6},{8,9},{9,8},{10,11... | collective-permute-start | bytes 1572872 | tf_op jit(solution)/shard_map/ppermute | solution.py:19
  51.8 29.6 %collective-permute-start.5 = (f32[64,2048]{1,0:T(8,128)S(1)}, f32[64,2048]{1,0:T(8,128)}, u32[]{:S(2)}, u32[]{:S(2)}) collective-permute-start(f32[64,2048]{1,0:T(8,128)S(1)} %collective-permute-done.4.refs_4_), channel_id=1, source_target_pairs={{0,1},{1,0},{2,3},{3,2},{4,5},{5,4},{6,7},{7,6},{8,9},{9,8},{10,11... | collective-permute-start | bytes 1572872 | tf_op jit(solution)/shard_map/ppermute | solution.py:19
  51.8 9.2 %collective-permute-start.11 = (f32[2,4,1024]{2,1,0:T(4,128)S(1)}, f32[2,4,1024]{2,1,0:T(4,128)S(1)}, u32[]{:S(2)}, u32[]{:S(2)}) collective-permute-start(f32[2,4,1024]{2,1,0:T(4,128)S(1)} %maximum_select_fusion.2), channel_id=1, source_target_pairs={{0,8},{4,12},{8,0},{12,4},{16,24},{20,28},{24,16},{28,20},{1,9},{5... | collective-permute-start | bytes 98312 | tf_op jit(solution)/shard_map/ppermute | solution.py:19
  61.0 48.3 %collective-permute-start.1 = (f32[128,2048]{1,0:T(8,128)}, f32[128,2048]{1,0:T(8,128)}, u32[]{:S(2)}, u32[]{:S(2)}) collective-permute-start(f32[128,2048]{1,0:T(8,128)} %collective-permute-done.refs_0_), channel_id=1, source_target_pairs={{0,1},{1,0},{2,3},{3,2},{4,5},{5,4},{6,7},{7,6},{8,9},{9,8},{10,11... | collective-permute-start | bytes 3145736 | tf_op jit(solution)/shard_map/ppermute | solution.py:19
  74.7 5.2 %collective-permute-start.12 = (f32[4,4,1024]{2,1,0:T(4,128)S(1)}, f32[4,4,1024]{2,1,0:T(4,128)S(1)}, u32[]{:S(2)}, u32[]{:S(2)}) collective-permute-start(f32[4,4,1024]{2,1,0:T(4,128)S(1)} %maximum_select_fusion.1), channel_id=1, source_target_pairs={{0,16},{4,20},{8,24},{12,28},{16,0},{20,4},{24,8},{28,12},{1,17},{... | collective-permute-start | bytes 196616 | tf_op jit(solution)/shard_map/ppermute | solution.py:19
  79.9 13.0 %collective-permute-start.19 = (f32[64,2048]{1,0:T(8,128)}, f32[64,2048]{1,0:T(8,128)}, u32[]{:S(2)}, u32[]{:S(2)}) collective-permute-start(f32[64,2048]{1,0:T(8,128)} %collective-permute-done.15.refs_2_), channel_id=1, source_target_pairs={{0,4},{4,0},{8,12},{12,8},{16,20},{20,16},{24,28},{28,24},{1,5},{5... | collective-permute-start | bytes 1572872 | tf_op jit(solution)/shard_map/ppermute | solution.py:19
  81.4 15.2 %collective-permute-start.8 = (f32[64,2048]{1,0:T(8,128)}, f32[64,2048]{1,0:T(8,128)}, u32[]{:S(2)}, u32[]{:S(2)}) collective-permute-start(f32[64,2048]{1,0:T(8,128)} %collective-permute-done.6.refs_6_), channel_id=1, source_target_pairs={{0,2},{1,3},{2,0},{3,1},{4,6},{5,7},{6,4},{7,5},{8,10},{9,11},{10,... | collective-permute-start | bytes 1572872 | tf_op jit(solution)/shard_map/ppermute | solution.py:19
  81.9 25.9 %collective-permute-start.17 = (f32[64,2048]{1,0:T(8,128)}, f32[64,2048]{1,0:T(8,128)}, u32[]{:S(2)}, u32[]{:S(2)}) collective-permute-start(f32[64,2048]{1,0:T(8,128)} %collective-permute-done.15.refs_2_), channel_id=1, source_target_pairs={{0,2},{1,3},{2,0},{3,1},{4,6},{5,7},{6,4},{7,5},{8,10},{9,11},{10,... | collective-permute-start | bytes 1572872 | tf_op jit(solution)/shard_map/ppermute | solution.py:19
  92.9 25.0 %collective-permute-start.20 = (f32[64,2048]{1,0:T(8,128)}, f32[64,2048]{1,0:T(8,128)S(1)}, u32[]{:S(2)}, u32[]{:S(2)}) collective-permute-start(f32[64,2048]{1,0:T(8,128)} %collective-permute-done.19.refs_0_), channel_id=1, source_target_pairs={{0,1},{1,0},{2,3},{3,2},{4,5},{5,4},{6,7},{7,6},{8,9},{9,8},{10,11... | collective-permute-start | bytes 1572872 | tf_op jit(solution)/shard_map/ppermute | solution.py:19
  96.5 20.0 %collective-permute-start.21 = (f32[64,2048]{1,0:T(8,128)}, f32[64,2048]{1,0:T(8,128)}, u32[]{:S(2)}, u32[]{:S(2)}) collective-permute-start(f32[64,2048]{1,0:T(8,128)} %collective-permute-done.19.refs_0_), channel_id=1, source_target_pairs={{0,2},{1,3},{2,0},{3,1},{4,6},{5,7},{6,4},{7,5},{8,10},{9,11},{10,... | collective-permute-start | bytes 1572872 | tf_op jit(solution)/shard_map/ppermute | solution.py:19
  107.8 8.8 %collective-permute-start.9 = (f32[64,2048]{1,0:T(8,128)}, f32[64,2048]{1,0:T(8,128)S(1)}, u32[]{:S(2)}, u32[]{:S(2)}) collective-permute-start(f32[64,2048]{1,0:T(8,128)} %collective-permute-done.8.refs_8_), channel_id=1, source_target_pairs={{0,1},{1,0},{2,3},{3,2},{4,5},{5,4},{6,7},{7,6},{8,9},{9,8},{10,11... | collective-permute-start | bytes 1572872 | tf_op jit(solution)/shard_map/ppermute | solution.py:19
  107.8 29.0 %collective-permute-start.14 = (f32[128,2048]{1,0:T(8,128)}, f32[128,2048]{1,0:T(8,128)}, u32[]{:S(2)}, u32[]{:S(2)}) collective-permute-start(f32[128,2048]{1,0:T(8,128)} %collective-permute-done.13.refs_0_), channel_id=1, source_target_pairs={{0,1},{1,0},{2,3},{3,2},{4,5},{5,4},{6,7},{7,6},{8,9},{9,8},{10,11... | collective-permute-start | bytes 3145736 | tf_op jit(solution)/shard_map/ppermute | solution.py:19
  109.3 40.3 %collective-permute-start.26 = (f32[2,256,512]{2,1,0:T(8,128)}, f32[2,256,512]{2,1,0:T(8,128)}, u32[]{:S(2)}, u32[]{:S(2)}) collective-permute-start(f32[2,256,512]{2,1,0:T(8,128)} %dynamic-slice_bitcast_fusion), channel_id=1, source_target_pairs={{0,1},{1,0},{2,3},{3,2},{4,5},{5,4},{6,7},{7,6},{8,9},{9,8},{10,11... | collective-permute-start | bytes 3145736 | tf_op jit(solution)/shard_map/ppermute | solution.py:19
  116.6 15.7 %collective-permute-start.22 = (f32[64,2048]{1,0:T(8,128)}, f32[64,2048]{1,0:T(8,128)}, u32[]{:S(2)}, u32[]{:S(2)}) collective-permute-start(f32[64,2048]{1,0:T(8,128)} %collective-permute-done.21.refs_2_), channel_id=1, source_target_pairs={{0,1},{1,0},{2,3},{3,2},{4,5},{5,4},{6,7},{7,6},{8,9},{9,8},{10,11... | collective-permute-start | bytes 1572872 | tf_op jit(solution)/shard_map/ppermute | solution.py:19
  117.4 19.4 %collective-permute-start.16 = (f32[64,2048]{1,0:T(8,128)}, f32[64,2048]{1,0:T(8,128)}, u32[]{:S(2)}, u32[]{:S(2)}) collective-permute-start(f32[64,2048]{1,0:T(8,128)} %collective-permute-done.15.refs_2_), channel_id=1, source_target_pairs={{0,1},{1,0},{2,3},{3,2},{4,5},{5,4},{6,7},{7,6},{8,9},{9,8},{10,11... | collective-permute-start | bytes 1572872 | tf_op jit(solution)/shard_map/ppermute | solution.py:19
  118.7 18.1 %collective-permute-start.18 = (f32[64,2048]{1,0:T(8,128)}, f32[64,2048]{1,0:T(8,128)}, u32[]{:S(2)}, u32[]{:S(2)}) collective-permute-start(f32[64,2048]{1,0:T(8,128)} %collective-permute-done.17.refs_4_), channel_id=1, source_target_pairs={{0,1},{1,0},{2,3},{3,2},{4,5},{5,4},{6,7},{7,6},{8,9},{9,8},{10,11... | collective-permute-start | bytes 1572872 | tf_op jit(solution)/shard_map/ppermute | solution.py:19
  145.8 49.0 %collective-permute-start.23 = (f32[256,1024]{1,0:T(8,128)}, f32[256,1024]{1,0:T(8,128)}, u32[]{:S(2)}, u32[]{:S(2)}) collective-permute-start(f32[256,1024]{1,0:T(8,128)} %in_grad.3), channel_id=1, source_target_pairs={{0,8},{4,12},{8,0},{12,4},{16,24},{20,28},{24,16},{28,20},{1,9},{5... | collective-permute-start | bytes 3145736 | tf_op jit(solution)/shard_map/ppermute | solution.py:19
  147.8 21.2 %copy-start.11 = (bf16[256,1024]{1,0:T(8,128)(2,1)S(1)}, bf16[256,1024]{1,0:T(8,128)(2,1)}, u32[]{:S(2)}) copy-start(bf16[256,1024]{1,0:T(8,128)(2,1)} %copy-done.9) | copy-start | bytes 1572868
  147.8 49.4 %collective-permute-start.24 = (f32[256,1024]{1,0:T(8,128)}, f32[256,1024]{1,0:T(8,128)}, u32[]{:S(2)}, u32[]{:S(2)}) collective-permute-start(f32[256,1024]{1,0:T(8,128)} %out_grad.3), channel_id=1, source_target_pairs={{0,8},{4,12},{8,0},{12,4},{16,24},{20,28},{24,16},{28,20},{1,9},{5... | collective-permute-start | bytes 3145736 | tf_op jit(solution)/shard_map/ppermute | solution.py:19
  152.9 14.1 %collective-permute-start.27 = (f32[1,256,512]{2,1,0:T(8,128)}, f32[1,256,512]{2,1,0:T(8,128)}, u32[]{:S(2)}, u32[]{:S(2)}) collective-permute-start(f32[1,256,512]{2,1,0:T(8,128)} %constant_dynamic-slice_fusion), channel_id=1, source_target_pairs={{0,2},{1,3},{2,0},{3,1},{4,6},{5,7},{6,4},{7,5},{8,10},{9,11},{10,... | collective-permute-start | bytes 1572872 | tf_op jit(solution)/shard_map/ppermute | solution.py:19
  153.4 40.8 %collective-permute-start.25 = (f32[1,1024]{1,0:T(1,128)S(1)}, f32[1,1024]{1,0:T(1,128)S(1)}, u32[]{:S(2)}, u32[]{:S(2)}) collective-permute-start(f32[1,1024]{1,0:T(1,128)S(1)} %add_add_fusion), channel_id=1, source_target_pairs={{0,8},{4,12},{8,0},{12,4},{16,24},{20,28},{24,16},{28,20},{1,9},{5... | collective-permute-start | bytes 12296 | tf_op jit(solution)/shard_map/ppermute | solution.py:19
  (48 other events, 204.7 us)

commit v3 on v2

v3 whole, which is shorter than its diff:
```python
import functools
import math

import jax
import jax.numpy as jnp
from jax import lax
from jax.experimental import pallas as pl
from jax.experimental.pallas import tpu as pltpu
from jax.sharding import PartitionSpec as P

F32 = jnp.float32
BF16 = jnp.bfloat16
SEG = 8
VMEM_LIMIT = 12 * 1024 * 1024


def swap(x, axis, bit):
    n = lax.axis_size(axis)
    return lax.ppermute(x, axis, [(k, k ^ bit) for k in range(n)])


def nn(a, b):
    return lax.dot_general(a, b, (((1,), (0,)), ((), ())), preferred_element_type=F32)


def nt(a, b):
    return lax.dot_general(a, b, (((1,), (1,)), ((), ())), preferred_element_type=F32)


def tn(a, b):
    return lax.dot_general(a, b, (((0,), (0,)), ((), ())), preferred_element_type=F32)


def order(rows, transpose=False):
    steps = rows // SEG
    r = lax.broadcasted_iota(jnp.int32, (rows, rows), 1 if transpose else 0)
    t = lax.broadcasted_iota(jnp.int32, (rows, rows), 0 if transpose else 1)
    return ((r % SEG) * steps + r // SEG == t).astype(F32).astype(BF16)


VMEM = pl.BlockSpec(memory_space=pltpu.VMEM)
SMEM = pl.BlockSpec(memory_space=pltpu.SMEM)


ANY = pl.BlockSpec(memory_space=pltpu.HBM)


def resident(kernel, out_shape, operands, name, scratch=(), scalars=1, anywhere=0, out_specs=None):
    return pl.pallas_call(
        kernel,
        out_shape=out_shape,
        in_specs=[SMEM] * scalars + [VMEM] * (len(operands) - scalars - anywhere) + [ANY] * anywhere,
        out_specs=jax.tree.map(lambda _: VMEM, out_shape) if out_specs is None else out_specs,
        scratch_shapes=scratch,
        compiler_params=pltpu.CompilerParams(vmem_limit_bytes=VMEM_LIMIT),
        cost_estimate=pl.CostEstimate(flops=0, transcendentals=0, bytes_accessed=0),
        name=name,
    )(*operands)


def prep_kernel(idx_ref, x_ref, p_ref, *refs, parts):
    full = refs[-1]
    rows, depth = x_ref.shape
    full[...] = nn(order(rows), x_ref[...])
    p_ref[...] = full[...].astype(BF16)
    half, quarter, width = rows // 2, rows // 4, depth // parts
    for k in range(parts):
        near = pl.ds(pl.multiple_of(idx_ref[2 + k] * width, width), width)
        away = pl.ds(pl.multiple_of(idx_ref[2 + parts - 1 - k] * width, width), width)
        refs[2 * k][...] = full[pl.ds(pl.multiple_of(idx_ref[0] * half, half), half), near]
        refs[2 * k + 1][...] = full[pl.ds(pl.multiple_of(idx_ref[1] * quarter, quarter), quarter), away]


def prep(idx, x, parts, name):
    rows, depth = x.shape
    shapes = [jax.ShapeDtypeStruct((rows, depth), BF16)]
    for _ in range(parts):
        shapes.append(jax.ShapeDtypeStruct((rows // 2, depth // parts), F32))
        shapes.append(jax.ShapeDtypeStruct((rows // 4, depth // parts), F32))
    kernel = functools.partial(prep_kernel, parts=parts)
    return resident(kernel, tuple(shapes), (idx, x), name, [pltpu.VMEM((rows, depth), F32)])


def pack_kernel(*refs):
    *pieces, out_ref, sems = refs
    copies, at = [], 0
    for k, ref in enumerate(pieces):
        copies.append(pltpu.make_async_copy(ref, out_ref.at[pl.ds(at, ref.shape[0]), :], sems.at[k]))
        at += ref.shape[0]
    for copy in copies:
        copy.start()
    for copy in copies:
        copy.wait()


def pack(pieces, name):
    shape = jax.ShapeDtypeStruct((sum(p.shape[0] for p in pieces), pieces[0].shape[1]), F32)
    return resident(pack_kernel, shape, tuple(pieces), name, [pltpu.SemaphoreType.DMA((len(pieces),))], scalars=0, anywhere=len(pieces))


def lanes_of(l):
    return slice(128 * l, 128 * (l + 1))


def scan_ends(src, retain_ref, base, decays, reverse):
    count, steps = src.shape[1] // 128, src.shape[0] // SEG

    def lap(k, carry):
        j = steps - 1 - k if reverse else k
        rows = pl.ds(pl.multiple_of(j * SEG, SEG), SEG)
        kept = retain_ref[pl.ds(pl.multiple_of(base + j * SEG, SEG), SEG), :]
        out = []
        for l in range(count):
            end, rate = carry[l]
            factor = kept * decays[l]
            value = src[rows, lanes_of(l)]
            end = factor * (value + end) if reverse else factor * end + value
            out.append((end, factor * rate))
        return tuple(out)

    start = tuple((jnp.zeros((SEG, 128), F32), jnp.ones((SEG, 128), F32)) for _ in range(count))
    ends = lax.fori_loop(0, steps, lap, start, unroll=4)
    return jnp.concatenate([e[0] for e in ends], axis=1), jnp.concatenate([e[1] for e in ends], axis=1)


def seg_starts(end, rate, entering, reverse):
    now = entering
    starts = [None] * SEG
    for k in range(SEG):
        s = SEG - 1 - k if reverse else k
        starts[s] = now
        now = end[s : s + 1] + rate[s : s + 1] * now
    return jnp.concatenate(starts, axis=0), now


def decay_tiles(decay_ref):
    width = decay_ref.shape[1]
    full = jnp.broadcast_to(decay_ref[...], (SEG, width))
    return [full[:, lanes_of(l)] for l in range(width // 128)]


def summary_kernel(x_ref, c_ref, w_ref, v_ref, scale_ref, decay_ref, retain_ref, out_ref, drive, scot, *, scaling):
    decays = decay_tiles(decay_ref)
    drive[...] = nn(x_ref[...], w_ref[...]) * scale_ref[...]
    scot[...] = nt(c_ref[...], v_ref[...]) * scaling
    zero = jnp.zeros(decay_ref.shape, F32)
    end, rate = scan_ends(drive, retain_ref, 0, decays, False)
    _, forward = seg_starts(end, rate, zero, False)
    back, _ = scan_ends(scot, retain_ref, 0, decays, True)
    _, backward = seg_starts(back, rate, zero, True)
    total = rate[0:1]
    for s in range(1, SEG):
        total = total * rate[s : s + 1]
    out_ref[...] = jnp.concatenate([total, forward, backward], axis=0)


def carries_kernel(idx_ref, sum_ref, fwd_ref, bwd_ref, retain_ref):
    blocks = sum_ref.shape[0]
    far = blocks // 2

    def row(b):
        away = idx_ref[0] ^ b
        top = away // far
        low = (away % 2) ^ top
        middle = ((away // 2) % (far // 2)) ^ low
        return sum_ref[middle + (far // 2) * low + far * top]

    now = jnp.zeros_like(fwd_ref[0:1, :])
    for b in range(blocks):
        fwd_ref[b : b + 1, :] = now
        ends = row(b)
        retain_ref[b : b + 1, :] = ends[3:4]
        now = ends[1:2] + ends[0:1] * now
    now = jnp.zeros_like(now)
    for b in range(blocks - 1, -1, -1):
        bwd_ref[b : b + 1, :] = now
        ends = row(b)
        now = ends[2:3] + ends[0:1] * now


def carries(me, table):
    shape = jax.ShapeDtypeStruct((table.shape[0], table.shape[2]), F32)
    return resident(carries_kernel, (shape,) * 3, (me, table), "carries")


def reach(devices):
    return [1 << k for k in range(1, devices.bit_length() - 2)] + [3, devices // 2 + 1]


def collect_kernel(idx_ref, *refs, layout):
    count = len(layout)
    outs = refs[count : count + 3]
    held, sems = refs[count + 3], refs[count + 4]
    copies, at = [], 0
    for k, ref in enumerate(refs[:count]):
        copies.append(pltpu.make_async_copy(ref, held.at[pl.ds(at, ref.shape[0]), :], sems.at[k]))
        at += ref.shape[0]
    for copy in copies:
        copy.start()
    start = 0
    for copy, parts in zip(copies, layout, strict=True):
        copy.wait()
        for role, slot, rows in parts:
            at = pl.multiple_of(idx_ref[slot] * rows, rows)
            outs[role][pl.ds(at, rows), :] = held[start : start + rows, :].astype(BF16)
            start += rows


def collected(place, pieces, name):
    rows = sum(part[2] for _, parts in pieces for part in parts)
    depth = pieces[0][0].shape[1]
    shape = jax.ShapeDtypeStruct((rows // 3, depth), BF16)
    kernel = functools.partial(collect_kernel, layout=[parts for _, parts in pieces])
    scratch = [pltpu.VMEM((rows, depth), F32), pltpu.SemaphoreType.DMA((len(pieces),))]
    return list(resident(kernel, (shape,) * 3, (place, *[array for array, _ in pieces]), name, scratch, anywhere=len(pieces)))


def forward_kernel(idx_ref, *refs, roles):
    xs = refs[:roles]
    w_ref, scale_ref, decay_ref, retain_ref, enter_ref = refs[roles : roles + 5]
    outs = refs[roles + 5 : -3]
    drive, held, sems = refs[-3:]
    copies = []
    decays = decay_tiles(decay_ref)
    count = len(decays)
    rows_all = drive.shape[0]
    steps = rows_all // SEG
    for role in range(roles):
        track_ref, low_ref = held.at[role], outs[2 * role + 1]
        block = idx_ref[role]
        base = block * rows_all
        drive[...] = nn(xs[role][...], w_ref[...]) * scale_ref[...]
        end, rate = scan_ends(drive, retain_ref, base, decays, False)
        start, _ = seg_starts(end, rate, enter_ref[pl.ds(block, 1), :], False)
        track_ref[0:SEG, :] = start

        def lap(j, before, base=base, track_ref=track_ref):
            at = pl.multiple_of(j * SEG, SEG)
            kept = retain_ref[pl.ds(pl.multiple_of(base + j * SEG, SEG), SEG), :]
            out = []
            for l in range(count):
                now = kept * decays[l] * before[l] + drive[pl.ds(at, SEG), lanes_of(l)]
                track_ref[pl.ds(pl.multiple_of(at + SEG, SEG), SEG), lanes_of(l)] = now
                out.append(now)
            return tuple(out)

        lax.fori_loop(0, steps, lap, tuple(start[:, lanes_of(l)] for l in range(count)), unroll=4)
        copies.append(pltpu.make_async_copy(track_ref, outs[2 * role], sems.at[role]))
        copies[-1].start()
        low_ref[...] = track_ref[SEG:, :].astype(BF16)
    for copy in copies:
        copy.wait()


def backward_kernel(idx_ref, side_ref, *refs, roles, parts, scaling):
    cs = refs[: roles * parts]
    v_ref, scale_ref, decay_ref, retain_ref, enter_ref = refs[roles * parts : roles * parts + 5]
    tracks = refs[roles * parts + 5 : roles * parts + 5 + roles]
    outs = refs[roles * parts + 5 + roles : -4]
    scot, adjoint, held, sems = refs[-4:]
    copies = [pltpu.make_async_copy(track, held.at[k], sems.at[k]) for k, track in enumerate(tracks)]
    for copy in copies:
        copy.start()
    decays = decay_tiles(decay_ref)
    count = len(decays)
    rows_all = scot.shape[0]
    steps = rows_all // SEG
    width = v_ref.shape[1] // parts
    for role in range(roles):
        scaled_ref, grad_ref = outs[2 * role : 2 * role + 2]
        block = idx_ref[role]
        base = block * rows_all
        if parts == 1:
            scot[...] = nt(cs[role][...], v_ref[...]) * scaling
        else:
            total = None
            for k in range(parts):
                cols = pl.ds(pl.multiple_of(side_ref[k] * width, width), width)
                part = nt(cs[parts * role + k][...], v_ref[:, cols])
                total = part if total is None else total + part
            scot[...] = total * scaling
        end, rate = scan_ends(scot, retain_ref, base, decays, True)
        start, _ = seg_starts(end, rate, enter_ref[pl.ds(block, 1), :], True)

        copies[role].wait()

        def lap(k, carry, base=base, track_ref=held.at[role]):
            at = (steps - 1 - k) * SEG
            rows = pl.ds(pl.multiple_of(at, SEG), SEG)
            kept = retain_ref[pl.ds(pl.multiple_of(base + at, SEG), SEG), :]
            out = []
            for l in range(count):
                follow, grad = carry[l]
                here = scot[rows, lanes_of(l)] + follow
                adjoint[rows, lanes_of(l)] = here
                part = kept * here
                out.append((part * decays[l], grad + part * track_ref[rows, lanes_of(l)]))
            return tuple(out)

        begin = tuple((start[:, lanes_of(l)], jnp.zeros((SEG, 128), F32)) for l in range(count))
        done = lax.fori_loop(0, steps, lap, begin, unroll=4)
        scaled_ref[...] = (adjoint[...] * scale_ref[...]).astype(BF16)
        grad_ref[...] = jnp.sum(jnp.concatenate([d[1] for d in done], axis=1), axis=0, keepdims=True)


def forward_call(blocks, xs, operands, name):
    channels = operands[1].shape[1]
    rows, roles = xs[0].shape[0], len(xs)
    shapes = (jax.ShapeDtypeStruct((SEG + rows, channels), F32), jax.ShapeDtypeStruct((rows, channels), BF16)) * roles
    out = resident(
        functools.partial(forward_kernel, roles=roles), shapes, (blocks, *xs, *operands), name,
        [
            pltpu.VMEM((rows, channels), F32),
            pltpu.VMEM((roles, SEG + rows, channels), F32),
            pltpu.SemaphoreType.DMA((roles,)),
        ],
        out_specs=(ANY, VMEM) * roles,
    )
    return list(out[::2]), list(out[1::2])


def backward_call(blocks, sides, cs, operands, tracks, scaling, name):
    channels = operands[1].shape[1]
    rows, roles = cs[0][0].shape[0], len(cs)
    kernel = functools.partial(backward_kernel, roles=roles, parts=len(cs[0]), scaling=scaling)
    shapes = (jax.ShapeDtypeStruct((rows, channels), BF16), jax.ShapeDtypeStruct((1, channels), F32)) * roles
    out = resident(
        kernel, shapes, (blocks, sides, *[part for c in cs for part in c], *operands, *tracks), name,
        [pltpu.VMEM((rows, channels), F32)] * 2
        + [pltpu.VMEM((roles, *tracks[0].shape), F32), pltpu.SemaphoreType.DMA((roles,))],
        scalars=2, anywhere=roles,
    )
    return list(out[::2]), list(out[1::2])


def grad_kernel(idx_ref, *refs, factor):
    half = (len(refs) - 1) // 2
    width = refs[-1].shape[0]
    at = pl.ds(pl.multiple_of(idx_ref[0] * width, width), width)
    total = tn(refs[0][:, at], refs[half][...])
    for k in range(1, half):
        total += tn(refs[k][:, at], refs[half + k][...])
    refs[-1][...] = total * factor if factor is not None else total


def grad_rows(at, features, values, rows_out, factor, name):
    channels = values[0].shape[1]
    rows = values[0].shape[0]
    if rows_out % 128:
        total = sum(
            tn(lax.dynamic_slice_in_dim(x, at * rows_out, rows_out, axis=1), v) for x, v in zip(features, values, strict=True)
        )
        return total * factor if factor is not None else total
    return resident(
        functools.partial(grad_kernel, factor=factor), jax.ShapeDtypeStruct((rows_out, channels), F32),
        (jnp.reshape(at, (1,)).astype(jnp.int32), *features, *values), name,
    )


def row_grad_kernel(a_ref, w_ref, out_ref):
    parts, rows, width = out_ref.shape
    a = nn(order(rows, True), a_ref[...]).astype(BF16)
    for k in range(parts):
        out_ref[k] = nt(a, w_ref[width * k : width * (k + 1), :])


def row_grad(scaled, in_proj, parts):
    rows, channels = scaled.shape
    depth = in_proj.shape[0]
    return resident(
        row_grad_kernel, jax.ShapeDtypeStruct((parts, rows, depth // parts), F32), (scaled, in_proj), "row_grad",
        scalars=0,
    )


def after(x, *others):
    return lax.optimization_barrier((x, *others))[0]


class Order:
    def __init__(self):
        self.last = None

    def behind(self, x):
        return x if self.last is None else lax.optimization_barrier((x, self.last))[0]

    def step(self, *results):
        held = results if self.last is None else (*results, self.last)
        results = lax.optimization_barrier(held)[: len(results)]
        self.last = results[0]
        return results[0] if len(results) == 1 else results

    def send(self, x, axis, bit):
        return swap(self.behind(x), axis, bit)


def per_device(inputs, cotangent, in_proj, out_proj, decays, input_scale, retain):
    rows, depth = inputs.shape
    channels = in_proj.shape[1]
    devices, lanes = lax.axis_size("tm"), lax.axis_size("chan")
    scaling = 1.0 / math.sqrt(rows * devices)
    me, lane = lax.axis_index("tm"), lax.axis_index("chan")
    far = devices // 2
    groups = devices // 4
    steps = rows // SEG
    scale = input_scale[None, :]
    decay_row = decays[None, :]
    side = me // far

    half, quarter = rows // 2, rows // 4
    rows_out = depth // devices
    core = lane % 2
    place = [core, 1 - core, lane, lane ^ 2, lane ^ 1, lane ^ 3, 2 * core, 2 * core + 1, 2 - 2 * core, 3 - 2 * core]
    place = jnp.stack(place).astype(jnp.int32)
    blocks = jnp.stack([me, me ^ 1, me ^ far, me ^ far ^ 1]).astype(jnp.int32)
    sides = jnp.stack([side, 1 - side]).astype(jnp.int32)
    mine_near, mine_1, mine_2, mine_3, mine_4 = (
        [(0, 0, half)], [(1, 2, quarter)], [(1, 3, quarter)], [(2, 2, quarter)], [(2, 3, quarter)],
    )
    their_near, their_1, their_2, their_3, their_4 = (
        [(0, 1, half)], [(1, 4, quarter)], [(1, 5, quarter)], [(2, 4, quarter)], [(2, 5, quarter)],
    )

    def ordered(r):
        return r.reshape(-1, SEG, steps).swapaxes(1, 2).reshape(-1, 1)

    line = Order()
    where = jnp.stack([lane % 2, lane, side * 0]).astype(jnp.int32)
    x_own, x_half, x_quarter = line.step(*prep(where, inputs, 1, "prep_inputs"))
    near_x = line.send(x_half, "tm", 1)
    away_x = line.send(x_quarter, "tm", far)
    where = jnp.stack([lane % 2, lane, side, 1 - side]).astype(jnp.int32)
    c_own, c_half_a, c_quarter_a, c_half_b, c_quarter_b = prep(where, line.behind(cotangent), 2, "prep_cotangent")
    ends = resident(
        functools.partial(summary_kernel, scaling=scaling), jax.ShapeDtypeStruct((3, channels), F32),
        (x_own, c_own, in_proj, out_proj, scale, decay_row, jnp.broadcast_to(ordered(retain), (rows, 128))), "summary",
        [pltpu.VMEM((rows, channels), F32)] * 2, scalars=0,
    )
    table = jnp.concatenate([ends, jnp.pad(retain, (0, channels - rows))[None, :]], axis=0)[None]
    for bit in reach(devices)[:-1]:
        table = jnp.concatenate([table, line.send(table, "tm", bit)])
    near_x, away_x, table = line.step(near_x, away_x, table)

    corner_x = line.send(away_x, "tm", 1)
    side_x = line.send(away_x, "chan", 2)
    away_a = line.send(c_quarter_a, "tm", far)
    table = jnp.concatenate([table, line.send(table, "tm", reach(devices)[-1])])
    enter_fwd, enter_bwd, retain_all = carries(me[None].astype(jnp.int32), table)
    corner_x, side_x, away_a, enter_fwd = line.step(corner_x, side_x, away_a, enter_fwd)

    near_a = line.send(c_half_a, "tm", 1)
    corner_a = line.send(away_a, "tm", 1)
    corner_side_x = line.send(corner_x, "chan", 2)
    away_b = line.send(c_quarter_b, "tm", far)
    retain_wide = jnp.broadcast_to(ordered(retain_all[:, :rows]), (devices * rows, 128))
    forward = (in_proj, scale, decay_row, retain_wide, enter_fwd)
    backward = (out_proj, scale, decay_row, retain_wide, enter_bwd)
    tracks, lows = forward_call(blocks[:1], [x_own], forward, "forward_own")
    scaled, grads = backward_call(blocks[:1], sides, [[c_own]], backward, tracks, scaling, "backward_own")
    parts = row_grad(scaled[0], in_proj, lanes)
    other_x = line.send(pack([near_x, away_x, side_x, corner_x], "pack_x"), "chan", 1)
    corner_side_x, corner_a, near_a, away_b, parts, other_x = line.step(corner_side_x, corner_a, near_a, away_b, parts, other_x)

    corner_b = line.send(away_b, "tm", 1)
    corner_side_a = line.send(corner_a, "chan", 2)
    side_a = line.send(away_a, "chan", 2)
    near_b1 = line.send(c_half_b[:quarter], "tm", 1)
    last_x = line.send(corner_side_x, "chan", 1)
    side_b = line.send(away_b, "chan", 2)
    xs = [x_own] + collected(place, [
        (near_x, mine_near), (away_x, mine_1), (side_x, mine_2), (corner_x, mine_3), (corner_side_x, mine_4),
        (other_x, their_near + their_1 + their_2 + their_3), (last_x, their_4),
    ], "collect_x")
    more, more_low = forward_call(blocks[1:], xs[1:], forward, "forward_group")
    tracks, lows = tracks + more, lows + more_low
    corner_side_a, side_a, side_b, corner_b, near_b1, lows[1] = line.step(corner_side_a, side_a, side_b, corner_b, near_b1, lows[1])

    corner_side_b = line.send(corner_b, "chan", 2)
    near_b2 = line.send(c_half_b[quarter:], "tm", 1)
    other_a = line.send(pack([near_a, away_a, side_a, corner_a, corner_side_a], "pack_a"), "chan", 1)
    own_a = lax.dynamic_slice_in_dim(c_own, side * (depth // 2), depth // 2, axis=1)
    ca = [own_a] + collected(place, [
        (near_a, mine_near), (away_a, mine_1), (side_a, mine_2), (corner_a, mine_3), (corner_side_a, mine_4),
        (other_a, their_near + their_1 + their_2 + their_3 + their_4),
    ], "collect_a")

    def shares(features, values, block, factor, name):
        return [grad_rows(block ^ (2 * k), features, values, rows_out, factor, name) for k in range(1, groups)]

    out_given = shares(ca, lows, me % far, scaling, "out_grad")
    out_given[0], corner_side_b, near_b2 = line.step(out_given[0], corner_side_b, near_b2)

    out_got = [line.send(part, "tm", 2 * (k + 1)) for k, part in enumerate(out_given)]
    other_b = line.send(pack([away_b, side_b, corner_b, corner_side_b, near_b1, near_b2], "pack_b"), "chan", 1)
    cb = collected(place, [
        (near_b1, [(0, 6, quarter)]), (near_b2, [(0, 7, quarter)]),
        (away_b, mine_1), (side_b, mine_2), (corner_b, mine_3), (corner_side_b, mine_4),
        (other_b, their_1 + their_2 + their_3 + their_4 + [(0, 8, quarter), (0, 9, quarter)]),
    ], "collect_b")
    cs = [list(pair) for pair in zip(ca[1:], cb, strict=True)]
    more, more_grads = backward_call(blocks[1:], sides, cs, backward, tracks[1:], scaling, "backward_group")
    scaled, grads = scaled + more, grads + more_grads
    in_given = shares(xs, scaled, me, None, "in_grad")
    in_given[0] = line.step(in_given[0])
    in_got = [line.send(part, "tm", 2 * (k + 1)) for k, part in enumerate(in_given)]
    out_got[0] = line.step(out_got[0])
    decay_grad = (grads[0] + grads[1]) + (grads[2] + grads[3])
    bit = 2
    while bit < far:
        decay_grad += line.send(decay_grad, "tm", bit)
        bit *= 2
    bit = 1
    while bit < lanes:
        parts = parts.reshape(-1, 2, *parts.shape[1:])
        turn = (lane // bit) % 2
        keep = lax.dynamic_index_in_dim(parts, turn, axis=1, keepdims=False)
        give = lax.dynamic_index_in_dim(parts, 1 - turn, axis=1, keepdims=False)
        parts = keep + line.send(give, "chan", bit)
        bit *= 2
    input_grad = parts[0].astype(BF16)
    in_got[0] = after(in_got[0], input_grad)

    out_proj_grad = sum(out_got, grad_rows(me % far, [line.behind(ca[0]), *ca[1:]], lows, rows_out, scaling, "out_grad"))
    in_proj_grad = sum(in_got, grad_rows(me, [line.behind(xs[0]), *xs[1:]], scaled, rows_out, None, "in_grad"))
    return (in_proj_grad, out_proj_grad, decay_grad[0], input_grad)


def solution(mesh):
    return jax.shard_map(
        per_device,
        mesh=mesh,
        in_specs=(
            P("tm", None),
            P("tm", None),
            P(None, "chan"),
            P("chan", None),
            P("chan"),
            P("chan"),
            P("tm"),
        ),
        out_specs=(P("tm", "chan"), P("tm", "chan"), P("chan"), P("tm", "chan")),
        check_vma=False,
    )
```

time: 201 us -> 175 us (0.87)
  waiting for transfers between devices: 99.3 us -> 53.4 us
  Pallas kernels: 37.6 us -> 47.1 us
  local copies, waits for them, and re-layouts: 30.6 us -> 37.6 us
  starting transfers between devices: 21.7 us -> 25.1 us
    ppermute x28, waiting for transfers between devices: 99.3 us -> 53.4 us  [swap(): return lax.ppermute(x, axis, [(k, k ^ bit) for k in range(n)])]
    pallas_call x14 -> x19, Pallas kernels: 37.6 us -> 47.1 us  [resident(): pl.pallas_call(kernel, out_shape=out_shape, in_specs=[SMEM] * scalars + [...]
    unnamed x104 -> x136, local copies, waits for them, and re-layouts: 26.3 us -> 30 us
    ppermute x28, starting transfers between devices: 21.7 us -> 25.1 us  [swap(): return lax.ppermute(x, axis, [(k, k ^ bit) for k in range(n)])]
  transfers between devices with their start and end apart: 28 -> 28, of which waited for: 11 -> 12; matrix products, arithmetic and copies ran while one was open for 6% -> 8% of each run, Pallas kernels for 18% -> 21%
where the time goes in v3:
time: 175 us; the launch traced here: 174 us
  waiting for transfers between devices  53.4 us (31%)
  Pallas kernels  47.1 us (27%)
  local copies, waits for them, and re-layouts  37.6 us (21%)
  starting transfers between devices  25.1 us (14%)
  other arithmetic  9.36 us (5%)
    ppermute x28, waiting for transfers between devices, swap(): return lax.ppermute(x, axis, [(k, k ^ bit) for k in range(n)])  53.4 us
    pallas_call x19, Pallas kernels, resident(): pl.pallas_call(kernel, out_shape=out_shape, in_specs=[SMEM] * scalars + [...  47.1 us
    unnamed x136, local copies, waits for them, and re-layouts  30 us
    ppermute x28, starting transfers between devices, swap(): return lax.ppermute(x, axis, [(k, k ^ bit) for k in range(n)])  25.1 us
  transfers between devices with their start and end apart: 28, of which 12 were waited for; matrix products, arithmetic and copies ran while one was open for 8% of the time, Pallas kernels for 21%

profile of v3, /device:TPU:0, one launch (start us, length us, event | category | flops | bytes accessed | tf_op | source)
XLA Modules:
  0.0 174.0 jit_solution(9265200091768039897)
XLA Ops:
  2.0 2.3 %prep_inputs.1 = (bf16[256,2048]{1,0:T(8,128)(2,1)S(1)}, f32[128,2048]{1,0:T(8,128)}, f32[64,2048]{1,0:T(8,128)}) custom-call(s32[3]{0:T(128)S(1)} %pad_add_fusion.idx_ref, bf16[256,2048]{1,0:T(8,128)(2,1)S(1)} %copy-done.57), custom_call_target="tpu_custom_call" | custom-call | tf_op jit(solution)/shard_map/prep_inputs/pallas_call | solution.py:49
  4.2 2.9 %collective-permute-start = (f32[128,2048]{1,0:T(8,128)}, f32[128,2048]{1,0:T(8,128)S(1)}, u32[]{:S(2)}, u32[]{:S(2)}) collective-permute-start(f32[128,2048]{1,0:T(8,128)} %get-tuple-element.98), channel_id=1, source_target_pairs={{0,4},{4,0},{8,12},{12,8},{16,20},{20,16},{24,28},{28,24},{1,5},{5... | collective-permute-start | bytes 3145736 | tf_op jit(solution)/shard_map/ppermute | solution.py:19
  7.2 2.6 %collective-permute-start.1 = (f32[64,2048]{1,0:T(8,128)}, f32[64,2048]{1,0:T(8,128)}, u32[]{:S(2)}, u32[]{:S(2)}) collective-permute-start(f32[64,2048]{1,0:T(8,128)} %get-tuple-element.100), channel_id=1, source_target_pairs={{0,16},{4,20},{8,24},{12,28},{16,0},{20,4},{24,8},{28,12},{1,17},{... | collective-permute-start | bytes 1572872 | tf_op jit(solution)/shard_map/ppermute | solution.py:19
  12.7 2.0 %prep_cotangent.1 = (bf16[256,2048]{1,0:T(8,128)(2,1)S(1)}, f32[128,1024]{1,0:T(8,128)}, f32[64,1024]{1,0:T(8,128)S(1)}, f32[128,1024]{1,0:T(8,128)S(1)}, f32[64,1024]{1,0:T(8,128)}) custom-call(s32[4]{0:T(128)S(1)} %pad_add_fusion.1.idx_ref, bf16[256,2048]{1,0:T(8,128)(2,1)S(1)} %copy-done.58), custom_call_target="tpu_custom_call" | custom-call | tf_op jit(solution)/shard_map/prep_cotangent/pallas_call | solution.py:49
  15.6 2.5 %copy-done = bf16[2048,1024]{1,0:T(8,128)(2,1)S(1)} copy-done((bf16[2048,1024]{1,0:T(8,128)(2,1)S(1)}, bf16[2048,1024]{1,0:T(8,128)(2,1)}, u32[]{:S(2)}) %copy-start) | copy-done | bytes 4194328
  18.1 2.2 %copy-done.4 = bf16[1024,2048]{1,0:T(8,128)(2,1)S(1)} copy-done((bf16[1024,2048]{1,0:T(8,128)(2,1)S(1)}, bf16[1024,2048]{1,0:T(8,128)(2,1)}, u32[]{:S(2)}) %copy-start.4) | copy-done | bytes 4194328
  20.3 2.9 %summary.1 = f32[3,1024]{1,0:T(4,128)S(1)} custom-call(bf16[256,2048]{1,0:T(8,128)(2,1)S(1)} %get-tuple-element.172.x_ref.refs_0_, bf16[256,2048]{1,0:T(8,128)(2,1)S(1)} %get-tuple-element.96.c_ref.refs_0_, bf16[2048,1024]{1,0:T(8,128)(2,1)S(1)} %copy-done, bf16[1024,2048]{1,0:T(8,128)(2,1)S(1)} %copy-done.4, f32[1,1024]{1,0:T(1,128)S(1)} %bitcast.36, ...), custom_call_target="tpu_custom_call" | custom-call | tf_op jit(solution)/shard_map/summary/pallas_call | solution.py:49
  24.9 8.4 %collective-permute-done.2 = f32[1,4,1024]{2,1,0:T(4,128)S(1)} collective-permute-done((f32[1,4,1024]{2,1,0:T(4,128)S(1)}, f32[1,4,1024]{2,1,0:T(4,128)S(1)}, u32[]{:S(2)}, u32[]{:S(2)}) %collective-permute-start.2) | collective-permute-done | bytes 16416 | tf_op jit(solution)/shard_map/ppermute | solution.py:19
  33.4 4.8 %collective-permute-done.3 = f32[2,4,1024]{2,1,0:T(4,128)S(1)} collective-permute-done((f32[2,4,1024]{2,1,0:T(4,128)S(1)}, f32[2,4,1024]{2,1,0:T(4,128)S(1)}, u32[]{:S(2)}, u32[]{:S(2)}) %collective-permute-start.3) | collective-permute-done | bytes 32800 | tf_op jit(solution)/shard_map/ppermute | solution.py:19
  40.3 2.1 %collective-permute-start.6 = (f32[64,1024]{1,0:T(8,128)S(1)}, f32[64,1024]{1,0:T(8,128)}, u32[]{:S(2)}, u32[]{:S(2)}) collective-permute-start(f32[64,1024]{1,0:T(8,128)S(1)} %get-tuple-element.107), channel_id=1, source_target_pairs={{0,16},{4,20},{8,24},{12,28},{16,0},{20,4},{24,8},{28,12},{1,17},{... | collective-permute-start | bytes 786440 | tf_op jit(solution)/shard_map/ppermute | solution.py:19
  42.4 1.8 %collective-permute-start.7 = (f32[4,4,1024]{2,1,0:T(4,128)S(1)}, f32[4,4,1024]{2,1,0:T(4,128)S(1)}, u32[]{:S(2)}, u32[]{:S(2)}) collective-permute-start(f32[4,4,1024]{2,1,0:T(4,128)S(1)} %pad_maximum_fusion.1), channel_id=1, source_target_pairs={{0,20},{4,16},{8,28},{12,24},{16,4},{20,0},{24,12},{28,8},{1,21},{... | collective-permute-start | bytes 196616 | tf_op jit(solution)/shard_map/ppermute | solution.py:19
  44.2 12.9 %collective-permute-done.7 = f32[4,4,1024]{2,1,0:T(4,128)S(1)} collective-permute-done((f32[4,4,1024]{2,1,0:T(4,128)S(1)}, f32[4,4,1024]{2,1,0:T(4,128)S(1)}, u32[]{:S(2)}, u32[]{:S(2)}) %collective-permute-start.7) | collective-permute-done | bytes 65568 | tf_op jit(solution)/shard_map/ppermute | solution.py:19
  57.3 3.0 %pack_x.1 = f32[320,2048]{1,0:T(8,128)} custom-call(f32[128,2048]{1,0:T(8,128)S(1)} %collective-permute-done.refs_0_, f32[64,2048]{1,0:T(8,128)} %collective-permute-done.1.refs_1_, f32[64,2048]{1,0:T(8,128)S(1)} %collective-permute-done.5.refs_2_, f32[64,2048]{1,0:T(8,128)} %collective-permute-done.4.refs_3_), custom_call_target="tpu_custom_call" | custom-call | tf_op jit(solution)/shard_map/pack_x/pallas_call | solution.py:49
  63.7 2.2 %copy-done.1 = bf16[2048,1024]{1,0:T(8,128)(2,1)S(1)} copy-done((bf16[2048,1024]{1,0:T(8,128)(2,1)S(1)}, bf16[2048,1024]{1,0:T(8,128)(2,1)}, u32[]{:S(2)}) %copy-start.1) | copy-done | bytes 4194328
  65.9 1.8 %forward_own.1 = (f32[264,1024]{1,0:T(8,128)S(1)}, bf16[256,1024]{1,0:T(8,128)(2,1)S(1)}) custom-call(s32[1]{0:T(128)} %bitcast.idx_ref, bf16[256,2048]{1,0:T(8,128)(2,1)S(1)} %get-tuple-element.172.x_ref.refs_0_, bf16[2048,1024]{1,0:T(8,128)(2,1)S(1)} %copy-done.1, f32[1,1024]{1,0:T(1,128)S(1)} %bitcast.37, f32[1,1024]{1,0:T(1,128)S(1)} %bitcast.42, ...), custom_call_target="tpu_custom_call" | custom-call | tf_op jit(solution)/shard_map/forward_own/pallas_call | solution.py:49
  68.5 2.5 %backward_own.1 = (bf16[256,1024]{1,0:T(8,128)(2,1)S(1)}, f32[1,1024]{1,0:T(1,128)S(1)}) custom-call(s32[1]{0:T(128)} %bitcast.idx_ref, s32[2]{0:T(128)S(1)} %pad_add_fusion.2.side_ref, bf16[256,2048]{1,0:T(8,128)(2,1)S(1)} %get-tuple-element.96.c_ref.refs_0_, bf16[1024,2048]{1,0:T(8,128)(2,1)S(1)} %copy-done.5, f32[1,1024]{1,0:T(1,128)S(1)} %bitcast.38, ...), custom_call_target="tpu_custom_call" | custom-call | tf_op jit(solution)/shard_map/backward_own/pallas_call | solution.py:49
  73.9 2.4 %collective-permute-done.11.refs_0_.refs_2_ = f32[64,1024]{1,0:T(8,128)S(1)} collective-permute-done((f32[64,1024]{1,0:T(8,128)}, f32[64,1024]{1,0:T(8,128)S(1)}, u32[]{:S(2)}, u32[]{:S(2)}) %collective-permute-start.11) | collective-permute-done | bytes 262176 | tf_op jit(solution)/shard_map/ppermute | solution.py:19
  76.3 4.4 %collective-permute-done.9.refs_3_ = f32[64,1024]{1,0:T(8,128)} collective-permute-done((f32[64,1024]{1,0:T(8,128)}, f32[64,1024]{1,0:T(8,128)}, u32[]{:S(2)}, u32[]{:S(2)}) %collective-permute-start.9) | collective-permute-done | bytes 262176 | tf_op jit(solution)/shard_map/ppermute | solution.py:19
  90.5 3.3 %collect_x.1 = (bf16[256,2048]{1,0:T(8,128)(2,1)S(1)}, bf16[256,2048]{1,0:T(8,128)(2,1)S(1)}, bf16[256,2048]{1,0:T(8,128)(2,1)S(1)}) custom-call(s32[10]{0:T(128)S(1)} %stack.81.idx_ref, f32[128,2048]{1,0:T(8,128)S(1)} %copy-done.30, f32[64,2048]{1,0:T(8,128)} %collective-permute-done.1.refs_1_, f32[64,2048]{1,0:T(8,128)S(1)} %copy-done.32, ...), custom_call_target="tpu_custom_call" | custom-call | tf_op jit(solution)/shard_map/collect_x/pallas_call | solution.py:49
  93.9 6.0 %forward_group.1 = (f32[264,1024]{1,0:T(8,128)S(1)}, bf16[256,1024]{1,0:T(8,128)(2,1)S(1)}, f32[264,1024]{1,0:T(8,128)S(1)}, bf16[256,1024]{1,0:T(8,128)(2,1)S(1...) custom-call(s32[3]{0:T(128)S(1)} %pad_add_fusion.3.idx_ref, ...), custom_call_target="tpu_custom_call" | custom-call | tf_op jit(solution)/shard_map/forward_group/pallas_call | solution.py:49
  102.0 3.4 %pack_a.1 = f32[384,1024]{1,0:T(8,128)} custom-call(f32[128,1024]{1,0:T(8,128)} %collective-permute-done.10.refs_0_, f32[64,1024]{1,0:T(8,128)} %collective-permute-done.6.refs_1_, f32[64,1024]{1,0:T(8,128)} %collective-permute-done.14.refs_2_, f32[64,1024]{1,0:T(8,128)} %collective-permute-done.9.refs_3_, f32[64,1024]{1,0:T(8,128)} %collective-permute-done.13.refs_4_), custom_call_target="tpu_custom_call" | custom-call | tf_op jit(solution)/shard_map/pack_a/pallas_call | solution.py:49
  109.3 2.6 %collect_a.1 = (bf16[256,1024]{1,0:T(8,128)(2,1)S(1)}, bf16[256,1024]{1,0:T(8,128)(2,1)S(1)}, bf16[256,1024]{1,0:T(8,128)(2,1)S(1)}) custom-call(s32[10]{0:T(128)S(1)} %stack.81.idx_ref, f32[128,1024]{1,0:T(8,128)} %collective-permute-done.10.refs_0_, f32[64,1024]{1,0:T(8,128)} %collective-permute-done.6.refs_1_, ...), custom_call_target="tpu_custom_call" | custom-call | tf_op jit(solution)/shard_map/collect_a/pallas_call | solution.py:49
  114.8 2.5 %pack_b.1 = f32[384,1024]{1,0:T(8,128)} custom-call(f32[64,1024]{1,0:T(8,128)S(1)} %collective-permute-done.11.refs_0_.refs_2_, f32[64,1024]{1,0:T(8,128)} %collective-permute-done.15.refs_1_.refs_3_, f32[64,1024]{1,0:T(8,128)} %collective-permute-done.16.refs_2_.refs_4_, f32[64,1024]{1,0:T(8,128)} %collective-permute-done.20.refs_3_.refs_5_, ...), custom_call_target="tpu_custom_call" | custom-call | tf_op jit(solution)/shard_map/pack_b/pallas_call | solution.py:49
  117.5 2.4 %dynamic-slice_bitcast_fusion = f32[2,256,512]{2,1,0:T(8,128)} fusion(f32[2,2,256,512]{3,2,1,0:T(8,128)} %bitcast.34, s32[]{:T(128)S(6)} %select_n.53), kind=kLoop, calls=%fused_computation.1 | loop fusion | bytes 2097156 | tf_op jit(solution)/shard_map/jit(dynamic_index_in_dim)/squeeze | solution.py:517
  121.1 2.5 %collect_b.1 = (bf16[256,1024]{1,0:T(8,128)(2,1)S(1)}, bf16[256,1024]{1,0:T(8,128)(2,1)S(1)}, bf16[256,1024]{1,0:T(8,128)(2,1)S(1)}) custom-call(s32[10]{0:T(128)S(1)} %stack.81.idx_ref, f32[64,1024]{1,0:T(8,128)} %collective-permute-done.17.refs_4_.refs_0_, f32[64,1024]{1,0:T(8,128)} %collective-permute-done.21.refs_5_.refs_1_, ...), custom_call_target="tpu_custom_call" | custom-call | tf_op jit(solution)/shard_map/collect_b/pallas_call | solution.py:49
  128.4 6.7 %backward_group.1 = (bf16[256,1024]{1,0:T(8,128)(2,1)S(1)}, f32[1,1024]{1,0:T(1,128)S(1)}, bf16[256,1024]{1,0:T(8,128)(2,1)S(1)}, f32[1,1024]{1,0:T(1,128)S(1)},...) custom-call(s32[3]{0:T(128)S(1)} %pad_add_fusion.3.idx_ref, s32[2]{0:T(128)S(1)} %pad_add_fusion.2.side_ref, ...), custom_call_target="tpu_custom_call" | custom-call | tf_op jit(solution)/shard_map/backward_group/pallas_call | solution.py:49
  136.3 6.9 %collective-permute-done.22 = f32[256,1024]{1,0:T(8,128)} collective-permute-done((f32[256,1024]{1,0:T(8,128)}, f32[256,1024]{1,0:T(8,128)}, u32[]{:S(2)}, u32[]{:S(2)}) %collective-permute-start.22) | collective-permute-done | bytes 1048608 | tf_op jit(solution)/shard_map/ppermute | solution.py:19
  143.6 2.7 %collective-permute-done.25 = f32[2,256,512]{2,1,0:T(8,128)} collective-permute-done((f32[2,256,512]{2,1,0:T(8,128)}, f32[2,256,512]{2,1,0:T(8,128)}, u32[]{:S(2)}, u32[]{:S(2)}) %collective-permute-start.25) | collective-permute-done | bytes 1048608 | tf_op jit(solution)/shard_map/ppermute | solution.py:19
  158.0 2.5 %add.77 = f32[256,1024]{1,0:T(8,128)} add(f32[256,1024]{1,0:T(8,128)S(1)} %out_grad.3, f32[256,1024]{1,0:T(8,128)} %collective-permute-done.22) | non-fusion elementwise | flops 262144 | bytes 3145728 | tf_op jit(solution)/shard_map/add | solution.py:523
  161.2 8.0 %collective-permute-done.27 = f32[1,1024]{1,0:T(1,128)S(1)} collective-permute-done((f32[1,1024]{1,0:T(1,128)S(1)}, f32[1,1024]{1,0:T(1,128)S(1)}, u32[]{:S(2)}, u32[]{:S(2)}) %collective-permute-start.27) | collective-permute-done | bytes 4128 | tf_op jit(solution)/shard_map/ppermute | solution.py:19
  169.9 1.8 %fusion = bf16[256,512]{1,0:T(8,128)(2,1)} fusion(f32[1,256,512]{2,1,0:T(8,128)} %collective-permute-done.26, f32[2,256,512]{2,1,0:T(8,128)S(1)} %copy-done.67, s32[]{:T(128)S(6)} %select_n.56), kind=kLoop, calls=%fused_computation.3 | loop fusion | flops 262144 | bytes 1310724 | tf_op jit(solution)/shard_map/convert_element_type | solution.py:520
  171.7 2.3 %add.76 = f32[256,1024]{1,0:T(8,128)} add(f32[256,1024]{1,0:T(8,128)S(1)} %in_grad.3, f32[256,1024]{1,0:T(8,128)} %collective-permute-done.24) | non-fusion elementwise | flops 262144 | bytes 3145728 | tf_op jit(solution)/shard_map/add | solution.py:524
  (208 shorter events, 55.1 us)
Async XLA Ops:
  0.6 15.0 %copy-start.64 = (f32[1024]{0:T(1024)S(1)}, f32[1024]{0:T(1024)}, u32[]{:S(2)}) copy-start(f32[1024]{0:T(1024)} %param.12) | copy-start | bytes 12292
  0.6 15.0 %copy-start.65 = (f32[1024]{0:T(1024)S(1)}, f32[1024]{0:T(1024)}, u32[]{:S(2)}) copy-start(f32[1024]{0:T(1024)} %param.11) | copy-start | bytes 12292
  4.2 33.9 %collective-permute-start = (f32[128,2048]{1,0:T(8,128)}, f32[128,2048]{1,0:T(8,128)S(1)}, u32[]{:S(2)}, u32[]{:S(2)}) collective-permute-start(f32[128,2048]{1,0:T(8,128)} %get-tuple-element.98), channel_id=1, source_target_pairs={{0,4},{4,0},{8,12},{12,8},{16,20},{20,16},{24,28},{28,24},{1,5},{5... | collective-permute-start | bytes 3145736 | tf_op jit(solution)/shard_map/ppermute | solution.py:19
  7.2 31.0 %collective-permute-start.1 = (f32[64,2048]{1,0:T(8,128)}, f32[64,2048]{1,0:T(8,128)}, u32[]{:S(2)}, u32[]{:S(2)}) collective-permute-start(f32[64,2048]{1,0:T(8,128)} %get-tuple-element.100), channel_id=1, source_target_pairs={{0,16},{4,20},{8,24},{12,28},{16,0},{20,4},{24,8},{28,12},{1,17},{... | collective-permute-start | bytes 1572872 | tf_op jit(solution)/shard_map/ppermute | solution.py:19
  15.5 53.0 %copy-start.14 = (bf16[256,2048]{1,0:T(8,128)(2,1)}, bf16[256,2048]{1,0:T(8,128)(2,1)S(1)}, u32[]{:S(2)}) copy-start(bf16[256,2048]{1,0:T(8,128)(2,1)S(1)} %get-tuple-element.96.c_ref.refs_0_) | copy-start | bytes 3145732
  23.2 10.0 %collective-permute-start.2 = (f32[1,4,1024]{2,1,0:T(4,128)S(1)}, f32[1,4,1024]{2,1,0:T(4,128)S(1)}, u32[]{:S(2)}, u32[]{:S(2)}) collective-permute-start(f32[1,4,1024]{2,1,0:T(4,128)S(1)} %maximum_bitcast_fusion), channel_id=1, source_target_pairs={{0,8},{4,12},{8,0},{12,4},{16,24},{20,28},{24,16},{28,20},{1,9},{5... | collective-permute-start | bytes 49160 | tf_op jit(solution)/shard_map/ppermute | solution.py:19
  33.3 4.9 %collective-permute-start.3 = (f32[2,4,1024]{2,1,0:T(4,128)S(1)}, f32[2,4,1024]{2,1,0:T(4,128)S(1)}, u32[]{:S(2)}, u32[]{:S(2)}) collective-permute-start(f32[2,4,1024]{2,1,0:T(4,128)S(1)} %pad_maximum_fusion.2), channel_id=1, source_target_pairs={{0,12},{4,8},{8,4},{12,0},{16,28},{20,24},{24,20},{28,16},{1,13},{... | collective-permute-start | bytes 98312 | tf_op jit(solution)/shard_map/ppermute | solution.py:19
  38.2 22.1 %copy-start.29 = (f32[128,2048]{1,0:T(8,128)}, f32[128,2048]{1,0:T(8,128)S(1)}, u32[]{:S(2)}) copy-start(f32[128,2048]{1,0:T(8,128)S(1)} %collective-permute-done.refs_0_) | copy-start | bytes 3145732
  38.2 19.1 %collective-permute-start.4 = (f32[64,2048]{1,0:T(8,128)}, f32[64,2048]{1,0:T(8,128)}, u32[]{:S(2)}, u32[]{:S(2)}) collective-permute-start(f32[64,2048]{1,0:T(8,128)} %collective-permute-done.1.refs_1_), channel_id=1, source_target_pairs={{0,4},{4,0},{8,12},{12,8},{16,20},{20,16},{24,28},{28,24},{1,5},{5... | collective-permute-start | bytes 1572872 | tf_op jit(solution)/shard_map/ppermute | solution.py:19
  38.8 18.6 %collective-permute-start.5 = (f32[64,2048]{1,0:T(8,128)}, f32[64,2048]{1,0:T(8,128)S(1)}, u32[]{:S(2)}, u32[]{:S(2)}) collective-permute-start(f32[64,2048]{1,0:T(8,128)} %collective-permute-done.1.refs_1_), channel_id=1, source_target_pairs={{0,2},{1,3},{2,0},{3,1},{4,6},{5,7},{6,4},{7,5},{8,10},{9,11},{10,... | collective-permute-start | bytes 1572872 | tf_op jit(solution)/shard_map/ppermute | solution.py:19
  40.3 17.0 %collective-permute-start.6 = (f32[64,1024]{1,0:T(8,128)S(1)}, f32[64,1024]{1,0:T(8,128)}, u32[]{:S(2)}, u32[]{:S(2)}) collective-permute-start(f32[64,1024]{1,0:T(8,128)S(1)} %get-tuple-element.107), channel_id=1, source_target_pairs={{0,16},{4,20},{8,24},{12,28},{16,0},{20,4},{24,8},{28,12},{1,17},{... | collective-permute-start | bytes 786440 | tf_op jit(solution)/shard_map/ppermute | solution.py:19
  42.4 14.7 %collective-permute-start.7 = (f32[4,4,1024]{2,1,0:T(4,128)S(1)}, f32[4,4,1024]{2,1,0:T(4,128)S(1)}, u32[]{:S(2)}, u32[]{:S(2)}) collective-permute-start(f32[4,4,1024]{2,1,0:T(4,128)S(1)} %pad_maximum_fusion.1), channel_id=1, source_target_pairs={{0,20},{4,16},{8,28},{12,24},{16,4},{20,0},{24,12},{28,8},{1,21},{... | collective-permute-start | bytes 196616 | tf_op jit(solution)/shard_map/ppermute | solution.py:19
  60.3 20.4 %collective-permute-start.12 = (f32[320,2048]{1,0:T(8,128)}, f32[320,2048]{1,0:T(8,128)}, u32[]{:S(2)}, u32[]{:S(2)}) collective-permute-start(f32[320,2048]{1,0:T(8,128)} %pack_x.1), channel_id=1, source_target_pairs={{0,1},{1,0},{2,3},{3,2},{4,5},{5,4},{6,7},{7,6},{8,9},{9,8},{10,11... | collective-permute-start | bytes 7864328 | tf_op jit(solution)/shard_map/ppermute | solution.py:19
  60.4 20.3 %collective-permute-start.10 = (f32[128,1024]{1,0:T(8,128)}, f32[128,1024]{1,0:T(8,128)}, u32[]{:S(2)}, u32[]{:S(2)}) collective-permute-start(f32[128,1024]{1,0:T(8,128)} %get-tuple-element.116), channel_id=1, source_target_pairs={{0,4},{4,0},{8,12},{12,8},{16,20},{20,16},{24,28},{28,24},{1,5},{5... | collective-permute-start | bytes 1572872 | tf_op jit(solution)/shard_map/ppermute | solution.py:19
  61.0 19.7 %collective-permute-start.8 = (f32[64,2048]{1,0:T(8,128)}, f32[64,2048]{1,0:T(8,128)}, u32[]{:S(2)}, u32[]{:S(2)}) collective-permute-start(f32[64,2048]{1,0:T(8,128)} %collective-permute-done.4.refs_3_), channel_id=1, source_target_pairs={{0,2},{1,3},{2,0},{3,1},{4,6},{5,7},{6,4},{7,5},{8,10},{9,11},{10,... | collective-permute-start | bytes 1572872 | tf_op jit(solution)/shard_map/ppermute | solution.py:19
  61.5 14.8 %collective-permute-start.11 = (f32[64,1024]{1,0:T(8,128)}, f32[64,1024]{1,0:T(8,128)S(1)}, u32[]{:S(2)}, u32[]{:S(2)}) collective-permute-start(f32[64,1024]{1,0:T(8,128)} %get-tuple-element.118), channel_id=1, source_target_pairs={{0,16},{4,20},{8,24},{12,28},{16,0},{20,4},{24,8},{28,12},{1,17},{... | collective-permute-start | bytes 786440 | tf_op jit(solution)/shard_map/ppermute | solution.py:19
  61.5 19.2 %collective-permute-start.9 = (f32[64,1024]{1,0:T(8,128)}, f32[64,1024]{1,0:T(8,128)}, u32[]{:S(2)}, u32[]{:S(2)}) collective-permute-start(f32[64,1024]{1,0:T(8,128)} %collective-permute-done.6.refs_1_), channel_id=1, source_target_pairs={{0,4},{4,0},{8,12},{12,8},{16,20},{20,16},{24,28},{28,24},{1,5},{5... | collective-permute-start | bytes 786440 | tf_op jit(solution)/shard_map/ppermute | solution.py:19
  80.7 5.0 %collective-permute-start.18 = (f32[64,2048]{1,0:T(8,128)}, f32[64,2048]{1,0:T(8,128)S(1)}, u32[]{:S(2)}, u32[]{:S(2)}) collective-permute-start(f32[64,2048]{1,0:T(8,128)} %collective-permute-done.8.refs_4_), channel_id=1, source_target_pairs={{0,1},{1,0},{2,3},{3,2},{4,5},{5,4},{6,7},{7,6},{8,9},{9,8},{10,11... | collective-permute-start | bytes 1572872 | tf_op jit(solution)/shard_map/ppermute | solution.py:19
  81.6 20.4 %collective-permute-start.15 = (f32[64,1024]{1,0:T(8,128)S(1)}, f32[64,1024]{1,0:T(8,128)}, u32[]{:S(2)}, u32[]{:S(2)}) collective-permute-start(f32[64,1024]{1,0:T(8,128)S(1)} %collective-permute-done.11.refs_0_.refs_2_), channel_id=1, source_target_pairs={{0,2},{1,3},{2,0},{3,1},{4,6},{5,7},{6,4},{7,5},{8,10},{9,11},{10,... | collective-permute-start | bytes 786440 | tf_op jit(solution)/shard_map/ppermute | solution.py:19
  82.1 19.9 %collective-permute-start.16 = (f32[64,1024]{1,0:T(8,128)S(1)}, f32[64,1024]{1,0:T(8,128)}, u32[]{:S(2)}, u32[]{:S(2)}) collective-permute-start(f32[64,1024]{1,0:T(8,128)S(1)} %collective-permute-done.11.refs_0_.refs_2_), channel_id=1, source_target_pairs={{0,4},{4,0},{8,12},{12,8},{16,20},{20,16},{24,28},{28,24},{1,5},{5... | collective-permute-start | bytes 786440 | tf_op jit(solution)/shard_map/ppermute | solution.py:19
  82.6 19.4 %collective-permute-start.17 = (f32[64,1024]{1,0:T(8,128)}, f32[64,1024]{1,0:T(8,128)}, u32[]{:S(2)}, u32[]{:S(2)}) collective-permute-start(f32[64,1024]{1,0:T(8,128)} %get-tuple-element.134), channel_id=1, source_target_pairs={{0,4},{4,0},{8,12},{12,8},{16,20},{20,16},{24,28},{28,24},{1,5},{5... | collective-permute-start | bytes 786440 | tf_op jit(solution)/shard_map/ppermute | solution.py:19
  84.1 17.9 %collective-permute-start.14 = (f32[64,1024]{1,0:T(8,128)}, f32[64,1024]{1,0:T(8,128)}, u32[]{:S(2)}, u32[]{:S(2)}) collective-permute-start(f32[64,1024]{1,0:T(8,128)} %collective-permute-done.6.refs_1_), channel_id=1, source_target_pairs={{0,2},{1,3},{2,0},{3,1},{4,6},{5,7},{6,4},{7,5},{8,10},{9,11},{10,... | collective-permute-start | bytes 786440 | tf_op jit(solution)/shard_map/ppermute | solution.py:19
  86.5 15.5 %collective-permute-start.13 = (f32[64,1024]{1,0:T(8,128)}, f32[64,1024]{1,0:T(8,128)}, u32[]{:S(2)}, u32[]{:S(2)}) collective-permute-start(f32[64,1024]{1,0:T(8,128)} %collective-permute-done.9.refs_3_), channel_id=1, source_target_pairs={{0,2},{1,3},{2,0},{3,1},{4,6},{5,7},{6,4},{7,5},{8,10},{9,11},{10,... | collective-permute-start | bytes 786440 | tf_op jit(solution)/shard_map/ppermute | solution.py:19
  105.5 3.8 %collective-permute-start.19 = (f32[384,1024]{1,0:T(8,128)}, f32[384,1024]{1,0:T(8,128)}, u32[]{:S(2)}, u32[]{:S(2)}) collective-permute-start(f32[384,1024]{1,0:T(8,128)} %pack_a.1), channel_id=1, source_target_pairs={{0,1},{1,0},{2,3},{3,2},{4,5},{5,4},{6,7},{7,6},{8,9},{9,8},{10,11... | collective-permute-start | bytes 4718600 | tf_op jit(solution)/shard_map/ppermute | solution.py:19
  105.6 9.0 %collective-permute-start.21 = (f32[64,1024]{1,0:T(8,128)}, f32[64,1024]{1,0:T(8,128)}, u32[]{:S(2)}, u32[]{:S(2)}) collective-permute-start(f32[64,1024]{1,0:T(8,128)} %get-tuple-element.153), channel_id=1, source_target_pairs={{0,4},{4,0},{8,12},{12,8},{16,20},{20,16},{24,28},{28,24},{1,5},{5... | collective-permute-start | bytes 786440 | tf_op jit(solution)/shard_map/ppermute | solution.py:19
  106.1 8.7 %collective-permute-start.20 = (f32[64,1024]{1,0:T(8,128)}, f32[64,1024]{1,0:T(8,128)}, u32[]{:S(2)}, u32[]{:S(2)}) collective-permute-start(f32[64,1024]{1,0:T(8,128)} %collective-permute-done.16.refs_2_.refs_4_), channel_id=1, source_target_pairs={{0,2},{1,3},{2,0},{3,1},{4,6},{5,7},{6,4},{7,5},{8,10},{9,11},{10,... | collective-permute-start | bytes 786440 | tf_op jit(solution)/shard_map/ppermute | solution.py:19
  117.3 3.8 %collective-permute-start.23 = (f32[384,1024]{1,0:T(8,128)}, f32[384,1024]{1,0:T(8,128)}, u32[]{:S(2)}, u32[]{:S(2)}) collective-permute-start(f32[384,1024]{1,0:T(8,128)} %pack_b.1), channel_id=1, source_target_pairs={{0,1},{1,0},{2,3},{3,2},{4,5},{5,4},{6,7},{7,6},{8,9},{9,8},{10,11... | collective-permute-start | bytes 4718600 | tf_op jit(solution)/shard_map/ppermute | solution.py:19
  117.4 25.9 %collective-permute-start.22 = (f32[256,1024]{1,0:T(8,128)}, f32[256,1024]{1,0:T(8,128)}, u32[]{:S(2)}, u32[]{:S(2)}) collective-permute-start(f32[256,1024]{1,0:T(8,128)} %out_grad.2), channel_id=1, source_target_pairs={{0,8},{4,12},{8,0},{12,4},{16,24},{20,28},{24,16},{28,20},{1,9},{5... | collective-permute-start | bytes 3145736 | tf_op jit(solution)/shard_map/ppermute | solution.py:19
  143.3 3.0 %collective-permute-start.25 = (f32[2,256,512]{2,1,0:T(8,128)}, f32[2,256,512]{2,1,0:T(8,128)}, u32[]{:S(2)}, u32[]{:S(2)}) collective-permute-start(f32[2,256,512]{2,1,0:T(8,128)} %dynamic-slice_bitcast_fusion), channel_id=1, source_target_pairs={{0,1},{1,0},{2,3},{3,2},{4,5},{5,4},{6,7},{7,6},{8,9},{9,8},{10,11... | collective-permute-start | bytes 3145736 | tf_op jit(solution)/shard_map/ppermute | solution.py:19
  143.3 28.4 %collective-permute-start.24 = (f32[256,1024]{1,0:T(8,128)}, f32[256,1024]{1,0:T(8,128)}, u32[]{:S(2)}, u32[]{:S(2)}) collective-permute-start(f32[256,1024]{1,0:T(8,128)} %copy-done.59), channel_id=1, source_target_pairs={{0,8},{4,12},{8,0},{12,4},{16,24},{20,28},{24,16},{28,20},{1,9},{5... | collective-permute-start | bytes 3145736 | tf_op jit(solution)/shard_map/ppermute | solution.py:19
  149.0 20.9 %collective-permute-start.26 = (f32[1,256,512]{2,1,0:T(8,128)}, f32[1,256,512]{2,1,0:T(8,128)}, u32[]{:S(2)}, u32[]{:S(2)}) collective-permute-start(f32[1,256,512]{2,1,0:T(8,128)} %constant_dynamic-slice_fusion), channel_id=1, source_target_pairs={{0,2},{1,3},{2,0},{3,1},{4,6},{5,7},{6,4},{7,5},{8,10},{9,11},{10,... | collective-permute-start | bytes 1572872 | tf_op jit(solution)/shard_map/ppermute | solution.py:19
  150.6 18.7 %collective-permute-start.27 = (f32[1,1024]{1,0:T(1,128)S(1)}, f32[1,1024]{1,0:T(1,128)S(1)}, u32[]{:S(2)}, u32[]{:S(2)}) collective-permute-start(f32[1,1024]{1,0:T(1,128)S(1)} %add_add_fusion), channel_id=1, source_target_pairs={{0,8},{4,12},{8,0},{12,4},{16,24},{20,28},{24,16},{28,20},{1,9},{5... | collective-permute-start | bytes 12296 | tf_op jit(solution)/shard_map/ppermute | solution.py:19
  (64 other events, 187.3 us)

commit v4 on v3

--- a/solution.py
+++ b/solution.py
@@ -42,15 +42,15 @@
 SMEM = pl.BlockSpec(memory_space=pltpu.SMEM)
 
 
-ANY = pl.BlockSpec(memory_space=pltpu.HBM)
-
-
-def resident(kernel, out_shape, operands, name, scratch=(), scalars=1, anywhere=0, out_specs=None):
+ANY = pl.BlockSpec(memory_space=pl.ANY)
+
+
+def resident(kernel, out_shape, operands, name, scratch=(), scalars=1, anywhere=0):
     return pl.pallas_call(
         kernel,
         out_shape=out_shape,
         in_specs=[SMEM] * scalars + [VMEM] * (len(operands) - scalars - anywhere) + [ANY] * anywhere,
-        out_specs=jax.tree.map(lambda _: VMEM, out_shape) if out_specs is None else out_specs,
+        out_specs=jax.tree.map(lambda _: VMEM, out_shape),
         scratch_shapes=scratch,
         compiler_params=pltpu.CompilerParams(vmem_limit_bytes=VMEM_LIMIT),
         cost_estimate=pl.CostEstimate(flops=0, transcendentals=0, bytes_accessed=0),
@@ -58,27 +58,37 @@
     )(*operands)
 
 
-def prep_kernel(idx_ref, x_ref, p_ref, *refs, parts):
-    full = refs[-1]
-    rows, depth = x_ref.shape
-    full[...] = nn(order(rows), x_ref[...])
+def ordered_rows(x_ref, p_ref, full):
+    full[...] = nn(order(x_ref.shape[0]), x_ref[...])
     p_ref[...] = full[...].astype(BF16)
-    half, quarter, width = rows // 2, rows // 4, depth // parts
-    for k in range(parts):
-        near = pl.ds(pl.multiple_of(idx_ref[2 + k] * width, width), width)
-        away = pl.ds(pl.multiple_of(idx_ref[2 + parts - 1 - k] * width, width), width)
-        refs[2 * k][...] = full[pl.ds(pl.multiple_of(idx_ref[0] * half, half), half), near]
-        refs[2 * k + 1][...] = full[pl.ds(pl.multiple_of(idx_ref[1] * quarter, quarter), quarter), away]
-
-
-def prep(idx, x, parts, name):
+
+
+def prep_inputs_kernel(idx_ref, x_ref, p_ref, half_ref, quarter_ref, full):
+    ordered_rows(x_ref, p_ref, full)
+    half, quarter = half_ref.shape[0], quarter_ref.shape[0]
+    half_ref[...] = full[pl.ds(pl.multiple_of(idx_ref[0] * half, half), half), :]
+    quarter_ref[...] = full[pl.ds(pl.multiple_of(idx_ref[1] * quarter, quarter), quarter), :]
+
+
+def prep_cotangent_kernel(idx_ref, x_ref, p_ref, first_a_ref, first_b_ref, second_ref, away_a_ref, away_b_ref, full):
+    ordered_rows(x_ref, p_ref, full)
+    quarter, width = first_a_ref.shape
+    cols = [pl.ds(pl.multiple_of(idx_ref[2 + k] * width, width), width) for k in range(2)]
+    first = pl.ds(pl.multiple_of(idx_ref[0] * 2 * quarter, quarter), quarter)
+    second = pl.ds(pl.multiple_of(idx_ref[0] * 2 * quarter + quarter, quarter), quarter)
+    away = pl.ds(pl.multiple_of(idx_ref[1] * quarter, quarter), quarter)
+    first_a_ref[...] = full[first, cols[0]]
+    first_b_ref[...] = full[first, cols[1]]
+    second_ref[:, :width] = full[second, cols[0]]
+    second_ref[:, width:] = full[second, cols[1]]
+    away_a_ref[...] = full[away, cols[1]]
+    away_b_ref[...] = full[away, cols[0]]
+
+
+def prep(kernel, idx, x, shapes, name):
     rows, depth = x.shape
-    shapes = [jax.ShapeDtypeStruct((rows, depth), BF16)]
-    for _ in range(parts):
-        shapes.append(jax.ShapeDtypeStruct((rows // 2, depth // parts), F32))
-        shapes.append(jax.ShapeDtypeStruct((rows // 4, depth // parts), F32))
-    kernel = functools.partial(prep_kernel, parts=parts)
-    return resident(kernel, tuple(shapes), (idx, x), name, [pltpu.VMEM((rows, depth), F32)])
+    shapes = (jax.ShapeDtypeStruct((rows, depth), BF16), *[jax.ShapeDtypeStruct(shape, F32) for shape in shapes])
+    return resident(kernel, shapes, (idx, x), name, [pltpu.VMEM((rows, depth), F32)])
 
 
 def pack_kernel(*refs):
@@ -218,49 +228,41 @@
 def forward_kernel(idx_ref, *refs, roles):
     xs = refs[:roles]
     w_ref, scale_ref, decay_ref, retain_ref, enter_ref = refs[roles : roles + 5]
-    outs = refs[roles + 5 : -3]
-    drive, held, sems = refs[-3:]
-    copies = []
+    outs = refs[roles + 5 : -2]
+    drive, state = refs[-2:]
     decays = decay_tiles(decay_ref)
     count = len(decays)
     rows_all = drive.shape[0]
     steps = rows_all // SEG
     for role in range(roles):
-        track_ref, low_ref = held.at[role], outs[2 * role + 1]
+        start_ref, low_ref = outs[2 * role : 2 * role + 2]
         block = idx_ref[role]
         base = block * rows_all
         drive[...] = nn(xs[role][...], w_ref[...]) * scale_ref[...]
         end, rate = scan_ends(drive, retain_ref, base, decays, False)
         start, _ = seg_starts(end, rate, enter_ref[pl.ds(block, 1), :], False)
-        track_ref[0:SEG, :] = start
-
-        def lap(j, before, base=base, track_ref=track_ref):
+        start_ref[...] = start
+
+        def lap(j, before, base=base):
             at = pl.multiple_of(j * SEG, SEG)
             kept = retain_ref[pl.ds(pl.multiple_of(base + j * SEG, SEG), SEG), :]
             out = []
             for l in range(count):
                 now = kept * decays[l] * before[l] + drive[pl.ds(at, SEG), lanes_of(l)]
-                track_ref[pl.ds(pl.multiple_of(at + SEG, SEG), SEG), lanes_of(l)] = now
+                state[pl.ds(at, SEG), lanes_of(l)] = now
                 out.append(now)
             return tuple(out)
 
         lax.fori_loop(0, steps, lap, tuple(start[:, lanes_of(l)] for l in range(count)), unroll=4)
-        copies.append(pltpu.make_async_copy(track_ref, outs[2 * role], sems.at[role]))
-        copies[-1].start()
-        low_ref[...] = track_ref[SEG:, :].astype(BF16)
-    for copy in copies:
-        copy.wait()
+        low_ref[...] = state[...].astype(BF16)
 
 
 def backward_kernel(idx_ref, side_ref, *refs, roles, parts, scaling):
     cs = refs[: roles * parts]
     v_ref, scale_ref, decay_ref, retain_ref, enter_ref = refs[roles * parts : roles * parts + 5]
-    tracks = refs[roles * parts + 5 : roles * parts + 5 + roles]
-    outs = refs[roles * parts + 5 + roles : -4]
-    scot, adjoint, held, sems = refs[-4:]
-    copies = [pltpu.make_async_copy(track, held.at[k], sems.at[k]) for k, track in enumerate(tracks)]
-    for copy in copies:
-        copy.start()
+    entering = refs[roles * parts + 5 : roles * parts + 5 + 2 * roles]
+    outs = refs[roles * parts + 5 + 2 * roles : -3]
+    scot, adjoint, track = refs[-3:]
     decays = decay_tiles(decay_ref)
     count = len(decays)
     rows_all = scot.shape[0]
@@ -282,9 +284,11 @@
         end, rate = scan_ends(scot, retain_ref, base, decays, True)
         start, _ = seg_starts(end, rate, enter_ref[pl.ds(block, 1), :], True)
 
-        copies[role].wait()
-
-        def lap(k, carry, base=base, track_ref=held.at[role]):
+        start_ref, low_ref = entering[2 * role : 2 * role + 2]
+        track[0:SEG, :] = start_ref[...]
+        track[SEG:, :] = low_ref[...].astype(F32)
+
+        def lap(k, carry, base=base):
             at = (steps - 1 - k) * SEG
             rows = pl.ds(pl.multiple_of(at, SEG), SEG)
             kept = retain_ref[pl.ds(pl.multiple_of(base + at, SEG), SEG), :]
@@ -294,7 +298,7 @@
                 here = scot[rows, lanes_of(l)] + follow
                 adjoint[rows, lanes_of(l)] = here
                 part = kept * here
-                out.append((part * decays[l], grad + part * track_ref[rows, lanes_of(l)]))
+                out.append((part * decays[l], grad + part * track[rows, lanes_of(l)]))
             return tuple(out)
 
         begin = tuple((start[:, lanes_of(l)], jnp.zeros((SEG, 128), F32)) for l in range(count))
@@ -306,54 +310,54 @@
 def forward_call(blocks, xs, operands, name):
     channels = operands[1].shape[1]
     rows, roles = xs[0].shape[0], len(xs)
-    shapes = (jax.ShapeDtypeStruct((SEG + rows, channels), F32), jax.ShapeDtypeStruct((rows, channels), BF16)) * roles
+    shapes = (jax.ShapeDtypeStruct((SEG, channels), F32), jax.ShapeDtypeStruct((rows, channels), BF16)) * roles
     out = resident(
         functools.partial(forward_kernel, roles=roles), shapes, (blocks, *xs, *operands), name,
-        [
-            pltpu.VMEM((rows, channels), F32),
-            pltpu.VMEM((roles, SEG + rows, channels), F32),
-            pltpu.SemaphoreType.DMA((roles,)),
-        ],
-        out_specs=(ANY, VMEM) * roles,
+        [pltpu.VMEM((rows, channels), F32)] * 2,
     )
     return list(out[::2]), list(out[1::2])
 
 
-def backward_call(blocks, sides, cs, operands, tracks, scaling, name):
+def backward_call(blocks, sides, cs, operands, starts, lows, scaling, name):
     channels = operands[1].shape[1]
     rows, roles = cs[0][0].shape[0], len(cs)
     kernel = functools.partial(backward_kernel, roles=roles, parts=len(cs[0]), scaling=scaling)
     shapes = (jax.ShapeDtypeStruct((rows, channels), BF16), jax.ShapeDtypeStruct((1, channels), F32)) * roles
     out = resident(
-        kernel, shapes, (blocks, sides, *[part for c in cs for part in c], *operands, *tracks), name,
-        [pltpu.VMEM((rows, channels), F32)] * 2
-        + [pltpu.VMEM((roles, *tracks[0].shape), F32), pltpu.SemaphoreType.DMA((roles,))],
-        scalars=2, anywhere=roles,
+        kernel, shapes, (blocks, sides, *[part for c in cs for part in c], *operands, *[r for pair in zip(starts, lows, strict=True) for r in pair]), name,
+        [pltpu.VMEM((rows, channels), F32)] * 2 + [pltpu.VMEM((SEG + rows, channels), F32)], scalars=2,
     )
     return list(out[::2]), list(out[1::2])
 
 
-def grad_kernel(idx_ref, *refs, factor):
-    half = (len(refs) - 1) // 2
-    width = refs[-1].shape[0]
+def grad_kernel(idx_ref, *refs, count, factor):
+    features, values, sums, out_ref = refs[:count], refs[count : 2 * count], refs[2 * count : -1], refs[-1]
+    width = out_ref.shape[0] - (SEG if sums else 0)
     at = pl.ds(pl.multiple_of(idx_ref[0] * width, width), width)
-    total = tn(refs[0][:, at], refs[half][...])
-    for k in range(1, half):
-        total += tn(refs[k][:, at], refs[half + k][...])
-    refs[-1][...] = total * factor if factor is not None else total
-
-
-def grad_rows(at, features, values, rows_out, factor, name):
+    total = tn(features[0][:, at], values[0][...])
+    for k in range(1, count):
+        total += tn(features[k][:, at], values[k][...])
+    out_ref[0:width, :] = total * factor if factor is not None else total
+    if sums:
+        row = (sums[0][...] + sums[1][...]) + (sums[2][...] + sums[3][...])
+        out_ref[width:, :] = jnp.broadcast_to(row, (SEG, row.shape[1]))
+
+
+def grad_rows(at, features, values, rows_out, factor, name, sums=()):
     channels = values[0].shape[1]
-    rows = values[0].shape[0]
     if rows_out % 128:
         total = sum(
             tn(lax.dynamic_slice_in_dim(x, at * rows_out, rows_out, axis=1), v) for x, v in zip(features, values, strict=True)
         )
-        return total * factor if factor is not None else total
+        total = total * factor if factor is not None else total
+        if sums:
+            row = (sums[0] + sums[1]) + (sums[2] + sums[3])
+            total = jnp.concatenate([total, jnp.broadcast_to(row, (SEG, channels))], axis=0)
+        return total
     return resident(
-        functools.partial(grad_kernel, factor=factor), jax.ShapeDtypeStruct((rows_out, channels), F32),
-        (jnp.reshape(at, (1,)).astype(jnp.int32), *features, *values), name,
+        functools.partial(grad_kernel, count=len(values), factor=factor),
+        jax.ShapeDtypeStruct((rows_out + (SEG if sums else 0), channels), F32),
+        (jnp.reshape(at, (1,)).astype(jnp.int32), *features, *values, *sums), name,
     )
 
 
@@ -426,19 +430,27 @@
 
     line = Order()
     where = jnp.stack([lane % 2, lane, side * 0]).astype(jnp.int32)
-    x_own, x_half, x_quarter = line.step(*prep(where, inputs, 1, "prep_inputs"))
+    x_own, x_half, x_quarter = line.step(
+        *prep(prep_inputs_kernel, where, inputs, [(half, depth), (quarter, depth)], "prep_inputs")
+    )
     near_x = line.send(x_half, "tm", 1)
     away_x = line.send(x_quarter, "tm", far)
     where = jnp.stack([lane % 2, lane, side, 1 - side]).astype(jnp.int32)
-    c_own, c_half_a, c_quarter_a, c_half_b, c_quarter_b = prep(where, line.behind(cotangent), 2, "prep_cotangent")
+    part = (quarter, depth // 2)
+    c_own, c_first_a, c_first_b, c_second, c_quarter_a, c_quarter_b = prep(
+        prep_cotangent_kernel, where, line.behind(cotangent), [part, part, (quarter, depth), part, part], "prep_cotangent"
+    )
     ends = resident(
         functools.partial(summary_kernel, scaling=scaling), jax.ShapeDtypeStruct((3, channels), F32),
         (x_own, c_own, in_proj, out_proj, scale, decay_row, jnp.broadcast_to(ordered(retain), (rows, 128))), "summary",
         [pltpu.VMEM((rows, channels), F32)] * 2, scalars=0,
     )
     table = jnp.concatenate([ends, jnp.pad(retain, (0, channels - rows))[None, :]], axis=0)[None]
-    for bit in reach(devices)[:-1]:
-        table = jnp.concatenate([table, line.send(table, "tm", bit)])
+    if groups == 2:
+        table = jnp.concatenate([table] + [line.send(table, "tm", bit) for bit in (2, 3, 1)])
+    else:
+        for bit in reach(devices)[:-1]:
+            table = jnp.concatenate([table, line.send(table, "tm", bit)])
     near_x, away_x, table = line.step(near_x, away_x, table)
 
     corner_x = line.send(away_x, "tm", 1)
@@ -448,23 +460,23 @@
     enter_fwd, enter_bwd, retain_all = carries(me[None].astype(jnp.int32), table)
     corner_x, side_x, away_a, enter_fwd = line.step(corner_x, side_x, away_a, enter_fwd)
 
-    near_a = line.send(c_half_a, "tm", 1)
+    near_a1 = line.send(c_first_a, "tm", 1)
     corner_a = line.send(away_a, "tm", 1)
     corner_side_x = line.send(corner_x, "chan", 2)
     away_b = line.send(c_quarter_b, "tm", far)
     retain_wide = jnp.broadcast_to(ordered(retain_all[:, :rows]), (devices * rows, 128))
     forward = (in_proj, scale, decay_row, retain_wide, enter_fwd)
     backward = (out_proj, scale, decay_row, retain_wide, enter_bwd)
-    tracks, lows = forward_call(blocks[:1], [x_own], forward, "forward_own")
-    scaled, grads = backward_call(blocks[:1], sides, [[c_own]], backward, tracks, scaling, "backward_own")
+    starts, lows = forward_call(blocks[:1], [x_own], forward, "forward_own")
+    scaled, grads = backward_call(blocks[:1], sides, [[c_own]], backward, starts, lows, scaling, "backward_own")
     parts = row_grad(scaled[0], in_proj, lanes)
     other_x = line.send(pack([near_x, away_x, side_x, corner_x], "pack_x"), "chan", 1)
-    corner_side_x, corner_a, near_a, away_b, parts, other_x = line.step(corner_side_x, corner_a, near_a, away_b, parts, other_x)
+    corner_side_x, corner_a, near_a1, away_b, parts, other_x = line.step(corner_side_x, corner_a, near_a1, away_b, parts, other_x)
 
     corner_b = line.send(away_b, "tm", 1)
     corner_side_a = line.send(corner_a, "chan", 2)
     side_a = line.send(away_a, "chan", 2)
-    near_b1 = line.send(c_half_b[:quarter], "tm", 1)
+    near_2 = line.send(c_second, "tm", 1)
     last_x = line.send(corner_side_x, "chan", 1)
     side_b = line.send(away_b, "chan", 2)
     xs = [x_own] + collected(place, [
@@ -472,43 +484,44 @@
         (other_x, their_near + their_1 + their_2 + their_3), (last_x, their_4),
     ], "collect_x")
     more, more_low = forward_call(blocks[1:], xs[1:], forward, "forward_group")
-    tracks, lows = tracks + more, lows + more_low
-    corner_side_a, side_a, side_b, corner_b, near_b1, lows[1] = line.step(corner_side_a, side_a, side_b, corner_b, near_b1, lows[1])
+    starts, lows = starts + more, lows + more_low
+    corner_side_a, side_a, side_b, corner_b, near_2, lows[1] = line.step(corner_side_a, side_a, side_b, corner_b, near_2, lows[1])
+    near_a2, near_b2 = near_2[:, : depth // 2], near_2[:, depth // 2 :]
 
     corner_side_b = line.send(corner_b, "chan", 2)
-    near_b2 = line.send(c_half_b[quarter:], "tm", 1)
-    other_a = line.send(pack([near_a, away_a, side_a, corner_a, corner_side_a], "pack_a"), "chan", 1)
+    near_b1 = line.send(c_first_b, "tm", 1)
+    other_a = line.send(pack([near_a1, near_a2, away_a, side_a, corner_a, corner_side_a], "pack_a"), "chan", 1)
     own_a = lax.dynamic_slice_in_dim(c_own, side * (depth // 2), depth // 2, axis=1)
     ca = [own_a] + collected(place, [
-        (near_a, mine_near), (away_a, mine_1), (side_a, mine_2), (corner_a, mine_3), (corner_side_a, mine_4),
-        (other_a, their_near + their_1 + their_2 + their_3 + their_4),
+        (near_a1, [(0, 6, quarter)]), (near_a2, [(0, 7, quarter)]),
+        (away_a, mine_1), (side_a, mine_2), (corner_a, mine_3), (corner_side_a, mine_4),
+        (other_a, [(0, 8, quarter), (0, 9, quarter)] + their_1 + their_2 + their_3 + their_4),
     ], "collect_a")
 
-    def shares(features, values, block, factor, name):
-        return [grad_rows(block ^ (2 * k), features, values, rows_out, factor, name) for k in range(1, groups)]
+    def shares(features, values, block, factor, name, sums=()):
+        return [grad_rows(block ^ (2 * k), features, values, rows_out, factor, name, sums) for k in range(1, groups)]
 
     out_given = shares(ca, lows, me % far, scaling, "out_grad")
-    out_given[0], corner_side_b, near_b2 = line.step(out_given[0], corner_side_b, near_b2)
+    out_given[0], corner_side_b, near_b1 = line.step(out_given[0], corner_side_b, near_b1)
 
     out_got = [line.send(part, "tm", 2 * (k + 1)) for k, part in enumerate(out_given)]
-    other_b = line.send(pack([away_b, side_b, corner_b, corner_side_b, near_b1, near_b2], "pack_b"), "chan", 1)
+    near_b1_other = line.send(near_b1, "chan", 1)
+    near_b2_other = line.send(near_b2, "chan", 1)
+    away_b_other = line.send(away_b, "chan", 1)
+    other_b = line.send(pack([side_b, corner_b, corner_side_b], "pack_b"), "chan", 1)
     cb = collected(place, [
         (near_b1, [(0, 6, quarter)]), (near_b2, [(0, 7, quarter)]),
         (away_b, mine_1), (side_b, mine_2), (corner_b, mine_3), (corner_side_b, mine_4),
-        (other_b, their_1 + their_2 + their_3 + their_4 + [(0, 8, quarter), (0, 9, quarter)]),
+        (near_b1_other, [(0, 8, quarter)]), (near_b2_other, [(0, 9, quarter)]), (away_b_other, their_1),
+        (other_b, their_2 + their_3 + their_4),
     ], "collect_b")
     cs = [list(pair) for pair in zip(ca[1:], cb, strict=True)]
-    more, more_grads = backward_call(blocks[1:], sides, cs, backward, tracks[1:], scaling, "backward_group")
+    more, more_grads = backward_call(blocks[1:], sides, cs, backward, starts[1:], lows[1:], scaling, "backward_group")
     scaled, grads = scaled + more, grads + more_grads
-    in_given = shares(xs, scaled, me, None, "in_grad")
+    in_given = shares(xs, scaled, me, None, "in_grad", grads)
     in_given[0] = line.step(in_given[0])
     in_got = [line.send(part, "tm", 2 * (k + 1)) for k, part in enumerate(in_given)]
     out_got[0] = line.step(out_got[0])
-    decay_grad = (grads[0] + grads[1]) + (grads[2] + grads[3])
-    bit = 2
-    while bit < far:
-        decay_grad += line.send(decay_grad, "tm", bit)
-        bit *= 2
     bit = 1
     while bit < lanes:
         parts = parts.reshape(-1, 2, *parts.shape[1:])
@@ -521,8 +534,16 @@
     in_got[0] = after(in_got[0], input_grad)
 
     out_proj_grad = sum(out_got, grad_rows(me % far, [line.behind(ca[0]), *ca[1:]], lows, rows_out, scaling, "out_grad"))
-    in_proj_grad = sum(in_got, grad_rows(me, [line.behind(xs[0]), *xs[1:]], scaled, rows_out, None, "in_grad"))
-    return (in_proj_grad, out_proj_grad, decay_grad[0], input_grad)
+    in_mine = grad_rows(me, [line.behind(xs[0]), *xs[1:]], scaled, rows_out, None, "in_grad", grads)
+    in_proj_grad = sum((part[:rows_out] for part in in_got), in_mine[:rows_out])
+    decay_grad = sum((part[rows_out] for part in in_got), in_mine[rows_out])
+    if groups > 2:
+        decay_grad = in_mine[rows_out]
+        bit = 2
+        while bit < far:
+            decay_grad += swap(decay_grad, "tm", bit)
+            bit *= 2
+    return (in_proj_grad, out_proj_grad, decay_grad, input_grad)
 
 
 def solution(mesh):

time: 175 us -> 164 us (0.937)
  waiting for transfers between devices: 53.4 us -> 37.4 us
  starting transfers between devices: 25.1 us -> 32 us
  Pallas kernels: 47.1 us -> 44.8 us
    ppermute x28 -> x31, waiting for transfers between devices: 53.4 us -> 37.4 us  [swap(): return lax.ppermute(x, axis, [(k, k ^ bit) for k in range(n)])]
    ppermute x28 -> x31, starting transfers between devices: 25.1 us -> 32 us  [swap(): return lax.ppermute(x, axis, [(k, k ^ bit) for k in range(n)])]
    pallas_call x19, Pallas kernels: 47.1 us -> 44.8 us  [resident(): pl.pallas_call(kernel, out_shape=out_shape, in_specs=[SMEM] * scalars + [...]
    unnamed x136 -> x146, local copies, waits for them, and re-layouts: 30 us -> 28.8 us
    add x3 -> x2, other arithmetic: 2.94 us -> 3.71 us  [the longest x1 2.36 us: per_device(): in_proj_grad = sum((part[:rows_out] for part in in_got), in_mine[:rows_out])]
  transfers between devices with their start and end apart: 28 -> 31, of which waited for: 12 -> 12; matrix products, arithmetic and copies ran while one was open for 8% -> 8% of each run, Pallas kernels for 21% -> 23%
where the time goes in v4:
time: 164 us; the launch traced here: 163 us
  Pallas kernels  44.8 us (27%)
  waiting for transfers between devices  37.4 us (23%)
  local copies, waits for them, and re-layouts  37.2 us (23%)
  starting transfers between devices  32 us (20%)
  other arithmetic  10.1 us (6%)
    pallas_call x19, Pallas kernels, resident(): pl.pallas_call(kernel, out_shape=out_shape, in_specs=[SMEM] * scalars + [...  44.8 us
    ppermute x31, waiting for transfers between devices, swap(): return lax.ppermute(x, axis, [(k, k ^ bit) for k in range(n)])  37.4 us
    ppermute x31, starting transfers between devices, swap(): return lax.ppermute(x, axis, [(k, k ^ bit) for k in range(n)])  32 us
    unnamed x146, local copies, waits for them, and re-layouts  28.8 us
  transfers between devices with their start and end apart: 31, of which 12 were waited for; matrix products, arithmetic and copies ran while one was open for 8% of the time, Pallas kernels for 23%

profile of v4, /device:TPU:0, one launch (start us, length us, event | category | flops | bytes accessed | tf_op | source)
XLA Modules:
  0.0 163.0 jit_solution(15347862747472222996)
XLA Ops:
  2.0 2.3 %prep_inputs.1 = (bf16[256,2048]{1,0:T(8,128)(2,1)S(1)}, f32[128,2048]{1,0:T(8,128)}, f32[64,2048]{1,0:T(8,128)}) custom-call(s32[3]{0:T(128)S(1)} %pad_add_fusion.idx_ref, bf16[256,2048]{1,0:T(8,128)(2,1)S(1)} %copy-done.55), custom_call_target="tpu_custom_call" | custom-call | tf_op jit(solution)/shard_map/prep_inputs/pallas_call | solution.py:49
  4.2 2.9 %collective-permute-start = (f32[128,2048]{1,0:T(8,128)}, f32[128,2048]{1,0:T(8,128)S(1)}, u32[]{:S(2)}, u32[]{:S(2)}) collective-permute-start(f32[128,2048]{1,0:T(8,128)} %get-tuple-element.100), channel_id=1, source_target_pairs={{0,4},{4,0},{8,12},{12,8},{16,20},{20,16},{24,28},{28,24},{1,5},{5... | collective-permute-start | bytes 3145736 | tf_op jit(solution)/shard_map/ppermute | solution.py:19
  7.2 2.6 %collective-permute-start.1 = (f32[64,2048]{1,0:T(8,128)}, f32[64,2048]{1,0:T(8,128)}, u32[]{:S(2)}, u32[]{:S(2)}) collective-permute-start(f32[64,2048]{1,0:T(8,128)} %get-tuple-element.102), channel_id=1, source_target_pairs={{0,16},{4,20},{8,24},{12,28},{16,0},{20,4},{24,8},{28,12},{1,17},{... | collective-permute-start | bytes 1572872 | tf_op jit(solution)/shard_map/ppermute | solution.py:19
  12.7 2.2 %prep_cotangent.1 = (bf16[256,2048]{1,0:T(8,128)(2,1)S(1)}, f32[64,1024]{1,0:T(8,128)}, f32[64,1024]{1,0:T(8,128)}, f32[64,2048]{1,0:T(8,128)}, f32[64,1024]{1,0:T(8,128)S(1)}, /*index=5*/f32[64,1024]{1,0:T(8,128)}) custom-call(s32[4]{0:T(128)S(1)} %pad_add_fusion.1.idx_ref, bf16[256,2048]{1,0:T(8,128)(2,1)S(1)} %copy-done.56), custom_call_target="tpu_custom_call" | custom-call | tf_op jit(solution)/shard_map/prep_cotangent/pallas_call | solution.py:49
  15.0 2.5 %copy-done = bf16[2048,1024]{1,0:T(8,128)(2,1)S(1)} copy-done((bf16[2048,1024]{1,0:T(8,128)(2,1)S(1)}, bf16[2048,1024]{1,0:T(8,128)(2,1)}, u32[]{:S(2)}) %copy-start) | copy-done | bytes 4194328
  17.4 2.2 %copy-done.4 = bf16[1024,2048]{1,0:T(8,128)(2,1)S(1)} copy-done((bf16[1024,2048]{1,0:T(8,128)(2,1)S(1)}, bf16[1024,2048]{1,0:T(8,128)(2,1)}, u32[]{:S(2)}) %copy-start.4) | copy-done | bytes 4194328
  19.6 2.9 %summary.1 = f32[3,1024]{1,0:T(4,128)S(1)} custom-call(bf16[256,2048]{1,0:T(8,128)(2,1)S(1)} %get-tuple-element.181.x_ref.refs_0_, bf16[256,2048]{1,0:T(8,128)(2,1)S(1)} %get-tuple-element.98.c_ref.refs_0_, bf16[2048,1024]{1,0:T(8,128)(2,1)S(1)} %copy-done, bf16[1024,2048]{1,0:T(8,128)(2,1)S(1)} %copy-done.4, f32[1,1024]{1,0:T(1,128)S(1)} %bitcast.36, ...), custom_call_target="tpu_custom_call" | custom-call | tf_op jit(solution)/shard_map/summary/pallas_call | solution.py:49
  26.1 7.2 %collective-permute-done.2 = f32[1,4,1024]{2,1,0:T(4,128)S(1)} collective-permute-done((f32[1,4,1024]{2,1,0:T(4,128)S(1)}, f32[1,4,1024]{2,1,0:T(4,128)S(1)}, u32[]{:S(2)}, u32[]{:S(2)}) %collective-permute-start.2) | collective-permute-done | bytes 16416 | tf_op jit(solution)/shard_map/ppermute | solution.py:19
  37.4 2.2 %collective-permute-start.8 = (f32[4,4,1024]{2,1,0:T(4,128)S(1)}, f32[4,4,1024]{2,1,0:T(4,128)S(1)}, u32[]{:S(2)}, u32[]{:S(2)}) collective-permute-start(f32[4,4,1024]{2,1,0:T(4,128)S(1)} %pad_maximum_fusion.1), channel_id=1, source_target_pairs={{0,20},{4,16},{8,28},{12,24},{16,4},{20,0},{24,12},{28,8},{1,21},{... | collective-permute-start | bytes 196616 | tf_op jit(solution)/shard_map/ppermute | solution.py:19
  39.6 14.1 %collective-permute-done.8 = f32[4,4,1024]{2,1,0:T(4,128)S(1)} collective-permute-done((f32[4,4,1024]{2,1,0:T(4,128)S(1)}, f32[4,4,1024]{2,1,0:T(4,128)S(1)}, u32[]{:S(2)}, u32[]{:S(2)}) %collective-permute-start.8) | collective-permute-done | bytes 65568 | tf_op jit(solution)/shard_map/ppermute | solution.py:19
  53.9 2.9 %pack_x.1 = f32[320,2048]{1,0:T(8,128)} custom-call(f32[128,2048]{1,0:T(8,128)S(1)} %collective-permute-done.refs_0_, f32[64,2048]{1,0:T(8,128)} %collective-permute-done.1.refs_1_, f32[64,2048]{1,0:T(8,128)S(1)} %collective-permute-done.6.refs_2_, f32[64,2048]{1,0:T(8,128)} %collective-permute-done.5.refs_3_), custom_call_target="tpu_custom_call" | custom-call | tf_op jit(solution)/shard_map/pack_x/pallas_call | solution.py:49
  60.2 2.2 %copy-done.1 = bf16[2048,1024]{1,0:T(8,128)(2,1)S(1)} copy-done((bf16[2048,1024]{1,0:T(8,128)(2,1)S(1)}, bf16[2048,1024]{1,0:T(8,128)(2,1)}, u32[]{:S(2)}) %copy-start.1) | copy-done | bytes 4194328
  64.6 2.4 %backward_own.1 = (bf16[256,1024]{1,0:T(8,128)(2,1)S(1)}, f32[1,1024]{1,0:T(1,128)S(1)}) custom-call(s32[1]{0:T(128)} %bitcast.idx_ref, s32[2]{0:T(128)S(1)} %pad_add_fusion.2.side_ref, bf16[256,2048]{1,0:T(8,128)(2,1)S(1)} %get-tuple-element.98.c_ref.refs_0_, bf16[1024,2048]{1,0:T(8,128)(2,1)S(1)} %copy-done.5, f32[1,1024]{1,0:T(1,128)S(1)} %bitcast.38, ...), custom_call_target="tpu_custom_call" | custom-call | tf_op jit(solution)/shard_map/backward_own/pallas_call | solution.py:49
  69.8 2.6 %collective-permute-done.12.refs_2_ = f32[64,1024]{1,0:T(8,128)} collective-permute-done((f32[64,1024]{1,0:T(8,128)}, f32[64,1024]{1,0:T(8,128)}, u32[]{:S(2)}, u32[]{:S(2)}) %collective-permute-start.12) | collective-permute-done | bytes 262176 | tf_op jit(solution)/shard_map/ppermute | solution.py:19
  82.5 3.3 %collect_x.1 = (bf16[256,2048]{1,0:T(8,128)(2,1)S(1)}, bf16[256,2048]{1,0:T(8,128)(2,1)S(1)}, bf16[256,2048]{1,0:T(8,128)(2,1)S(1)}) custom-call(s32[10]{0:T(128)S(1)} %stack.81.idx_ref, f32[128,2048]{1,0:T(8,128)S(1)} %copy-done.45, f32[64,2048]{1,0:T(8,128)} %collective-permute-done.1.refs_1_, f32[64,2048]{1,0:T(8,128)S(1)} %copy-done.47, ...), custom_call_target="tpu_custom_call" | custom-call | tf_op jit(solution)/shard_map/collect_x/pallas_call | solution.py:49
  86.0 5.6 %forward_group.1 = (f32[8,1024]{1,0:T(8,128)S(1)}, bf16[256,1024]{1,0:T(8,128)(2,1)S(1)}, f32[8,1024]{1,0:T(8,128)S(1)}, bf16[256,1024]{1,0:T(8,128)(2,1)S(1)}, ...) custom-call(s32[3]{0:T(128)S(1)} %pad_add_fusion.3.idx_ref, ...), custom_call_target="tpu_custom_call" | custom-call | tf_op jit(solution)/shard_map/forward_group/pallas_call | solution.py:49
  93.4 1.8 %fusion.1 = (f32[64,1024]{1,0:T(8,128)}, f32[64,1024]{1,0:T(8,128)S(1)}) fusion(f32[64,2048]{1,0:T(8,128)} %collective-permute-done.18), kind=kLoop, calls=%fused_computation.15 | loop fusion | bytes 1048576 | tf_op jit(solution)/shard_map/slice | solution.py:489
  95.1 2.4 %pack_a.1 = f32[384,1024]{1,0:T(8,128)} custom-call(f32[64,1024]{1,0:T(8,128)} %collective-permute-done.11.refs_0_, f32[64,1024]{1,0:T(8,128)S(1)} %get-tuple-element.189.refs_1_, f32[64,1024]{1,0:T(8,128)S(1)} %copy-done.58, f32[64,1024]{1,0:T(8,128)} %collective-permute-done.15.refs_3_, f32[64,1024]{1,0:T(8,128)} %collective-permute-done.10.refs_4_, ...), custom_call_target="tpu_custom_call" | custom-call | tf_op jit(solution)/shard_map/pack_a/pallas_call | solution.py:49
  102.8 2.4 %collect_a.1 = (bf16[256,1024]{1,0:T(8,128)(2,1)S(1)}, bf16[256,1024]{1,0:T(8,128)(2,1)S(1)}, bf16[256,1024]{1,0:T(8,128)(2,1)S(1)}) custom-call(s32[10]{0:T(128)S(1)} %stack.81.idx_ref, f32[64,1024]{1,0:T(8,128)} %collective-permute-done.11.refs_0_, f32[64,1024]{1,0:T(8,128)S(1)} %get-tuple-element.189.refs_1_, f32[64,1024]{1,0:T(8,128)S(1)} %copy-done.59, ...), custom_call_target="tpu_custom_call" | custom-call | tf_op jit(solution)/shard_map/collect_a/pallas_call | solution.py:49
  105.3 1.8 %out_grad.2 = f32[256,1024]{1,0:T(8,128)} custom-call(s32[1]{0:T(128)} %bitcast.3.idx_ref, bf16[256,1024]{1,0:T(8,128)(2,1)S(1)} %constant_dynamic-slice_fusion.1.refs_0_, bf16[256,1024]{1,0:T(8,128)(2,1)S(1)} %get-tuple-element.147.refs_1_.refs_0_, bf16[256,1024]{1,0:T(8,128)(2,1)S(1)} %get-tuple-element.148.refs_2_, ...), custom_call_target="tpu_custom_call" | custom-call | tf_op jit(solution)/shard_map/out_grad/pallas_call | solution.py:49
  109.6 2.0 %pack_b.1 = f32[192,1024]{1,0:T(8,128)} custom-call(f32[64,1024]{1,0:T(8,128)} %collective-permute-done.16.refs_0_.refs_3_, f32[64,1024]{1,0:T(8,128)} %collective-permute-done.17.refs_1_.refs_4_, f32[64,1024]{1,0:T(8,128)} %collective-permute-done.21.refs_2_.refs_5_), custom_call_target="tpu_custom_call" | custom-call | tf_op jit(solution)/shard_map/pack_b/pallas_call | solution.py:49
  112.8 2.4 %dynamic-slice_bitcast_fusion = f32[2,256,512]{2,1,0:T(8,128)} fusion(f32[2,2,256,512]{3,2,1,0:T(8,128)} %bitcast.34, s32[]{:T(128)S(6)} %select_n.53), kind=kLoop, calls=%fused_computation.2 | loop fusion | bytes 2097156 | tf_op jit(solution)/shard_map/jit(dynamic_index_in_dim)/squeeze | solution.py:530
  115.5 2.6 %collect_b.1 = (bf16[256,1024]{1,0:T(8,128)(2,1)S(1)}, bf16[256,1024]{1,0:T(8,128)(2,1)S(1)}, bf16[256,1024]{1,0:T(8,128)(2,1)S(1)}) custom-call(s32[10]{0:T(128)S(1)} %stack.81.idx_ref, f32[64,1024]{1,0:T(8,128)} %collective-permute-done.22.refs_0_, f32[64,1024]{1,0:T(8,128)S(1)} %copy-done.60, f32[64,1024]{1,0:T(8,128)} %collective-permute-done.12.refs_2_, ...), custom_call_target="tpu_custom_call" | custom-call | tf_op jit(solution)/shard_map/collect_b/pallas_call | solution.py:49
  122.4 6.3 %backward_group.1 = (bf16[256,1024]{1,0:T(8,128)(2,1)S(1)}, f32[1,1024]{1,0:T(1,128)S(1)}, bf16[256,1024]{1,0:T(8,128)(2,1)S(1)}, f32[1,1024]{1,0:T(1,128)S(1)},...) custom-call(s32[3]{0:T(128)S(1)} %copy-done.68, s32[2]{0:T(128)S(1)} %copy-done.70, ...), custom_call_target="tpu_custom_call" | custom-call | tf_op jit(solution)/shard_map/backward_group/pallas_call | solution.py:49
  129.8 2.8 %collective-permute-done.23 = f32[256,1024]{1,0:T(8,128)} collective-permute-done((f32[256,1024]{1,0:T(8,128)}, f32[256,1024]{1,0:T(8,128)}, u32[]{:S(2)}, u32[]{:S(2)}) %collective-permute-start.23) | collective-permute-done | bytes 1048608 | tf_op jit(solution)/shard_map/ppermute | solution.py:19
  132.7 1.8 %collective-permute-start.28 = (f32[264,1024]{1,0:T(8,128)}, f32[264,1024]{1,0:T(8,128)}, u32[]{:S(2)}, u32[]{:S(2)}) collective-permute-start(f32[264,1024]{1,0:T(8,128)} %copy-done.54), channel_id=1, source_target_pairs={{0,8},{4,12},{8,0},{12,4},{16,24},{20,28},{24,16},{28,20},{1,9},{5... | collective-permute-start | bytes 3244040 | tf_op jit(solution)/shard_map/ppermute | solution.py:19
  135.7 1.7 %bitcast_add_fusion = f32[2,256,512]{2,1,0:T(8,128)S(1)} fusion(f32[2,256,512]{2,1,0:T(8,128)} %collective-permute-done.29, f32[2,2,256,512]{3,2,1,0:T(8,128)} %bitcast.35, s32[]{:T(128)S(6)} %select_n.52), kind=kLoop, calls=%fused_computation.1 | loop fusion | flops 262144 | bytes 3145732 | tf_op jit(solution)/shard_map/add | solution.py:531
  148.7 2.5 %add.71 = f32[256,1024]{1,0:T(8,128)} add(f32[256,1024]{1,0:T(8,128)S(1)} %out_grad.3, f32[256,1024]{1,0:T(8,128)} %collective-permute-done.23) | non-fusion elementwise | flops 262144 | bytes 3145728 | tf_op jit(solution)/shard_map/add | solution.py:536
  151.1 2.4 %collective-permute-done.30 = f32[1,256,512]{2,1,0:T(8,128)} collective-permute-done((f32[1,256,512]{2,1,0:T(8,128)}, f32[1,256,512]{2,1,0:T(8,128)}, u32[]{:S(2)}, u32[]{:S(2)}) %collective-permute-start.30) | collective-permute-done | bytes 524320 | tf_op jit(solution)/shard_map/ppermute | solution.py:19
  153.5 1.8 %fusion = bf16[256,512]{1,0:T(8,128)(2,1)} fusion(f32[1,256,512]{2,1,0:T(8,128)} %collective-permute-done.30, f32[2,256,512]{2,1,0:T(8,128)S(1)} %copy-done.72, s32[]{:T(128)S(6)} %select_n.56), kind=kLoop, calls=%fused_computation.4 | loop fusion | flops 262144 | bytes 1310724 | tf_op jit(solution)/shard_map/convert_element_type | solution.py:533
  155.3 3.9 %collective-permute-done.28 = f32[264,1024]{1,0:T(8,128)} collective-permute-done((f32[264,1024]{1,0:T(8,128)}, f32[264,1024]{1,0:T(8,128)}, u32[]{:S(2)}, u32[]{:S(2)}) %collective-permute-start.28) | collective-permute-done | bytes 1081376 | tf_op jit(solution)/shard_map/ppermute | solution.py:19
  160.6 2.4 %slice_add_fusion = f32[256,1024]{1,0:T(8,128)} fusion(f32[264,1024]{1,0:T(8,128)S(1)} %in_grad.3, f32[264,1024]{1,0:T(8,128)} %collective-permute-done.28), kind=kLoop, calls=%fused_computation | loop fusion | flops 262144 | bytes 3145728 | tf_op jit(solution)/shard_map/add | solution.py:538
  (222 shorter events, 60.2 us)
Async XLA Ops:
  4.2 29.3 %collective-permute-start = (f32[128,2048]{1,0:T(8,128)}, f32[128,2048]{1,0:T(8,128)S(1)}, u32[]{:S(2)}, u32[]{:S(2)}) collective-permute-start(f32[128,2048]{1,0:T(8,128)} %get-tuple-element.100), channel_id=1, source_target_pairs={{0,4},{4,0},{8,12},{12,8},{16,20},{20,16},{24,28},{28,24},{1,5},{5... | collective-permute-start | bytes 3145736 | tf_op jit(solution)/shard_map/ppermute | solution.py:19
  7.2 26.4 %collective-permute-start.1 = (f32[64,2048]{1,0:T(8,128)}, f32[64,2048]{1,0:T(8,128)}, u32[]{:S(2)}, u32[]{:S(2)}) collective-permute-start(f32[64,2048]{1,0:T(8,128)} %get-tuple-element.102), channel_id=1, source_target_pairs={{0,16},{4,20},{8,24},{12,28},{16,0},{20,4},{24,8},{28,12},{1,17},{... | collective-permute-start | bytes 1572872 | tf_op jit(solution)/shard_map/ppermute | solution.py:19
  14.8 49.3 %copy-start.14 = (bf16[256,2048]{1,0:T(8,128)(2,1)}, bf16[256,2048]{1,0:T(8,128)(2,1)S(1)}, u32[]{:S(2)}) copy-start(bf16[256,2048]{1,0:T(8,128)(2,1)S(1)} %get-tuple-element.98.c_ref.refs_0_) | copy-start | bytes 3145732
  22.6 10.8 %collective-permute-start.2 = (f32[1,4,1024]{2,1,0:T(4,128)S(1)}, f32[1,4,1024]{2,1,0:T(4,128)S(1)}, u32[]{:S(2)}, u32[]{:S(2)}) collective-permute-start(f32[1,4,1024]{2,1,0:T(4,128)S(1)} %maximum_bitcast_fusion), channel_id=1, source_target_pairs={{0,8},{4,12},{8,0},{12,4},{16,24},{20,28},{24,16},{28,20},{1,9},{5... | collective-permute-start | bytes 49160 | tf_op jit(solution)/shard_map/ppermute | solution.py:19
  24.2 9.3 %collective-permute-start.3 = (f32[1,4,1024]{2,1,0:T(4,128)S(1)}, f32[1,4,1024]{2,1,0:T(4,128)S(1)}, u32[]{:S(2)}, u32[]{:S(2)}) collective-permute-start(f32[1,4,1024]{2,1,0:T(4,128)S(1)} %maximum_bitcast_fusion), channel_id=1, source_target_pairs={{0,12},{4,8},{8,4},{12,0},{16,28},{20,24},{24,20},{28,16},{1,13},{... | collective-permute-start | bytes 49160 | tf_op jit(solution)/shard_map/ppermute | solution.py:19
  24.6 8.9 %collective-permute-start.4 = (f32[1,4,1024]{2,1,0:T(4,128)S(1)}, f32[1,4,1024]{2,1,0:T(4,128)S(1)}, u32[]{:S(2)}, u32[]{:S(2)}) collective-permute-start(f32[1,4,1024]{2,1,0:T(4,128)S(1)} %maximum_bitcast_fusion), channel_id=1, source_target_pairs={{0,4},{4,0},{8,12},{12,8},{16,20},{20,16},{24,28},{28,24},{1,5},{5... | collective-permute-start | bytes 49160 | tf_op jit(solution)/shard_map/ppermute | solution.py:19
  33.6 20.3 %collective-permute-start.5 = (f32[64,2048]{1,0:T(8,128)}, f32[64,2048]{1,0:T(8,128)}, u32[]{:S(2)}, u32[]{:S(2)}) collective-permute-start(f32[64,2048]{1,0:T(8,128)} %collective-permute-done.1.refs_1_), channel_id=1, source_target_pairs={{0,4},{4,0},{8,12},{12,8},{16,20},{20,16},{24,28},{28,24},{1,5},{5... | collective-permute-start | bytes 1572872 | tf_op jit(solution)/shard_map/ppermute | solution.py:19
  35.2 18.7 %collective-permute-start.6 = (f32[64,2048]{1,0:T(8,128)}, f32[64,2048]{1,0:T(8,128)S(1)}, u32[]{:S(2)}, u32[]{:S(2)}) collective-permute-start(f32[64,2048]{1,0:T(8,128)} %collective-permute-done.1.refs_1_), channel_id=1, source_target_pairs={{0,2},{1,3},{2,0},{3,1},{4,6},{5,7},{6,4},{7,5},{8,10},{9,11},{10,... | collective-permute-start | bytes 1572872 | tf_op jit(solution)/shard_map/ppermute | solution.py:19
  36.7 17.2 %collective-permute-start.7 = (f32[64,1024]{1,0:T(8,128)S(1)}, f32[64,1024]{1,0:T(8,128)S(1)}, u32[]{:S(2)}, u32[]{:S(2)}) collective-permute-start(f32[64,1024]{1,0:T(8,128)S(1)} %get-tuple-element.108), channel_id=1, source_target_pairs={{0,16},{4,20},{8,24},{12,28},{16,0},{20,4},{24,8},{28,12},{1,17},{... | collective-permute-start | bytes 786440 | tf_op jit(solution)/shard_map/ppermute | solution.py:19
  37.4 16.3 %collective-permute-start.8 = (f32[4,4,1024]{2,1,0:T(4,128)S(1)}, f32[4,4,1024]{2,1,0:T(4,128)S(1)}, u32[]{:S(2)}, u32[]{:S(2)}) collective-permute-start(f32[4,4,1024]{2,1,0:T(4,128)S(1)} %pad_maximum_fusion.1), channel_id=1, source_target_pairs={{0,20},{4,16},{8,28},{12,24},{16,4},{20,0},{24,12},{28,8},{1,21},{... | collective-permute-start | bytes 196616 | tf_op jit(solution)/shard_map/ppermute | solution.py:19
  56.9 15.6 %collective-permute-start.13 = (f32[320,2048]{1,0:T(8,128)}, f32[320,2048]{1,0:T(8,128)}, u32[]{:S(2)}, u32[]{:S(2)}) collective-permute-start(f32[320,2048]{1,0:T(8,128)} %pack_x.1), channel_id=1, source_target_pairs={{0,1},{1,0},{2,3},{3,2},{4,5},{5,4},{6,7},{7,6},{8,9},{9,8},{10,11... | collective-permute-start | bytes 7864328 | tf_op jit(solution)/shard_map/ppermute | solution.py:19
  57.0 15.5 %collective-permute-start.9 = (f32[64,2048]{1,0:T(8,128)}, f32[64,2048]{1,0:T(8,128)}, u32[]{:S(2)}, u32[]{:S(2)}) collective-permute-start(f32[64,2048]{1,0:T(8,128)} %collective-permute-done.5.refs_3_), channel_id=1, source_target_pairs={{0,2},{1,3},{2,0},{3,1},{4,6},{5,7},{6,4},{7,5},{8,10},{9,11},{10,... | collective-permute-start | bytes 1572872 | tf_op jit(solution)/shard_map/ppermute | solution.py:19
  57.5 15.0 %collective-permute-start.12 = (f32[64,1024]{1,0:T(8,128)}, f32[64,1024]{1,0:T(8,128)}, u32[]{:S(2)}, u32[]{:S(2)}) collective-permute-start(f32[64,1024]{1,0:T(8,128)} %get-tuple-element.119), channel_id=1, source_target_pairs={{0,16},{4,20},{8,24},{12,28},{16,0},{20,4},{24,8},{28,12},{1,17},{... | collective-permute-start | bytes 786440 | tf_op jit(solution)/shard_map/ppermute | solution.py:19
  57.5 15.0 %collective-permute-start.11 = (f32[64,1024]{1,0:T(8,128)}, f32[64,1024]{1,0:T(8,128)}, u32[]{:S(2)}, u32[]{:S(2)}) collective-permute-start(f32[64,1024]{1,0:T(8,128)} %get-tuple-element.117), channel_id=1, source_target_pairs={{0,4},{4,0},{8,12},{12,8},{16,20},{20,16},{24,28},{28,24},{1,5},{5... | collective-permute-start | bytes 786440 | tf_op jit(solution)/shard_map/ppermute | solution.py:19
  59.1 13.4 %collective-permute-start.10 = (f32[64,1024]{1,0:T(8,128)S(1)}, f32[64,1024]{1,0:T(8,128)}, u32[]{:S(2)}, u32[]{:S(2)}) collective-permute-start(f32[64,1024]{1,0:T(8,128)S(1)} %collective-permute-done.7.refs_2_), channel_id=1, source_target_pairs={{0,4},{4,0},{8,12},{12,8},{16,20},{20,16},{24,28},{28,24},{1,5},{5... | collective-permute-start | bytes 786440 | tf_op jit(solution)/shard_map/ppermute | solution.py:19
  72.5 4.2 %collective-permute-start.19 = (f32[64,2048]{1,0:T(8,128)}, f32[64,2048]{1,0:T(8,128)S(1)}, u32[]{:S(2)}, u32[]{:S(2)}) collective-permute-start(f32[64,2048]{1,0:T(8,128)} %collective-permute-done.9.refs_4_), channel_id=1, source_target_pairs={{0,1},{1,0},{2,3},{3,2},{4,5},{5,4},{6,7},{7,6},{8,9},{9,8},{10,11... | collective-permute-start | bytes 1572872 | tf_op jit(solution)/shard_map/ppermute | solution.py:19
  72.6 20.8 %collective-permute-start.18 = (f32[64,2048]{1,0:T(8,128)}, f32[64,2048]{1,0:T(8,128)}, u32[]{:S(2)}, u32[]{:S(2)}) collective-permute-start(f32[64,2048]{1,0:T(8,128)} %get-tuple-element.136), channel_id=1, source_target_pairs={{0,4},{4,0},{8,12},{12,8},{16,20},{20,16},{24,28},{28,24},{1,5},{5... | collective-permute-start | bytes 1572872 | tf_op jit(solution)/shard_map/ppermute | solution.py:19
  73.4 18.2 %collective-permute-start.16 = (f32[64,1024]{1,0:T(8,128)}, f32[64,1024]{1,0:T(8,128)}, u32[]{:S(2)}, u32[]{:S(2)}) collective-permute-start(f32[64,1024]{1,0:T(8,128)} %collective-permute-done.12.refs_2_), channel_id=1, source_target_pairs={{0,2},{1,3},{2,0},{3,1},{4,6},{5,7},{6,4},{7,5},{8,10},{9,11},{10,... | collective-permute-start | bytes 786440 | tf_op jit(solution)/shard_map/ppermute | solution.py:19
  75.0 17.9 %collective-permute-start.17 = (f32[64,1024]{1,0:T(8,128)}, f32[64,1024]{1,0:T(8,128)}, u32[]{:S(2)}, u32[]{:S(2)}) collective-permute-start(f32[64,1024]{1,0:T(8,128)} %collective-permute-done.12.refs_2_), channel_id=1, source_target_pairs={{0,4},{4,0},{8,12},{12,8},{16,20},{20,16},{24,28},{28,24},{1,5},{5... | collective-permute-start | bytes 786440 | tf_op jit(solution)/shard_map/ppermute | solution.py:19
  76.2 16.7 %collective-permute-start.15 = (f32[64,1024]{1,0:T(8,128)S(1)}, f32[64,1024]{1,0:T(8,128)}, u32[]{:S(2)}, u32[]{:S(2)}) collective-permute-start(f32[64,1024]{1,0:T(8,128)S(1)} %collective-permute-done.7.refs_2_), channel_id=1, source_target_pairs={{0,2},{1,3},{2,0},{3,1},{4,6},{5,7},{6,4},{7,5},{8,10},{9,11},{10,... | collective-permute-start | bytes 786440 | tf_op jit(solution)/shard_map/ppermute | solution.py:19
  77.5 15.9 %collective-permute-start.14 = (f32[64,1024]{1,0:T(8,128)}, f32[64,1024]{1,0:T(8,128)}, u32[]{:S(2)}, u32[]{:S(2)}) collective-permute-start(f32[64,1024]{1,0:T(8,128)} %collective-permute-done.10.refs_4_), channel_id=1, source_target_pairs={{0,2},{1,3},{2,0},{3,1},{4,6},{5,7},{6,4},{7,5},{8,10},{9,11},{10,... | collective-permute-start | bytes 786440 | tf_op jit(solution)/shard_map/ppermute | solution.py:19
  97.6 4.0 %collective-permute-start.20 = (f32[384,1024]{1,0:T(8,128)}, f32[384,1024]{1,0:T(8,128)}, u32[]{:S(2)}, u32[]{:S(2)}) collective-permute-start(f32[384,1024]{1,0:T(8,128)} %pack_a.1), channel_id=1, source_target_pairs={{0,1},{1,0},{2,3},{3,2},{4,5},{5,4},{6,7},{7,6},{8,9},{9,8},{10,11... | collective-permute-start | bytes 4718600 | tf_op jit(solution)/shard_map/ppermute | solution.py:19
  97.7 9.4 %collective-permute-start.21 = (f32[64,1024]{1,0:T(8,128)}, f32[64,1024]{1,0:T(8,128)}, u32[]{:S(2)}, u32[]{:S(2)}) collective-permute-start(f32[64,1024]{1,0:T(8,128)} %collective-permute-done.17.refs_1_.refs_4_), channel_id=1, source_target_pairs={{0,2},{1,3},{2,0},{3,1},{4,6},{5,7},{6,4},{7,5},{8,10},{9,11},{10,... | collective-permute-start | bytes 786440 | tf_op jit(solution)/shard_map/ppermute | solution.py:19
  99.3 8.7 %collective-permute-start.22 = (f32[64,1024]{1,0:T(8,128)}, f32[64,1024]{1,0:T(8,128)}, u32[]{:S(2)}, u32[]{:S(2)}) collective-permute-start(f32[64,1024]{1,0:T(8,128)} %get-tuple-element.156), channel_id=1, source_target_pairs={{0,4},{4,0},{8,12},{12,8},{16,20},{20,16},{24,28},{28,24},{1,5},{5... | collective-permute-start | bytes 786440 | tf_op jit(solution)/shard_map/ppermute | solution.py:19
  108.0 24.7 %collective-permute-start.23 = (f32[256,1024]{1,0:T(8,128)}, f32[256,1024]{1,0:T(8,128)}, u32[]{:S(2)}, u32[]{:S(2)}) collective-permute-start(f32[256,1024]{1,0:T(8,128)} %out_grad.2), channel_id=1, source_target_pairs={{0,8},{4,12},{8,0},{12,4},{16,24},{20,28},{24,16},{28,20},{1,9},{5... | collective-permute-start | bytes 3145736 | tf_op jit(solution)/shard_map/ppermute | solution.py:19
  111.7 3.8 %collective-permute-start.27 = (f32[192,1024]{1,0:T(8,128)}, f32[192,1024]{1,0:T(8,128)}, u32[]{:S(2)}, u32[]{:S(2)}) collective-permute-start(f32[192,1024]{1,0:T(8,128)} %pack_b.1), channel_id=1, source_target_pairs={{0,1},{1,0},{2,3},{3,2},{4,5},{5,4},{6,7},{7,6},{8,9},{9,8},{10,11... | collective-permute-start | bytes 2359304 | tf_op jit(solution)/shard_map/ppermute | solution.py:19
  111.8 3.4 %collective-permute-start.26 = (f32[64,1024]{1,0:T(8,128)}, f32[64,1024]{1,0:T(8,128)}, u32[]{:S(2)}, u32[]{:S(2)}) collective-permute-start(f32[64,1024]{1,0:T(8,128)} %collective-permute-done.12.refs_2_), channel_id=1, source_target_pairs={{0,1},{1,0},{2,3},{3,2},{4,5},{5,4},{6,7},{7,6},{8,9},{9,8},{10,11... | collective-permute-start | bytes 786440 | tf_op jit(solution)/shard_map/ppermute | solution.py:19
  112.3 2.9 %collective-permute-start.25 = (f32[64,1024]{1,0:T(8,128)S(1)}, f32[64,1024]{1,0:T(8,128)}, u32[]{:S(2)}, u32[]{:S(2)}) collective-permute-start(f32[64,1024]{1,0:T(8,128)S(1)} %copy-done.60), channel_id=1, source_target_pairs={{0,1},{1,0},{2,3},{3,2},{4,5},{5,4},{6,7},{7,6},{8,9},{9,8},{10,11... | collective-permute-start | bytes 786440 | tf_op jit(solution)/shard_map/ppermute | solution.py:19
  112.3 3.2 %collective-permute-start.24 = (f32[64,1024]{1,0:T(8,128)}, f32[64,1024]{1,0:T(8,128)}, u32[]{:S(2)}, u32[]{:S(2)}) collective-permute-start(f32[64,1024]{1,0:T(8,128)} %collective-permute-done.22.refs_0_), channel_id=1, source_target_pairs={{0,1},{1,0},{2,3},{3,2},{4,5},{5,4},{6,7},{7,6},{8,9},{9,8},{10,11... | collective-permute-start | bytes 786440 | tf_op jit(solution)/shard_map/ppermute | solution.py:19
  132.7 3.0 %collective-permute-start.29 = (f32[2,256,512]{2,1,0:T(8,128)}, f32[2,256,512]{2,1,0:T(8,128)}, u32[]{:S(2)}, u32[]{:S(2)}) collective-permute-start(f32[2,256,512]{2,1,0:T(8,128)} %dynamic-slice_bitcast_fusion), channel_id=1, source_target_pairs={{0,1},{1,0},{2,3},{3,2},{4,5},{5,4},{6,7},{7,6},{8,9},{9,8},{10,11... | collective-permute-start | bytes 3145736 | tf_op jit(solution)/shard_map/ppermute | solution.py:19
  132.7 26.6 %collective-permute-start.28 = (f32[264,1024]{1,0:T(8,128)}, f32[264,1024]{1,0:T(8,128)}, u32[]{:S(2)}, u32[]{:S(2)}) collective-permute-start(f32[264,1024]{1,0:T(8,128)} %copy-done.54), channel_id=1, source_target_pairs={{0,8},{4,12},{8,0},{12,4},{16,24},{20,28},{24,16},{28,20},{1,9},{5... | collective-permute-start | bytes 3244040 | tf_op jit(solution)/shard_map/ppermute | solution.py:19
  139.2 14.3 %collective-permute-start.30 = (f32[1,256,512]{2,1,0:T(8,128)}, f32[1,256,512]{2,1,0:T(8,128)}, u32[]{:S(2)}, u32[]{:S(2)}) collective-permute-start(f32[1,256,512]{2,1,0:T(8,128)} %constant_dynamic-slice_fusion), channel_id=1, source_target_pairs={{0,2},{1,3},{2,0},{3,1},{4,6},{5,7},{6,4},{7,5},{8,10},{9,11},{10,... | collective-permute-start | bytes 1572872 | tf_op jit(solution)/shard_map/ppermute | solution.py:19
  (72 other events, 273.6 us)

commit v5 on v4

--- a/solution.py
+++ b/solution.py
@@ -11,6 +11,7 @@
 F32 = jnp.float32
 BF16 = jnp.bfloat16
 SEG = 8
+CORE, LANE, SIDES, PLACES, BLOCKS, SELF, ROWS = 0, 1, 2, 4, 14, 18, 19
 VMEM_LIMIT = 12 * 1024 * 1024
 
 
@@ -31,11 +32,15 @@
     return lax.dot_general(a, b, (((0,), (0,)), ((), ())), preferred_element_type=F32)
 
 
-def order(rows, transpose=False):
+def order_of(rows, transpose=False):
     steps = rows // SEG
     r = lax.broadcasted_iota(jnp.int32, (rows, rows), 1 if transpose else 0)
     t = lax.broadcasted_iota(jnp.int32, (rows, rows), 0 if transpose else 1)
-    return ((r % SEG) * steps + r // SEG == t).astype(F32).astype(BF16)
+    return (r % SEG) * steps + r // SEG == t
+
+
+def order(rows, transpose=False):
+    return order_of(rows, transpose).astype(F32).astype(BF16)
 
 
 VMEM = pl.BlockSpec(memory_space=pltpu.VMEM)
@@ -66,17 +71,18 @@
 def prep_inputs_kernel(idx_ref, x_ref, p_ref, half_ref, quarter_ref, full):
     ordered_rows(x_ref, p_ref, full)
     half, quarter = half_ref.shape[0], quarter_ref.shape[0]
-    half_ref[...] = full[pl.ds(pl.multiple_of(idx_ref[0] * half, half), half), :]
-    quarter_ref[...] = full[pl.ds(pl.multiple_of(idx_ref[1] * quarter, quarter), quarter), :]
-
-
-def prep_cotangent_kernel(idx_ref, x_ref, p_ref, first_a_ref, first_b_ref, second_ref, away_a_ref, away_b_ref, full):
+    half_ref[...] = full[pl.ds(pl.multiple_of(idx_ref[CORE] * half, half), half), :]
+    quarter_ref[...] = full[pl.ds(pl.multiple_of(idx_ref[LANE] * quarter, quarter), quarter), :]
+
+
+def prep_cotangent_kernel(idx_ref, x_ref, p_ref, own_a_ref, first_a_ref, first_b_ref, second_ref, away_a_ref, away_b_ref, full):
     ordered_rows(x_ref, p_ref, full)
     quarter, width = first_a_ref.shape
-    cols = [pl.ds(pl.multiple_of(idx_ref[2 + k] * width, width), width) for k in range(2)]
-    first = pl.ds(pl.multiple_of(idx_ref[0] * 2 * quarter, quarter), quarter)
-    second = pl.ds(pl.multiple_of(idx_ref[0] * 2 * quarter + quarter, quarter), quarter)
-    away = pl.ds(pl.multiple_of(idx_ref[1] * quarter, quarter), quarter)
+    cols = [pl.ds(pl.multiple_of(idx_ref[SIDES + k] * width, width), width) for k in range(2)]
+    first = pl.ds(pl.multiple_of(idx_ref[CORE] * 2 * quarter, quarter), quarter)
+    second = pl.ds(pl.multiple_of(idx_ref[CORE] * 2 * quarter + quarter, quarter), quarter)
+    away = pl.ds(pl.multiple_of(idx_ref[LANE] * quarter, quarter), quarter)
+    own_a_ref[...] = full[:, cols[0]].astype(BF16)
     first_a_ref[...] = full[first, cols[0]]
     first_b_ref[...] = full[first, cols[1]]
     second_ref[:, :width] = full[second, cols[0]]
@@ -87,8 +93,8 @@
 
 def prep(kernel, idx, x, shapes, name):
     rows, depth = x.shape
-    shapes = (jax.ShapeDtypeStruct((rows, depth), BF16), *[jax.ShapeDtypeStruct(shape, F32) for shape in shapes])
-    return resident(kernel, shapes, (idx, x), name, [pltpu.VMEM((rows, depth), F32)])
+    shapes = [jax.ShapeDtypeStruct(shape, kind) for shape, kind in shapes]
+    return resident(kernel, (jax.ShapeDtypeStruct((rows, depth), BF16), *shapes), (idx, x), name, [pltpu.VMEM((rows, depth), F32)])
 
 
 def pack_kernel(*refs):
@@ -149,8 +155,15 @@
     return [full[:, lanes_of(l)] for l in range(width // 128)]
 
 
-def summary_kernel(x_ref, c_ref, w_ref, v_ref, scale_ref, decay_ref, retain_ref, out_ref, drive, scot, *, scaling):
+def spread_rows(row, out_ref, at):
+    rows = row.shape[1]
+    column = jnp.sum(jnp.where(order_of(rows), row, 0.0), axis=1, keepdims=True)
+    out_ref[at : at + rows, :] = jnp.broadcast_to(column, (rows, 128))
+
+
+def summary_kernel(x_ref, c_ref, w_ref, v_ref, scale_ref, decay_ref, kept_ref, out_ref, drive, scot, retain_ref, *, scaling):
     decays = decay_tiles(decay_ref)
+    spread_rows(kept_ref[...], retain_ref, 0)
     drive[...] = nn(x_ref[...], w_ref[...]) * scale_ref[...]
     scot[...] = nt(c_ref[...], v_ref[...]) * scaling
     zero = jnp.zeros(decay_ref.shape, F32)
@@ -161,36 +174,39 @@
     total = rate[0:1]
     for s in range(1, SEG):
         total = total * rate[s : s + 1]
-    out_ref[...] = jnp.concatenate([total, forward, backward], axis=0)
+    rest = zero.shape[1] - kept_ref.shape[1]
+    kept = jnp.concatenate([kept_ref[...], zero[:, :rest]], axis=1) if rest else kept_ref[...]
+    out_ref[0] = jnp.concatenate([total, forward, backward, kept], axis=0)
 
 
 def carries_kernel(idx_ref, sum_ref, fwd_ref, bwd_ref, retain_ref):
     blocks = sum_ref.shape[0]
     far = blocks // 2
-
-    def row(b):
-        away = idx_ref[0] ^ b
+    rows = retain_ref.shape[0] // 4
+
+    def row(away):
         top = away // far
         low = (away % 2) ^ top
         middle = ((away // 2) % (far // 2)) ^ low
         return sum_ref[middle + (far // 2) * low + far * top]
 
+    for role, away in enumerate((0, 1, far, far + 1)):
+        spread_rows(row(away)[3:4, :rows], retain_ref, role * rows)
     now = jnp.zeros_like(fwd_ref[0:1, :])
     for b in range(blocks):
         fwd_ref[b : b + 1, :] = now
-        ends = row(b)
-        retain_ref[b : b + 1, :] = ends[3:4]
+        ends = row(idx_ref[SELF] ^ b)
         now = ends[1:2] + ends[0:1] * now
     now = jnp.zeros_like(now)
     for b in range(blocks - 1, -1, -1):
         bwd_ref[b : b + 1, :] = now
-        ends = row(b)
+        ends = row(idx_ref[SELF] ^ b)
         now = ends[2:3] + ends[0:1] * now
 
 
-def carries(me, table):
+def carries(idx, table, rows):
     shape = jax.ShapeDtypeStruct((table.shape[0], table.shape[2]), F32)
-    return resident(carries_kernel, (shape,) * 3, (me, table), "carries")
+    return resident(carries_kernel, (shape, shape, jax.ShapeDtypeStruct((4 * rows, 128), F32)), (idx, table), "carries")
 
 
 def reach(devices):
@@ -211,21 +227,21 @@
     for copy, parts in zip(copies, layout, strict=True):
         copy.wait()
         for role, slot, rows in parts:
-            at = pl.multiple_of(idx_ref[slot] * rows, rows)
+            at = pl.multiple_of(idx_ref[PLACES + slot] * rows, rows)
             outs[role][pl.ds(at, rows), :] = held[start : start + rows, :].astype(BF16)
             start += rows
 
 
-def collected(place, pieces, name):
+def collected(idx, pieces, name):
     rows = sum(part[2] for _, parts in pieces for part in parts)
     depth = pieces[0][0].shape[1]
     shape = jax.ShapeDtypeStruct((rows // 3, depth), BF16)
     kernel = functools.partial(collect_kernel, layout=[parts for _, parts in pieces])
     scratch = [pltpu.VMEM((rows, depth), F32), pltpu.SemaphoreType.DMA((len(pieces),))]
-    return list(resident(kernel, (shape,) * 3, (place, *[array for array, _ in pieces]), name, scratch, anywhere=len(pieces)))
-
-
-def forward_kernel(idx_ref, *refs, roles):
+    return list(resident(kernel, (shape,) * 3, (idx, *[array for array, _ in pieces]), name, scratch, anywhere=len(pieces)))
+
+
+def forward_kernel(idx_ref, *refs, roles, first):
     xs = refs[:roles]
     w_ref, scale_ref, decay_ref, retain_ref, enter_ref = refs[roles : roles + 5]
     outs = refs[roles + 5 : -2]
@@ -236,8 +252,8 @@
     steps = rows_all // SEG
     for role in range(roles):
         start_ref, low_ref = outs[2 * role : 2 * role + 2]
-        block = idx_ref[role]
-        base = block * rows_all
+        block = idx_ref[BLOCKS + first + role]
+        base = (first + role) * rows_all
         drive[...] = nn(xs[role][...], w_ref[...]) * scale_ref[...]
         end, rate = scan_ends(drive, retain_ref, base, decays, False)
         start, _ = seg_starts(end, rate, enter_ref[pl.ds(block, 1), :], False)
@@ -257,7 +273,7 @@
         low_ref[...] = state[...].astype(BF16)
 
 
-def backward_kernel(idx_ref, side_ref, *refs, roles, parts, scaling):
+def backward_kernel(idx_ref, *refs, roles, parts, scaling, first):
     cs = refs[: roles * parts]
     v_ref, scale_ref, decay_ref, retain_ref, enter_ref = refs[roles * parts : roles * parts + 5]
     entering = refs[roles * parts + 5 : roles * parts + 5 + 2 * roles]
@@ -270,14 +286,14 @@
     width = v_ref.shape[1] // parts
     for role in range(roles):
         scaled_ref, grad_ref = outs[2 * role : 2 * role + 2]
-        block = idx_ref[role]
-        base = block * rows_all
+        block = idx_ref[BLOCKS + first + role]
+        base = (first + role) * rows_all
         if parts == 1:
             scot[...] = nt(cs[role][...], v_ref[...]) * scaling
         else:
             total = None
             for k in range(parts):
-                cols = pl.ds(pl.multiple_of(side_ref[k] * width, width), width)
+                cols = pl.ds(pl.multiple_of(idx_ref[SIDES + k] * width, width), width)
                 part = nt(cs[parts * role + k][...], v_ref[:, cols])
                 total = part if total is None else total + part
             scot[...] = total * scaling
@@ -307,33 +323,33 @@
         grad_ref[...] = jnp.sum(jnp.concatenate([d[1] for d in done], axis=1), axis=0, keepdims=True)
 
 
-def forward_call(blocks, xs, operands, name):
+def forward_call(idx, first, xs, operands, name):
     channels = operands[1].shape[1]
     rows, roles = xs[0].shape[0], len(xs)
     shapes = (jax.ShapeDtypeStruct((SEG, channels), F32), jax.ShapeDtypeStruct((rows, channels), BF16)) * roles
     out = resident(
-        functools.partial(forward_kernel, roles=roles), shapes, (blocks, *xs, *operands), name,
+        functools.partial(forward_kernel, roles=roles, first=first), shapes, (idx, *xs, *operands), name,
         [pltpu.VMEM((rows, channels), F32)] * 2,
     )
     return list(out[::2]), list(out[1::2])
 
 
-def backward_call(blocks, sides, cs, operands, starts, lows, scaling, name):
+def backward_call(idx, first, cs, operands, starts, lows, scaling, name):
     channels = operands[1].shape[1]
     rows, roles = cs[0][0].shape[0], len(cs)
-    kernel = functools.partial(backward_kernel, roles=roles, parts=len(cs[0]), scaling=scaling)
+    kernel = functools.partial(backward_kernel, roles=roles, parts=len(cs[0]), scaling=scaling, first=first)
     shapes = (jax.ShapeDtypeStruct((rows, channels), BF16), jax.ShapeDtypeStruct((1, channels), F32)) * roles
     out = resident(
-        kernel, shapes, (blocks, sides, *[part for c in cs for part in c], *operands, *[r for pair in zip(starts, lows, strict=True) for r in pair]), name,
-        [pltpu.VMEM((rows, channels), F32)] * 2 + [pltpu.VMEM((SEG + rows, channels), F32)], scalars=2,
+        kernel, shapes, (idx, *[part for c in cs for part in c], *operands, *[r for pair in zip(starts, lows, strict=True) for r in pair]), name,
+        [pltpu.VMEM((rows, channels), F32)] * 2 + [pltpu.VMEM((SEG + rows, channels), F32)],
     )
     return list(out[::2]), list(out[1::2])
 
 
-def grad_kernel(idx_ref, *refs, count, factor):
+def grad_kernel(idx_ref, *refs, count, factor, which):
     features, values, sums, out_ref = refs[:count], refs[count : 2 * count], refs[2 * count : -1], refs[-1]
     width = out_ref.shape[0] - (SEG if sums else 0)
-    at = pl.ds(pl.multiple_of(idx_ref[0] * width, width), width)
+    at = pl.ds(pl.multiple_of(idx_ref[which] * width, width), width)
     total = tn(features[0][:, at], values[0][...])
     for k in range(1, count):
         total += tn(features[k][:, at], values[k][...])
@@ -343,11 +359,11 @@
         out_ref[width:, :] = jnp.broadcast_to(row, (SEG, row.shape[1]))
 
 
-def grad_rows(at, features, values, rows_out, factor, name, sums=()):
+def grad_rows(idx, which, features, values, rows_out, factor, name, sums=()):
     channels = values[0].shape[1]
     if rows_out % 128:
         total = sum(
-            tn(lax.dynamic_slice_in_dim(x, at * rows_out, rows_out, axis=1), v) for x, v in zip(features, values, strict=True)
+            tn(lax.dynamic_slice_in_dim(x, idx[which] * rows_out, rows_out, axis=1), v) for x, v in zip(features, values, strict=True)
         )
         total = total * factor if factor is not None else total
         if sums:
@@ -355,26 +371,25 @@
             total = jnp.concatenate([total, jnp.broadcast_to(row, (SEG, channels))], axis=0)
         return total
     return resident(
-        functools.partial(grad_kernel, count=len(values), factor=factor),
+        functools.partial(grad_kernel, count=len(values), factor=factor, which=which),
         jax.ShapeDtypeStruct((rows_out + (SEG if sums else 0), channels), F32),
-        (jnp.reshape(at, (1,)).astype(jnp.int32), *features, *values, *sums), name,
-    )
-
-
-def row_grad_kernel(a_ref, w_ref, out_ref):
-    parts, rows, width = out_ref.shape
+        (idx, *features, *values, *sums), name,
+    )
+
+
+def row_grad_kernel(idx_ref, a_ref, w_ref, keep_ref, give_ref):
+    count, rows, width = keep_ref.shape
     a = nn(order(rows, True), a_ref[...]).astype(BF16)
-    for k in range(parts):
-        out_ref[k] = nt(a, w_ref[width * k : width * (k + 1), :])
-
-
-def row_grad(scaled, in_proj, parts):
+    for k in range(count):
+        for ref, flip in ((keep_ref, 0), (give_ref, 1)):
+            at = (idx_ref[LANE] ^ (2 * k) ^ flip) * width
+            ref[k] = nt(a, w_ref[pl.ds(pl.multiple_of(at, width), width), :])
+
+
+def row_grad(idx, scaled, in_proj, parts):
     rows, channels = scaled.shape
-    depth = in_proj.shape[0]
-    return resident(
-        row_grad_kernel, jax.ShapeDtypeStruct((parts, rows, depth // parts), F32), (scaled, in_proj), "row_grad",
-        scalars=0,
-    )
+    shape = jax.ShapeDtypeStruct((parts // 2, rows, in_proj.shape[0] // parts), F32)
+    return resident(row_grad_kernel, (shape, shape), (idx, scaled, in_proj), "row_grad")
 
 
 def after(x, *others):
@@ -414,10 +429,11 @@
     half, quarter = rows // 2, rows // 4
     rows_out = depth // devices
     core = lane % 2
-    place = [core, 1 - core, lane, lane ^ 2, lane ^ 1, lane ^ 3, 2 * core, 2 * core + 1, 2 - 2 * core, 3 - 2 * core]
-    place = jnp.stack(place).astype(jnp.int32)
-    blocks = jnp.stack([me, me ^ 1, me ^ far, me ^ far ^ 1]).astype(jnp.int32)
-    sides = jnp.stack([side, 1 - side]).astype(jnp.int32)
+    idx = [core, lane, side, 1 - side]
+    idx += [core, 1 - core, lane, lane ^ 2, lane ^ 1, lane ^ 3, 2 * core, 2 * core + 1, 2 - 2 * core, 3 - 2 * core]
+    idx += [me, me ^ 1, me ^ far, me ^ far ^ 1, me]
+    idx += [me ^ (2 * k) for k in range(groups)] + [(me % far) ^ (2 * k) for k in range(groups)]
+    idx, inputs, cotangent = lax.optimization_barrier((jnp.stack(idx).astype(jnp.int32), inputs, cotangent))
     mine_near, mine_1, mine_2, mine_3, mine_4 = (
         [(0, 0, half)], [(1, 2, quarter)], [(1, 3, quarter)], [(2, 2, quarter)], [(2, 3, quarter)],
     )
@@ -425,27 +441,22 @@
         [(0, 1, half)], [(1, 4, quarter)], [(1, 5, quarter)], [(2, 4, quarter)], [(2, 5, quarter)],
     )
 
-    def ordered(r):
-        return r.reshape(-1, SEG, steps).swapaxes(1, 2).reshape(-1, 1)
-
     line = Order()
-    where = jnp.stack([lane % 2, lane, side * 0]).astype(jnp.int32)
     x_own, x_half, x_quarter = line.step(
-        *prep(prep_inputs_kernel, where, inputs, [(half, depth), (quarter, depth)], "prep_inputs")
+        *prep(prep_inputs_kernel, idx, inputs, [((half, depth), F32), ((quarter, depth), F32)], "prep_inputs")
     )
     near_x = line.send(x_half, "tm", 1)
     away_x = line.send(x_quarter, "tm", far)
-    where = jnp.stack([lane % 2, lane, side, 1 - side]).astype(jnp.int32)
-    part = (quarter, depth // 2)
-    c_own, c_first_a, c_first_b, c_second, c_quarter_a, c_quarter_b = prep(
-        prep_cotangent_kernel, where, line.behind(cotangent), [part, part, (quarter, depth), part, part], "prep_cotangent"
-    )
-    ends = resident(
-        functools.partial(summary_kernel, scaling=scaling), jax.ShapeDtypeStruct((3, channels), F32),
-        (x_own, c_own, in_proj, out_proj, scale, decay_row, jnp.broadcast_to(ordered(retain), (rows, 128))), "summary",
-        [pltpu.VMEM((rows, channels), F32)] * 2, scalars=0,
-    )
-    table = jnp.concatenate([ends, jnp.pad(retain, (0, channels - rows))[None, :]], axis=0)[None]
+    part = ((quarter, depth // 2), F32)
+    c_own, own_a, c_first_a, c_first_b, c_second, c_quarter_a, c_quarter_b = prep(
+        prep_cotangent_kernel, idx, line.behind(cotangent),
+        [((rows, depth // 2), BF16), part, part, ((quarter, depth), F32), part, part], "prep_cotangent",
+    )
+    table = resident(
+        functools.partial(summary_kernel, scaling=scaling), jax.ShapeDtypeStruct((1, 4, channels), F32),
+        (x_own, c_own, in_proj, out_proj, scale, decay_row, retain[None, :]), "summary",
+        [pltpu.VMEM((rows, channels), F32)] * 2 + [pltpu.VMEM((rows, 128), F32)], scalars=0,
+    )
     if groups == 2:
         table = jnp.concatenate([table] + [line.send(table, "tm", bit) for bit in (2, 3, 1)])
     else:
@@ -457,21 +468,20 @@
     side_x = line.send(away_x, "chan", 2)
     away_a = line.send(c_quarter_a, "tm", far)
     table = jnp.concatenate([table, line.send(table, "tm", reach(devices)[-1])])
-    enter_fwd, enter_bwd, retain_all = carries(me[None].astype(jnp.int32), table)
+    enter_fwd, enter_bwd, retain_wide = carries(idx, table, rows)
     corner_x, side_x, away_a, enter_fwd = line.step(corner_x, side_x, away_a, enter_fwd)
 
     near_a1 = line.send(c_first_a, "tm", 1)
     corner_a = line.send(away_a, "tm", 1)
     corner_side_x = line.send(corner_x, "chan", 2)
     away_b = line.send(c_quarter_b, "tm", far)
-    retain_wide = jnp.broadcast_to(ordered(retain_all[:, :rows]), (devices * rows, 128))
     forward = (in_proj, scale, decay_row, retain_wide, enter_fwd)
     backward = (out_proj, scale, decay_row, retain_wide, enter_bwd)
-    starts, lows = forward_call(blocks[:1], [x_own], forward, "forward_own")
-    scaled, grads = backward_call(blocks[:1], sides, [[c_own]], backward, starts, lows, scaling, "backward_own")
-    parts = row_grad(scaled[0], in_proj, lanes)
+    starts, lows = forward_call(idx, 0, [x_own], forward, "forward_own")
+    scaled, grads = backward_call(idx, 0, [[c_own]], backward, starts, lows, scaling, "backward_own")
+    keep, give = row_grad(idx, scaled[0], in_proj, lanes)
     other_x = line.send(pack([near_x, away_x, side_x, corner_x], "pack_x"), "chan", 1)
-    corner_side_x, corner_a, near_a1, away_b, parts, other_x = line.step(corner_side_x, corner_a, near_a1, away_b, parts, other_x)
+    corner_side_x, corner_a, near_a1, away_b, give, other_x = line.step(corner_side_x, corner_a, near_a1, away_b, give, other_x)
 
     corner_b = line.send(away_b, "tm", 1)
     corner_side_a = line.send(corner_a, "chan", 2)
@@ -479,11 +489,11 @@
     near_2 = line.send(c_second, "tm", 1)
     last_x = line.send(corner_side_x, "chan", 1)
     side_b = line.send(away_b, "chan", 2)
-    xs = [x_own] + collected(place, [
+    xs = [x_own] + collected(idx, [
         (near_x, mine_near), (away_x, mine_1), (side_x, mine_2), (corner_x, mine_3), (corner_side_x, mine_4),
         (other_x, their_near + their_1 + their_2 + their_3), (last_x, their_4),
     ], "collect_x")
-    more, more_low = forward_call(blocks[1:], xs[1:], forward, "forward_group")
+    more, more_low = forward_call(idx, 1, xs[1:], forward, "forward_group")
     starts, lows = starts + more, lows + more_low
     corner_side_a, side_a, side_b, corner_b, near_2, lows[1] = line.step(corner_side_a, side_a, side_b, corner_b, near_2, lows[1])
     near_a2, near_b2 = near_2[:, : depth // 2], near_2[:, depth // 2 :]
@@ -491,17 +501,16 @@
     corner_side_b = line.send(corner_b, "chan", 2)
     near_b1 = line.send(c_first_b, "tm", 1)
     other_a = line.send(pack([near_a1, near_a2, away_a, side_a, corner_a, corner_side_a], "pack_a"), "chan", 1)
-    own_a = lax.dynamic_slice_in_dim(c_own, side * (depth // 2), depth // 2, axis=1)
-    ca = [own_a] + collected(place, [
+    ca = [own_a] + collected(idx, [
         (near_a1, [(0, 6, quarter)]), (near_a2, [(0, 7, quarter)]),
         (away_a, mine_1), (side_a, mine_2), (corner_a, mine_3), (corner_side_a, mine_4),
         (other_a, [(0, 8, quarter), (0, 9, quarter)] + their_1 + their_2 + their_3 + their_4),
     ], "collect_a")
 
-    def shares(features, values, block, factor, name, sums=()):
-        return [grad_rows(block ^ (2 * k), features, values, rows_out, factor, name, sums) for k in range(1, groups)]
-
-    out_given = shares(ca, lows, me % far, scaling, "out_grad")
+    def shares(first, features, values, factor, name, sums=()):
+        return [grad_rows(idx, first + k, features, values, rows_out, factor, name, sums) for k in range(1, groups)]
+
+    out_given = shares(ROWS + groups, ca, lows, scaling, "out_grad")
     out_given[0], corner_side_b, near_b1 = line.step(out_given[0], corner_side_b, near_b1)
 
     out_got = [line.send(part, "tm", 2 * (k + 1)) for k, part in enumerate(out_given)]
@@ -509,32 +518,26 @@
     near_b2_other = line.send(near_b2, "chan", 1)
     away_b_other = line.send(away_b, "chan", 1)
     other_b = line.send(pack([side_b, corner_b, corner_side_b], "pack_b"), "chan", 1)
-    cb = collected(place, [
+    cb = collected(idx, [
         (near_b1, [(0, 6, quarter)]), (near_b2, [(0, 7, quarter)]),
         (away_b, mine_1), (side_b, mine_2), (corner_b, mine_3), (corner_side_b, mine_4),
         (near_b1_other, [(0, 8, quarter)]), (near_b2_other, [(0, 9, quarter)]), (away_b_other, their_1),
         (other_b, their_2 + their_3 + their_4),
     ], "collect_b")
     cs = [list(pair) for pair in zip(ca[1:], cb, strict=True)]
-    more, more_grads = backward_call(blocks[1:], sides, cs, backward, starts[1:], lows[1:], scaling, "backward_group")
+    more, more_grads = backward_call(idx, 1, cs, backward, starts[1:], lows[1:], scaling, "backward_group")
     scaled, grads = scaled + more, grads + more_grads
-    in_given = shares(xs, scaled, me, None, "in_grad", grads)
+    in_given = shares(ROWS, xs, scaled, None, "in_grad", grads)
     in_given[0] = line.step(in_given[0])
     in_got = [line.send(part, "tm", 2 * (k + 1)) for k, part in enumerate(in_given)]
     out_got[0] = line.step(out_got[0])
-    bit = 1
-    while bit < lanes:
-        parts = parts.reshape(-1, 2, *parts.shape[1:])
-        turn = (lane // bit) % 2
-        keep = lax.dynamic_index_in_dim(parts, turn, axis=1, keepdims=False)
-        give = lax.dynamic_index_in_dim(parts, 1 - turn, axis=1, keepdims=False)
-        parts = keep + line.send(give, "chan", bit)
-        bit *= 2
-    input_grad = parts[0].astype(BF16)
+    parts = keep + line.send(give, "chan", 1)
+    columns = parts[0] + line.send(parts[1], "chan", 2)
+    input_grad = columns.astype(BF16)
     in_got[0] = after(in_got[0], input_grad)
 
-    out_proj_grad = sum(out_got, grad_rows(me % far, [line.behind(ca[0]), *ca[1:]], lows, rows_out, scaling, "out_grad"))
-    in_mine = grad_rows(me, [line.behind(xs[0]), *xs[1:]], scaled, rows_out, None, "in_grad", grads)
+    out_proj_grad = sum(out_got, grad_rows(idx, ROWS + groups, [line.behind(ca[0]), *ca[1:]], lows, rows_out, scaling, "out_grad"))
+    in_mine = grad_rows(idx, ROWS, [line.behind(xs[0]), *xs[1:]], scaled, rows_out, None, "in_grad", grads)
     in_proj_grad = sum((part[:rows_out] for part in in_got), in_mine[:rows_out])
     decay_grad = sum((part[rows_out] for part in in_got), in_mine[rows_out])
     if groups > 2:

time: 164 us -> 151 us (0.921)
  waiting for transfers between devices: 37.4 us -> 74.3 us
  local copies, waits for them, and re-layouts: 37.2 us -> 5.79 us
  Pallas kernels: 44.8 us -> 33.9 us
  other arithmetic: 10.1 us -> 3.89 us
    ppermute x31, waiting for transfers between devices: 37.4 us -> 74.3 us  [swap(): return lax.ppermute(x, axis, [(k, k ^ bit) for k in range(n)])]
    unnamed x146 -> x18, local copies, waits for them, and re-layouts: 28.8 us -> 5.62 us
    pallas_call x19, Pallas kernels: 44.8 us -> 33.9 us  [resident(): pl.pallas_call(kernel, out_shape=out_shape, in_specs=[SMEM] * scalars + [...]
    squeeze x2 -> x1, local copies, waits for them, and re-layouts: 3.23 us -> 0.04 us  [per_device(): columns = parts[0] + line.send(parts[1], 'chan', 2)]
    add x2, other arithmetic: 4.21 us -> 1.34 us  [the longest x1 1.13 us: per_device(): sum(out_got, grad_rows(idx, ROWS + groups, [line.behind(ca[0]), *ca[1:]],...]
    slice x1, local copies, waits for them, and re-layouts: 1.78 us -> 0.03 us  [per_device(): near_a2, near_b2 = (near_2[:, :depth // 2], near_2[:, depth // 2:])]
  transfers between devices with their start and end apart: 31 -> 31, of which waited for: 12 -> 16; matrix products, arithmetic and copies ran while one was open for 8% -> 1% of each run, Pallas kernels for 23% -> 21%
where the time goes in v5:
time: 151 us
  waiting for transfers between devices  74.3 us (49%)
  Pallas kernels  33.9 us (22%)
  starting transfers between devices  32.1 us (21%)
  local copies, waits for them, and re-layouts  5.79 us (4%)
  other arithmetic  3.89 us (3%)
    ppermute x31, waiting for transfers between devices, swap(): return lax.ppermute(x, axis, [(k, k ^ bit) for k in range(n)])  74.3 us
    pallas_call x19, Pallas kernels, resident(): pl.pallas_call(kernel, out_shape=out_shape, in_specs=[SMEM] * scalars + [...  33.9 us
    ppermute x31, starting transfers between devices, swap(): return lax.ppermute(x, axis, [(k, k ^ bit) for k in range(n)])  32.1 us
    unnamed x18, local copies, waits for them, and re-layouts  5.62 us
  transfers between devices with their start and end apart: 31, of which 16 were waited for; matrix products, arithmetic and copies ran while one was open for 1% of the time, Pallas kernels for 21%

profile of v5, /device:TPU:0, one launch (start us, length us, event | category | flops | bytes accessed | tf_op | source)
XLA Modules:
  0.0 151.0 jit_solution(13899463465761312543)
XLA Ops:
  3.1 3.0 %collective-permute-start = (f32[128,2048]{1,0:T(8,128)S(1)}, f32[128,2048]{1,0:T(8,128)S(1)}, u32[]{:S(2)}, u32[]{:S(2)}) collective-permute-start(f32[128,2048]{1,0:T(8,128)S(1)} %get-tuple-element.109), channel_id=1, source_target_pairs={{0,4},{4,0},{8,12},{12,8},{16,20},{20,16},{24,28},{28,24},{1,5},{5... | collective-permute-start | bytes 3145736 | tf_op jit(solution)/shard_map/ppermute | solution.py:20
  6.1 2.6 %collective-permute-start.1 = (f32[64,2048]{1,0:T(8,128)S(1)}, f32[64,2048]{1,0:T(8,128)S(1)}, u32[]{:S(2)}, u32[]{:S(2)}) collective-permute-start(f32[64,2048]{1,0:T(8,128)S(1)} %get-tuple-element.111), channel_id=1, source_target_pairs={{0,16},{4,20},{8,24},{12,28},{16,0},{20,4},{24,8},{28,12},{1,17},{... | collective-permute-start | bytes 1572872 | tf_op jit(solution)/shard_map/ppermute | solution.py:20
  9.9 2.2 %copy-done = bf16[2048,1024]{1,0:T(8,128)(2,1)S(1)} copy-done((bf16[2048,1024]{1,0:T(8,128)(2,1)S(1)}, bf16[2048,1024]{1,0:T(8,128)(2,1)}, u32[]{:S(2)}) %copy-start) | copy-done | bytes 4194328
  12.1 2.2 %copy-done.2 = bf16[1024,2048]{1,0:T(8,128)(2,1)S(1)} copy-done((bf16[1024,2048]{1,0:T(8,128)(2,1)S(1)}, bf16[1024,2048]{1,0:T(8,128)(2,1)}, u32[]{:S(2)}) %copy-start.2) | copy-done | bytes 4194328
  14.3 2.9 %summary.1 = f32[1,4,1024]{2,1,0:T(4,128)S(1)} custom-call(bf16[256,2048]{1,0:T(8,128)(2,1)S(1)} %get-tuple-element.192.x_ref.refs_0_, bf16[256,2048]{1,0:T(8,128)(2,1)S(1)} %get-tuple-element.112.c_ref.refs_0_, bf16[2048,1024]{1,0:T(8,128)(2,1)S(1)} %copy-done, bf16[1024,2048]{1,0:T(8,128)(2,1)S(1)} %copy-done.2, f32[1,1024]{1,0:T(1,128)S(1)} %bitcast.31, ...), custom_call_target="tpu_custom_call" | custom-call | tf_op jit(solution)/shard_map/summary/pallas_call | solution.py:54
  17.2 1.6 %collective-permute-start.2 = (f32[1,4,1024]{2,1,0:T(4,128)S(1)}, f32[1,4,1024]{2,1,0:T(4,128)S(1)}, u32[]{:S(2)}, u32[]{:S(2)}) collective-permute-start(f32[1,4,1024]{2,1,0:T(4,128)S(1)} %summary.1), channel_id=1, source_target_pairs={{0,8},{4,12},{8,0},{12,4},{16,24},{20,28},{24,16},{28,20},{1,9},{5... | collective-permute-start | bytes 49160 | tf_op jit(solution)/shard_map/ppermute | solution.py:20
  19.3 1.5 collective-permute-start.4
  21.0 10.7 %collective-permute-done.3 = f32[1,4,1024]{2,1,0:T(4,128)S(1)} collective-permute-done((f32[1,4,1024]{2,1,0:T(4,128)S(1)}, f32[1,4,1024]{2,1,0:T(4,128)S(1)}, u32[]{:S(2)}, u32[]{:S(2)}) %collective-permute-start.3) | collective-permute-done | bytes 16416 | tf_op jit(solution)/shard_map/ppermute | solution.py:20
  31.8 1.6 %collective-permute-start.5 = (f32[64,2048]{1,0:T(8,128)S(1)}, f32[64,2048]{1,0:T(8,128)S(1)}, u32[]{:S(2)}, u32[]{:S(2)}) collective-permute-start(f32[64,2048]{1,0:T(8,128)S(1)} %collective-permute-done.1.refs_1_), channel_id=1, source_target_pairs={{0,4},{4,0},{8,12},{12,8},{16,20},{20,16},{24,28},{28,24},{1,5},{5... | collective-permute-start | bytes 1572872 | tf_op jit(solution)/shard_map/ppermute | solution.py:20
  33.4 1.5 %collective-permute-start.6 = (f32[64,2048]{1,0:T(8,128)S(1)}, f32[64,2048]{1,0:T(8,128)S(1)}, u32[]{:S(2)}, u32[]{:S(2)}) collective-permute-start(f32[64,2048]{1,0:T(8,128)S(1)} %collective-permute-done.1.refs_1_), channel_id=1, source_target_pairs={{0,2},{1,3},{2,0},{3,1},{4,6},{5,7},{6,4},{7,5},{8,10},{9,11},{10,... | collective-permute-start | bytes 1572872 | tf_op jit(solution)/shard_map/ppermute | solution.py:20
  35.9 1.9 %collective-permute-start.8 = (f32[4,4,1024]{2,1,0:T(4,128)S(1)}, f32[4,4,1024]{2,1,0:T(4,128)S(1)}, u32[]{:S(2)}, u32[]{:S(2)}) collective-permute-start(f32[4,4,1024]{2,1,0:T(4,128)S(1)} %pad_maximum_fusion.1), channel_id=1, source_target_pairs={{0,20},{4,16},{8,28},{12,24},{16,4},{20,0},{24,12},{28,8},{1,21},{... | collective-permute-start | bytes 196616 | tf_op jit(solution)/shard_map/ppermute | solution.py:20
  37.8 12.8 %collective-permute-done.8 = f32[4,4,1024]{2,1,0:T(4,128)S(1)} collective-permute-done((f32[4,4,1024]{2,1,0:T(4,128)S(1)}, f32[4,4,1024]{2,1,0:T(4,128)S(1)}, u32[]{:S(2)}, u32[]{:S(2)}) %collective-permute-start.8) | collective-permute-done | bytes 65568 | tf_op jit(solution)/shard_map/ppermute | solution.py:20
  52.9 1.5 %collective-permute-start.10 = (f32[64,1024]{1,0:T(8,128)S(1)}, f32[64,1024]{1,0:T(8,128)S(1)}, u32[]{:S(2)}, u32[]{:S(2)}) collective-permute-start(f32[64,1024]{1,0:T(8,128)S(1)} %collective-permute-done.7.refs_2_), channel_id=1, source_target_pairs={{0,4},{4,0},{8,12},{12,8},{16,20},{20,16},{24,28},{28,24},{1,5},{5... | collective-permute-start | bytes 786440 | tf_op jit(solution)/shard_map/ppermute | solution.py:20
  54.4 2.2 %forward_own.1 = (f32[8,1024]{1,0:T(8,128)S(1)}, bf16[256,1024]{1,0:T(8,128)(2,1)S(1)}) custom-call(s32[23]{0:T(128)S(1)} %stack.83.idx_ref, bf16[256,2048]{1,0:T(8,128)(2,1)S(1)} %get-tuple-element.192.x_ref.refs_0_, bf16[2048,1024]{1,0:T(8,128)(2,1)S(1)} %copy-done.1, f32[1,1024]{1,0:T(1,128)S(1)} %bitcast.32, f32[1,1024]{1,0:T(1,128)S(1)} %bitcast.37, ...), custom_call_target="tpu_custom_call" | custom-call | tf_op jit(solution)/shard_map/forward_own/pallas_call | solution.py:54
  56.7 2.4 %backward_own.1 = (bf16[256,1024]{1,0:T(8,128)(2,1)S(1)}, f32[1,1024]{1,0:T(1,128)S(1)}) custom-call(s32[23]{0:T(128)S(1)} %stack.83.idx_ref, bf16[256,2048]{1,0:T(8,128)(2,1)S(1)} %get-tuple-element.112.c_ref.refs_0_, bf16[1024,2048]{1,0:T(8,128)(2,1)S(1)} %copy-done.3, f32[1,1024]{1,0:T(1,128)S(1)} %bitcast.33, f32[1,1024]{1,0:T(1,128)S(1)} %bitcast.38, ...), custom_call_target="tpu_custom_call" | custom-call | tf_op jit(solution)/shard_map/backward_own/pallas_call | solution.py:54
  59.2 1.9 %row_grad.1 = (f32[2,256,512]{2,1,0:T(8,128)S(1)}, f32[2,256,512]{2,1,0:T(8,128)S(1)}) custom-call(s32[23]{0:T(128)S(1)} %stack.83.idx_ref, bf16[256,1024]{1,0:T(8,128)(2,1)S(1)} %get-tuple-element.135.a_ref.refs_4_, bf16[2048,1024]{1,0:T(8,128)(2,1)S(1)} %copy-done.1), custom_call_target="tpu_custom_call" | custom-call | tf_op jit(solution)/shard_map/row_grad/pallas_call | solution.py:54
  61.1 5.7 %collective-permute-done.12.refs_2_ = f32[64,1024]{1,0:T(8,128)S(1)} collective-permute-done((f32[64,1024]{1,0:T(8,128)S(1)}, f32[64,1024]{1,0:T(8,128)S(1)}, u32[]{:S(2)}, u32[]{:S(2)}) %collective-permute-start.12) | collective-permute-done | bytes 262176 | tf_op jit(solution)/shard_map/ppermute | solution.py:20
  68.0 1.5 %collective-permute-start.16 = (f32[64,1024]{1,0:T(8,128)S(1)}, f32[64,1024]{1,0:T(8,128)S(1)}, u32[]{:S(2)}, u32[]{:S(2)}) collective-permute-start(f32[64,1024]{1,0:T(8,128)S(1)} %collective-permute-done.12.refs_2_), channel_id=1, source_target_pairs={{0,2},{1,3},{2,0},{3,1},{4,6},{5,7},{6,4},{7,5},{8,10},{9,11},{10,... | collective-permute-start | bytes 786440 | tf_op jit(solution)/shard_map/ppermute | solution.py:20
  71.0 1.5 %collective-permute-start.14 = (f32[64,1024]{1,0:T(8,128)S(1)}, f32[64,1024]{1,0:T(8,128)S(1)}, u32[]{:S(2)}, u32[]{:S(2)}) collective-permute-start(f32[64,1024]{1,0:T(8,128)S(1)} %collective-permute-done.10.refs_4_), channel_id=1, source_target_pairs={{0,2},{1,3},{2,0},{3,1},{4,6},{5,7},{6,4},{7,5},{8,10},{9,11},{10,... | collective-permute-start | bytes 786440 | tf_op jit(solution)/shard_map/ppermute | solution.py:20
  72.6 1.4 collect_x.1
  73.9 5.6 %forward_group.1 = (f32[8,1024]{1,0:T(8,128)S(1)}, bf16[256,1024]{1,0:T(8,128)(2,1)S(1)}, f32[8,1024]{1,0:T(8,128)S(1)}, bf16[256,1024]{1,0:T(8,128)(2,1)S(1)}, ...) custom-call(s32[23]{0:T(128)S(1)} %stack.83.idx_ref, bf16[256,2048]{1,0:T(8,128)(2,1)S(1)} %get-tuple-element.150.refs_0_.refs_1_, ...), custom_call_target="tpu_custom_call" | custom-call | tf_op jit(solution)/shard_map/forward_group/pallas_call | solution.py:54
  79.6 7.3 %collective-permute-done.17.refs_1_.refs_4_ = f32[64,1024]{1,0:T(8,128)S(1)} collective-permute-done((f32[64,1024]{1,0:T(8,128)S(1)}, f32[64,1024]{1,0:T(8,128)S(1)}, u32[]{:S(2)}, u32[]{:S(2)}) %collective-permute-start.17) | collective-permute-done | bytes 262176 | tf_op jit(solution)/shard_map/ppermute | solution.py:20
  87.9 1.6 %collective-permute-start.21 = (f32[64,1024]{1,0:T(8,128)S(1)}, f32[64,1024]{1,0:T(8,128)S(1)}, u32[]{:S(2)}, u32[]{:S(2)}) collective-permute-start(f32[64,1024]{1,0:T(8,128)S(1)} %collective-permute-done.17.refs_1_.refs_4_), channel_id=1, source_target_pairs={{0,2},{1,3},{2,0},{3,1},{4,6},{5,7},{6,4},{7,5},{8,10},{9,11},{10,... | collective-permute-start | bytes 786440 | tf_op jit(solution)/shard_map/ppermute | solution.py:20
  92.3 1.3 out_grad.2
  93.6 3.0 %collective-permute-done.21.refs_2_.refs_5_ = f32[64,1024]{1,0:T(8,128)S(1)} collective-permute-done((f32[64,1024]{1,0:T(8,128)S(1)}, f32[64,1024]{1,0:T(8,128)S(1)}, u32[]{:S(2)}, u32[]{:S(2)}) %collective-permute-start.21) | collective-permute-done | bytes 262176 | tf_op jit(solution)/shard_map/ppermute | solution.py:20
  97.9 2.4 %collective-permute-start.23 = (f32[256,1024]{1,0:T(8,128)S(1)}, f32[256,1024]{1,0:T(8,128)S(1)}, u32[]{:S(2)}, u32[]{:S(2)}) collective-permute-start(f32[256,1024]{1,0:T(8,128)S(1)} %out_grad.2), channel_id=1, source_target_pairs={{0,8},{4,12},{8,0},{12,4},{16,24},{20,28},{24,16},{28,20},{1,9},{5... | collective-permute-start | bytes 3145736 | tf_op jit(solution)/shard_map/ppermute | solution.py:20
  101.5 1.6 %collective-permute-done.26.refs_8_ = f32[64,1024]{1,0:T(8,128)S(1)} collective-permute-done((f32[64,1024]{1,0:T(8,128)S(1)}, f32[64,1024]{1,0:T(8,128)S(1)}, u32[]{:S(2)}, u32[]{:S(2)}) %collective-permute-start.26) | collective-permute-done | bytes 262176 | tf_op jit(solution)/shard_map/ppermute | solution.py:20
  105.1 6.4 %backward_group.1 = (bf16[256,1024]{1,0:T(8,128)(2,1)S(1)}, f32[1,1024]{1,0:T(1,128)S(1)}, bf16[256,1024]{1,0:T(8,128)(2,1)S(1)}, f32[1,1024]{1,0:T(1,128)S(1)},...) custom-call(s32[23]{0:T(128)S(1)} %stack.83.idx_ref, bf16[256,1024]{1,0:T(8,128)(2,1)S(1)} %get-tuple-element.158.refs_1_.refs_0_, ...), custom_call_target="tpu_custom_call" | custom-call | tf_op jit(solution)/shard_map/backward_group/pallas_call | solution.py:54
  112.8 10.2 %collective-permute-done.23 = f32[256,1024]{1,0:T(8,128)S(1)} collective-permute-done((f32[256,1024]{1,0:T(8,128)S(1)}, f32[256,1024]{1,0:T(8,128)S(1)}, u32[]{:S(2)}, u32[]{:S(2)}) %collective-permute-start.23) | collective-permute-done | bytes 1048608 | tf_op jit(solution)/shard_map/ppermute | solution.py:20
  123.0 1.7 %collective-permute-start.28 = (f32[264,1024]{1,0:T(8,128)S(1)}, f32[264,1024]{1,0:T(8,128)S(1)}, u32[]{:S(2)}, u32[]{:S(2)}) collective-permute-start(f32[264,1024]{1,0:T(8,128)S(1)} %in_grad.2), channel_id=1, source_target_pairs={{0,8},{4,12},{8,0},{12,4},{16,24},{20,28},{24,16},{28,20},{1,9},{5... | collective-permute-start | bytes 3244040 | tf_op jit(solution)/shard_map/ppermute | solution.py:20
  130.2 9.7 %collective-permute-done.30 = f32[256,512]{1,0:T(8,128)S(1)} collective-permute-done((f32[256,512]{1,0:T(8,128)S(1)}, f32[256,512]{1,0:T(8,128)S(1)}, u32[]{:S(2)}, u32[]{:S(2)}) %collective-permute-start.30) | collective-permute-done | bytes 524320 | tf_op jit(solution)/shard_map/ppermute | solution.py:20
  140.7 8.6 %collective-permute-done.28 = f32[264,1024]{1,0:T(8,128)S(1)} collective-permute-done((f32[264,1024]{1,0:T(8,128)S(1)}, f32[264,1024]{1,0:T(8,128)S(1)}, u32[]{:S(2)}, u32[]{:S(2)}) %collective-permute-start.28) | collective-permute-done | bytes 1081376 | tf_op jit(solution)/shard_map/ppermute | solution.py:20
  (77 shorter events, 27.8 us)
Async XLA Ops:
  0.7 9.2 %copy-start.6 = (f32[1024]{0:T(1024)S(1)}, f32[1024]{0:T(1024)}, u32[]{:S(2)}) copy-start(f32[1024]{0:T(1024)} %param.12) | copy-start | bytes 12292
  3.1 28.7 %collective-permute-start = (f32[128,2048]{1,0:T(8,128)S(1)}, f32[128,2048]{1,0:T(8,128)S(1)}, u32[]{:S(2)}, u32[]{:S(2)}) collective-permute-start(f32[128,2048]{1,0:T(8,128)S(1)} %get-tuple-element.109), channel_id=1, source_target_pairs={{0,4},{4,0},{8,12},{12,8},{16,20},{20,16},{24,28},{28,24},{1,5},{5... | collective-permute-start | bytes 3145736 | tf_op jit(solution)/shard_map/ppermute | solution.py:20
  6.1 25.6 %collective-permute-start.1 = (f32[64,2048]{1,0:T(8,128)S(1)}, f32[64,2048]{1,0:T(8,128)S(1)}, u32[]{:S(2)}, u32[]{:S(2)}) collective-permute-start(f32[64,2048]{1,0:T(8,128)S(1)} %get-tuple-element.111), channel_id=1, source_target_pairs={{0,16},{4,20},{8,24},{12,28},{16,0},{20,4},{24,8},{28,12},{1,17},{... | collective-permute-start | bytes 1572872 | tf_op jit(solution)/shard_map/ppermute | solution.py:20
  17.2 3.8 %collective-permute-start.2 = (f32[1,4,1024]{2,1,0:T(4,128)S(1)}, f32[1,4,1024]{2,1,0:T(4,128)S(1)}, u32[]{:S(2)}, u32[]{:S(2)}) collective-permute-start(f32[1,4,1024]{2,1,0:T(4,128)S(1)} %summary.1), channel_id=1, source_target_pairs={{0,8},{4,12},{8,0},{12,4},{16,24},{20,28},{24,16},{28,20},{1,9},{5... | collective-permute-start | bytes 49160 | tf_op jit(solution)/shard_map/ppermute | solution.py:20
  18.9 12.9 %collective-permute-start.3 = (f32[1,4,1024]{2,1,0:T(4,128)S(1)}, f32[1,4,1024]{2,1,0:T(4,128)S(1)}, u32[]{:S(2)}, u32[]{:S(2)}) collective-permute-start(f32[1,4,1024]{2,1,0:T(4,128)S(1)} %summary.1), channel_id=1, source_target_pairs={{0,12},{4,8},{8,4},{12,0},{16,28},{20,24},{24,20},{28,16},{1,13},{... | collective-permute-start | bytes 49160 | tf_op jit(solution)/shard_map/ppermute | solution.py:20
  19.3 12.5 %collective-permute-start.4 = (f32[1,4,1024]{2,1,0:T(4,128)S(1)}, f32[1,4,1024]{2,1,0:T(4,128)S(1)}, u32[]{:S(2)}, u32[]{:S(2)}) collective-permute-start(f32[1,4,1024]{2,1,0:T(4,128)S(1)} %summary.1), channel_id=1, source_target_pairs={{0,4},{4,0},{8,12},{12,8},{16,20},{20,16},{24,28},{28,24},{1,5},{5... | collective-permute-start | bytes 49160 | tf_op jit(solution)/shard_map/ppermute | solution.py:20
  31.8 19.7 %collective-permute-start.5 = (f32[64,2048]{1,0:T(8,128)S(1)}, f32[64,2048]{1,0:T(8,128)S(1)}, u32[]{:S(2)}, u32[]{:S(2)}) collective-permute-start(f32[64,2048]{1,0:T(8,128)S(1)} %collective-permute-done.1.refs_1_), channel_id=1, source_target_pairs={{0,4},{4,0},{8,12},{12,8},{16,20},{20,16},{24,28},{28,24},{1,5},{5... | collective-permute-start | bytes 1572872 | tf_op jit(solution)/shard_map/ppermute | solution.py:20
  33.4 18.1 %collective-permute-start.6 = (f32[64,2048]{1,0:T(8,128)S(1)}, f32[64,2048]{1,0:T(8,128)S(1)}, u32[]{:S(2)}, u32[]{:S(2)}) collective-permute-start(f32[64,2048]{1,0:T(8,128)S(1)} %collective-permute-done.1.refs_1_), channel_id=1, source_target_pairs={{0,2},{1,3},{2,0},{3,1},{4,6},{5,7},{6,4},{7,5},{8,10},{9,11},{10,... | collective-permute-start | bytes 1572872 | tf_op jit(solution)/shard_map/ppermute | solution.py:20
  34.9 16.6 %collective-permute-start.7 = (f32[64,1024]{1,0:T(8,128)S(1)}, f32[64,1024]{1,0:T(8,128)S(1)}, u32[]{:S(2)}, u32[]{:S(2)}) collective-permute-start(f32[64,1024]{1,0:T(8,128)S(1)} %get-tuple-element.118), channel_id=1, source_target_pairs={{0,16},{4,20},{8,24},{12,28},{16,0},{20,4},{24,8},{28,12},{1,17},{... | collective-permute-start | bytes 786440 | tf_op jit(solution)/shard_map/ppermute | solution.py:20
  35.9 14.7 %collective-permute-start.8 = (f32[4,4,1024]{2,1,0:T(4,128)S(1)}, f32[4,4,1024]{2,1,0:T(4,128)S(1)}, u32[]{:S(2)}, u32[]{:S(2)}) collective-permute-start(f32[4,4,1024]{2,1,0:T(4,128)S(1)} %pad_maximum_fusion.1), channel_id=1, source_target_pairs={{0,20},{4,16},{8,28},{12,24},{16,4},{20,0},{24,12},{28,8},{1,21},{... | collective-permute-start | bytes 196616 | tf_op jit(solution)/shard_map/ppermute | solution.py:20
  51.8 15.1 %collective-permute-start.13 = (f32[320,2048]{1,0:T(8,128)S(1)}, f32[320,2048]{1,0:T(8,128)S(1)}, u32[]{:S(2)}, u32[]{:S(2)}) collective-permute-start(f32[320,2048]{1,0:T(8,128)S(1)} %pack_x.1), channel_id=1, source_target_pairs={{0,1},{1,0},{2,3},{3,2},{4,5},{5,4},{6,7},{7,6},{8,9},{9,8},{10,11... | collective-permute-start | bytes 7864328 | tf_op jit(solution)/shard_map/ppermute | solution.py:20
  51.8 15.0 %collective-permute-start.9 = (f32[64,2048]{1,0:T(8,128)S(1)}, f32[64,2048]{1,0:T(8,128)S(1)}, u32[]{:S(2)}, u32[]{:S(2)}) collective-permute-start(f32[64,2048]{1,0:T(8,128)S(1)} %collective-permute-done.5.refs_3_), channel_id=1, source_target_pairs={{0,2},{1,3},{2,0},{3,1},{4,6},{5,7},{6,4},{7,5},{8,10},{9,11},{10,... | collective-permute-start | bytes 1572872 | tf_op jit(solution)/shard_map/ppermute | solution.py:20
  52.4 14.4 %collective-permute-start.12 = (f32[64,1024]{1,0:T(8,128)S(1)}, f32[64,1024]{1,0:T(8,128)S(1)}, u32[]{:S(2)}, u32[]{:S(2)}) collective-permute-start(f32[64,1024]{1,0:T(8,128)S(1)} %get-tuple-element.129), channel_id=1, source_target_pairs={{0,16},{4,20},{8,24},{12,28},{16,0},{20,4},{24,8},{28,12},{1,17},{... | collective-permute-start | bytes 786440 | tf_op jit(solution)/shard_map/ppermute | solution.py:20
  52.4 14.4 %collective-permute-start.11 = (f32[64,1024]{1,0:T(8,128)S(1)}, f32[64,1024]{1,0:T(8,128)S(1)}, u32[]{:S(2)}, u32[]{:S(2)}) collective-permute-start(f32[64,1024]{1,0:T(8,128)S(1)} %get-tuple-element.127), channel_id=1, source_target_pairs={{0,4},{4,0},{8,12},{12,8},{16,20},{20,16},{24,28},{28,24},{1,5},{5... | collective-permute-start | bytes 786440 | tf_op jit(solution)/shard_map/ppermute | solution.py:20
  52.9 13.9 %collective-permute-start.10 = (f32[64,1024]{1,0:T(8,128)S(1)}, f32[64,1024]{1,0:T(8,128)S(1)}, u32[]{:S(2)}, u32[]{:S(2)}) collective-permute-start(f32[64,1024]{1,0:T(8,128)S(1)} %collective-permute-done.7.refs_2_), channel_id=1, source_target_pairs={{0,4},{4,0},{8,12},{12,8},{16,20},{20,16},{24,28},{28,24},{1,5},{5... | collective-permute-start | bytes 786440 | tf_op jit(solution)/shard_map/ppermute | solution.py:20
  66.8 4.2 %collective-permute-start.19 = (f32[64,2048]{1,0:T(8,128)S(1)}, f32[64,2048]{1,0:T(8,128)S(1)}, u32[]{:S(2)}, u32[]{:S(2)}) collective-permute-start(f32[64,2048]{1,0:T(8,128)S(1)} %collective-permute-done.9.refs_4_), channel_id=1, source_target_pairs={{0,1},{1,0},{2,3},{3,2},{4,5},{5,4},{6,7},{7,6},{8,9},{9,8},{10,11... | collective-permute-start | bytes 1572872 | tf_op jit(solution)/shard_map/ppermute | solution.py:20
  66.9 20.7 %collective-permute-start.18 = (f32[64,2048]{1,0:T(8,128)S(1)}, f32[64,2048]{1,0:T(8,128)S(1)}, u32[]{:S(2)}, u32[]{:S(2)}) collective-permute-start(f32[64,2048]{1,0:T(8,128)S(1)} %get-tuple-element.147), channel_id=1, source_target_pairs={{0,4},{4,0},{8,12},{12,8},{16,20},{20,16},{24,28},{28,24},{1,5},{5... | collective-permute-start | bytes 1572872 | tf_op jit(solution)/shard_map/ppermute | solution.py:20
  68.0 11.6 %collective-permute-start.16 = (f32[64,1024]{1,0:T(8,128)S(1)}, f32[64,1024]{1,0:T(8,128)S(1)}, u32[]{:S(2)}, u32[]{:S(2)}) collective-permute-start(f32[64,1024]{1,0:T(8,128)S(1)} %collective-permute-done.12.refs_2_), channel_id=1, source_target_pairs={{0,2},{1,3},{2,0},{3,1},{4,6},{5,7},{6,4},{7,5},{8,10},{9,11},{10,... | collective-permute-start | bytes 786440 | tf_op jit(solution)/shard_map/ppermute | solution.py:20
  69.5 17.3 %collective-permute-start.17 = (f32[64,1024]{1,0:T(8,128)S(1)}, f32[64,1024]{1,0:T(8,128)S(1)}, u32[]{:S(2)}, u32[]{:S(2)}) collective-permute-start(f32[64,1024]{1,0:T(8,128)S(1)} %collective-permute-done.12.refs_2_), channel_id=1, source_target_pairs={{0,4},{4,0},{8,12},{12,8},{16,20},{20,16},{24,28},{28,24},{1,5},{5... | collective-permute-start | bytes 786440 | tf_op jit(solution)/shard_map/ppermute | solution.py:20
  70.5 16.3 %collective-permute-start.15 = (f32[64,1024]{1,0:T(8,128)S(1)}, f32[64,1024]{1,0:T(8,128)S(1)}, u32[]{:S(2)}, u32[]{:S(2)}) collective-permute-start(f32[64,1024]{1,0:T(8,128)S(1)} %collective-permute-done.7.refs_2_), channel_id=1, source_target_pairs={{0,2},{1,3},{2,0},{3,1},{4,6},{5,7},{6,4},{7,5},{8,10},{9,11},{10,... | collective-permute-start | bytes 786440 | tf_op jit(solution)/shard_map/ppermute | solution.py:20
  71.0 16.6 %collective-permute-start.14 = (f32[64,1024]{1,0:T(8,128)S(1)}, f32[64,1024]{1,0:T(8,128)S(1)}, u32[]{:S(2)}, u32[]{:S(2)}) collective-permute-start(f32[64,1024]{1,0:T(8,128)S(1)} %collective-permute-done.10.refs_4_), channel_id=1, source_target_pairs={{0,2},{1,3},{2,0},{3,1},{4,6},{5,7},{6,4},{7,5},{8,10},{9,11},{10,... | collective-permute-start | bytes 786440 | tf_op jit(solution)/shard_map/ppermute | solution.py:20
  87.8 3.5 %collective-permute-start.20 = (f32[384,1024]{1,0:T(8,128)S(1)}, f32[384,1024]{1,0:T(8,128)S(1)}, u32[]{:S(2)}, u32[]{:S(2)}) collective-permute-start(f32[384,1024]{1,0:T(8,128)S(1)} %pack_a.1), channel_id=1, source_target_pairs={{0,1},{1,0},{2,3},{3,2},{4,5},{5,4},{6,7},{7,6},{8,9},{9,8},{10,11... | collective-permute-start | bytes 4718600 | tf_op jit(solution)/shard_map/ppermute | solution.py:20
  87.9 8.7 %collective-permute-start.21 = (f32[64,1024]{1,0:T(8,128)S(1)}, f32[64,1024]{1,0:T(8,128)S(1)}, u32[]{:S(2)}, u32[]{:S(2)}) collective-permute-start(f32[64,1024]{1,0:T(8,128)S(1)} %collective-permute-done.17.refs_1_.refs_4_), channel_id=1, source_target_pairs={{0,2},{1,3},{2,0},{3,1},{4,6},{5,7},{6,4},{7,5},{8,10},{9,11},{10,... | collective-permute-start | bytes 786440 | tf_op jit(solution)/shard_map/ppermute | solution.py:20
  89.5 8.4 %collective-permute-start.22 = (f32[64,1024]{1,0:T(8,128)S(1)}, f32[64,1024]{1,0:T(8,128)S(1)}, u32[]{:S(2)}, u32[]{:S(2)}) collective-permute-start(f32[64,1024]{1,0:T(8,128)S(1)} %get-tuple-element.167), channel_id=1, source_target_pairs={{0,4},{4,0},{8,12},{12,8},{16,20},{20,16},{24,28},{28,24},{1,5},{5... | collective-permute-start | bytes 786440 | tf_op jit(solution)/shard_map/ppermute | solution.py:20
  97.9 25.1 %collective-permute-start.23 = (f32[256,1024]{1,0:T(8,128)S(1)}, f32[256,1024]{1,0:T(8,128)S(1)}, u32[]{:S(2)}, u32[]{:S(2)}) collective-permute-start(f32[256,1024]{1,0:T(8,128)S(1)} %out_grad.2), channel_id=1, source_target_pairs={{0,8},{4,12},{8,0},{12,4},{16,24},{20,28},{24,16},{28,20},{1,9},{5... | collective-permute-start | bytes 3145736 | tf_op jit(solution)/shard_map/ppermute | solution.py:20
  100.4 3.5 %collective-permute-start.27 = (f32[192,1024]{1,0:T(8,128)S(1)}, f32[192,1024]{1,0:T(8,128)S(1)}, u32[]{:S(2)}, u32[]{:S(2)}) collective-permute-start(f32[192,1024]{1,0:T(8,128)S(1)} %pack_b.1), channel_id=1, source_target_pairs={{0,1},{1,0},{2,3},{3,2},{4,5},{5,4},{6,7},{7,6},{8,9},{9,8},{10,11... | collective-permute-start | bytes 2359304 | tf_op jit(solution)/shard_map/ppermute | solution.py:20
  100.5 2.6 %collective-permute-start.26 = (f32[64,1024]{1,0:T(8,128)S(1)}, f32[64,1024]{1,0:T(8,128)S(1)}, u32[]{:S(2)}, u32[]{:S(2)}) collective-permute-start(f32[64,1024]{1,0:T(8,128)S(1)} %collective-permute-done.12.refs_2_), channel_id=1, source_target_pairs={{0,1},{1,0},{2,3},{3,2},{4,5},{5,4},{6,7},{7,6},{8,9},{9,8},{10,11... | collective-permute-start | bytes 786440 | tf_op jit(solution)/shard_map/ppermute | solution.py:20
  101.0 2.5 %collective-permute-start.25 = (f32[64,1024]{1,0:T(8,128)S(1)}, f32[64,1024]{1,0:T(8,128)S(1)}, u32[]{:S(2)}, u32[]{:S(2)}) collective-permute-start(f32[64,1024]{1,0:T(8,128)S(1)} %get-tuple-element.174.refs_1_), channel_id=1, source_target_pairs={{0,1},{1,0},{2,3},{3,2},{4,5},{5,4},{6,7},{7,6},{8,9},{9,8},{10,11... | collective-permute-start | bytes 786440 | tf_op jit(solution)/shard_map/ppermute | solution.py:20
  101.0 2.8 %collective-permute-start.24 = (f32[64,1024]{1,0:T(8,128)S(1)}, f32[64,1024]{1,0:T(8,128)S(1)}, u32[]{:S(2)}, u32[]{:S(2)}) collective-permute-start(f32[64,1024]{1,0:T(8,128)S(1)} %collective-permute-done.22.refs_0_), channel_id=1, source_target_pairs={{0,1},{1,0},{2,3},{3,2},{4,5},{5,4},{6,7},{7,6},{8,9},{9,8},{10,11... | collective-permute-start | bytes 786440 | tf_op jit(solution)/shard_map/ppermute | solution.py:20
  122.9 2.7 %collective-permute-start.29 = (f32[2,256,512]{2,1,0:T(8,128)S(1)}, f32[2,256,512]{2,1,0:T(8,128)S(1)}, u32[]{:S(2)}, u32[]{:S(2)}) collective-permute-start(f32[2,256,512]{2,1,0:T(8,128)S(1)} %get-tuple-element.196), channel_id=1, source_target_pairs={{0,1},{1,0},{2,3},{3,2},{4,5},{5,4},{6,7},{7,6},{8,9},{9,8},{10,11... | collective-permute-start | bytes 3145736 | tf_op jit(solution)/shard_map/ppermute | solution.py:20
  123.0 26.3 %collective-permute-start.28 = (f32[264,1024]{1,0:T(8,128)S(1)}, f32[264,1024]{1,0:T(8,128)S(1)}, u32[]{:S(2)}, u32[]{:S(2)}) collective-permute-start(f32[264,1024]{1,0:T(8,128)S(1)} %in_grad.2), channel_id=1, source_target_pairs={{0,8},{4,12},{8,0},{12,4},{16,24},{20,28},{24,16},{28,20},{1,9},{5... | collective-permute-start | bytes 3244040 | tf_op jit(solution)/shard_map/ppermute | solution.py:20
  125.9 14.0 %collective-permute-start.30 = (f32[256,512]{1,0:T(8,128)S(1)}, f32[256,512]{1,0:T(8,128)S(1)}, u32[]{:S(2)}, u32[]{:S(2)}) collective-permute-start(f32[256,512]{1,0:T(8,128)S(1)} %slice_bitcast_fusion), channel_id=1, source_target_pairs={{0,2},{1,3},{2,0},{3,1},{4,6},{5,7},{6,4},{7,5},{8,10},{9,11},{10,... | collective-permute-start | bytes 1572872 | tf_op jit(solution)/shard_map/ppermute | solution.py:20
  (8 other events, 35.9 us)

commit v6 on v5

--- a/solution.py
+++ b/solution.py
@@ -75,7 +75,7 @@
     quarter_ref[...] = full[pl.ds(pl.multiple_of(idx_ref[LANE] * quarter, quarter), quarter), :]
 
 
-def prep_cotangent_kernel(idx_ref, x_ref, p_ref, own_a_ref, first_a_ref, first_b_ref, second_ref, away_a_ref, away_b_ref, full):
+def prep_cotangent_kernel(idx_ref, x_ref, p_ref, own_a_ref, first_a_ref, first_b_ref, second_a_ref, second_b_ref, away_a_ref, away_b_ref, full):
     ordered_rows(x_ref, p_ref, full)
     quarter, width = first_a_ref.shape
     cols = [pl.ds(pl.multiple_of(idx_ref[SIDES + k] * width, width), width) for k in range(2)]
@@ -85,8 +85,8 @@
     own_a_ref[...] = full[:, cols[0]].astype(BF16)
     first_a_ref[...] = full[first, cols[0]]
     first_b_ref[...] = full[first, cols[1]]
-    second_ref[:, :width] = full[second, cols[0]]
-    second_ref[:, width:] = full[second, cols[1]]
+    second_a_ref[...] = full[second, cols[0]]
+    second_b_ref[...] = full[second, cols[1]]
     away_a_ref[...] = full[away, cols[1]]
     away_b_ref[...] = full[away, cols[0]]
 
@@ -448,9 +448,9 @@
     near_x = line.send(x_half, "tm", 1)
     away_x = line.send(x_quarter, "tm", far)
     part = ((quarter, depth // 2), F32)
-    c_own, own_a, c_first_a, c_first_b, c_second, c_quarter_a, c_quarter_b = prep(
+    c_own, own_a, c_first_a, c_first_b, c_second_a, c_second_b, c_quarter_a, c_quarter_b = prep(
         prep_cotangent_kernel, idx, line.behind(cotangent),
-        [((rows, depth // 2), BF16), part, part, ((quarter, depth), F32), part, part], "prep_cotangent",
+        [((rows, depth // 2), BF16), part, part, part, part, part, part], "prep_cotangent",
     )
     table = resident(
         functools.partial(summary_kernel, scaling=scaling), jax.ShapeDtypeStruct((1, 4, channels), F32),
@@ -486,19 +486,17 @@
     corner_b = line.send(away_b, "tm", 1)
     corner_side_a = line.send(corner_a, "chan", 2)
     side_a = line.send(away_a, "chan", 2)
-    near_2 = line.send(c_second, "tm", 1)
+    near_a2 = line.send(c_second_a, "tm", 1)
     last_x = line.send(corner_side_x, "chan", 1)
-    side_b = line.send(away_b, "chan", 2)
     xs = [x_own] + collected(idx, [
         (near_x, mine_near), (away_x, mine_1), (side_x, mine_2), (corner_x, mine_3), (corner_side_x, mine_4),
         (other_x, their_near + their_1 + their_2 + their_3), (last_x, their_4),
     ], "collect_x")
     more, more_low = forward_call(idx, 1, xs[1:], forward, "forward_group")
     starts, lows = starts + more, lows + more_low
-    corner_side_a, side_a, side_b, corner_b, near_2, lows[1] = line.step(corner_side_a, side_a, side_b, corner_b, near_2, lows[1])
-    near_a2, near_b2 = near_2[:, : depth // 2], near_2[:, depth // 2 :]
-
-    corner_side_b = line.send(corner_b, "chan", 2)
+    corner_side_a, side_a, corner_b, near_a2, lows[1] = line.step(corner_side_a, side_a, corner_b, near_a2, lows[1])
+
+    side_b = line.send(away_b, "chan", 2)
     near_b1 = line.send(c_first_b, "tm", 1)
     other_a = line.send(pack([near_a1, near_a2, away_a, side_a, corner_a, corner_side_a], "pack_a"), "chan", 1)
     ca = [own_a] + collected(idx, [
@@ -511,18 +509,24 @@
         return [grad_rows(idx, first + k, features, values, rows_out, factor, name, sums) for k in range(1, groups)]
 
     out_given = shares(ROWS + groups, ca, lows, scaling, "out_grad")
-    out_given[0], corner_side_b, near_b1 = line.step(out_given[0], corner_side_b, near_b1)
+    out_given[0], side_b, near_b1 = line.step(out_given[0], side_b, near_b1)
 
     out_got = [line.send(part, "tm", 2 * (k + 1)) for k, part in enumerate(out_given)]
+    near_b2 = line.send(c_second_b, "tm", 1)
+    corner_side_b = line.send(corner_b, "chan", 2)
     near_b1_other = line.send(near_b1, "chan", 1)
+    away_b_other = line.send(away_b, "chan", 1)
+    near_b2, corner_side_b, near_b1_other, away_b_other = line.step(near_b2, corner_side_b, near_b1_other, away_b_other)
+
     near_b2_other = line.send(near_b2, "chan", 1)
-    away_b_other = line.send(away_b, "chan", 1)
-    other_b = line.send(pack([side_b, corner_b, corner_side_b], "pack_b"), "chan", 1)
+    side_b_other = line.send(side_b, "chan", 1)
+    corner_b_other = line.send(corner_b, "chan", 1)
+    last_b = line.send(corner_side_b, "chan", 1)
     cb = collected(idx, [
         (near_b1, [(0, 6, quarter)]), (near_b2, [(0, 7, quarter)]),
         (away_b, mine_1), (side_b, mine_2), (corner_b, mine_3), (corner_side_b, mine_4),
-        (near_b1_other, [(0, 8, quarter)]), (near_b2_other, [(0, 9, quarter)]), (away_b_other, their_1),
-        (other_b, their_2 + their_3 + their_4),
+        (near_b1_other, [(0, 8, quarter)]), (near_b2_other, [(0, 9, quarter)]),
+        (away_b_other, their_1), (side_b_other, their_2), (corner_b_other, their_3), (last_b, their_4),
     ], "collect_b")
     cs = [list(pair) for pair in zip(ca[1:], cb, strict=True)]
     more, more_grads = backward_call(idx, 1, cs, backward, starts[1:], lows[1:], scaling, "backward_group")

time: 151 us -> 145 us (0.960)
  waiting for transfers between devices: 74.3 us -> 71 us
  starting transfers between devices: 32.1 us -> 29.5 us
    ppermute x31 -> x34, waiting for transfers between devices: 74.3 us -> 71 us  [swap(): return lax.ppermute(x, axis, [(k, k ^ bit) for k in range(n)])]
    ppermute x31 -> x34, starting transfers between devices: 32.1 us -> 29.5 us  [swap(): return lax.ppermute(x, axis, [(k, k ^ bit) for k in range(n)])]
    pallas_call x19 -> x18, Pallas kernels: 33.9 us -> 33.8 us  [resident(): pl.pallas_call(kernel, out_shape=out_shape, in_specs=[SMEM] * scalars + [...]
  transfers between devices with their start and end apart: 31 -> 34, of which waited for: 16 -> 20; matrix products, arithmetic and copies ran while one was open for 1% -> 1% of each run, Pallas kernels for 21% -> 22%
where the time goes in v6:
time: 145 us
  waiting for transfers between devices  71 us (49%)
  Pallas kernels  33.8 us (23%)
  starting transfers between devices  29.5 us (20%)
  local copies, waits for them, and re-layouts  5.76 us (4%)
  other arithmetic  3.86 us (3%)
    ppermute x34, waiting for transfers between devices, swap(): return lax.ppermute(x, axis, [(k, k ^ bit) for k in range(n)])  71 us
    pallas_call x18, Pallas kernels, resident(): pl.pallas_call(kernel, out_shape=out_shape, in_specs=[SMEM] * scalars + [...  33.8 us
    ppermute x34, starting transfers between devices, swap(): return lax.ppermute(x, axis, [(k, k ^ bit) for k in range(n)])  29.5 us
    unnamed x18, local copies, waits for them, and re-layouts  5.62 us
  transfers between devices with their start and end apart: 34, of which 20 were waited for; matrix products, arithmetic and copies ran while one was open for 1% of the time, Pallas kernels for 22%

profile of v6, /device:TPU:0, one launch (start us, length us, event | category | flops | bytes accessed | tf_op | source)
XLA Modules:
  0.0 145.0 jit_solution(10318372604662016081)
XLA Ops:
  3.1 3.0 %collective-permute-start = (f32[128,2048]{1,0:T(8,128)S(1)}, f32[128,2048]{1,0:T(8,128)S(1)}, u32[]{:S(2)}, u32[]{:S(2)}) collective-permute-start(f32[128,2048]{1,0:T(8,128)S(1)} %get-tuple-element.117), channel_id=1, source_target_pairs={{0,4},{4,0},{8,12},{12,8},{16,20},{20,16},{24,28},{28,24},{1,5},{5... | collective-permute-start | bytes 3145736 | tf_op jit(solution)/shard_map/ppermute | solution.py:20
  6.1 2.6 %collective-permute-start.1 = (f32[64,2048]{1,0:T(8,128)S(1)}, f32[64,2048]{1,0:T(8,128)S(1)}, u32[]{:S(2)}, u32[]{:S(2)}) collective-permute-start(f32[64,2048]{1,0:T(8,128)S(1)} %get-tuple-element.119), channel_id=1, source_target_pairs={{0,16},{4,20},{8,24},{12,28},{16,0},{20,4},{24,8},{28,12},{1,17},{... | collective-permute-start | bytes 1572872 | tf_op jit(solution)/shard_map/ppermute | solution.py:20
  9.9 2.2 %copy-done = bf16[2048,1024]{1,0:T(8,128)(2,1)S(1)} copy-done((bf16[2048,1024]{1,0:T(8,128)(2,1)S(1)}, bf16[2048,1024]{1,0:T(8,128)(2,1)}, u32[]{:S(2)}) %copy-start) | copy-done | bytes 4194328
  12.1 2.2 %copy-done.2 = bf16[1024,2048]{1,0:T(8,128)(2,1)S(1)} copy-done((bf16[1024,2048]{1,0:T(8,128)(2,1)S(1)}, bf16[1024,2048]{1,0:T(8,128)(2,1)}, u32[]{:S(2)}) %copy-start.2) | copy-done | bytes 4194328
  14.3 2.9 %summary.1 = f32[1,4,1024]{2,1,0:T(4,128)S(1)} custom-call(bf16[256,2048]{1,0:T(8,128)(2,1)S(1)} %get-tuple-element.208.x_ref.refs_0_, bf16[256,2048]{1,0:T(8,128)(2,1)S(1)} %get-tuple-element.120.c_ref.refs_0_, bf16[2048,1024]{1,0:T(8,128)(2,1)S(1)} %copy-done, bf16[1024,2048]{1,0:T(8,128)(2,1)S(1)} %copy-done.2, f32[1,1024]{1,0:T(1,128)S(1)} %bitcast.31, ...), custom_call_target="tpu_custom_call" | custom-call | tf_op jit(solution)/shard_map/summary/pallas_call | solution.py:54
  17.8 2.5 %collective-permute-start.3 = (f32[1,4,1024]{2,1,0:T(4,128)S(1)}, f32[1,4,1024]{2,1,0:T(4,128)S(1)}, u32[]{:S(2)}, u32[]{:S(2)}) collective-permute-start(f32[1,4,1024]{2,1,0:T(4,128)S(1)} %summary.1), channel_id=1, source_target_pairs={{0,12},{4,8},{8,4},{12,0},{16,28},{20,24},{24,20},{28,16},{1,13},{... | collective-permute-start | bytes 49160 | tf_op jit(solution)/shard_map/ppermute | solution.py:20
  20.8 9.1 %collective-permute-done.4 = f32[1,4,1024]{2,1,0:T(4,128)S(1)} collective-permute-done((f32[1,4,1024]{2,1,0:T(4,128)S(1)}, f32[1,4,1024]{2,1,0:T(4,128)S(1)}, u32[]{:S(2)}, u32[]{:S(2)}) %collective-permute-start.4) | collective-permute-done | bytes 16416 | tf_op jit(solution)/shard_map/ppermute | solution.py:20
  29.8 2.0 %collective-permute-done.3 = f32[1,4,1024]{2,1,0:T(4,128)S(1)} collective-permute-done((f32[1,4,1024]{2,1,0:T(4,128)S(1)}, f32[1,4,1024]{2,1,0:T(4,128)S(1)}, u32[]{:S(2)}, u32[]{:S(2)}) %collective-permute-start.3) | collective-permute-done | bytes 16416 | tf_op jit(solution)/shard_map/ppermute | solution.py:20
  32.1 1.6 %collective-permute-start.6 = (f32[64,2048]{1,0:T(8,128)S(1)}, f32[64,2048]{1,0:T(8,128)S(1)}, u32[]{:S(2)}, u32[]{:S(2)}) collective-permute-start(f32[64,2048]{1,0:T(8,128)S(1)} %collective-permute-done.1.refs_1_), channel_id=1, source_target_pairs={{0,2},{1,3},{2,0},{3,1},{4,6},{5,7},{6,4},{7,5},{8,10},{9,11},{10,... | collective-permute-start | bytes 1572872 | tf_op jit(solution)/shard_map/ppermute | solution.py:20
  33.7 1.3 collective-permute-start.5
  36.0 2.1 %collective-permute-start.8 = (f32[4,4,1024]{2,1,0:T(4,128)S(1)}, f32[4,4,1024]{2,1,0:T(4,128)S(1)}, u32[]{:S(2)}, u32[]{:S(2)}) collective-permute-start(f32[4,4,1024]{2,1,0:T(4,128)S(1)} %pad_maximum_fusion.1), channel_id=1, source_target_pairs={{0,20},{4,16},{8,28},{12,24},{16,4},{20,0},{24,12},{28,8},{1,21},{... | collective-permute-start | bytes 196616 | tf_op jit(solution)/shard_map/ppermute | solution.py:20
  38.1 12.5 %collective-permute-done.8 = f32[4,4,1024]{2,1,0:T(4,128)S(1)} collective-permute-done((f32[4,4,1024]{2,1,0:T(4,128)S(1)}, f32[4,4,1024]{2,1,0:T(4,128)S(1)}, u32[]{:S(2)}, u32[]{:S(2)}) %collective-permute-start.8) | collective-permute-done | bytes 65568 | tf_op jit(solution)/shard_map/ppermute | solution.py:20
  52.9 1.6 %collective-permute-start.10 = (f32[64,1024]{1,0:T(8,128)S(1)}, f32[64,1024]{1,0:T(8,128)S(1)}, u32[]{:S(2)}, u32[]{:S(2)}) collective-permute-start(f32[64,1024]{1,0:T(8,128)S(1)} %collective-permute-done.7.refs_2_), channel_id=1, source_target_pairs={{0,4},{4,0},{8,12},{12,8},{16,20},{20,16},{24,28},{28,24},{1,5},{5... | collective-permute-start | bytes 786440 | tf_op jit(solution)/shard_map/ppermute | solution.py:20
  54.5 2.2 %forward_own.1 = (f32[8,1024]{1,0:T(8,128)S(1)}, bf16[256,1024]{1,0:T(8,128)(2,1)S(1)}) custom-call(s32[23]{0:T(128)S(1)} %stack.83.idx_ref, bf16[256,2048]{1,0:T(8,128)(2,1)S(1)} %get-tuple-element.208.x_ref.refs_0_, bf16[2048,1024]{1,0:T(8,128)(2,1)S(1)} %copy-done.1, f32[1,1024]{1,0:T(1,128)S(1)} %bitcast.32, f32[1,1024]{1,0:T(1,128)S(1)} %bitcast.37, ...), custom_call_target="tpu_custom_call" | custom-call | tf_op jit(solution)/shard_map/forward_own/pallas_call | solution.py:54
  56.7 2.4 %backward_own.1 = (bf16[256,1024]{1,0:T(8,128)(2,1)S(1)}, f32[1,1024]{1,0:T(1,128)S(1)}) custom-call(s32[23]{0:T(128)S(1)} %stack.83.idx_ref, bf16[256,2048]{1,0:T(8,128)(2,1)S(1)} %get-tuple-element.120.c_ref.refs_0_, bf16[1024,2048]{1,0:T(8,128)(2,1)S(1)} %copy-done.3, f32[1,1024]{1,0:T(1,128)S(1)} %bitcast.33, f32[1,1024]{1,0:T(1,128)S(1)} %bitcast.38, ...), custom_call_target="tpu_custom_call" | custom-call | tf_op jit(solution)/shard_map/backward_own/pallas_call | solution.py:54
  59.2 1.9 %row_grad.1 = (f32[2,256,512]{2,1,0:T(8,128)S(1)}, f32[2,256,512]{2,1,0:T(8,128)S(1)}) custom-call(s32[23]{0:T(128)S(1)} %stack.83.idx_ref, bf16[256,1024]{1,0:T(8,128)(2,1)S(1)} %get-tuple-element.143.a_ref.refs_4_, bf16[2048,1024]{1,0:T(8,128)(2,1)S(1)} %copy-done.1), custom_call_target="tpu_custom_call" | custom-call | tf_op jit(solution)/shard_map/row_grad/pallas_call | solution.py:54
  61.6 5.9 %collective-permute-done.12.refs_2_ = f32[64,1024]{1,0:T(8,128)S(1)} collective-permute-done((f32[64,1024]{1,0:T(8,128)S(1)}, f32[64,1024]{1,0:T(8,128)S(1)}, u32[]{:S(2)}, u32[]{:S(2)}) %collective-permute-start.12) | collective-permute-done | bytes 262176 | tf_op jit(solution)/shard_map/ppermute | solution.py:20
  67.6 1.6 %collective-permute-start.15 = (f32[64,1024]{1,0:T(8,128)S(1)}, f32[64,1024]{1,0:T(8,128)S(1)}, u32[]{:S(2)}, u32[]{:S(2)}) collective-permute-start(f32[64,1024]{1,0:T(8,128)S(1)} %collective-permute-done.7.refs_2_), channel_id=1, source_target_pairs={{0,2},{1,3},{2,0},{3,1},{4,6},{5,7},{6,4},{7,5},{8,10},{9,11},{10,... | collective-permute-start | bytes 786440 | tf_op jit(solution)/shard_map/ppermute | solution.py:20
  71.7 1.4 collect_x.1
  73.1 5.6 %forward_group.1 = (f32[8,1024]{1,0:T(8,128)S(1)}, bf16[256,1024]{1,0:T(8,128)(2,1)S(1)}, f32[8,1024]{1,0:T(8,128)S(1)}, bf16[256,1024]{1,0:T(8,128)(2,1)S(1)}, ...) custom-call(s32[23]{0:T(128)S(1)} %stack.83.idx_ref, bf16[256,2048]{1,0:T(8,128)(2,1)S(1)} %get-tuple-element.158.refs_0_.refs_1_, ...), custom_call_target="tpu_custom_call" | custom-call | tf_op jit(solution)/shard_map/forward_group/pallas_call | solution.py:54
  78.8 4.5 %collective-permute-done.16.refs_4_ = f32[64,1024]{1,0:T(8,128)S(1)} collective-permute-done((f32[64,1024]{1,0:T(8,128)S(1)}, f32[64,1024]{1,0:T(8,128)S(1)}, u32[]{:S(2)}, u32[]{:S(2)}) %collective-permute-start.16) | collective-permute-done | bytes 262176 | tf_op jit(solution)/shard_map/ppermute | solution.py:20
  85.1 1.8 %collective-permute-done.19.refs_6_ = f32[384,1024]{1,0:T(8,128)S(1)} collective-permute-done((f32[384,1024]{1,0:T(8,128)S(1)}, f32[384,1024]{1,0:T(8,128)S(1)}, u32[]{:S(2)}, u32[]{:S(2)}) %collective-permute-start.19) | collective-permute-done | bytes 1572896 | tf_op jit(solution)/shard_map/ppermute | solution.py:20
  87.9 1.3 out_grad.2
  89.2 3.0 %collective-permute-done.20.refs_3_ = f32[64,1024]{1,0:T(8,128)S(1)} collective-permute-done((f32[64,1024]{1,0:T(8,128)S(1)}, f32[64,1024]{1,0:T(8,128)S(1)}, u32[]{:S(2)}, u32[]{:S(2)}) %collective-permute-start.20) | collective-permute-done | bytes 262176 | tf_op jit(solution)/shard_map/ppermute | solution.py:20
  93.5 1.5 %collective-permute-start.24 = (f32[64,1024]{1,0:T(8,128)S(1)}, f32[64,1024]{1,0:T(8,128)S(1)}, u32[]{:S(2)}, u32[]{:S(2)}) collective-permute-start(f32[64,1024]{1,0:T(8,128)S(1)} %collective-permute-done.16.refs_4_), channel_id=1, source_target_pairs={{0,2},{1,3},{2,0},{3,1},{4,6},{5,7},{6,4},{7,5},{8,10},{9,11},{10,... | collective-permute-start | bytes 786440 | tf_op jit(solution)/shard_map/ppermute | solution.py:20
  95.5 4.6 %collective-permute-done.23.refs_1_ = f32[64,1024]{1,0:T(8,128)S(1)} collective-permute-done((f32[64,1024]{1,0:T(8,128)S(1)}, f32[64,1024]{1,0:T(8,128)S(1)}, u32[]{:S(2)}, u32[]{:S(2)}) %collective-permute-start.23) | collective-permute-done | bytes 262176 | tf_op jit(solution)/shard_map/ppermute | solution.py:20
  104.8 6.4 %backward_group.1 = (bf16[256,1024]{1,0:T(8,128)(2,1)S(1)}, f32[1,1024]{1,0:T(1,128)S(1)}, bf16[256,1024]{1,0:T(8,128)(2,1)S(1)}, f32[1,1024]{1,0:T(1,128)S(1)},...) custom-call(s32[23]{0:T(128)S(1)} %stack.83.idx_ref, bf16[256,1024]{1,0:T(8,128)(2,1)S(1)} %get-tuple-element.166.refs_1_.refs_0_, ...), custom_call_target="tpu_custom_call" | custom-call | tf_op jit(solution)/shard_map/backward_group/pallas_call | solution.py:54
  112.4 4.5 %collective-permute-done.22 = f32[256,1024]{1,0:T(8,128)S(1)} collective-permute-done((f32[256,1024]{1,0:T(8,128)S(1)}, f32[256,1024]{1,0:T(8,128)S(1)}, u32[]{:S(2)}, u32[]{:S(2)}) %collective-permute-start.22) | collective-permute-done | bytes 1048608 | tf_op jit(solution)/shard_map/ppermute | solution.py:20
  117.2 2.4 %collective-permute-done.32 = f32[2,256,512]{2,1,0:T(8,128)S(1)} collective-permute-done((f32[2,256,512]{2,1,0:T(8,128)S(1)}, f32[2,256,512]{2,1,0:T(8,128)S(1)}, u32[]{:S(2)}, u32[]{:S(2)}) %collective-permute-start.32) | collective-permute-done | bytes 1048608 | tf_op jit(solution)/shard_map/ppermute | solution.py:20
  119.9 1.5 %collective-permute-start.33 = (f32[256,512]{1,0:T(8,128)S(1)}, f32[256,512]{1,0:T(8,128)S(1)}, u32[]{:S(2)}, u32[]{:S(2)}) collective-permute-start(f32[256,512]{1,0:T(8,128)S(1)} %slice_bitcast_fusion), channel_id=1, source_target_pairs={{0,2},{1,3},{2,0},{3,1},{4,6},{5,7},{6,4},{7,5},{8,10},{9,11},{10,... | collective-permute-start | bytes 1572872 | tf_op jit(solution)/shard_map/ppermute | solution.py:20
  125.0 8.9 %collective-permute-done.33 = f32[256,512]{1,0:T(8,128)S(1)} collective-permute-done((f32[256,512]{1,0:T(8,128)S(1)}, f32[256,512]{1,0:T(8,128)S(1)}, u32[]{:S(2)}, u32[]{:S(2)}) %collective-permute-start.33) | collective-permute-done | bytes 524320 | tf_op jit(solution)/shard_map/ppermute | solution.py:20
  134.7 8.6 %collective-permute-done.31 = f32[264,1024]{1,0:T(8,128)S(1)} collective-permute-done((f32[264,1024]{1,0:T(8,128)S(1)}, f32[264,1024]{1,0:T(8,128)S(1)}, u32[]{:S(2)}, u32[]{:S(2)}) %collective-permute-start.31) | collective-permute-done | bytes 1081376 | tf_op jit(solution)/shard_map/ppermute | solution.py:20
  (81 shorter events, 28.4 us)
Async XLA Ops:
  3.1 29.0 %collective-permute-start = (f32[128,2048]{1,0:T(8,128)S(1)}, f32[128,2048]{1,0:T(8,128)S(1)}, u32[]{:S(2)}, u32[]{:S(2)}) collective-permute-start(f32[128,2048]{1,0:T(8,128)S(1)} %get-tuple-element.117), channel_id=1, source_target_pairs={{0,4},{4,0},{8,12},{12,8},{16,20},{20,16},{24,28},{28,24},{1,5},{5... | collective-permute-start | bytes 3145736 | tf_op jit(solution)/shard_map/ppermute | solution.py:20
  6.1 26.0 %collective-permute-start.1 = (f32[64,2048]{1,0:T(8,128)S(1)}, f32[64,2048]{1,0:T(8,128)S(1)}, u32[]{:S(2)}, u32[]{:S(2)}) collective-permute-start(f32[64,2048]{1,0:T(8,128)S(1)} %get-tuple-element.119), channel_id=1, source_target_pairs={{0,16},{4,20},{8,24},{12,28},{16,0},{20,4},{24,8},{28,12},{1,17},{... | collective-permute-start | bytes 1572872 | tf_op jit(solution)/shard_map/ppermute | solution.py:20
  17.2 12.6 %collective-permute-start.4 = (f32[1,4,1024]{2,1,0:T(4,128)S(1)}, f32[1,4,1024]{2,1,0:T(4,128)S(1)}, u32[]{:S(2)}, u32[]{:S(2)}) collective-permute-start(f32[1,4,1024]{2,1,0:T(4,128)S(1)} %summary.1), channel_id=1, source_target_pairs={{0,4},{4,0},{8,12},{12,8},{16,20},{20,16},{24,28},{28,24},{1,5},{5... | collective-permute-start | bytes 49160 | tf_op jit(solution)/shard_map/ppermute | solution.py:20
  17.8 14.0 %collective-permute-start.3 = (f32[1,4,1024]{2,1,0:T(4,128)S(1)}, f32[1,4,1024]{2,1,0:T(4,128)S(1)}, u32[]{:S(2)}, u32[]{:S(2)}) collective-permute-start(f32[1,4,1024]{2,1,0:T(4,128)S(1)} %summary.1), channel_id=1, source_target_pairs={{0,12},{4,8},{8,4},{12,0},{16,28},{20,24},{24,20},{28,16},{1,13},{... | collective-permute-start | bytes 49160 | tf_op jit(solution)/shard_map/ppermute | solution.py:20
  20.3 11.8 %collective-permute-start.2 = (f32[1,4,1024]{2,1,0:T(4,128)S(1)}, f32[1,4,1024]{2,1,0:T(4,128)S(1)}, u32[]{:S(2)}, u32[]{:S(2)}) collective-permute-start(f32[1,4,1024]{2,1,0:T(4,128)S(1)} %summary.1), channel_id=1, source_target_pairs={{0,8},{4,12},{8,0},{12,4},{16,24},{20,28},{24,16},{28,20},{1,9},{5... | collective-permute-start | bytes 49160 | tf_op jit(solution)/shard_map/ppermute | solution.py:20
  32.1 19.4 %collective-permute-start.6 = (f32[64,2048]{1,0:T(8,128)S(1)}, f32[64,2048]{1,0:T(8,128)S(1)}, u32[]{:S(2)}, u32[]{:S(2)}) collective-permute-start(f32[64,2048]{1,0:T(8,128)S(1)} %collective-permute-done.1.refs_1_), channel_id=1, source_target_pairs={{0,2},{1,3},{2,0},{3,1},{4,6},{5,7},{6,4},{7,5},{8,10},{9,11},{10,... | collective-permute-start | bytes 1572872 | tf_op jit(solution)/shard_map/ppermute | solution.py:20
  33.7 17.8 %collective-permute-start.5 = (f32[64,2048]{1,0:T(8,128)S(1)}, f32[64,2048]{1,0:T(8,128)S(1)}, u32[]{:S(2)}, u32[]{:S(2)}) collective-permute-start(f32[64,2048]{1,0:T(8,128)S(1)} %collective-permute-done.1.refs_1_), channel_id=1, source_target_pairs={{0,4},{4,0},{8,12},{12,8},{16,20},{20,16},{24,28},{28,24},{1,5},{5... | collective-permute-start | bytes 1572872 | tf_op jit(solution)/shard_map/ppermute | solution.py:20
  35.0 16.5 %collective-permute-start.7 = (f32[64,1024]{1,0:T(8,128)S(1)}, f32[64,1024]{1,0:T(8,128)S(1)}, u32[]{:S(2)}, u32[]{:S(2)}) collective-permute-start(f32[64,1024]{1,0:T(8,128)S(1)} %get-tuple-element.126), channel_id=1, source_target_pairs={{0,16},{4,20},{8,24},{12,28},{16,0},{20,4},{24,8},{28,12},{1,17},{... | collective-permute-start | bytes 786440 | tf_op jit(solution)/shard_map/ppermute | solution.py:20
  36.0 14.6 %collective-permute-start.8 = (f32[4,4,1024]{2,1,0:T(4,128)S(1)}, f32[4,4,1024]{2,1,0:T(4,128)S(1)}, u32[]{:S(2)}, u32[]{:S(2)}) collective-permute-start(f32[4,4,1024]{2,1,0:T(4,128)S(1)} %pad_maximum_fusion.1), channel_id=1, source_target_pairs={{0,20},{4,16},{8,28},{12,24},{16,4},{20,0},{24,12},{28,8},{1,21},{... | collective-permute-start | bytes 196616 | tf_op jit(solution)/shard_map/ppermute | solution.py:20
  51.8 15.8 %collective-permute-start.13 = (f32[320,2048]{1,0:T(8,128)S(1)}, f32[320,2048]{1,0:T(8,128)S(1)}, u32[]{:S(2)}, u32[]{:S(2)}) collective-permute-start(f32[320,2048]{1,0:T(8,128)S(1)} %pack_x.1), channel_id=1, source_target_pairs={{0,1},{1,0},{2,3},{3,2},{4,5},{5,4},{6,7},{7,6},{8,9},{9,8},{10,11... | collective-permute-start | bytes 7864328 | tf_op jit(solution)/shard_map/ppermute | solution.py:20
  51.8 15.7 %collective-permute-start.9 = (f32[64,2048]{1,0:T(8,128)S(1)}, f32[64,2048]{1,0:T(8,128)S(1)}, u32[]{:S(2)}, u32[]{:S(2)}) collective-permute-start(f32[64,2048]{1,0:T(8,128)S(1)} %collective-permute-done.5.refs_3_), channel_id=1, source_target_pairs={{0,2},{1,3},{2,0},{3,1},{4,6},{5,7},{6,4},{7,5},{8,10},{9,11},{10,... | collective-permute-start | bytes 1572872 | tf_op jit(solution)/shard_map/ppermute | solution.py:20
  52.4 9.2 %collective-permute-start.11 = (f32[64,1024]{1,0:T(8,128)S(1)}, f32[64,1024]{1,0:T(8,128)S(1)}, u32[]{:S(2)}, u32[]{:S(2)}) collective-permute-start(f32[64,1024]{1,0:T(8,128)S(1)} %get-tuple-element.135), channel_id=1, source_target_pairs={{0,4},{4,0},{8,12},{12,8},{16,20},{20,16},{24,28},{28,24},{1,5},{5... | collective-permute-start | bytes 786440 | tf_op jit(solution)/shard_map/ppermute | solution.py:20
  52.9 14.6 %collective-permute-start.12 = (f32[64,1024]{1,0:T(8,128)S(1)}, f32[64,1024]{1,0:T(8,128)S(1)}, u32[]{:S(2)}, u32[]{:S(2)}) collective-permute-start(f32[64,1024]{1,0:T(8,128)S(1)} %get-tuple-element.137), channel_id=1, source_target_pairs={{0,16},{4,20},{8,24},{12,28},{16,0},{20,4},{24,8},{28,12},{1,17},{... | collective-permute-start | bytes 786440 | tf_op jit(solution)/shard_map/ppermute | solution.py:20
  52.9 14.6 %collective-permute-start.10 = (f32[64,1024]{1,0:T(8,128)S(1)}, f32[64,1024]{1,0:T(8,128)S(1)}, u32[]{:S(2)}, u32[]{:S(2)}) collective-permute-start(f32[64,1024]{1,0:T(8,128)S(1)} %collective-permute-done.7.refs_2_), channel_id=1, source_target_pairs={{0,4},{4,0},{8,12},{12,8},{16,20},{20,16},{24,28},{28,24},{1,5},{5... | collective-permute-start | bytes 786440 | tf_op jit(solution)/shard_map/ppermute | solution.py:20
  67.5 4.2 %collective-permute-start.18 = (f32[64,2048]{1,0:T(8,128)S(1)}, f32[64,2048]{1,0:T(8,128)S(1)}, u32[]{:S(2)}, u32[]{:S(2)}) collective-permute-start(f32[64,2048]{1,0:T(8,128)S(1)} %collective-permute-done.9.refs_4_), channel_id=1, source_target_pairs={{0,1},{1,0},{2,3},{3,2},{4,5},{5,4},{6,7},{7,6},{8,9},{9,8},{10,11... | collective-permute-start | bytes 1572872 | tf_op jit(solution)/shard_map/ppermute | solution.py:20
  67.6 11.1 %collective-permute-start.15 = (f32[64,1024]{1,0:T(8,128)S(1)}, f32[64,1024]{1,0:T(8,128)S(1)}, u32[]{:S(2)}, u32[]{:S(2)}) collective-permute-start(f32[64,1024]{1,0:T(8,128)S(1)} %collective-permute-done.7.refs_2_), channel_id=1, source_target_pairs={{0,2},{1,3},{2,0},{3,1},{4,6},{5,7},{6,4},{7,5},{8,10},{9,11},{10,... | collective-permute-start | bytes 786440 | tf_op jit(solution)/shard_map/ppermute | solution.py:20
  69.2 9.5 %collective-permute-start.17 = (f32[64,1024]{1,0:T(8,128)S(1)}, f32[64,1024]{1,0:T(8,128)S(1)}, u32[]{:S(2)}, u32[]{:S(2)}) collective-permute-start(f32[64,1024]{1,0:T(8,128)S(1)} %get-tuple-element.155), channel_id=1, source_target_pairs={{0,4},{4,0},{8,12},{12,8},{16,20},{20,16},{24,28},{28,24},{1,5},{5... | collective-permute-start | bytes 786440 | tf_op jit(solution)/shard_map/ppermute | solution.py:20
  70.2 13.0 %collective-permute-start.16 = (f32[64,1024]{1,0:T(8,128)S(1)}, f32[64,1024]{1,0:T(8,128)S(1)}, u32[]{:S(2)}, u32[]{:S(2)}) collective-permute-start(f32[64,1024]{1,0:T(8,128)S(1)} %collective-permute-done.12.refs_2_), channel_id=1, source_target_pairs={{0,4},{4,0},{8,12},{12,8},{16,20},{20,16},{24,28},{28,24},{1,5},{5... | collective-permute-start | bytes 786440 | tf_op jit(solution)/shard_map/ppermute | solution.py:20
  71.3 12.0 %collective-permute-start.14 = (f32[64,1024]{1,0:T(8,128)S(1)}, f32[64,1024]{1,0:T(8,128)S(1)}, u32[]{:S(2)}, u32[]{:S(2)}) collective-permute-start(f32[64,1024]{1,0:T(8,128)S(1)} %collective-permute-done.10.refs_4_), channel_id=1, source_target_pairs={{0,2},{1,3},{2,0},{3,1},{4,6},{5,7},{6,4},{7,5},{8,10},{9,11},{10,... | collective-permute-start | bytes 786440 | tf_op jit(solution)/shard_map/ppermute | solution.py:20
  83.4 3.5 %collective-permute-start.19 = (f32[384,1024]{1,0:T(8,128)S(1)}, f32[384,1024]{1,0:T(8,128)S(1)}, u32[]{:S(2)}, u32[]{:S(2)}) collective-permute-start(f32[384,1024]{1,0:T(8,128)S(1)} %pack_a.1), channel_id=1, source_target_pairs={{0,1},{1,0},{2,3},{3,2},{4,5},{5,4},{6,7},{7,6},{8,9},{9,8},{10,11... | collective-permute-start | bytes 4718600 | tf_op jit(solution)/shard_map/ppermute | solution.py:20
  83.5 8.7 %collective-permute-start.20 = (f32[64,1024]{1,0:T(8,128)S(1)}, f32[64,1024]{1,0:T(8,128)S(1)}, u32[]{:S(2)}, u32[]{:S(2)}) collective-permute-start(f32[64,1024]{1,0:T(8,128)S(1)} %collective-permute-done.12.refs_2_), channel_id=1, source_target_pairs={{0,2},{1,3},{2,0},{3,1},{4,6},{5,7},{6,4},{7,5},{8,10},{9,11},{10,... | collective-permute-start | bytes 786440 | tf_op jit(solution)/shard_map/ppermute | solution.py:20
  84.0 8.4 %collective-permute-start.21 = (f32[64,1024]{1,0:T(8,128)S(1)}, f32[64,1024]{1,0:T(8,128)S(1)}, u32[]{:S(2)}, u32[]{:S(2)}) collective-permute-start(f32[64,1024]{1,0:T(8,128)S(1)} %get-tuple-element.174), channel_id=1, source_target_pairs={{0,4},{4,0},{8,12},{12,8},{16,20},{20,16},{24,28},{28,24},{1,5},{5... | collective-permute-start | bytes 786440 | tf_op jit(solution)/shard_map/ppermute | solution.py:20
  92.4 24.5 %collective-permute-start.22 = (f32[256,1024]{1,0:T(8,128)S(1)}, f32[256,1024]{1,0:T(8,128)S(1)}, u32[]{:S(2)}, u32[]{:S(2)}) collective-permute-start(f32[256,1024]{1,0:T(8,128)S(1)} %out_grad.2), channel_id=1, source_target_pairs={{0,8},{4,12},{8,0},{12,4},{16,24},{20,28},{24,16},{28,20},{1,9},{5... | collective-permute-start | bytes 3145736 | tf_op jit(solution)/shard_map/ppermute | solution.py:20
  92.4 7.7 %collective-permute-start.23 = (f32[64,1024]{1,0:T(8,128)S(1)}, f32[64,1024]{1,0:T(8,128)S(1)}, u32[]{:S(2)}, u32[]{:S(2)}) collective-permute-start(f32[64,1024]{1,0:T(8,128)S(1)} %get-tuple-element.179), channel_id=1, source_target_pairs={{0,4},{4,0},{8,12},{12,8},{16,20},{20,16},{24,28},{28,24},{1,5},{5... | collective-permute-start | bytes 786440 | tf_op jit(solution)/shard_map/ppermute | solution.py:20
  93.5 7.4 %collective-permute-start.24 = (f32[64,1024]{1,0:T(8,128)S(1)}, f32[64,1024]{1,0:T(8,128)S(1)}, u32[]{:S(2)}, u32[]{:S(2)}) collective-permute-start(f32[64,1024]{1,0:T(8,128)S(1)} %collective-permute-done.16.refs_4_), channel_id=1, source_target_pairs={{0,2},{1,3},{2,0},{3,1},{4,6},{5,7},{6,4},{7,5},{8,10},{9,11},{10,... | collective-permute-start | bytes 786440 | tf_op jit(solution)/shard_map/ppermute | solution.py:20
  95.0 5.9 %collective-permute-start.26 = (f32[64,1024]{1,0:T(8,128)S(1)}, f32[64,1024]{1,0:T(8,128)S(1)}, u32[]{:S(2)}, u32[]{:S(2)}) collective-permute-start(f32[64,1024]{1,0:T(8,128)S(1)} %collective-permute-done.12.refs_2_), channel_id=1, source_target_pairs={{0,1},{1,0},{2,3},{3,2},{4,5},{5,4},{6,7},{7,6},{8,9},{9,8},{10,11... | collective-permute-start | bytes 786440 | tf_op jit(solution)/shard_map/ppermute | solution.py:20
  95.0 5.9 %collective-permute-start.25 = (f32[64,1024]{1,0:T(8,128)S(1)}, f32[64,1024]{1,0:T(8,128)S(1)}, u32[]{:S(2)}, u32[]{:S(2)}) collective-permute-start(f32[64,1024]{1,0:T(8,128)S(1)} %collective-permute-done.21.refs_0_), channel_id=1, source_target_pairs={{0,1},{1,0},{2,3},{3,2},{4,5},{5,4},{6,7},{7,6},{8,9},{9,8},{10,11... | collective-permute-start | bytes 786440 | tf_op jit(solution)/shard_map/ppermute | solution.py:20
  100.8 1.9 %collective-permute-start.28 = (f32[64,1024]{1,0:T(8,128)S(1)}, f32[64,1024]{1,0:T(8,128)S(1)}, u32[]{:S(2)}, u32[]{:S(2)}) collective-permute-start(f32[64,1024]{1,0:T(8,128)S(1)} %collective-permute-done.20.refs_3_), channel_id=1, source_target_pairs={{0,1},{1,0},{2,3},{3,2},{4,5},{5,4},{6,7},{7,6},{8,9},{9,8},{10,11... | collective-permute-start | bytes 786440 | tf_op jit(solution)/shard_map/ppermute | solution.py:20
  101.4 2.1 %collective-permute-start.30 = (f32[64,1024]{1,0:T(8,128)S(1)}, f32[64,1024]{1,0:T(8,128)S(1)}, u32[]{:S(2)}, u32[]{:S(2)}) collective-permute-start(f32[64,1024]{1,0:T(8,128)S(1)} %collective-permute-done.24.refs_5_), channel_id=1, source_target_pairs={{0,1},{1,0},{2,3},{3,2},{4,5},{5,4},{6,7},{7,6},{8,9},{9,8},{10,11... | collective-permute-start | bytes 786440 | tf_op jit(solution)/shard_map/ppermute | solution.py:20
  116.9 2.7 %collective-permute-start.32 = (f32[2,256,512]{2,1,0:T(8,128)S(1)}, f32[2,256,512]{2,1,0:T(8,128)S(1)}, u32[]{:S(2)}, u32[]{:S(2)}) collective-permute-start(f32[2,256,512]{2,1,0:T(8,128)S(1)} %get-tuple-element.212), channel_id=1, source_target_pairs={{0,1},{1,0},{2,3},{3,2},{4,5},{5,4},{6,7},{7,6},{8,9},{9,8},{10,11... | collective-permute-start | bytes 3145736 | tf_op jit(solution)/shard_map/ppermute | solution.py:20
  116.9 26.3 %collective-permute-start.31 = (f32[264,1024]{1,0:T(8,128)S(1)}, f32[264,1024]{1,0:T(8,128)S(1)}, u32[]{:S(2)}, u32[]{:S(2)}) collective-permute-start(f32[264,1024]{1,0:T(8,128)S(1)} %in_grad.2), channel_id=1, source_target_pairs={{0,8},{4,12},{8,0},{12,4},{16,24},{20,28},{24,16},{28,20},{1,9},{5... | collective-permute-start | bytes 3244040 | tf_op jit(solution)/shard_map/ppermute | solution.py:20
  119.9 14.0 %collective-permute-start.33 = (f32[256,512]{1,0:T(8,128)S(1)}, f32[256,512]{1,0:T(8,128)S(1)}, u32[]{:S(2)}, u32[]{:S(2)}) collective-permute-start(f32[256,512]{1,0:T(8,128)S(1)} %slice_bitcast_fusion), channel_id=1, source_target_pairs={{0,2},{1,3},{2,0},{3,1},{4,6},{5,7},{6,4},{7,5},{8,10},{9,11},{10,... | collective-permute-start | bytes 1572872 | tf_op jit(solution)/shard_map/ppermute | solution.py:20
  (11 other events, 48.4 us)

commit v7 on v6

--- a/solution.py
+++ b/solution.py
@@ -75,7 +75,7 @@
     quarter_ref[...] = full[pl.ds(pl.multiple_of(idx_ref[LANE] * quarter, quarter), quarter), :]
 
 
-def prep_cotangent_kernel(idx_ref, x_ref, p_ref, own_a_ref, first_a_ref, first_b_ref, second_a_ref, second_b_ref, away_a_ref, away_b_ref, full):
+def prep_cotangent_kernel(idx_ref, x_ref, p_ref, own_a_ref, first_a_ref, second_a_ref, half_b_ref, away_a_ref, away_b_ref, full):
     ordered_rows(x_ref, p_ref, full)
     quarter, width = first_a_ref.shape
     cols = [pl.ds(pl.multiple_of(idx_ref[SIDES + k] * width, width), width) for k in range(2)]
@@ -84,9 +84,8 @@
     away = pl.ds(pl.multiple_of(idx_ref[LANE] * quarter, quarter), quarter)
     own_a_ref[...] = full[:, cols[0]].astype(BF16)
     first_a_ref[...] = full[first, cols[0]]
-    first_b_ref[...] = full[first, cols[1]]
     second_a_ref[...] = full[second, cols[0]]
-    second_b_ref[...] = full[second, cols[1]]
+    half_b_ref[...] = full[pl.ds(pl.multiple_of(idx_ref[CORE] * 2 * quarter, quarter), 2 * quarter), cols[1]]
     away_a_ref[...] = full[away, cols[1]]
     away_b_ref[...] = full[away, cols[0]]
 
@@ -448,9 +447,9 @@
     near_x = line.send(x_half, "tm", 1)
     away_x = line.send(x_quarter, "tm", far)
     part = ((quarter, depth // 2), F32)
-    c_own, own_a, c_first_a, c_first_b, c_second_a, c_second_b, c_quarter_a, c_quarter_b = prep(
+    c_own, own_a, c_first_a, c_second_a, c_half_b, c_quarter_a, c_quarter_b = prep(
         prep_cotangent_kernel, idx, line.behind(cotangent),
-        [((rows, depth // 2), BF16), part, part, part, part, part, part], "prep_cotangent",
+        [((rows, depth // 2), BF16), part, part, ((half, depth // 2), F32), part, part], "prep_cotangent",
     )
     table = resident(
         functools.partial(summary_kernel, scaling=scaling), jax.ShapeDtypeStruct((1, 4, channels), F32),
@@ -496,8 +495,9 @@
     starts, lows = starts + more, lows + more_low
     corner_side_a, side_a, corner_b, near_a2, lows[1] = line.step(corner_side_a, side_a, corner_b, near_a2, lows[1])
 
-    side_b = line.send(away_b, "chan", 2)
-    near_b1 = line.send(c_first_b, "tm", 1)
+    far_b = pack([line.behind(away_b), corner_b], "pack_b")
+    side_b = line.send(far_b, "chan", 2)
+    near_b = line.send(c_half_b, "tm", 1)
     other_a = line.send(pack([near_a1, near_a2, away_a, side_a, corner_a, corner_side_a], "pack_a"), "chan", 1)
     ca = [own_a] + collected(idx, [
         (near_a1, [(0, 6, quarter)]), (near_a2, [(0, 7, quarter)]),
@@ -509,24 +509,17 @@
         return [grad_rows(idx, first + k, features, values, rows_out, factor, name, sums) for k in range(1, groups)]
 
     out_given = shares(ROWS + groups, ca, lows, scaling, "out_grad")
-    out_given[0], side_b, near_b1 = line.step(out_given[0], side_b, near_b1)
+    out_given[0] = line.step(out_given[0])
 
     out_got = [line.send(part, "tm", 2 * (k + 1)) for k, part in enumerate(out_given)]
-    near_b2 = line.send(c_second_b, "tm", 1)
-    corner_side_b = line.send(corner_b, "chan", 2)
-    near_b1_other = line.send(near_b1, "chan", 1)
-    away_b_other = line.send(away_b, "chan", 1)
-    near_b2, corner_side_b, near_b1_other, away_b_other = line.step(near_b2, corner_side_b, near_b1_other, away_b_other)
-
-    near_b2_other = line.send(near_b2, "chan", 1)
+    near_b, side_b = line.step(near_b, side_b)
+
+    near_b_other = line.send(near_b, "chan", 1)
+    far_b_other = line.send(far_b, "chan", 1)
     side_b_other = line.send(side_b, "chan", 1)
-    corner_b_other = line.send(corner_b, "chan", 1)
-    last_b = line.send(corner_side_b, "chan", 1)
     cb = collected(idx, [
-        (near_b1, [(0, 6, quarter)]), (near_b2, [(0, 7, quarter)]),
-        (away_b, mine_1), (side_b, mine_2), (corner_b, mine_3), (corner_side_b, mine_4),
-        (near_b1_other, [(0, 8, quarter)]), (near_b2_other, [(0, 9, quarter)]),
-        (away_b_other, their_1), (side_b_other, their_2), (corner_b_other, their_3), (last_b, their_4),
+        (near_b, mine_near), (far_b, mine_1 + mine_3), (side_b, mine_2 + mine_4),
+        (near_b_other, their_near), (far_b_other, their_1 + their_3), (side_b_other, their_2 + their_4),
     ], "collect_b")
     cs = [list(pair) for pair in zip(ca[1:], cb, strict=True)]
     more, more_grads = backward_call(idx, 1, cs, backward, starts[1:], lows[1:], scaling, "backward_group")

time: 145 us -> 143 us (0.986)
  starting transfers between devices: 29.5 us -> 25.1 us
  waiting for transfers between devices: 71 us -> 72.9 us
    ppermute x34 -> x29, starting transfers between devices: 29.5 us -> 25.1 us  [swap(): return lax.ppermute(x, axis, [(k, k ^ bit) for k in range(n)])]
    ppermute x34 -> x29, waiting for transfers between devices: 71 us -> 72.9 us  [swap(): return lax.ppermute(x, axis, [(k, k ^ bit) for k in range(n)])]
    pallas_call x18 -> x19, Pallas kernels: 33.8 us -> 33.8 us  [resident(): pl.pallas_call(kernel, out_shape=out_shape, in_specs=[SMEM] * scalars + [...]
  transfers between devices with their start and end apart: 34 -> 29, of which waited for: 20 -> 18; matrix products, arithmetic and copies ran while one was open for 1% -> 2% of each run, Pallas kernels for 22% -> 23%
where the time goes in v7:
time: 143 us; the launch traced here: 142 us
  waiting for transfers between devices  72.9 us (51%)
  Pallas kernels  33.8 us (24%)
  starting transfers between devices  25.1 us (18%)
  local copies, waits for them, and re-layouts  5.76 us (4%)
  other arithmetic  3.89 us (3%)
    ppermute x29, waiting for transfers between devices, swap(): return lax.ppermute(x, axis, [(k, k ^ bit) for k in range(n)])  72.9 us
    pallas_call x19, Pallas kernels, resident(): pl.pallas_call(kernel, out_shape=out_shape, in_specs=[SMEM] * scalars + [...  33.8 us
    ppermute x29, starting transfers between devices, swap(): return lax.ppermute(x, axis, [(k, k ^ bit) for k in range(n)])  25.1 us
    unnamed x18, local copies, waits for them, and re-layouts  5.62 us
  transfers between devices with their start and end apart: 29, of which 18 were waited for; matrix products, arithmetic and copies ran while one was open for 2% of the time, Pallas kernels for 23%

profile of v7, /device:TPU:0, one launch (start us, length us, event | category | flops | bytes accessed | tf_op | source)
XLA Modules:
  0.0 142.5 jit_solution(1264396357016096087)
XLA Ops:
  3.1 3.0 %collective-permute-start = (f32[128,2048]{1,0:T(8,128)S(1)}, f32[128,2048]{1,0:T(8,128)S(1)}, u32[]{:S(2)}, u32[]{:S(2)}) collective-permute-start(f32[128,2048]{1,0:T(8,128)S(1)} %get-tuple-element.108), channel_id=1, source_target_pairs={{0,4},{4,0},{8,12},{12,8},{16,20},{20,16},{24,28},{28,24},{1,5},{5... | collective-permute-start | bytes 3145736 | tf_op jit(solution)/shard_map/ppermute | solution.py:20
  6.1 2.6 %collective-permute-start.1 = (f32[64,2048]{1,0:T(8,128)S(1)}, f32[64,2048]{1,0:T(8,128)S(1)}, u32[]{:S(2)}, u32[]{:S(2)}) collective-permute-start(f32[64,2048]{1,0:T(8,128)S(1)} %get-tuple-element.110), channel_id=1, source_target_pairs={{0,16},{4,20},{8,24},{12,28},{16,0},{20,4},{24,8},{28,12},{1,17},{... | collective-permute-start | bytes 1572872 | tf_op jit(solution)/shard_map/ppermute | solution.py:20
  9.9 2.2 %copy-done = bf16[2048,1024]{1,0:T(8,128)(2,1)S(1)} copy-done((bf16[2048,1024]{1,0:T(8,128)(2,1)S(1)}, bf16[2048,1024]{1,0:T(8,128)(2,1)}, u32[]{:S(2)}) %copy-start) | copy-done | bytes 4194328
  12.1 2.2 %copy-done.2 = bf16[1024,2048]{1,0:T(8,128)(2,1)S(1)} copy-done((bf16[1024,2048]{1,0:T(8,128)(2,1)S(1)}, bf16[1024,2048]{1,0:T(8,128)(2,1)}, u32[]{:S(2)}) %copy-start.2) | copy-done | bytes 4194328
  14.3 3.0 %summary.1 = f32[1,4,1024]{2,1,0:T(4,128)S(1)} custom-call(bf16[256,2048]{1,0:T(8,128)(2,1)S(1)} %get-tuple-element.190.x_ref.refs_0_, bf16[256,2048]{1,0:T(8,128)(2,1)S(1)} %get-tuple-element.111.c_ref.refs_0_, bf16[2048,1024]{1,0:T(8,128)(2,1)S(1)} %copy-done, bf16[1024,2048]{1,0:T(8,128)(2,1)S(1)} %copy-done.2, f32[1,1024]{1,0:T(1,128)S(1)} %bitcast.31, ...), custom_call_target="tpu_custom_call" | custom-call | tf_op jit(solution)/shard_map/summary/pallas_call | solution.py:54
  17.8 2.5 %collective-permute-start.3 = (f32[1,4,1024]{2,1,0:T(4,128)S(1)}, f32[1,4,1024]{2,1,0:T(4,128)S(1)}, u32[]{:S(2)}, u32[]{:S(2)}) collective-permute-start(f32[1,4,1024]{2,1,0:T(4,128)S(1)} %summary.1), channel_id=1, source_target_pairs={{0,12},{4,8},{8,4},{12,0},{16,28},{20,24},{24,20},{28,16},{1,13},{... | collective-permute-start | bytes 49160 | tf_op jit(solution)/shard_map/ppermute | solution.py:20
  20.8 9.1 %collective-permute-done.4 = f32[1,4,1024]{2,1,0:T(4,128)S(1)} collective-permute-done((f32[1,4,1024]{2,1,0:T(4,128)S(1)}, f32[1,4,1024]{2,1,0:T(4,128)S(1)}, u32[]{:S(2)}, u32[]{:S(2)}) %collective-permute-start.4) | collective-permute-done | bytes 16416 | tf_op jit(solution)/shard_map/ppermute | solution.py:20
  29.8 2.0 %collective-permute-done.3 = f32[1,4,1024]{2,1,0:T(4,128)S(1)} collective-permute-done((f32[1,4,1024]{2,1,0:T(4,128)S(1)}, f32[1,4,1024]{2,1,0:T(4,128)S(1)}, u32[]{:S(2)}, u32[]{:S(2)}) %collective-permute-start.3) | collective-permute-done | bytes 16416 | tf_op jit(solution)/shard_map/ppermute | solution.py:20
  32.1 1.6 %collective-permute-start.6 = (f32[64,2048]{1,0:T(8,128)S(1)}, f32[64,2048]{1,0:T(8,128)S(1)}, u32[]{:S(2)}, u32[]{:S(2)}) collective-permute-start(f32[64,2048]{1,0:T(8,128)S(1)} %collective-permute-done.1.refs_1_), channel_id=1, source_target_pairs={{0,2},{1,3},{2,0},{3,1},{4,6},{5,7},{6,4},{7,5},{8,10},{9,11},{10,... | collective-permute-start | bytes 1572872 | tf_op jit(solution)/shard_map/ppermute | solution.py:20
  33.7 1.3 collective-permute-start.5
  36.0 2.1 %collective-permute-start.8 = (f32[4,4,1024]{2,1,0:T(4,128)S(1)}, f32[4,4,1024]{2,1,0:T(4,128)S(1)}, u32[]{:S(2)}, u32[]{:S(2)}) collective-permute-start(f32[4,4,1024]{2,1,0:T(4,128)S(1)} %pad_maximum_fusion.1), channel_id=1, source_target_pairs={{0,20},{4,16},{8,28},{12,24},{16,4},{20,0},{24,12},{28,8},{1,21},{... | collective-permute-start | bytes 196616 | tf_op jit(solution)/shard_map/ppermute | solution.py:20
  38.1 12.5 %collective-permute-done.8 = f32[4,4,1024]{2,1,0:T(4,128)S(1)} collective-permute-done((f32[4,4,1024]{2,1,0:T(4,128)S(1)}, f32[4,4,1024]{2,1,0:T(4,128)S(1)}, u32[]{:S(2)}, u32[]{:S(2)}) %collective-permute-start.8) | collective-permute-done | bytes 65568 | tf_op jit(solution)/shard_map/ppermute | solution.py:20
  52.9 1.6 %collective-permute-start.10 = (f32[64,1024]{1,0:T(8,128)S(1)}, f32[64,1024]{1,0:T(8,128)S(1)}, u32[]{:S(2)}, u32[]{:S(2)}) collective-permute-start(f32[64,1024]{1,0:T(8,128)S(1)} %collective-permute-done.7.refs_2_), channel_id=1, source_target_pairs={{0,4},{4,0},{8,12},{12,8},{16,20},{20,16},{24,28},{28,24},{1,5},{5... | collective-permute-start | bytes 786440 | tf_op jit(solution)/shard_map/ppermute | solution.py:20
  54.5 2.2 %forward_own.1 = (f32[8,1024]{1,0:T(8,128)S(1)}, bf16[256,1024]{1,0:T(8,128)(2,1)S(1)}) custom-call(s32[23]{0:T(128)S(1)} %stack.83.idx_ref, bf16[256,2048]{1,0:T(8,128)(2,1)S(1)} %get-tuple-element.190.x_ref.refs_0_, bf16[2048,1024]{1,0:T(8,128)(2,1)S(1)} %copy-done.1, f32[1,1024]{1,0:T(1,128)S(1)} %bitcast.32, f32[1,1024]{1,0:T(1,128)S(1)} %bitcast.37, ...), custom_call_target="tpu_custom_call" | custom-call | tf_op jit(solution)/shard_map/forward_own/pallas_call | solution.py:54
  56.7 2.5 %backward_own.1 = (bf16[256,1024]{1,0:T(8,128)(2,1)S(1)}, f32[1,1024]{1,0:T(1,128)S(1)}) custom-call(s32[23]{0:T(128)S(1)} %stack.83.idx_ref, bf16[256,2048]{1,0:T(8,128)(2,1)S(1)} %get-tuple-element.111.c_ref.refs_0_, bf16[1024,2048]{1,0:T(8,128)(2,1)S(1)} %copy-done.3, f32[1,1024]{1,0:T(1,128)S(1)} %bitcast.33, f32[1,1024]{1,0:T(1,128)S(1)} %bitcast.38, ...), custom_call_target="tpu_custom_call" | custom-call | tf_op jit(solution)/shard_map/backward_own/pallas_call | solution.py:54
  59.2 1.9 %row_grad.1 = (f32[2,256,512]{2,1,0:T(8,128)S(1)}, f32[2,256,512]{2,1,0:T(8,128)S(1)}) custom-call(s32[23]{0:T(128)S(1)} %stack.83.idx_ref, bf16[256,1024]{1,0:T(8,128)(2,1)S(1)} %get-tuple-element.134.a_ref.refs_4_, bf16[2048,1024]{1,0:T(8,128)(2,1)S(1)} %copy-done.1), custom_call_target="tpu_custom_call" | custom-call | tf_op jit(solution)/shard_map/row_grad/pallas_call | solution.py:54
  61.6 5.9 %collective-permute-done.12.refs_0_ = f32[64,1024]{1,0:T(8,128)S(1)} collective-permute-done((f32[64,1024]{1,0:T(8,128)S(1)}, f32[64,1024]{1,0:T(8,128)S(1)}, u32[]{:S(2)}, u32[]{:S(2)}) %collective-permute-start.12) | collective-permute-done | bytes 262176 | tf_op jit(solution)/shard_map/ppermute | solution.py:20
  67.6 1.6 %collective-permute-start.15 = (f32[64,1024]{1,0:T(8,128)S(1)}, f32[64,1024]{1,0:T(8,128)S(1)}, u32[]{:S(2)}, u32[]{:S(2)}) collective-permute-start(f32[64,1024]{1,0:T(8,128)S(1)} %collective-permute-done.7.refs_2_), channel_id=1, source_target_pairs={{0,2},{1,3},{2,0},{3,1},{4,6},{5,7},{6,4},{7,5},{8,10},{9,11},{10,... | collective-permute-start | bytes 786440 | tf_op jit(solution)/shard_map/ppermute | solution.py:20
  71.7 1.4 collect_x.1
  73.1 5.6 %forward_group.1 = (f32[8,1024]{1,0:T(8,128)S(1)}, bf16[256,1024]{1,0:T(8,128)(2,1)S(1)}, f32[8,1024]{1,0:T(8,128)S(1)}, bf16[256,1024]{1,0:T(8,128)(2,1)S(1)}, ...) custom-call(s32[23]{0:T(128)S(1)} %stack.83.idx_ref, bf16[256,2048]{1,0:T(8,128)(2,1)S(1)} %get-tuple-element.149.refs_0_.refs_1_, ...), custom_call_target="tpu_custom_call" | custom-call | tf_op jit(solution)/shard_map/forward_group/pallas_call | solution.py:54
  78.8 3.2 %collective-permute-done.14.refs_5_ = f32[64,1024]{1,0:T(8,128)S(1)} collective-permute-done((f32[64,1024]{1,0:T(8,128)S(1)}, f32[64,1024]{1,0:T(8,128)S(1)}, u32[]{:S(2)}, u32[]{:S(2)}) %collective-permute-start.14) | collective-permute-done | bytes 262176 | tf_op jit(solution)/shard_map/ppermute | solution.py:20
  85.1 1.8 %collective-permute-done.19.refs_6_ = f32[384,1024]{1,0:T(8,128)S(1)} collective-permute-done((f32[384,1024]{1,0:T(8,128)S(1)}, f32[384,1024]{1,0:T(8,128)S(1)}, u32[]{:S(2)}, u32[]{:S(2)}) %collective-permute-start.19) | collective-permute-done | bytes 1572896 | tf_op jit(solution)/shard_map/ppermute | solution.py:20
  87.9 1.3 out_grad.2
  89.3 8.7 %collective-permute-done.21.refs_0_ = f32[128,1024]{1,0:T(8,128)S(1)} collective-permute-done((f32[128,1024]{1,0:T(8,128)S(1)}, f32[128,1024]{1,0:T(8,128)S(1)}, u32[]{:S(2)}, u32[]{:S(2)}) %collective-permute-start.21) | collective-permute-done | bytes 524320 | tf_op jit(solution)/shard_map/ppermute | solution.py:20
  99.2 1.4 collective-permute-done.23.refs_3_
  103.3 6.4 %backward_group.1 = (bf16[256,1024]{1,0:T(8,128)(2,1)S(1)}, f32[1,1024]{1,0:T(1,128)S(1)}, bf16[256,1024]{1,0:T(8,128)(2,1)S(1)}, f32[1,1024]{1,0:T(1,128)S(1)},...) custom-call(s32[23]{0:T(128)S(1)} %stack.83.idx_ref, bf16[256,1024]{1,0:T(8,128)(2,1)S(1)} %get-tuple-element.157.refs_1_.refs_0_, ...), custom_call_target="tpu_custom_call" | custom-call | tf_op jit(solution)/shard_map/backward_group/pallas_call | solution.py:54
  109.7 1.3 in_grad.2
  111.0 3.5 %collective-permute-done.20 = f32[256,1024]{1,0:T(8,128)S(1)} collective-permute-done((f32[256,1024]{1,0:T(8,128)S(1)}, f32[256,1024]{1,0:T(8,128)S(1)}, u32[]{:S(2)}, u32[]{:S(2)}) %collective-permute-start.20) | collective-permute-done | bytes 1048608 | tf_op jit(solution)/shard_map/ppermute | solution.py:20
  114.8 2.4 %collective-permute-done.27 = f32[2,256,512]{2,1,0:T(8,128)S(1)} collective-permute-done((f32[2,256,512]{2,1,0:T(8,128)S(1)}, f32[2,256,512]{2,1,0:T(8,128)S(1)}, u32[]{:S(2)}, u32[]{:S(2)}) %collective-permute-start.27) | collective-permute-done | bytes 1048608 | tf_op jit(solution)/shard_map/ppermute | solution.py:20
  120.3 1.3 in_grad.3
  121.6 9.8 %collective-permute-done.28 = f32[256,512]{1,0:T(8,128)S(1)} collective-permute-done((f32[256,512]{1,0:T(8,128)S(1)}, f32[256,512]{1,0:T(8,128)S(1)}, u32[]{:S(2)}, u32[]{:S(2)}) %collective-permute-start.28) | collective-permute-done | bytes 524320 | tf_op jit(solution)/shard_map/ppermute | solution.py:20
  132.2 8.6 %collective-permute-done.26 = f32[264,1024]{1,0:T(8,128)S(1)} collective-permute-done((f32[264,1024]{1,0:T(8,128)S(1)}, f32[264,1024]{1,0:T(8,128)S(1)}, u32[]{:S(2)}, u32[]{:S(2)}) %collective-permute-start.26) | collective-permute-done | bytes 1081376 | tf_op jit(solution)/shard_map/ppermute | solution.py:20
  (72 shorter events, 25.3 us)
Async XLA Ops:
  0.7 9.2 %copy-start.6 = (f32[1024]{0:T(1024)S(1)}, f32[1024]{0:T(1024)}, u32[]{:S(2)}) copy-start(f32[1024]{0:T(1024)} %param.12) | copy-start | bytes 12292
  0.7 9.2 %copy-start.7 = (f32[1024]{0:T(1024)S(1)}, f32[1024]{0:T(1024)}, u32[]{:S(2)}) copy-start(f32[1024]{0:T(1024)} %param.11) | copy-start | bytes 12292
  0.7 9.2 %copy-start.8 = (f32[256]{0:T(256)S(1)}, f32[256]{0:T(256)}, u32[]{:S(2)}) copy-start(f32[256]{0:T(256)} %param.13) | copy-start | bytes 3076
  3.1 29.0 %collective-permute-start = (f32[128,2048]{1,0:T(8,128)S(1)}, f32[128,2048]{1,0:T(8,128)S(1)}, u32[]{:S(2)}, u32[]{:S(2)}) collective-permute-start(f32[128,2048]{1,0:T(8,128)S(1)} %get-tuple-element.108), channel_id=1, source_target_pairs={{0,4},{4,0},{8,12},{12,8},{16,20},{20,16},{24,28},{28,24},{1,5},{5... | collective-permute-start | bytes 3145736 | tf_op jit(solution)/shard_map/ppermute | solution.py:20
  6.1 26.0 %collective-permute-start.1 = (f32[64,2048]{1,0:T(8,128)S(1)}, f32[64,2048]{1,0:T(8,128)S(1)}, u32[]{:S(2)}, u32[]{:S(2)}) collective-permute-start(f32[64,2048]{1,0:T(8,128)S(1)} %get-tuple-element.110), channel_id=1, source_target_pairs={{0,16},{4,20},{8,24},{12,28},{16,0},{20,4},{24,8},{28,12},{1,17},{... | collective-permute-start | bytes 1572872 | tf_op jit(solution)/shard_map/ppermute | solution.py:20
  17.2 12.6 %collective-permute-start.4 = (f32[1,4,1024]{2,1,0:T(4,128)S(1)}, f32[1,4,1024]{2,1,0:T(4,128)S(1)}, u32[]{:S(2)}, u32[]{:S(2)}) collective-permute-start(f32[1,4,1024]{2,1,0:T(4,128)S(1)} %summary.1), channel_id=1, source_target_pairs={{0,4},{4,0},{8,12},{12,8},{16,20},{20,16},{24,28},{28,24},{1,5},{5... | collective-permute-start | bytes 49160 | tf_op jit(solution)/shard_map/ppermute | solution.py:20
  17.8 14.0 %collective-permute-start.3 = (f32[1,4,1024]{2,1,0:T(4,128)S(1)}, f32[1,4,1024]{2,1,0:T(4,128)S(1)}, u32[]{:S(2)}, u32[]{:S(2)}) collective-permute-start(f32[1,4,1024]{2,1,0:T(4,128)S(1)} %summary.1), channel_id=1, source_target_pairs={{0,12},{4,8},{8,4},{12,0},{16,28},{20,24},{24,20},{28,16},{1,13},{... | collective-permute-start | bytes 49160 | tf_op jit(solution)/shard_map/ppermute | solution.py:20
  20.3 11.8 %collective-permute-start.2 = (f32[1,4,1024]{2,1,0:T(4,128)S(1)}, f32[1,4,1024]{2,1,0:T(4,128)S(1)}, u32[]{:S(2)}, u32[]{:S(2)}) collective-permute-start(f32[1,4,1024]{2,1,0:T(4,128)S(1)} %summary.1), channel_id=1, source_target_pairs={{0,8},{4,12},{8,0},{12,4},{16,24},{20,28},{24,16},{28,20},{1,9},{5... | collective-permute-start | bytes 49160 | tf_op jit(solution)/shard_map/ppermute | solution.py:20
  32.1 19.4 %collective-permute-start.6 = (f32[64,2048]{1,0:T(8,128)S(1)}, f32[64,2048]{1,0:T(8,128)S(1)}, u32[]{:S(2)}, u32[]{:S(2)}) collective-permute-start(f32[64,2048]{1,0:T(8,128)S(1)} %collective-permute-done.1.refs_1_), channel_id=1, source_target_pairs={{0,2},{1,3},{2,0},{3,1},{4,6},{5,7},{6,4},{7,5},{8,10},{9,11},{10,... | collective-permute-start | bytes 1572872 | tf_op jit(solution)/shard_map/ppermute | solution.py:20
  33.7 17.8 %collective-permute-start.5 = (f32[64,2048]{1,0:T(8,128)S(1)}, f32[64,2048]{1,0:T(8,128)S(1)}, u32[]{:S(2)}, u32[]{:S(2)}) collective-permute-start(f32[64,2048]{1,0:T(8,128)S(1)} %collective-permute-done.1.refs_1_), channel_id=1, source_target_pairs={{0,4},{4,0},{8,12},{12,8},{16,20},{20,16},{24,28},{28,24},{1,5},{5... | collective-permute-start | bytes 1572872 | tf_op jit(solution)/shard_map/ppermute | solution.py:20
  35.0 16.5 %collective-permute-start.7 = (f32[64,1024]{1,0:T(8,128)S(1)}, f32[64,1024]{1,0:T(8,128)S(1)}, u32[]{:S(2)}, u32[]{:S(2)}) collective-permute-start(f32[64,1024]{1,0:T(8,128)S(1)} %get-tuple-element.117), channel_id=1, source_target_pairs={{0,16},{4,20},{8,24},{12,28},{16,0},{20,4},{24,8},{28,12},{1,17},{... | collective-permute-start | bytes 786440 | tf_op jit(solution)/shard_map/ppermute | solution.py:20
  36.0 14.6 %collective-permute-start.8 = (f32[4,4,1024]{2,1,0:T(4,128)S(1)}, f32[4,4,1024]{2,1,0:T(4,128)S(1)}, u32[]{:S(2)}, u32[]{:S(2)}) collective-permute-start(f32[4,4,1024]{2,1,0:T(4,128)S(1)} %pad_maximum_fusion.1), channel_id=1, source_target_pairs={{0,20},{4,16},{8,28},{12,24},{16,4},{20,0},{24,12},{28,8},{1,21},{... | collective-permute-start | bytes 196616 | tf_op jit(solution)/shard_map/ppermute | solution.py:20
  51.8 15.8 %collective-permute-start.13 = (f32[320,2048]{1,0:T(8,128)S(1)}, f32[320,2048]{1,0:T(8,128)S(1)}, u32[]{:S(2)}, u32[]{:S(2)}) collective-permute-start(f32[320,2048]{1,0:T(8,128)S(1)} %pack_x.1), channel_id=1, source_target_pairs={{0,1},{1,0},{2,3},{3,2},{4,5},{5,4},{6,7},{7,6},{8,9},{9,8},{10,11... | collective-permute-start | bytes 7864328 | tf_op jit(solution)/shard_map/ppermute | solution.py:20
  51.8 15.7 %collective-permute-start.9 = (f32[64,2048]{1,0:T(8,128)S(1)}, f32[64,2048]{1,0:T(8,128)S(1)}, u32[]{:S(2)}, u32[]{:S(2)}) collective-permute-start(f32[64,2048]{1,0:T(8,128)S(1)} %collective-permute-done.5.refs_3_), channel_id=1, source_target_pairs={{0,2},{1,3},{2,0},{3,1},{4,6},{5,7},{6,4},{7,5},{8,10},{9,11},{10,... | collective-permute-start | bytes 1572872 | tf_op jit(solution)/shard_map/ppermute | solution.py:20
  52.4 9.2 %collective-permute-start.11 = (f32[64,1024]{1,0:T(8,128)S(1)}, f32[64,1024]{1,0:T(8,128)S(1)}, u32[]{:S(2)}, u32[]{:S(2)}) collective-permute-start(f32[64,1024]{1,0:T(8,128)S(1)} %get-tuple-element.126), channel_id=1, source_target_pairs={{0,4},{4,0},{8,12},{12,8},{16,20},{20,16},{24,28},{28,24},{1,5},{5... | collective-permute-start | bytes 786440 | tf_op jit(solution)/shard_map/ppermute | solution.py:20
  52.9 14.6 %collective-permute-start.12 = (f32[64,1024]{1,0:T(8,128)S(1)}, f32[64,1024]{1,0:T(8,128)S(1)}, u32[]{:S(2)}, u32[]{:S(2)}) collective-permute-start(f32[64,1024]{1,0:T(8,128)S(1)} %get-tuple-element.128), channel_id=1, source_target_pairs={{0,16},{4,20},{8,24},{12,28},{16,0},{20,4},{24,8},{28,12},{1,17},{... | collective-permute-start | bytes 786440 | tf_op jit(solution)/shard_map/ppermute | solution.py:20
  52.9 14.6 %collective-permute-start.10 = (f32[64,1024]{1,0:T(8,128)S(1)}, f32[64,1024]{1,0:T(8,128)S(1)}, u32[]{:S(2)}, u32[]{:S(2)}) collective-permute-start(f32[64,1024]{1,0:T(8,128)S(1)} %collective-permute-done.7.refs_2_), channel_id=1, source_target_pairs={{0,4},{4,0},{8,12},{12,8},{16,20},{20,16},{24,28},{28,24},{1,5},{5... | collective-permute-start | bytes 786440 | tf_op jit(solution)/shard_map/ppermute | solution.py:20
  67.5 4.2 %collective-permute-start.18 = (f32[64,2048]{1,0:T(8,128)S(1)}, f32[64,2048]{1,0:T(8,128)S(1)}, u32[]{:S(2)}, u32[]{:S(2)}) collective-permute-start(f32[64,2048]{1,0:T(8,128)S(1)} %collective-permute-done.9.refs_4_), channel_id=1, source_target_pairs={{0,1},{1,0},{2,3},{3,2},{4,5},{5,4},{6,7},{7,6},{8,9},{9,8},{10,11... | collective-permute-start | bytes 1572872 | tf_op jit(solution)/shard_map/ppermute | solution.py:20
  67.6 11.1 %collective-permute-start.15 = (f32[64,1024]{1,0:T(8,128)S(1)}, f32[64,1024]{1,0:T(8,128)S(1)}, u32[]{:S(2)}, u32[]{:S(2)}) collective-permute-start(f32[64,1024]{1,0:T(8,128)S(1)} %collective-permute-done.7.refs_2_), channel_id=1, source_target_pairs={{0,2},{1,3},{2,0},{3,1},{4,6},{5,7},{6,4},{7,5},{8,10},{9,11},{10,... | collective-permute-start | bytes 786440 | tf_op jit(solution)/shard_map/ppermute | solution.py:20
  69.2 9.5 %collective-permute-start.17 = (f32[64,1024]{1,0:T(8,128)S(1)}, f32[64,1024]{1,0:T(8,128)S(1)}, u32[]{:S(2)}, u32[]{:S(2)}) collective-permute-start(f32[64,1024]{1,0:T(8,128)S(1)} %get-tuple-element.146), channel_id=1, source_target_pairs={{0,4},{4,0},{8,12},{12,8},{16,20},{20,16},{24,28},{28,24},{1,5},{5... | collective-permute-start | bytes 786440 | tf_op jit(solution)/shard_map/ppermute | solution.py:20
  70.2 11.7 %collective-permute-start.14 = (f32[64,1024]{1,0:T(8,128)S(1)}, f32[64,1024]{1,0:T(8,128)S(1)}, u32[]{:S(2)}, u32[]{:S(2)}) collective-permute-start(f32[64,1024]{1,0:T(8,128)S(1)} %collective-permute-done.10.refs_4_), channel_id=1, source_target_pairs={{0,2},{1,3},{2,0},{3,1},{4,6},{5,7},{6,4},{7,5},{8,10},{9,11},{10,... | collective-permute-start | bytes 786440 | tf_op jit(solution)/shard_map/ppermute | solution.py:20
  70.8 12.5 %collective-permute-start.16 = (f32[64,1024]{1,0:T(8,128)S(1)}, f32[64,1024]{1,0:T(8,128)S(1)}, u32[]{:S(2)}, u32[]{:S(2)}) collective-permute-start(f32[64,1024]{1,0:T(8,128)S(1)} %collective-permute-done.12.refs_0_), channel_id=1, source_target_pairs={{0,4},{4,0},{8,12},{12,8},{16,20},{20,16},{24,28},{28,24},{1,5},{5... | collective-permute-start | bytes 786440 | tf_op jit(solution)/shard_map/ppermute | solution.py:20
  83.4 3.5 %collective-permute-start.19 = (f32[384,1024]{1,0:T(8,128)S(1)}, f32[384,1024]{1,0:T(8,128)S(1)}, u32[]{:S(2)}, u32[]{:S(2)}) collective-permute-start(f32[384,1024]{1,0:T(8,128)S(1)} %pack_a.1), channel_id=1, source_target_pairs={{0,1},{1,0},{2,3},{3,2},{4,5},{5,4},{6,7},{7,6},{8,9},{9,8},{10,11... | collective-permute-start | bytes 4718600 | tf_op jit(solution)/shard_map/ppermute | solution.py:20
  83.6 14.4 %collective-permute-start.21 = (f32[128,1024]{1,0:T(8,128)S(1)}, f32[128,1024]{1,0:T(8,128)S(1)}, u32[]{:S(2)}, u32[]{:S(2)}) collective-permute-start(f32[128,1024]{1,0:T(8,128)S(1)} %get-tuple-element.166), channel_id=1, source_target_pairs={{0,4},{4,0},{8,12},{12,8},{16,20},{20,16},{24,28},{28,24},{1,5},{5... | collective-permute-start | bytes 1572872 | tf_op jit(solution)/shard_map/ppermute | solution.py:20
  84.6 14.0 %collective-permute-start.22 = (f32[128,1024]{1,0:T(8,128)S(1)}, f32[128,1024]{1,0:T(8,128)S(1)}, u32[]{:S(2)}, u32[]{:S(2)}) collective-permute-start(f32[128,1024]{1,0:T(8,128)S(1)} %pack_b.1.refs_1_), channel_id=1, source_target_pairs={{0,2},{1,3},{2,0},{3,1},{4,6},{5,7},{6,4},{7,5},{8,10},{9,11},{10,... | collective-permute-start | bytes 1572872 | tf_op jit(solution)/shard_map/ppermute | solution.py:20
  89.2 25.3 %collective-permute-start.20 = (f32[256,1024]{1,0:T(8,128)S(1)}, f32[256,1024]{1,0:T(8,128)S(1)}, u32[]{:S(2)}, u32[]{:S(2)}) collective-permute-start(f32[256,1024]{1,0:T(8,128)S(1)} %out_grad.2), channel_id=1, source_target_pairs={{0,8},{4,12},{8,0},{12,4},{16,24},{20,28},{24,16},{28,20},{1,9},{5... | collective-permute-start | bytes 3145736 | tf_op jit(solution)/shard_map/ppermute | solution.py:20
  98.7 1.9 %collective-permute-start.23 = (f32[128,1024]{1,0:T(8,128)S(1)}, f32[128,1024]{1,0:T(8,128)S(1)}, u32[]{:S(2)}, u32[]{:S(2)}) collective-permute-start(f32[128,1024]{1,0:T(8,128)S(1)} %collective-permute-done.21.refs_0_), channel_id=1, source_target_pairs={{0,1},{1,0},{2,3},{3,2},{4,5},{5,4},{6,7},{7,6},{8,9},{9,8},{10,11... | collective-permute-start | bytes 1572872 | tf_op jit(solution)/shard_map/ppermute | solution.py:20
  98.7 2.7 %collective-permute-start.24 = (f32[128,1024]{1,0:T(8,128)S(1)}, f32[128,1024]{1,0:T(8,128)S(1)}, u32[]{:S(2)}, u32[]{:S(2)}) collective-permute-start(f32[128,1024]{1,0:T(8,128)S(1)} %pack_b.1.refs_1_), channel_id=1, source_target_pairs={{0,1},{1,0},{2,3},{3,2},{4,5},{5,4},{6,7},{7,6},{8,9},{9,8},{10,11... | collective-permute-start | bytes 1572872 | tf_op jit(solution)/shard_map/ppermute | solution.py:20
  99.2 2.9 %collective-permute-start.25 = (f32[128,1024]{1,0:T(8,128)S(1)}, f32[128,1024]{1,0:T(8,128)S(1)}, u32[]{:S(2)}, u32[]{:S(2)}) collective-permute-start(f32[128,1024]{1,0:T(8,128)S(1)} %collective-permute-done.22.refs_2_), channel_id=1, source_target_pairs={{0,1},{1,0},{2,3},{3,2},{4,5},{5,4},{6,7},{7,6},{8,9},{9,8},{10,11... | collective-permute-start | bytes 1572872 | tf_op jit(solution)/shard_map/ppermute | solution.py:20
  114.5 2.7 %collective-permute-start.27 = (f32[2,256,512]{2,1,0:T(8,128)S(1)}, f32[2,256,512]{2,1,0:T(8,128)S(1)}, u32[]{:S(2)}, u32[]{:S(2)}) collective-permute-start(f32[2,256,512]{2,1,0:T(8,128)S(1)} %get-tuple-element.194), channel_id=1, source_target_pairs={{0,1},{1,0},{2,3},{3,2},{4,5},{5,4},{6,7},{7,6},{8,9},{9,8},{10,11... | collective-permute-start | bytes 3145736 | tf_op jit(solution)/shard_map/ppermute | solution.py:20
  114.5 26.3 %collective-permute-start.26 = (f32[264,1024]{1,0:T(8,128)S(1)}, f32[264,1024]{1,0:T(8,128)S(1)}, u32[]{:S(2)}, u32[]{:S(2)}) collective-permute-start(f32[264,1024]{1,0:T(8,128)S(1)} %in_grad.2), channel_id=1, source_target_pairs={{0,8},{4,12},{8,0},{12,4},{16,24},{20,28},{24,16},{28,20},{1,9},{5... | collective-permute-start | bytes 3244040 | tf_op jit(solution)/shard_map/ppermute | solution.py:20
  117.4 14.0 %collective-permute-start.28 = (f32[256,512]{1,0:T(8,128)S(1)}, f32[256,512]{1,0:T(8,128)S(1)}, u32[]{:S(2)}, u32[]{:S(2)}) collective-permute-start(f32[256,512]{1,0:T(8,128)S(1)} %slice_bitcast_fusion), channel_id=1, source_target_pairs={{0,2},{1,3},{2,0},{3,1},{4,6},{5,7},{6,4},{7,5},{8,10},{9,11},{10,... | collective-permute-start | bytes 1572872 | tf_op jit(solution)/shard_map/ppermute | solution.py:20
  (6 other events, 17.5 us)

commit v8 on v7

--- a/solution.py
+++ b/solution.py
@@ -96,12 +96,12 @@
     return resident(kernel, (jax.ShapeDtypeStruct((rows, depth), BF16), *shapes), (idx, x), name, [pltpu.VMEM((rows, depth), F32)])
 
 
-def pack_kernel(*refs):
+def pack_kernel(*refs, spans):
     *pieces, out_ref, sems = refs
     copies, at = [], 0
-    for k, ref in enumerate(pieces):
-        copies.append(pltpu.make_async_copy(ref, out_ref.at[pl.ds(at, ref.shape[0]), :], sems.at[k]))
-        at += ref.shape[0]
+    for k, (ref, (start, rows)) in enumerate(zip(pieces, spans, strict=True)):
+        copies.append(pltpu.make_async_copy(ref.at[pl.ds(start, rows), :], out_ref.at[pl.ds(at, rows), :], sems.at[k]))
+        at += rows
     for copy in copies:
         copy.start()
     for copy in copies:
@@ -109,8 +109,11 @@
 
 
 def pack(pieces, name):
-    shape = jax.ShapeDtypeStruct((sum(p.shape[0] for p in pieces), pieces[0].shape[1]), F32)
-    return resident(pack_kernel, shape, tuple(pieces), name, [pltpu.SemaphoreType.DMA((len(pieces),))], scalars=0, anywhere=len(pieces))
+    pieces = [p if isinstance(p, tuple) else (p, 0, p.shape[0]) for p in pieces]
+    shape = jax.ShapeDtypeStruct((sum(p[2] for p in pieces), pieces[0][0].shape[1]), F32)
+    kernel = functools.partial(pack_kernel, spans=[p[1:] for p in pieces])
+    arrays = tuple(p[0] for p in pieces)
+    return resident(kernel, shape, arrays, name, [pltpu.SemaphoreType.DMA((len(pieces),))], scalars=0, anywhere=len(pieces))
 
 
 def lanes_of(l):
@@ -184,10 +187,7 @@
     rows = retain_ref.shape[0] // 4
 
     def row(away):
-        top = away // far
-        low = (away % 2) ^ top
-        middle = ((away // 2) % (far // 2)) ^ low
-        return sum_ref[middle + (far // 2) * low + far * top]
+        return sum_ref[(away % 2) * far + away // 2]
 
     for role, away in enumerate((0, 1, far, far + 1)):
         spread_rows(row(away)[3:4, :rows], retain_ref, role * rows)
@@ -209,7 +209,7 @@
 
 
 def reach(devices):
-    return [1 << k for k in range(1, devices.bit_length() - 2)] + [3, devices // 2 + 1]
+    return [1 << k for k in range(1, devices.bit_length() - 1)] + [1]
 
 
 def collect_kernel(idx_ref, *refs, layout):
@@ -457,7 +457,7 @@
         [pltpu.VMEM((rows, channels), F32)] * 2 + [pltpu.VMEM((rows, 128), F32)], scalars=0,
     )
     if groups == 2:
-        table = jnp.concatenate([table] + [line.send(table, "tm", bit) for bit in (2, 3, 1)])
+        table = jnp.concatenate([table] + [line.send(table, "tm", bit) for bit in (2, 4, 6)])
     else:
         for bit in reach(devices)[:-1]:
             table = jnp.concatenate([table, line.send(table, "tm", bit)])
@@ -470,8 +470,7 @@
     enter_fwd, enter_bwd, retain_wide = carries(idx, table, rows)
     corner_x, side_x, away_a, enter_fwd = line.step(corner_x, side_x, away_a, enter_fwd)
 
-    near_a1 = line.send(c_first_a, "tm", 1)
-    corner_a = line.send(away_a, "tm", 1)
+    mixed_a = line.send(pack([c_first_a, line.behind(away_a)], "pack_mixed"), "tm", 1)
     corner_side_x = line.send(corner_x, "chan", 2)
     away_b = line.send(c_quarter_b, "tm", far)
     forward = (in_proj, scale, decay_row, retain_wide, enter_fwd)
@@ -480,12 +479,11 @@
     scaled, grads = backward_call(idx, 0, [[c_own]], backward, starts, lows, scaling, "backward_own")
     keep, give = row_grad(idx, scaled[0], in_proj, lanes)
     other_x = line.send(pack([near_x, away_x, side_x, corner_x], "pack_x"), "chan", 1)
-    corner_side_x, corner_a, near_a1, away_b, give, other_x = line.step(corner_side_x, corner_a, near_a1, away_b, give, other_x)
-
-    corner_b = line.send(away_b, "tm", 1)
-    corner_side_a = line.send(corner_a, "chan", 2)
-    side_a = line.send(away_a, "chan", 2)
-    near_a2 = line.send(c_second_a, "tm", 1)
+    corner_side_x, mixed_a, away_b, give, other_x = line.step(corner_side_x, mixed_a, away_b, give, other_x)
+
+    mixed_b = line.send(pack([c_second_a, line.behind(away_b)], "pack_mixed"), "tm", 1)
+    far_a = pack([line.behind(away_a), (mixed_a, quarter, quarter)], "pack_far")
+    side_a = line.send(far_a, "chan", 2)
     last_x = line.send(corner_side_x, "chan", 1)
     xs = [x_own] + collected(idx, [
         (near_x, mine_near), (away_x, mine_1), (side_x, mine_2), (corner_x, mine_3), (corner_side_x, mine_4),
@@ -493,16 +491,17 @@
     ], "collect_x")
     more, more_low = forward_call(idx, 1, xs[1:], forward, "forward_group")
     starts, lows = starts + more, lows + more_low
-    corner_side_a, side_a, corner_b, near_a2, lows[1] = line.step(corner_side_a, side_a, corner_b, near_a2, lows[1])
-
-    far_b = pack([line.behind(away_b), corner_b], "pack_b")
+    side_a, mixed_b, lows[1] = line.step(side_a, mixed_b, lows[1])
+
+    far_b = pack([line.behind(away_b), (mixed_b, quarter, quarter)], "pack_far")
     side_b = line.send(far_b, "chan", 2)
     near_b = line.send(c_half_b, "tm", 1)
-    other_a = line.send(pack([near_a1, near_a2, away_a, side_a, corner_a, corner_side_a], "pack_a"), "chan", 1)
+    rest_a = pack([(mixed_a, 0, quarter), (mixed_b, 0, quarter), side_a], "pack_rest")
+    far_a_other = line.send(far_a, "chan", 1)
+    rest_a_other = line.send(rest_a, "chan", 1)
     ca = [own_a] + collected(idx, [
-        (near_a1, [(0, 6, quarter)]), (near_a2, [(0, 7, quarter)]),
-        (away_a, mine_1), (side_a, mine_2), (corner_a, mine_3), (corner_side_a, mine_4),
-        (other_a, [(0, 8, quarter), (0, 9, quarter)] + their_1 + their_2 + their_3 + their_4),
+        (far_a, mine_1 + mine_3), (rest_a, [(0, 6, quarter), (0, 7, quarter)] + mine_2 + mine_4),
+        (far_a_other, their_1 + their_3), (rest_a_other, [(0, 8, quarter), (0, 9, quarter)] + their_2 + their_4),
     ], "collect_a")
 
     def shares(first, features, values, factor, name, sums=()):

time: 143 us -> 142 us (level)
  waiting for transfers between devices: 72.9 us -> 68.8 us
  starting transfers between devices: 25.1 us -> 28.2 us
    ppermute x29 -> x27, waiting for transfers between devices: 72.9 us -> 68.8 us  [swap(): return lax.ppermute(x, axis, [(k, k ^ bit) for k in range(n)])]
    ppermute x29 -> x27, starting transfers between devices: 25.1 us -> 28.2 us  [swap(): return lax.ppermute(x, axis, [(k, k ^ bit) for k in range(n)])]
    pallas_call x19 -> x22, Pallas kernels: 33.8 us -> 33.8 us  [resident(): pl.pallas_call(kernel, out_shape=out_shape, in_specs=[SMEM] * scalars + [...]
  transfers between devices with their start and end apart: 29 -> 27, of which waited for: 18 -> 16; matrix products, arithmetic and copies ran while one was open for 2% -> 2% of each run, Pallas kernels for 23% -> 23%
where the time goes in v8:
time: 142 us; the launch traced here: 141 us
  waiting for transfers between devices  68.8 us (48%)
  Pallas kernels  33.8 us (24%)
  starting transfers between devices  28.2 us (20%)
  local copies, waits for them, and re-layouts  5.75 us (4%)
  other arithmetic  3.89 us (3%)
    ppermute x27, waiting for transfers between devices, swap(): return lax.ppermute(x, axis, [(k, k ^ bit) for k in range(n)])  68.8 us
    pallas_call x22, Pallas kernels, resident(): pl.pallas_call(kernel, out_shape=out_shape, in_specs=[SMEM] * scalars + [...  33.8 us
    ppermute x27, starting transfers between devices, swap(): return lax.ppermute(x, axis, [(k, k ^ bit) for k in range(n)])  28.2 us
    unnamed x18, local copies, waits for them, and re-layouts  5.62 us
  transfers between devices with their start and end apart: 27, of which 16 were waited for; matrix products, arithmetic and copies ran while one was open for 2% of the time, Pallas kernels for 23%

profile of v8, /device:TPU:0, one launch (start us, length us, event | category | flops | bytes accessed | tf_op | source)
XLA Modules:
  0.0 141.4 jit_solution(2806301936278433517)
XLA Ops:
  3.1 3.0 %collective-permute-start = (f32[128,2048]{1,0:T(8,128)S(1)}, f32[128,2048]{1,0:T(8,128)S(1)}, u32[]{:S(2)}, u32[]{:S(2)}) collective-permute-start(f32[128,2048]{1,0:T(8,128)S(1)} %get-tuple-element.106), channel_id=1, source_target_pairs={{0,4},{4,0},{8,12},{12,8},{16,20},{20,16},{24,28},{28,24},{1,5},{5... | collective-permute-start | bytes 3145736 | tf_op jit(solution)/shard_map/ppermute | solution.py:20
  6.1 2.6 %collective-permute-start.1 = (f32[64,2048]{1,0:T(8,128)S(1)}, f32[64,2048]{1,0:T(8,128)S(1)}, u32[]{:S(2)}, u32[]{:S(2)}) collective-permute-start(f32[64,2048]{1,0:T(8,128)S(1)} %get-tuple-element.108), channel_id=1, source_target_pairs={{0,16},{4,20},{8,24},{12,28},{16,0},{20,4},{24,8},{28,12},{1,17},{... | collective-permute-start | bytes 1572872 | tf_op jit(solution)/shard_map/ppermute | solution.py:20
  9.9 2.2 %copy-done = bf16[2048,1024]{1,0:T(8,128)(2,1)S(1)} copy-done((bf16[2048,1024]{1,0:T(8,128)(2,1)S(1)}, bf16[2048,1024]{1,0:T(8,128)(2,1)}, u32[]{:S(2)}) %copy-start) | copy-done | bytes 4194328
  12.1 2.2 %copy-done.2 = bf16[1024,2048]{1,0:T(8,128)(2,1)S(1)} copy-done((bf16[1024,2048]{1,0:T(8,128)(2,1)S(1)}, bf16[1024,2048]{1,0:T(8,128)(2,1)}, u32[]{:S(2)}) %copy-start.2) | copy-done | bytes 4194328
  14.3 2.9 %summary.1 = f32[1,4,1024]{2,1,0:T(4,128)S(1)} custom-call(bf16[256,2048]{1,0:T(8,128)(2,1)S(1)} %get-tuple-element.186.x_ref.refs_0_, bf16[256,2048]{1,0:T(8,128)(2,1)S(1)} %get-tuple-element.109.c_ref.refs_0_, bf16[2048,1024]{1,0:T(8,128)(2,1)S(1)} %copy-done, bf16[1024,2048]{1,0:T(8,128)(2,1)S(1)} %copy-done.2, f32[1,1024]{1,0:T(1,128)S(1)} %bitcast.31, ...), custom_call_target="tpu_custom_call" | custom-call | tf_op jit(solution)/shard_map/summary/pallas_call | solution.py:54
  17.2 1.6 %collective-permute-start.2 = (f32[1,4,1024]{2,1,0:T(4,128)S(1)}, f32[1,4,1024]{2,1,0:T(4,128)S(1)}, u32[]{:S(2)}, u32[]{:S(2)}) collective-permute-start(f32[1,4,1024]{2,1,0:T(4,128)S(1)} %summary.1), channel_id=1, source_target_pairs={{0,8},{4,12},{8,0},{12,4},{16,24},{20,28},{24,16},{28,20},{1,9},{5... | collective-permute-start | bytes 49160 | tf_op jit(solution)/shard_map/ppermute | solution.py:20
  19.2 2.5 %collective-permute-start.4 = (f32[1,4,1024]{2,1,0:T(4,128)S(1)}, f32[1,4,1024]{2,1,0:T(4,128)S(1)}, u32[]{:S(2)}, u32[]{:S(2)}) collective-permute-start(f32[1,4,1024]{2,1,0:T(4,128)S(1)} %summary.1), channel_id=1, source_target_pairs={{0,24},{4,28},{8,16},{12,20},{16,8},{20,12},{24,0},{28,4},{1,25},{... | collective-permute-start | bytes 49160 | tf_op jit(solution)/shard_map/ppermute | solution.py:20
  21.7 11.2 %collective-permute-done.3 = f32[1,4,1024]{2,1,0:T(4,128)S(1)} collective-permute-done((f32[1,4,1024]{2,1,0:T(4,128)S(1)}, f32[1,4,1024]{2,1,0:T(4,128)S(1)}, u32[]{:S(2)}, u32[]{:S(2)}) %collective-permute-start.3) | collective-permute-done | bytes 16416 | tf_op jit(solution)/shard_map/ppermute | solution.py:20
  33.5 1.6 %collective-permute-start.6 = (f32[64,2048]{1,0:T(8,128)S(1)}, f32[64,2048]{1,0:T(8,128)S(1)}, u32[]{:S(2)}, u32[]{:S(2)}) collective-permute-start(f32[64,2048]{1,0:T(8,128)S(1)} %collective-permute-done.1.refs_1_), channel_id=1, source_target_pairs={{0,2},{1,3},{2,0},{3,1},{4,6},{5,7},{6,4},{7,5},{8,10},{9,11},{10,... | collective-permute-start | bytes 1572872 | tf_op jit(solution)/shard_map/ppermute | solution.py:20
  35.0 2.8 %collective-permute-start.7 = (f32[64,1024]{1,0:T(8,128)S(1)}, f32[64,1024]{1,0:T(8,128)S(1)}, u32[]{:S(2)}, u32[]{:S(2)}) collective-permute-start(f32[64,1024]{1,0:T(8,128)S(1)} %get-tuple-element.115), channel_id=1, source_target_pairs={{0,16},{4,20},{8,24},{12,28},{16,0},{20,4},{24,8},{28,12},{1,17},{... | collective-permute-start | bytes 786440 | tf_op jit(solution)/shard_map/ppermute | solution.py:20
  37.8 1.5 %collective-permute-start.8 = (f32[4,4,1024]{2,1,0:T(4,128)S(1)}, f32[4,4,1024]{2,1,0:T(4,128)S(1)}, u32[]{:S(2)}, u32[]{:S(2)}) collective-permute-start(f32[4,4,1024]{2,1,0:T(4,128)S(1)} %pad_maximum_fusion.1), channel_id=1, source_target_pairs={{0,4},{4,0},{8,12},{12,8},{16,20},{20,16},{24,28},{28,24},{1,5},{5... | collective-permute-start | bytes 196616 | tf_op jit(solution)/shard_map/ppermute | solution.py:20
  39.3 7.7 %collective-permute-done.8 = f32[4,4,1024]{2,1,0:T(4,128)S(1)} collective-permute-done((f32[4,4,1024]{2,1,0:T(4,128)S(1)}, f32[4,4,1024]{2,1,0:T(4,128)S(1)}, u32[]{:S(2)}, u32[]{:S(2)}) %collective-permute-start.8) | collective-permute-done | bytes 65568 | tf_op jit(solution)/shard_map/ppermute | solution.py:20
  47.8 1.5 %collective-permute-done.7.refs_1_.refs_0_ = f32[64,1024]{1,0:T(8,128)S(1)} collective-permute-done((f32[64,1024]{1,0:T(8,128)S(1)}, f32[64,1024]{1,0:T(8,128)S(1)}, u32[]{:S(2)}, u32[]{:S(2)}) %collective-permute-start.7) | collective-permute-done | bytes 262176 | tf_op jit(solution)/shard_map/ppermute | solution.py:20
  49.7 1.6 %collective-permute-start.10 = (f32[128,1024]{1,0:T(8,128)S(1)}, f32[128,1024]{1,0:T(8,128)S(1)}, u32[]{:S(2)}, u32[]{:S(2)}) collective-permute-start(f32[128,1024]{1,0:T(8,128)S(1)} %pack_mixed.2), channel_id=1, source_target_pairs={{0,4},{4,0},{8,12},{12,8},{16,20},{20,16},{24,28},{28,24},{1,5},{5... | collective-permute-start | bytes 1572872 | tf_op jit(solution)/shard_map/ppermute | solution.py:20
  51.8 2.6 %collective-permute-start.11 = (f32[64,1024]{1,0:T(8,128)S(1)}, f32[64,1024]{1,0:T(8,128)S(1)}, u32[]{:S(2)}, u32[]{:S(2)}) collective-permute-start(f32[64,1024]{1,0:T(8,128)S(1)} %get-tuple-element.126), channel_id=1, source_target_pairs={{0,16},{4,20},{8,24},{12,28},{16,0},{20,4},{24,8},{28,12},{1,17},{... | collective-permute-start | bytes 786440 | tf_op jit(solution)/shard_map/ppermute | solution.py:20
  54.4 2.2 %forward_own.1 = (f32[8,1024]{1,0:T(8,128)S(1)}, bf16[256,1024]{1,0:T(8,128)(2,1)S(1)}) custom-call(s32[23]{0:T(128)S(1)} %stack.83.idx_ref, bf16[256,2048]{1,0:T(8,128)(2,1)S(1)} %get-tuple-element.186.x_ref.refs_0_, bf16[2048,1024]{1,0:T(8,128)(2,1)S(1)} %copy-done.1, f32[1,1024]{1,0:T(1,128)S(1)} %bitcast.32, f32[1,1024]{1,0:T(1,128)S(1)} %bitcast.37, ...), custom_call_target="tpu_custom_call" | custom-call | tf_op jit(solution)/shard_map/forward_own/pallas_call | solution.py:54
  56.6 2.5 %backward_own.1 = (bf16[256,1024]{1,0:T(8,128)(2,1)S(1)}, f32[1,1024]{1,0:T(1,128)S(1)}) custom-call(s32[23]{0:T(128)S(1)} %stack.83.idx_ref, bf16[256,2048]{1,0:T(8,128)(2,1)S(1)} %get-tuple-element.109.c_ref.refs_0_, bf16[1024,2048]{1,0:T(8,128)(2,1)S(1)} %copy-done.3, f32[1,1024]{1,0:T(1,128)S(1)} %bitcast.33, f32[1,1024]{1,0:T(1,128)S(1)} %bitcast.38, ...), custom_call_target="tpu_custom_call" | custom-call | tf_op jit(solution)/shard_map/backward_own/pallas_call | solution.py:54
  59.1 1.9 %row_grad.1 = (f32[2,256,512]{2,1,0:T(8,128)S(1)}, f32[2,256,512]{2,1,0:T(8,128)S(1)}) custom-call(s32[23]{0:T(128)S(1)} %stack.83.idx_ref, bf16[256,1024]{1,0:T(8,128)(2,1)S(1)} %get-tuple-element.132.a_ref.refs_4_, bf16[2048,1024]{1,0:T(8,128)(2,1)S(1)} %copy-done.1), custom_call_target="tpu_custom_call" | custom-call | tf_op jit(solution)/shard_map/row_grad/pallas_call | solution.py:54
  61.0 5.4 %collective-permute-done.11.refs_1_.refs_0_ = f32[64,1024]{1,0:T(8,128)S(1)} collective-permute-done((f32[64,1024]{1,0:T(8,128)S(1)}, f32[64,1024]{1,0:T(8,128)S(1)}, u32[]{:S(2)}, u32[]{:S(2)}) %collective-permute-start.11) | collective-permute-done | bytes 262176 | tf_op jit(solution)/shard_map/ppermute | solution.py:20
  66.6 1.5 %collective-permute-start.14 = (f32[128,1024]{1,0:T(8,128)S(1)}, f32[128,1024]{1,0:T(8,128)S(1)}, u32[]{:S(2)}, u32[]{:S(2)}) collective-permute-start(f32[128,1024]{1,0:T(8,128)S(1)} %pack_mixed.3), channel_id=1, source_target_pairs={{0,4},{4,0},{8,12},{12,8},{16,20},{20,16},{24,28},{28,24},{1,5},{5... | collective-permute-start | bytes 1572872 | tf_op jit(solution)/shard_map/ppermute | solution.py:20
  68.9 1.4 collect_x.1
  70.2 5.6 %forward_group.1 = (f32[8,1024]{1,0:T(8,128)S(1)}, bf16[256,1024]{1,0:T(8,128)(2,1)S(1)}, f32[8,1024]{1,0:T(8,128)S(1)}, bf16[256,1024]{1,0:T(8,128)(2,1)S(1)}, ...) custom-call(s32[23]{0:T(128)S(1)} %stack.83.idx_ref, bf16[256,2048]{1,0:T(8,128)(2,1)S(1)} %get-tuple-element.146.refs_0_.refs_1_, ...), custom_call_target="tpu_custom_call" | custom-call | tf_op jit(solution)/shard_map/forward_group/pallas_call | solution.py:54
  75.9 5.1 %collective-permute-done.14.refs_1_ = f32[128,1024]{1,0:T(8,128)S(1)} collective-permute-done((f32[128,1024]{1,0:T(8,128)S(1)}, f32[128,1024]{1,0:T(8,128)S(1)}, u32[]{:S(2)}, u32[]{:S(2)}) %collective-permute-start.14) | collective-permute-done | bytes 524320 | tf_op jit(solution)/shard_map/ppermute | solution.py:20
  83.7 1.5 %collective-permute-start.19 = (f32[128,1024]{1,0:T(8,128)S(1)}, f32[128,1024]{1,0:T(8,128)S(1)}, u32[]{:S(2)}, u32[]{:S(2)}) collective-permute-start(f32[128,1024]{1,0:T(8,128)S(1)} %get-tuple-element.163), channel_id=1, source_target_pairs={{0,4},{4,0},{8,12},{12,8},{16,20},{20,16},{24,28},{28,24},{1,5},{5... | collective-permute-start | bytes 1572872 | tf_op jit(solution)/shard_map/ppermute | solution.py:20
  86.8 1.3 out_grad.2
  88.6 8.4 %collective-permute-done.20.refs_2_ = f32[128,1024]{1,0:T(8,128)S(1)} collective-permute-done((f32[128,1024]{1,0:T(8,128)S(1)}, f32[128,1024]{1,0:T(8,128)S(1)}, u32[]{:S(2)}, u32[]{:S(2)}) %collective-permute-start.20) | collective-permute-done | bytes 524320 | tf_op jit(solution)/shard_map/ppermute | solution.py:20
  97.9 1.4 collective-permute-done.23.refs_5_
  101.8 6.6 %backward_group.1 = (bf16[256,1024]{1,0:T(8,128)(2,1)S(1)}, f32[1,1024]{1,0:T(1,128)S(1)}, bf16[256,1024]{1,0:T(8,128)(2,1)S(1)}, f32[1,1024]{1,0:T(1,128)S(1)},...) custom-call(s32[23]{0:T(128)S(1)} %stack.83.idx_ref, bf16[256,1024]{1,0:T(8,128)(2,1)S(1)} %get-tuple-element.154.refs_1_.refs_0_, ...), custom_call_target="tpu_custom_call" | custom-call | tf_op jit(solution)/shard_map/backward_group/pallas_call | solution.py:54
  109.6 3.7 %collective-permute-done.18 = f32[256,1024]{1,0:T(8,128)S(1)} collective-permute-done((f32[256,1024]{1,0:T(8,128)S(1)}, f32[256,1024]{1,0:T(8,128)S(1)}, u32[]{:S(2)}, u32[]{:S(2)}) %collective-permute-start.18) | collective-permute-done | bytes 1048608 | tf_op jit(solution)/shard_map/ppermute | solution.py:20
  113.8 2.3 %collective-permute-done.25 = f32[2,256,512]{2,1,0:T(8,128)S(1)} collective-permute-done((f32[2,256,512]{2,1,0:T(8,128)S(1)}, f32[2,256,512]{2,1,0:T(8,128)S(1)}, u32[]{:S(2)}, u32[]{:S(2)}) %collective-permute-start.25) | collective-permute-done | bytes 1048608 | tf_op jit(solution)/shard_map/ppermute | solution.py:20
  120.7 9.6 %collective-permute-done.26 = f32[256,512]{1,0:T(8,128)S(1)} collective-permute-done((f32[256,512]{1,0:T(8,128)S(1)}, f32[256,512]{1,0:T(8,128)S(1)}, u32[]{:S(2)}, u32[]{:S(2)}) %collective-permute-start.26) | collective-permute-done | bytes 524320 | tf_op jit(solution)/shard_map/ppermute | solution.py:20
  131.1 8.6 %collective-permute-done.24 = f32[264,1024]{1,0:T(8,128)S(1)} collective-permute-done((f32[264,1024]{1,0:T(8,128)S(1)}, f32[264,1024]{1,0:T(8,128)S(1)}, u32[]{:S(2)}, u32[]{:S(2)}) %collective-permute-start.24) | collective-permute-done | bytes 1081376 | tf_op jit(solution)/shard_map/ppermute | solution.py:20
  (71 shorter events, 23.9 us)
Async XLA Ops:
  0.7 9.2 %copy-start.6 = (f32[1024]{0:T(1024)S(1)}, f32[1024]{0:T(1024)}, u32[]{:S(2)}) copy-start(f32[1024]{0:T(1024)} %param.12) | copy-start | bytes 12292
  0.7 9.2 %copy-start.7 = (f32[1024]{0:T(1024)S(1)}, f32[1024]{0:T(1024)}, u32[]{:S(2)}) copy-start(f32[1024]{0:T(1024)} %param.11) | copy-start | bytes 12292
  0.7 9.2 %copy-start.8 = (f32[256]{0:T(256)S(1)}, f32[256]{0:T(256)}, u32[]{:S(2)}) copy-start(f32[256]{0:T(256)} %param.13) | copy-start | bytes 3076
  2.0 6.7 %copy-start.5 = (bf16[256,2048]{1,0:T(8,128)(2,1)S(1)}, bf16[256,2048]{1,0:T(8,128)(2,1)}, u32[]{:S(2)}) copy-start(bf16[256,2048]{1,0:T(8,128)(2,1)} %x_ref.1) | copy-start | bytes 3145732
  3.1 29.8 %collective-permute-start = (f32[128,2048]{1,0:T(8,128)S(1)}, f32[128,2048]{1,0:T(8,128)S(1)}, u32[]{:S(2)}, u32[]{:S(2)}) collective-permute-start(f32[128,2048]{1,0:T(8,128)S(1)} %get-tuple-element.106), channel_id=1, source_target_pairs={{0,4},{4,0},{8,12},{12,8},{16,20},{20,16},{24,28},{28,24},{1,5},{5... | collective-permute-start | bytes 3145736 | tf_op jit(solution)/shard_map/ppermute | solution.py:20
  6.1 26.8 %collective-permute-start.1 = (f32[64,2048]{1,0:T(8,128)S(1)}, f32[64,2048]{1,0:T(8,128)S(1)}, u32[]{:S(2)}, u32[]{:S(2)}) collective-permute-start(f32[64,2048]{1,0:T(8,128)S(1)} %get-tuple-element.108), channel_id=1, source_target_pairs={{0,16},{4,20},{8,24},{12,28},{16,0},{20,4},{24,8},{28,12},{1,17},{... | collective-permute-start | bytes 1572872 | tf_op jit(solution)/shard_map/ppermute | solution.py:20
  17.2 4.5 %collective-permute-start.2 = (f32[1,4,1024]{2,1,0:T(4,128)S(1)}, f32[1,4,1024]{2,1,0:T(4,128)S(1)}, u32[]{:S(2)}, u32[]{:S(2)}) collective-permute-start(f32[1,4,1024]{2,1,0:T(4,128)S(1)} %summary.1), channel_id=1, source_target_pairs={{0,8},{4,12},{8,0},{12,4},{16,24},{20,28},{24,16},{28,20},{1,9},{5... | collective-permute-start | bytes 49160 | tf_op jit(solution)/shard_map/ppermute | solution.py:20
  18.9 14.0 %collective-permute-start.3 = (f32[1,4,1024]{2,1,0:T(4,128)S(1)}, f32[1,4,1024]{2,1,0:T(4,128)S(1)}, u32[]{:S(2)}, u32[]{:S(2)}) collective-permute-start(f32[1,4,1024]{2,1,0:T(4,128)S(1)} %summary.1), channel_id=1, source_target_pairs={{0,16},{4,20},{8,24},{12,28},{16,0},{20,4},{24,8},{28,12},{1,17},{... | collective-permute-start | bytes 49160 | tf_op jit(solution)/shard_map/ppermute | solution.py:20
  19.2 13.7 %collective-permute-start.4 = (f32[1,4,1024]{2,1,0:T(4,128)S(1)}, f32[1,4,1024]{2,1,0:T(4,128)S(1)}, u32[]{:S(2)}, u32[]{:S(2)}) collective-permute-start(f32[1,4,1024]{2,1,0:T(4,128)S(1)} %summary.1), channel_id=1, source_target_pairs={{0,24},{4,28},{8,16},{12,20},{16,8},{20,12},{24,0},{28,4},{1,25},{... | collective-permute-start | bytes 49160 | tf_op jit(solution)/shard_map/ppermute | solution.py:20
  32.9 16.4 %collective-permute-start.5 = (f32[64,2048]{1,0:T(8,128)S(1)}, f32[64,2048]{1,0:T(8,128)S(1)}, u32[]{:S(2)}, u32[]{:S(2)}) collective-permute-start(f32[64,2048]{1,0:T(8,128)S(1)} %collective-permute-done.1.refs_1_), channel_id=1, source_target_pairs={{0,4},{4,0},{8,12},{12,8},{16,20},{20,16},{24,28},{28,24},{1,5},{5... | collective-permute-start | bytes 1572872 | tf_op jit(solution)/shard_map/ppermute | solution.py:20
  33.5 15.9 %collective-permute-start.6 = (f32[64,2048]{1,0:T(8,128)S(1)}, f32[64,2048]{1,0:T(8,128)S(1)}, u32[]{:S(2)}, u32[]{:S(2)}) collective-permute-start(f32[64,2048]{1,0:T(8,128)S(1)} %collective-permute-done.1.refs_1_), channel_id=1, source_target_pairs={{0,2},{1,3},{2,0},{3,1},{4,6},{5,7},{6,4},{7,5},{8,10},{9,11},{10,... | collective-permute-start | bytes 1572872 | tf_op jit(solution)/shard_map/ppermute | solution.py:20
  35.0 14.3 %collective-permute-start.7 = (f32[64,1024]{1,0:T(8,128)S(1)}, f32[64,1024]{1,0:T(8,128)S(1)}, u32[]{:S(2)}, u32[]{:S(2)}) collective-permute-start(f32[64,1024]{1,0:T(8,128)S(1)} %get-tuple-element.115), channel_id=1, source_target_pairs={{0,16},{4,20},{8,24},{12,28},{16,0},{20,4},{24,8},{28,12},{1,17},{... | collective-permute-start | bytes 786440 | tf_op jit(solution)/shard_map/ppermute | solution.py:20
  37.8 9.2 %collective-permute-start.8 = (f32[4,4,1024]{2,1,0:T(4,128)S(1)}, f32[4,4,1024]{2,1,0:T(4,128)S(1)}, u32[]{:S(2)}, u32[]{:S(2)}) collective-permute-start(f32[4,4,1024]{2,1,0:T(4,128)S(1)} %pad_maximum_fusion.1), channel_id=1, source_target_pairs={{0,4},{4,0},{8,12},{12,8},{16,20},{20,16},{24,28},{28,24},{1,5},{5... | collective-permute-start | bytes 196616 | tf_op jit(solution)/shard_map/ppermute | solution.py:20
  49.3 5.0 %copy-start.1 = (bf16[2048,1024]{1,0:T(8,128)(2,1)S(1)}, bf16[2048,1024]{1,0:T(8,128)(2,1)}, u32[]{:S(2)}) copy-start(bf16[2048,1024]{1,0:T(8,128)(2,1)} %refs_3_.1) | copy-start | bytes 12582916
  49.6 16.9 %collective-permute-start.12 = (f32[320,2048]{1,0:T(8,128)S(1)}, f32[320,2048]{1,0:T(8,128)S(1)}, u32[]{:S(2)}, u32[]{:S(2)}) collective-permute-start(f32[320,2048]{1,0:T(8,128)S(1)} %pack_x.1), channel_id=1, source_target_pairs={{0,1},{1,0},{2,3},{3,2},{4,5},{5,4},{6,7},{7,6},{8,9},{9,8},{10,11... | collective-permute-start | bytes 7864328 | tf_op jit(solution)/shard_map/ppermute | solution.py:20
  49.7 16.7 %collective-permute-start.10 = (f32[128,1024]{1,0:T(8,128)S(1)}, f32[128,1024]{1,0:T(8,128)S(1)}, u32[]{:S(2)}, u32[]{:S(2)}) collective-permute-start(f32[128,1024]{1,0:T(8,128)S(1)} %pack_mixed.2), channel_id=1, source_target_pairs={{0,4},{4,0},{8,12},{12,8},{16,20},{20,16},{24,28},{28,24},{1,5},{5... | collective-permute-start | bytes 1572872 | tf_op jit(solution)/shard_map/ppermute | solution.py:20
  51.3 15.2 %collective-permute-start.9 = (f32[64,2048]{1,0:T(8,128)S(1)}, f32[64,2048]{1,0:T(8,128)S(1)}, u32[]{:S(2)}, u32[]{:S(2)}) collective-permute-start(f32[64,2048]{1,0:T(8,128)S(1)} %collective-permute-done.5.refs_3_), channel_id=1, source_target_pairs={{0,2},{1,3},{2,0},{3,1},{4,6},{5,7},{6,4},{7,5},{8,10},{9,11},{10,... | collective-permute-start | bytes 1572872 | tf_op jit(solution)/shard_map/ppermute | solution.py:20
  51.8 14.7 %collective-permute-start.11 = (f32[64,1024]{1,0:T(8,128)S(1)}, f32[64,1024]{1,0:T(8,128)S(1)}, u32[]{:S(2)}, u32[]{:S(2)}) collective-permute-start(f32[64,1024]{1,0:T(8,128)S(1)} %get-tuple-element.126), channel_id=1, source_target_pairs={{0,16},{4,20},{8,24},{12,28},{16,0},{20,4},{24,8},{28,12},{1,17},{... | collective-permute-start | bytes 786440 | tf_op jit(solution)/shard_map/ppermute | solution.py:20
  66.5 2.4 %collective-permute-start.15 = (f32[64,2048]{1,0:T(8,128)S(1)}, f32[64,2048]{1,0:T(8,128)S(1)}, u32[]{:S(2)}, u32[]{:S(2)}) collective-permute-start(f32[64,2048]{1,0:T(8,128)S(1)} %collective-permute-done.9.refs_4_), channel_id=1, source_target_pairs={{0,1},{1,0},{2,3},{3,2},{4,5},{5,4},{6,7},{7,6},{8,9},{9,8},{10,11... | collective-permute-start | bytes 1572872 | tf_op jit(solution)/shard_map/ppermute | solution.py:20
  66.6 14.4 %collective-permute-start.14 = (f32[128,1024]{1,0:T(8,128)S(1)}, f32[128,1024]{1,0:T(8,128)S(1)}, u32[]{:S(2)}, u32[]{:S(2)}) collective-permute-start(f32[128,1024]{1,0:T(8,128)S(1)} %pack_mixed.3), channel_id=1, source_target_pairs={{0,4},{4,0},{8,12},{12,8},{16,20},{20,16},{24,28},{28,24},{1,5},{5... | collective-permute-start | bytes 1572872 | tf_op jit(solution)/shard_map/ppermute | solution.py:20
  68.2 14.1 %collective-permute-start.13 = (f32[128,1024]{1,0:T(8,128)S(1)}, f32[128,1024]{1,0:T(8,128)S(1)}, u32[]{:S(2)}, u32[]{:S(2)}) collective-permute-start(f32[128,1024]{1,0:T(8,128)S(1)} %pack_far.2.refs_0_), channel_id=1, source_target_pairs={{0,2},{1,3},{2,0},{3,1},{4,6},{5,7},{6,4},{7,5},{8,10},{9,11},{10,... | collective-permute-start | bytes 1572872 | tf_op jit(solution)/shard_map/ppermute | solution.py:20
  82.4 3.5 %collective-permute-start.17 = (f32[256,1024]{1,0:T(8,128)S(1)}, f32[256,1024]{1,0:T(8,128)S(1)}, u32[]{:S(2)}, u32[]{:S(2)}) collective-permute-start(f32[256,1024]{1,0:T(8,128)S(1)} %pack_rest.1.refs_1_), channel_id=1, source_target_pairs={{0,1},{1,0},{2,3},{3,2},{4,5},{5,4},{6,7},{7,6},{8,9},{9,8},{10,11... | collective-permute-start | bytes 3145736 | tf_op jit(solution)/shard_map/ppermute | solution.py:20
  82.5 3.4 %collective-permute-start.16 = (f32[128,1024]{1,0:T(8,128)S(1)}, f32[128,1024]{1,0:T(8,128)S(1)}, u32[]{:S(2)}, u32[]{:S(2)}) collective-permute-start(f32[128,1024]{1,0:T(8,128)S(1)} %pack_far.2.refs_0_), channel_id=1, source_target_pairs={{0,1},{1,0},{2,3},{3,2},{4,5},{5,4},{6,7},{7,6},{8,9},{9,8},{10,11... | collective-permute-start | bytes 1572872 | tf_op jit(solution)/shard_map/ppermute | solution.py:20
  83.0 14.0 %collective-permute-start.20 = (f32[128,1024]{1,0:T(8,128)S(1)}, f32[128,1024]{1,0:T(8,128)S(1)}, u32[]{:S(2)}, u32[]{:S(2)}) collective-permute-start(f32[128,1024]{1,0:T(8,128)S(1)} %pack_far.3.refs_1_), channel_id=1, source_target_pairs={{0,2},{1,3},{2,0},{3,1},{4,6},{5,7},{6,4},{7,5},{8,10},{9,11},{10,... | collective-permute-start | bytes 1572872 | tf_op jit(solution)/shard_map/ppermute | solution.py:20
  83.7 13.6 %collective-permute-start.19 = (f32[128,1024]{1,0:T(8,128)S(1)}, f32[128,1024]{1,0:T(8,128)S(1)}, u32[]{:S(2)}, u32[]{:S(2)}) collective-permute-start(f32[128,1024]{1,0:T(8,128)S(1)} %get-tuple-element.163), channel_id=1, source_target_pairs={{0,4},{4,0},{8,12},{12,8},{16,20},{20,16},{24,28},{28,24},{1,5},{5... | collective-permute-start | bytes 1572872 | tf_op jit(solution)/shard_map/ppermute | solution.py:20
  88.1 25.3 %collective-permute-start.18 = (f32[256,1024]{1,0:T(8,128)S(1)}, f32[256,1024]{1,0:T(8,128)S(1)}, u32[]{:S(2)}, u32[]{:S(2)}) collective-permute-start(f32[256,1024]{1,0:T(8,128)S(1)} %out_grad.2), channel_id=1, source_target_pairs={{0,8},{4,12},{8,0},{12,4},{16,24},{20,28},{24,16},{28,20},{1,9},{5... | collective-permute-start | bytes 3145736 | tf_op jit(solution)/shard_map/ppermute | solution.py:20
  97.4 1.9 %collective-permute-start.23 = (f32[128,1024]{1,0:T(8,128)S(1)}, f32[128,1024]{1,0:T(8,128)S(1)}, u32[]{:S(2)}, u32[]{:S(2)}) collective-permute-start(f32[128,1024]{1,0:T(8,128)S(1)} %collective-permute-done.20.refs_2_), channel_id=1, source_target_pairs={{0,1},{1,0},{2,3},{3,2},{4,5},{5,4},{6,7},{7,6},{8,9},{9,8},{10,11... | collective-permute-start | bytes 1572872 | tf_op jit(solution)/shard_map/ppermute | solution.py:20
  97.4 2.7 %collective-permute-start.22 = (f32[128,1024]{1,0:T(8,128)S(1)}, f32[128,1024]{1,0:T(8,128)S(1)}, u32[]{:S(2)}, u32[]{:S(2)}) collective-permute-start(f32[128,1024]{1,0:T(8,128)S(1)} %pack_far.3.refs_1_), channel_id=1, source_target_pairs={{0,1},{1,0},{2,3},{3,2},{4,5},{5,4},{6,7},{7,6},{8,9},{9,8},{10,11... | collective-permute-start | bytes 1572872 | tf_op jit(solution)/shard_map/ppermute | solution.py:20
  97.9 2.9 %collective-permute-start.21 = (f32[128,1024]{1,0:T(8,128)S(1)}, f32[128,1024]{1,0:T(8,128)S(1)}, u32[]{:S(2)}, u32[]{:S(2)}) collective-permute-start(f32[128,1024]{1,0:T(8,128)S(1)} %collective-permute-done.19.refs_0_), channel_id=1, source_target_pairs={{0,1},{1,0},{2,3},{3,2},{4,5},{5,4},{6,7},{7,6},{8,9},{9,8},{10,11... | collective-permute-start | bytes 1572872 | tf_op jit(solution)/shard_map/ppermute | solution.py:20
  113.4 2.7 %collective-permute-start.25 = (f32[2,256,512]{2,1,0:T(8,128)S(1)}, f32[2,256,512]{2,1,0:T(8,128)S(1)}, u32[]{:S(2)}, u32[]{:S(2)}) collective-permute-start(f32[2,256,512]{2,1,0:T(8,128)S(1)} %get-tuple-element.190), channel_id=1, source_target_pairs={{0,1},{1,0},{2,3},{3,2},{4,5},{5,4},{6,7},{7,6},{8,9},{9,8},{10,11... | collective-permute-start | bytes 3145736 | tf_op jit(solution)/shard_map/ppermute | solution.py:20
  113.4 26.3 %collective-permute-start.24 = (f32[264,1024]{1,0:T(8,128)S(1)}, f32[264,1024]{1,0:T(8,128)S(1)}, u32[]{:S(2)}, u32[]{:S(2)}) collective-permute-start(f32[264,1024]{1,0:T(8,128)S(1)} %in_grad.2), channel_id=1, source_target_pairs={{0,8},{4,12},{8,0},{12,4},{16,24},{20,28},{24,16},{28,20},{1,9},{5... | collective-permute-start | bytes 3244040 | tf_op jit(solution)/shard_map/ppermute | solution.py:20
  116.3 14.0 %collective-permute-start.26 = (f32[256,512]{1,0:T(8,128)S(1)}, f32[256,512]{1,0:T(8,128)S(1)}, u32[]{:S(2)}, u32[]{:S(2)}) collective-permute-start(f32[256,512]{1,0:T(8,128)S(1)} %slice_bitcast_fusion), channel_id=1, source_target_pairs={{0,2},{1,3},{2,0},{3,1},{4,6},{5,7},{6,4},{7,5},{8,10},{9,11},{10,... | collective-permute-start | bytes 1572872 | tf_op jit(solution)/shard_map/ppermute | solution.py:20
  (4 other events, 7.9 us)

commit v9 on v8

--- a/solution.py
+++ b/solution.py
@@ -498,6 +498,7 @@
     near_b = line.send(c_half_b, "tm", 1)
     rest_a = pack([(mixed_a, 0, quarter), (mixed_b, 0, quarter), side_a], "pack_rest")
     far_a_other = line.send(far_a, "chan", 1)
+    given = line.send(give, "chan", 1)
     rest_a_other = line.send(rest_a, "chan", 1)
     ca = [own_a] + collected(idx, [
         (far_a, mine_1 + mine_3), (rest_a, [(0, 6, quarter), (0, 7, quarter)] + mine_2 + mine_4),
@@ -508,7 +509,7 @@
         return [grad_rows(idx, first + k, features, values, rows_out, factor, name, sums) for k in range(1, groups)]
 
     out_given = shares(ROWS + groups, ca, lows, scaling, "out_grad")
-    out_given[0] = line.step(out_given[0])
+    out_given[0], given = line.step(out_given[0], given)
 
     out_got = [line.send(part, "tm", 2 * (k + 1)) for k, part in enumerate(out_given)]
     near_b, side_b = line.step(near_b, side_b)
@@ -527,7 +528,7 @@
     in_given[0] = line.step(in_given[0])
     in_got = [line.send(part, "tm", 2 * (k + 1)) for k, part in enumerate(in_given)]
     out_got[0] = line.step(out_got[0])
-    parts = keep + line.send(give, "chan", 1)
+    parts = keep + given
     columns = parts[0] + line.send(parts[1], "chan", 2)
     input_grad = columns.astype(BF16)
     in_got[0] = after(in_got[0], input_grad)

time: 142 us -> 140 us (0.986)
  waiting for transfers between devices: 68.8 us -> 67.2 us
    ppermute x27, waiting for transfers between devices: 68.8 us -> 67.2 us  [swap(): return lax.ppermute(x, axis, [(k, k ^ bit) for k in range(n)])]
  transfers between devices with their start and end apart: 27 -> 27, of which waited for: 16 -> 15; matrix products, arithmetic and copies ran while one was open for 2% -> 2% of each run, Pallas kernels for 23% -> 23%
where the time goes in v9:
time: 140 us
  waiting for transfers between devices  67.2 us (48%)
  Pallas kernels  33.8 us (24%)
  starting transfers between devices  28.2 us (20%)
  local copies, waits for them, and re-layouts  5.75 us (4%)
  other arithmetic  3.84 us (3%)
    ppermute x27, waiting for transfers between devices, swap(): return lax.ppermute(x, axis, [(k, k ^ bit) for k in range(n)])  67.2 us
    pallas_call x22, Pallas kernels, resident(): pl.pallas_call(kernel, out_shape=out_shape, in_specs=[SMEM] * scalars + [...  33.8 us
    ppermute x27, starting transfers between devices, swap(): return lax.ppermute(x, axis, [(k, k ^ bit) for k in range(n)])  28.2 us
    unnamed x18, local copies, waits for them, and re-layouts  5.62 us
  transfers between devices with their start and end apart: 27, of which 15 were waited for; matrix products, arithmetic and copies ran while one was open for 2% of the time, Pallas kernels for 23%

profile of v9, /device:TPU:0, one launch (start us, length us, event | category | flops | bytes accessed | tf_op | source)
XLA Modules:
  0.0 139.8 jit_solution(3225055996145266143)
XLA Ops:
  3.1 3.0 %collective-permute-start = (f32[128,2048]{1,0:T(8,128)S(1)}, f32[128,2048]{1,0:T(8,128)S(1)}, u32[]{:S(2)}, u32[]{:S(2)}) collective-permute-start(f32[128,2048]{1,0:T(8,128)S(1)} %get-tuple-element.107), channel_id=1, source_target_pairs={{0,4},{4,0},{8,12},{12,8},{16,20},{20,16},{24,28},{28,24},{1,5},{5... | collective-permute-start | bytes 3145736 | tf_op jit(solution)/shard_map/ppermute | solution.py:20
  6.1 2.6 %collective-permute-start.1 = (f32[64,2048]{1,0:T(8,128)S(1)}, f32[64,2048]{1,0:T(8,128)S(1)}, u32[]{:S(2)}, u32[]{:S(2)}) collective-permute-start(f32[64,2048]{1,0:T(8,128)S(1)} %get-tuple-element.109), channel_id=1, source_target_pairs={{0,16},{4,20},{8,24},{12,28},{16,0},{20,4},{24,8},{28,12},{1,17},{... | collective-permute-start | bytes 1572872 | tf_op jit(solution)/shard_map/ppermute | solution.py:20
  9.9 2.2 %copy-done = bf16[2048,1024]{1,0:T(8,128)(2,1)S(1)} copy-done((bf16[2048,1024]{1,0:T(8,128)(2,1)S(1)}, bf16[2048,1024]{1,0:T(8,128)(2,1)}, u32[]{:S(2)}) %copy-start) | copy-done | bytes 4194328
  12.1 2.2 %copy-done.2 = bf16[1024,2048]{1,0:T(8,128)(2,1)S(1)} copy-done((bf16[1024,2048]{1,0:T(8,128)(2,1)S(1)}, bf16[1024,2048]{1,0:T(8,128)(2,1)}, u32[]{:S(2)}) %copy-start.2) | copy-done | bytes 4194328
  14.3 2.9 %summary.1 = f32[1,4,1024]{2,1,0:T(4,128)S(1)} custom-call(bf16[256,2048]{1,0:T(8,128)(2,1)S(1)} %get-tuple-element.189.x_ref.refs_0_, bf16[256,2048]{1,0:T(8,128)(2,1)S(1)} %get-tuple-element.110.c_ref.refs_0_, bf16[2048,1024]{1,0:T(8,128)(2,1)S(1)} %copy-done, bf16[1024,2048]{1,0:T(8,128)(2,1)S(1)} %copy-done.2, f32[1,1024]{1,0:T(1,128)S(1)} %bitcast.31, ...), custom_call_target="tpu_custom_call" | custom-call | tf_op jit(solution)/shard_map/summary/pallas_call | solution.py:54
  17.2 1.6 %collective-permute-start.2 = (f32[1,4,1024]{2,1,0:T(4,128)S(1)}, f32[1,4,1024]{2,1,0:T(4,128)S(1)}, u32[]{:S(2)}, u32[]{:S(2)}) collective-permute-start(f32[1,4,1024]{2,1,0:T(4,128)S(1)} %summary.1), channel_id=1, source_target_pairs={{0,8},{4,12},{8,0},{12,4},{16,24},{20,28},{24,16},{28,20},{1,9},{5... | collective-permute-start | bytes 49160 | tf_op jit(solution)/shard_map/ppermute | solution.py:20
  19.2 2.5 %collective-permute-start.4 = (f32[1,4,1024]{2,1,0:T(4,128)S(1)}, f32[1,4,1024]{2,1,0:T(4,128)S(1)}, u32[]{:S(2)}, u32[]{:S(2)}) collective-permute-start(f32[1,4,1024]{2,1,0:T(4,128)S(1)} %summary.1), channel_id=1, source_target_pairs={{0,24},{4,28},{8,16},{12,20},{16,8},{20,12},{24,0},{28,4},{1,25},{... | collective-permute-start | bytes 49160 | tf_op jit(solution)/shard_map/ppermute | solution.py:20
  21.7 11.2 %collective-permute-done.3 = f32[1,4,1024]{2,1,0:T(4,128)S(1)} collective-permute-done((f32[1,4,1024]{2,1,0:T(4,128)S(1)}, f32[1,4,1024]{2,1,0:T(4,128)S(1)}, u32[]{:S(2)}, u32[]{:S(2)}) %collective-permute-start.3) | collective-permute-done | bytes 16416 | tf_op jit(solution)/shard_map/ppermute | solution.py:20
  33.5 1.6 %collective-permute-start.6 = (f32[64,2048]{1,0:T(8,128)S(1)}, f32[64,2048]{1,0:T(8,128)S(1)}, u32[]{:S(2)}, u32[]{:S(2)}) collective-permute-start(f32[64,2048]{1,0:T(8,128)S(1)} %collective-permute-done.1.refs_1_), channel_id=1, source_target_pairs={{0,2},{1,3},{2,0},{3,1},{4,6},{5,7},{6,4},{7,5},{8,10},{9,11},{10,... | collective-permute-start | bytes 1572872 | tf_op jit(solution)/shard_map/ppermute | solution.py:20
  35.0 2.8 %collective-permute-start.7 = (f32[64,1024]{1,0:T(8,128)S(1)}, f32[64,1024]{1,0:T(8,128)S(1)}, u32[]{:S(2)}, u32[]{:S(2)}) collective-permute-start(f32[64,1024]{1,0:T(8,128)S(1)} %get-tuple-element.116), channel_id=1, source_target_pairs={{0,16},{4,20},{8,24},{12,28},{16,0},{20,4},{24,8},{28,12},{1,17},{... | collective-permute-start | bytes 786440 | tf_op jit(solution)/shard_map/ppermute | solution.py:20
  37.8 1.5 %collective-permute-start.8 = (f32[4,4,1024]{2,1,0:T(4,128)S(1)}, f32[4,4,1024]{2,1,0:T(4,128)S(1)}, u32[]{:S(2)}, u32[]{:S(2)}) collective-permute-start(f32[4,4,1024]{2,1,0:T(4,128)S(1)} %pad_maximum_fusion.1), channel_id=1, source_target_pairs={{0,4},{4,0},{8,12},{12,8},{16,20},{20,16},{24,28},{28,24},{1,5},{5... | collective-permute-start | bytes 196616 | tf_op jit(solution)/shard_map/ppermute | solution.py:20
  39.3 7.7 %collective-permute-done.8 = f32[4,4,1024]{2,1,0:T(4,128)S(1)} collective-permute-done((f32[4,4,1024]{2,1,0:T(4,128)S(1)}, f32[4,4,1024]{2,1,0:T(4,128)S(1)}, u32[]{:S(2)}, u32[]{:S(2)}) %collective-permute-start.8) | collective-permute-done | bytes 65568 | tf_op jit(solution)/shard_map/ppermute | solution.py:20
  47.8 1.5 %collective-permute-done.7.refs_1_.refs_0_ = f32[64,1024]{1,0:T(8,128)S(1)} collective-permute-done((f32[64,1024]{1,0:T(8,128)S(1)}, f32[64,1024]{1,0:T(8,128)S(1)}, u32[]{:S(2)}, u32[]{:S(2)}) %collective-permute-start.7) | collective-permute-done | bytes 262176 | tf_op jit(solution)/shard_map/ppermute | solution.py:20
  49.7 1.6 %collective-permute-start.10 = (f32[128,1024]{1,0:T(8,128)S(1)}, f32[128,1024]{1,0:T(8,128)S(1)}, u32[]{:S(2)}, u32[]{:S(2)}) collective-permute-start(f32[128,1024]{1,0:T(8,128)S(1)} %pack_mixed.2), channel_id=1, source_target_pairs={{0,4},{4,0},{8,12},{12,8},{16,20},{20,16},{24,28},{28,24},{1,5},{5... | collective-permute-start | bytes 1572872 | tf_op jit(solution)/shard_map/ppermute | solution.py:20
  51.8 2.6 %collective-permute-start.11 = (f32[64,1024]{1,0:T(8,128)S(1)}, f32[64,1024]{1,0:T(8,128)S(1)}, u32[]{:S(2)}, u32[]{:S(2)}) collective-permute-start(f32[64,1024]{1,0:T(8,128)S(1)} %get-tuple-element.127), channel_id=1, source_target_pairs={{0,16},{4,20},{8,24},{12,28},{16,0},{20,4},{24,8},{28,12},{1,17},{... | collective-permute-start | bytes 786440 | tf_op jit(solution)/shard_map/ppermute | solution.py:20
  54.4 2.2 %forward_own.1 = (f32[8,1024]{1,0:T(8,128)S(1)}, bf16[256,1024]{1,0:T(8,128)(2,1)S(1)}) custom-call(s32[23]{0:T(128)S(1)} %stack.83.idx_ref, bf16[256,2048]{1,0:T(8,128)(2,1)S(1)} %get-tuple-element.189.x_ref.refs_0_, bf16[2048,1024]{1,0:T(8,128)(2,1)S(1)} %copy-done.1, f32[1,1024]{1,0:T(1,128)S(1)} %bitcast.32, f32[1,1024]{1,0:T(1,128)S(1)} %bitcast.37, ...), custom_call_target="tpu_custom_call" | custom-call | tf_op jit(solution)/shard_map/forward_own/pallas_call | solution.py:54
  56.6 2.5 %backward_own.1 = (bf16[256,1024]{1,0:T(8,128)(2,1)S(1)}, f32[1,1024]{1,0:T(1,128)S(1)}) custom-call(s32[23]{0:T(128)S(1)} %stack.83.idx_ref, bf16[256,2048]{1,0:T(8,128)(2,1)S(1)} %get-tuple-element.110.c_ref.refs_0_, bf16[1024,2048]{1,0:T(8,128)(2,1)S(1)} %copy-done.3, f32[1,1024]{1,0:T(1,128)S(1)} %bitcast.33, f32[1,1024]{1,0:T(1,128)S(1)} %bitcast.38, ...), custom_call_target="tpu_custom_call" | custom-call | tf_op jit(solution)/shard_map/backward_own/pallas_call | solution.py:54
  59.1 1.9 %row_grad.1 = (f32[2,256,512]{2,1,0:T(8,128)S(1)}, f32[2,256,512]{2,1,0:T(8,128)S(1)}) custom-call(s32[23]{0:T(128)S(1)} %stack.83.idx_ref, bf16[256,1024]{1,0:T(8,128)(2,1)S(1)} %get-tuple-element.133.a_ref.refs_4_, bf16[2048,1024]{1,0:T(8,128)(2,1)S(1)} %copy-done.1), custom_call_target="tpu_custom_call" | custom-call | tf_op jit(solution)/shard_map/row_grad/pallas_call | solution.py:54
  61.0 5.4 %collective-permute-done.11.refs_1_.refs_0_ = f32[64,1024]{1,0:T(8,128)S(1)} collective-permute-done((f32[64,1024]{1,0:T(8,128)S(1)}, f32[64,1024]{1,0:T(8,128)S(1)}, u32[]{:S(2)}, u32[]{:S(2)}) %collective-permute-start.11) | collective-permute-done | bytes 262176 | tf_op jit(solution)/shard_map/ppermute | solution.py:20
  66.6 1.5 %collective-permute-start.14 = (f32[128,1024]{1,0:T(8,128)S(1)}, f32[128,1024]{1,0:T(8,128)S(1)}, u32[]{:S(2)}, u32[]{:S(2)}) collective-permute-start(f32[128,1024]{1,0:T(8,128)S(1)} %pack_mixed.3), channel_id=1, source_target_pairs={{0,4},{4,0},{8,12},{12,8},{16,20},{20,16},{24,28},{28,24},{1,5},{5... | collective-permute-start | bytes 1572872 | tf_op jit(solution)/shard_map/ppermute | solution.py:20
  68.9 1.4 collect_x.1
  70.2 5.6 %forward_group.1 = (f32[8,1024]{1,0:T(8,128)S(1)}, bf16[256,1024]{1,0:T(8,128)(2,1)S(1)}, f32[8,1024]{1,0:T(8,128)S(1)}, bf16[256,1024]{1,0:T(8,128)(2,1)S(1)}, ...) custom-call(s32[23]{0:T(128)S(1)} %stack.83.idx_ref, bf16[256,2048]{1,0:T(8,128)(2,1)S(1)} %get-tuple-element.147.refs_0_.refs_1_, ...), custom_call_target="tpu_custom_call" | custom-call | tf_op jit(solution)/shard_map/forward_group/pallas_call | solution.py:54
  75.9 5.1 %collective-permute-done.14.refs_1_ = f32[128,1024]{1,0:T(8,128)S(1)} collective-permute-done((f32[128,1024]{1,0:T(8,128)S(1)}, f32[128,1024]{1,0:T(8,128)S(1)}, u32[]{:S(2)}, u32[]{:S(2)}) %collective-permute-start.14) | collective-permute-done | bytes 524320 | tf_op jit(solution)/shard_map/ppermute | solution.py:20
  83.8 1.5 %collective-permute-start.20 = (f32[128,1024]{1,0:T(8,128)S(1)}, f32[128,1024]{1,0:T(8,128)S(1)}, u32[]{:S(2)}, u32[]{:S(2)}) collective-permute-start(f32[128,1024]{1,0:T(8,128)S(1)} %get-tuple-element.166), channel_id=1, source_target_pairs={{0,4},{4,0},{8,12},{12,8},{16,20},{20,16},{24,28},{28,24},{1,5},{5... | collective-permute-start | bytes 1572872 | tf_op jit(solution)/shard_map/ppermute | solution.py:20
  85.3 2.0 %collective-permute-done.16.refs_2_ = f32[128,1024]{1,0:T(8,128)S(1)} collective-permute-done((f32[128,1024]{1,0:T(8,128)S(1)}, f32[128,1024]{1,0:T(8,128)S(1)}, u32[]{:S(2)}, u32[]{:S(2)}) %collective-permute-start.16) | collective-permute-done | bytes 524320 | tf_op jit(solution)/shard_map/ppermute | solution.py:20
  88.3 1.3 out_grad.2
  90.1 7.4 %collective-permute-done.21.refs_2_ = f32[128,1024]{1,0:T(8,128)S(1)} collective-permute-done((f32[128,1024]{1,0:T(8,128)S(1)}, f32[128,1024]{1,0:T(8,128)S(1)}, u32[]{:S(2)}, u32[]{:S(2)}) %collective-permute-start.21) | collective-permute-done | bytes 524320 | tf_op jit(solution)/shard_map/ppermute | solution.py:20
  98.3 1.4 collective-permute-done.24.refs_5_
  102.2 6.6 %backward_group.1 = (bf16[256,1024]{1,0:T(8,128)(2,1)S(1)}, f32[1,1024]{1,0:T(1,128)S(1)}, bf16[256,1024]{1,0:T(8,128)(2,1)S(1)}, f32[1,1024]{1,0:T(1,128)S(1)},...) custom-call(s32[23]{0:T(128)S(1)} %stack.83.idx_ref, bf16[256,1024]{1,0:T(8,128)(2,1)S(1)} %get-tuple-element.155.refs_1_.refs_0_, ...), custom_call_target="tpu_custom_call" | custom-call | tf_op jit(solution)/shard_map/backward_group/pallas_call | solution.py:54
  110.8 4.9 %collective-permute-done.19 = f32[256,1024]{1,0:T(8,128)S(1)} collective-permute-done((f32[256,1024]{1,0:T(8,128)S(1)}, f32[256,1024]{1,0:T(8,128)S(1)}, u32[]{:S(2)}, u32[]{:S(2)}) %collective-permute-start.19) | collective-permute-done | bytes 1048608 | tf_op jit(solution)/shard_map/ppermute | solution.py:20
  120.0 8.0 %collective-permute-done.26 = f32[256,512]{1,0:T(8,128)S(1)} collective-permute-done((f32[256,512]{1,0:T(8,128)S(1)}, f32[256,512]{1,0:T(8,128)S(1)}, u32[]{:S(2)}, u32[]{:S(2)}) %collective-permute-start.26) | collective-permute-done | bytes 524320 | tf_op jit(solution)/shard_map/ppermute | solution.py:20
  128.8 9.3 %collective-permute-done.25 = f32[264,1024]{1,0:T(8,128)S(1)} collective-permute-done((f32[264,1024]{1,0:T(8,128)S(1)}, f32[264,1024]{1,0:T(8,128)S(1)}, u32[]{:S(2)}, u32[]{:S(2)}) %collective-permute-start.25) | collective-permute-done | bytes 1081376 | tf_op jit(solution)/shard_map/ppermute | solution.py:20
  (71 shorter events, 23.3 us)
Async XLA Ops:
  0.7 9.2 %copy-start.6 = (f32[1024]{0:T(1024)S(1)}, f32[1024]{0:T(1024)}, u32[]{:S(2)}) copy-start(f32[1024]{0:T(1024)} %param.12) | copy-start | bytes 12292
  0.7 9.2 %copy-start.7 = (f32[1024]{0:T(1024)S(1)}, f32[1024]{0:T(1024)}, u32[]{:S(2)}) copy-start(f32[1024]{0:T(1024)} %param.11) | copy-start | bytes 12292
  0.7 9.2 %copy-start.8 = (f32[256]{0:T(256)S(1)}, f32[256]{0:T(256)}, u32[]{:S(2)}) copy-start(f32[256]{0:T(256)} %param.13) | copy-start | bytes 3076
  2.0 6.7 %copy-start.5 = (bf16[256,2048]{1,0:T(8,128)(2,1)S(1)}, bf16[256,2048]{1,0:T(8,128)(2,1)}, u32[]{:S(2)}) copy-start(bf16[256,2048]{1,0:T(8,128)(2,1)} %x_ref.1) | copy-start | bytes 3145732
  3.1 29.8 %collective-permute-start = (f32[128,2048]{1,0:T(8,128)S(1)}, f32[128,2048]{1,0:T(8,128)S(1)}, u32[]{:S(2)}, u32[]{:S(2)}) collective-permute-start(f32[128,2048]{1,0:T(8,128)S(1)} %get-tuple-element.107), channel_id=1, source_target_pairs={{0,4},{4,0},{8,12},{12,8},{16,20},{20,16},{24,28},{28,24},{1,5},{5... | collective-permute-start | bytes 3145736 | tf_op jit(solution)/shard_map/ppermute | solution.py:20
  6.1 26.8 %collective-permute-start.1 = (f32[64,2048]{1,0:T(8,128)S(1)}, f32[64,2048]{1,0:T(8,128)S(1)}, u32[]{:S(2)}, u32[]{:S(2)}) collective-permute-start(f32[64,2048]{1,0:T(8,128)S(1)} %get-tuple-element.109), channel_id=1, source_target_pairs={{0,16},{4,20},{8,24},{12,28},{16,0},{20,4},{24,8},{28,12},{1,17},{... | collective-permute-start | bytes 1572872 | tf_op jit(solution)/shard_map/ppermute | solution.py:20
  17.2 4.5 %collective-permute-start.2 = (f32[1,4,1024]{2,1,0:T(4,128)S(1)}, f32[1,4,1024]{2,1,0:T(4,128)S(1)}, u32[]{:S(2)}, u32[]{:S(2)}) collective-permute-start(f32[1,4,1024]{2,1,0:T(4,128)S(1)} %summary.1), channel_id=1, source_target_pairs={{0,8},{4,12},{8,0},{12,4},{16,24},{20,28},{24,16},{28,20},{1,9},{5... | collective-permute-start | bytes 49160 | tf_op jit(solution)/shard_map/ppermute | solution.py:20
  18.9 14.0 %collective-permute-start.3 = (f32[1,4,1024]{2,1,0:T(4,128)S(1)}, f32[1,4,1024]{2,1,0:T(4,128)S(1)}, u32[]{:S(2)}, u32[]{:S(2)}) collective-permute-start(f32[1,4,1024]{2,1,0:T(4,128)S(1)} %summary.1), channel_id=1, source_target_pairs={{0,16},{4,20},{8,24},{12,28},{16,0},{20,4},{24,8},{28,12},{1,17},{... | collective-permute-start | bytes 49160 | tf_op jit(solution)/shard_map/ppermute | solution.py:20
  19.2 13.7 %collective-permute-start.4 = (f32[1,4,1024]{2,1,0:T(4,128)S(1)}, f32[1,4,1024]{2,1,0:T(4,128)S(1)}, u32[]{:S(2)}, u32[]{:S(2)}) collective-permute-start(f32[1,4,1024]{2,1,0:T(4,128)S(1)} %summary.1), channel_id=1, source_target_pairs={{0,24},{4,28},{8,16},{12,20},{16,8},{20,12},{24,0},{28,4},{1,25},{... | collective-permute-start | bytes 49160 | tf_op jit(solution)/shard_map/ppermute | solution.py:20
  32.9 16.4 %collective-permute-start.5 = (f32[64,2048]{1,0:T(8,128)S(1)}, f32[64,2048]{1,0:T(8,128)S(1)}, u32[]{:S(2)}, u32[]{:S(2)}) collective-permute-start(f32[64,2048]{1,0:T(8,128)S(1)} %collective-permute-done.1.refs_1_), channel_id=1, source_target_pairs={{0,4},{4,0},{8,12},{12,8},{16,20},{20,16},{24,28},{28,24},{1,5},{5... | collective-permute-start | bytes 1572872 | tf_op jit(solution)/shard_map/ppermute | solution.py:20
  33.5 15.9 %collective-permute-start.6 = (f32[64,2048]{1,0:T(8,128)S(1)}, f32[64,2048]{1,0:T(8,128)S(1)}, u32[]{:S(2)}, u32[]{:S(2)}) collective-permute-start(f32[64,2048]{1,0:T(8,128)S(1)} %collective-permute-done.1.refs_1_), channel_id=1, source_target_pairs={{0,2},{1,3},{2,0},{3,1},{4,6},{5,7},{6,4},{7,5},{8,10},{9,11},{10,... | collective-permute-start | bytes 1572872 | tf_op jit(solution)/shard_map/ppermute | solution.py:20
  35.0 14.3 %collective-permute-start.7 = (f32[64,1024]{1,0:T(8,128)S(1)}, f32[64,1024]{1,0:T(8,128)S(1)}, u32[]{:S(2)}, u32[]{:S(2)}) collective-permute-start(f32[64,1024]{1,0:T(8,128)S(1)} %get-tuple-element.116), channel_id=1, source_target_pairs={{0,16},{4,20},{8,24},{12,28},{16,0},{20,4},{24,8},{28,12},{1,17},{... | collective-permute-start | bytes 786440 | tf_op jit(solution)/shard_map/ppermute | solution.py:20
  37.8 9.2 %collective-permute-start.8 = (f32[4,4,1024]{2,1,0:T(4,128)S(1)}, f32[4,4,1024]{2,1,0:T(4,128)S(1)}, u32[]{:S(2)}, u32[]{:S(2)}) collective-permute-start(f32[4,4,1024]{2,1,0:T(4,128)S(1)} %pad_maximum_fusion.1), channel_id=1, source_target_pairs={{0,4},{4,0},{8,12},{12,8},{16,20},{20,16},{24,28},{28,24},{1,5},{5... | collective-permute-start | bytes 196616 | tf_op jit(solution)/shard_map/ppermute | solution.py:20
  49.3 5.0 %copy-start.1 = (bf16[2048,1024]{1,0:T(8,128)(2,1)S(1)}, bf16[2048,1024]{1,0:T(8,128)(2,1)}, u32[]{:S(2)}) copy-start(bf16[2048,1024]{1,0:T(8,128)(2,1)} %refs_3_.1) | copy-start | bytes 12582916
  49.6 16.9 %collective-permute-start.12 = (f32[320,2048]{1,0:T(8,128)S(1)}, f32[320,2048]{1,0:T(8,128)S(1)}, u32[]{:S(2)}, u32[]{:S(2)}) collective-permute-start(f32[320,2048]{1,0:T(8,128)S(1)} %pack_x.1), channel_id=1, source_target_pairs={{0,1},{1,0},{2,3},{3,2},{4,5},{5,4},{6,7},{7,6},{8,9},{9,8},{10,11... | collective-permute-start | bytes 7864328 | tf_op jit(solution)/shard_map/ppermute | solution.py:20
  49.7 16.7 %collective-permute-start.10 = (f32[128,1024]{1,0:T(8,128)S(1)}, f32[128,1024]{1,0:T(8,128)S(1)}, u32[]{:S(2)}, u32[]{:S(2)}) collective-permute-start(f32[128,1024]{1,0:T(8,128)S(1)} %pack_mixed.2), channel_id=1, source_target_pairs={{0,4},{4,0},{8,12},{12,8},{16,20},{20,16},{24,28},{28,24},{1,5},{5... | collective-permute-start | bytes 1572872 | tf_op jit(solution)/shard_map/ppermute | solution.py:20
  51.3 15.2 %collective-permute-start.9 = (f32[64,2048]{1,0:T(8,128)S(1)}, f32[64,2048]{1,0:T(8,128)S(1)}, u32[]{:S(2)}, u32[]{:S(2)}) collective-permute-start(f32[64,2048]{1,0:T(8,128)S(1)} %collective-permute-done.5.refs_3_), channel_id=1, source_target_pairs={{0,2},{1,3},{2,0},{3,1},{4,6},{5,7},{6,4},{7,5},{8,10},{9,11},{10,... | collective-permute-start | bytes 1572872 | tf_op jit(solution)/shard_map/ppermute | solution.py:20
  51.8 14.7 %collective-permute-start.11 = (f32[64,1024]{1,0:T(8,128)S(1)}, f32[64,1024]{1,0:T(8,128)S(1)}, u32[]{:S(2)}, u32[]{:S(2)}) collective-permute-start(f32[64,1024]{1,0:T(8,128)S(1)} %get-tuple-element.127), channel_id=1, source_target_pairs={{0,16},{4,20},{8,24},{12,28},{16,0},{20,4},{24,8},{28,12},{1,17},{... | collective-permute-start | bytes 786440 | tf_op jit(solution)/shard_map/ppermute | solution.py:20
  66.5 2.4 %collective-permute-start.15 = (f32[64,2048]{1,0:T(8,128)S(1)}, f32[64,2048]{1,0:T(8,128)S(1)}, u32[]{:S(2)}, u32[]{:S(2)}) collective-permute-start(f32[64,2048]{1,0:T(8,128)S(1)} %collective-permute-done.9.refs_4_), channel_id=1, source_target_pairs={{0,1},{1,0},{2,3},{3,2},{4,5},{5,4},{6,7},{7,6},{8,9},{9,8},{10,11... | collective-permute-start | bytes 1572872 | tf_op jit(solution)/shard_map/ppermute | solution.py:20
  66.6 14.4 %collective-permute-start.14 = (f32[128,1024]{1,0:T(8,128)S(1)}, f32[128,1024]{1,0:T(8,128)S(1)}, u32[]{:S(2)}, u32[]{:S(2)}) collective-permute-start(f32[128,1024]{1,0:T(8,128)S(1)} %pack_mixed.3), channel_id=1, source_target_pairs={{0,4},{4,0},{8,12},{12,8},{16,20},{20,16},{24,28},{28,24},{1,5},{5... | collective-permute-start | bytes 1572872 | tf_op jit(solution)/shard_map/ppermute | solution.py:20
  68.2 14.1 %collective-permute-start.13 = (f32[128,1024]{1,0:T(8,128)S(1)}, f32[128,1024]{1,0:T(8,128)S(1)}, u32[]{:S(2)}, u32[]{:S(2)}) collective-permute-start(f32[128,1024]{1,0:T(8,128)S(1)} %pack_far.2.refs_0_), channel_id=1, source_target_pairs={{0,2},{1,3},{2,0},{3,1},{4,6},{5,7},{6,4},{7,5},{8,10},{9,11},{10,... | collective-permute-start | bytes 1572872 | tf_op jit(solution)/shard_map/ppermute | solution.py:20
  82.4 5.0 %collective-permute-start.17 = (f32[256,1024]{1,0:T(8,128)S(1)}, f32[256,1024]{1,0:T(8,128)S(1)}, u32[]{:S(2)}, u32[]{:S(2)}) collective-permute-start(f32[256,1024]{1,0:T(8,128)S(1)} %pack_rest.1.refs_1_), channel_id=1, source_target_pairs={{0,1},{1,0},{2,3},{3,2},{4,5},{5,4},{6,7},{7,6},{8,9},{9,8},{10,11... | collective-permute-start | bytes 3145736 | tf_op jit(solution)/shard_map/ppermute | solution.py:20
  82.5 7.2 %collective-permute-start.18 = (f32[2,256,512]{2,1,0:T(8,128)S(1)}, f32[2,256,512]{2,1,0:T(8,128)S(1)}, u32[]{:S(2)}, u32[]{:S(2)}) collective-permute-start(f32[2,256,512]{2,1,0:T(8,128)S(1)} %get-tuple-element.162), channel_id=1, source_target_pairs={{0,1},{1,0},{2,3},{3,2},{4,5},{5,4},{6,7},{7,6},{8,9},{9,8},{10,11... | collective-permute-start | bytes 3145736 | tf_op jit(solution)/shard_map/ppermute | solution.py:20
  82.9 4.4 %collective-permute-start.16 = (f32[128,1024]{1,0:T(8,128)S(1)}, f32[128,1024]{1,0:T(8,128)S(1)}, u32[]{:S(2)}, u32[]{:S(2)}) collective-permute-start(f32[128,1024]{1,0:T(8,128)S(1)} %pack_far.2.refs_0_), channel_id=1, source_target_pairs={{0,1},{1,0},{2,3},{3,2},{4,5},{5,4},{6,7},{7,6},{8,9},{9,8},{10,11... | collective-permute-start | bytes 1572872 | tf_op jit(solution)/shard_map/ppermute | solution.py:20
  83.1 14.3 %collective-permute-start.21 = (f32[128,1024]{1,0:T(8,128)S(1)}, f32[128,1024]{1,0:T(8,128)S(1)}, u32[]{:S(2)}, u32[]{:S(2)}) collective-permute-start(f32[128,1024]{1,0:T(8,128)S(1)} %pack_far.3.refs_1_), channel_id=1, source_target_pairs={{0,2},{1,3},{2,0},{3,1},{4,6},{5,7},{6,4},{7,5},{8,10},{9,11},{10,... | collective-permute-start | bytes 1572872 | tf_op jit(solution)/shard_map/ppermute | solution.py:20
  83.8 14.0 %collective-permute-start.20 = (f32[128,1024]{1,0:T(8,128)S(1)}, f32[128,1024]{1,0:T(8,128)S(1)}, u32[]{:S(2)}, u32[]{:S(2)}) collective-permute-start(f32[128,1024]{1,0:T(8,128)S(1)} %get-tuple-element.166), channel_id=1, source_target_pairs={{0,4},{4,0},{8,12},{12,8},{16,20},{20,16},{24,28},{28,24},{1,5},{5... | collective-permute-start | bytes 1572872 | tf_op jit(solution)/shard_map/ppermute | solution.py:20
  89.6 26.1 %collective-permute-start.19 = (f32[256,1024]{1,0:T(8,128)S(1)}, f32[256,1024]{1,0:T(8,128)S(1)}, u32[]{:S(2)}, u32[]{:S(2)}) collective-permute-start(f32[256,1024]{1,0:T(8,128)S(1)} %out_grad.2), channel_id=1, source_target_pairs={{0,8},{4,12},{8,0},{12,4},{16,24},{20,28},{24,16},{28,20},{1,9},{5... | collective-permute-start | bytes 3145736 | tf_op jit(solution)/shard_map/ppermute | solution.py:20
  97.8 1.9 %collective-permute-start.24 = (f32[128,1024]{1,0:T(8,128)S(1)}, f32[128,1024]{1,0:T(8,128)S(1)}, u32[]{:S(2)}, u32[]{:S(2)}) collective-permute-start(f32[128,1024]{1,0:T(8,128)S(1)} %collective-permute-done.21.refs_2_), channel_id=1, source_target_pairs={{0,1},{1,0},{2,3},{3,2},{4,5},{5,4},{6,7},{7,6},{8,9},{9,8},{10,11... | collective-permute-start | bytes 1572872 | tf_op jit(solution)/shard_map/ppermute | solution.py:20
  97.8 2.7 %collective-permute-start.23 = (f32[128,1024]{1,0:T(8,128)S(1)}, f32[128,1024]{1,0:T(8,128)S(1)}, u32[]{:S(2)}, u32[]{:S(2)}) collective-permute-start(f32[128,1024]{1,0:T(8,128)S(1)} %pack_far.3.refs_1_), channel_id=1, source_target_pairs={{0,1},{1,0},{2,3},{3,2},{4,5},{5,4},{6,7},{7,6},{8,9},{9,8},{10,11... | collective-permute-start | bytes 1572872 | tf_op jit(solution)/shard_map/ppermute | solution.py:20
  98.3 2.9 %collective-permute-start.22 = (f32[128,1024]{1,0:T(8,128)S(1)}, f32[128,1024]{1,0:T(8,128)S(1)}, u32[]{:S(2)}, u32[]{:S(2)}) collective-permute-start(f32[128,1024]{1,0:T(8,128)S(1)} %collective-permute-done.20.refs_0_), channel_id=1, source_target_pairs={{0,1},{1,0},{2,3},{3,2},{4,5},{5,4},{6,7},{7,6},{8,9},{9,8},{10,11... | collective-permute-start | bytes 1572872 | tf_op jit(solution)/shard_map/ppermute | solution.py:20
  110.1 28.0 %collective-permute-start.25 = (f32[264,1024]{1,0:T(8,128)S(1)}, f32[264,1024]{1,0:T(8,128)S(1)}, u32[]{:S(2)}, u32[]{:S(2)}) collective-permute-start(f32[264,1024]{1,0:T(8,128)S(1)} %in_grad.2), channel_id=1, source_target_pairs={{0,8},{4,12},{8,0},{12,4},{16,24},{20,28},{24,16},{28,20},{1,9},{5... | collective-permute-start | bytes 3244040 | tf_op jit(solution)/shard_map/ppermute | solution.py:20
  115.7 12.3 %collective-permute-start.26 = (f32[256,512]{1,0:T(8,128)S(1)}, f32[256,512]{1,0:T(8,128)S(1)}, u32[]{:S(2)}, u32[]{:S(2)}) collective-permute-start(f32[256,512]{1,0:T(8,128)S(1)} %slice_bitcast_fusion), channel_id=1, source_target_pairs={{0,2},{1,3},{2,0},{3,1},{4,6},{5,7},{6,4},{7,5},{8,10},{9,11},{10,... | collective-permute-start | bytes 1572872 | tf_op jit(solution)/shard_map/ppermute | solution.py:20
  (4 other events, 7.9 us)
